TPU v7x, 32 devices: a whole 2x2x4 slice. The times are simulated.
32 devices in a mesh: wide: 8 (over z, x), narrow: 4 (over y, core).
Axes of the slice: x: 2, y: 2, z: 4, core: 2. Of those that a mesh axis runs over, the one named last changes fastest.
Arguments:
- block_in: bfloat16 [160, 200, 768], P(('wide', 'narrow')), may hold values from -6 to 6
- out_grad: bfloat16 [160, 200, 768], P(('wide', 'narrow')), may hold values from -6 to 6
- mim_mask: int32 [160, 200], P(('wide', 'narrow')), may hold values from 0 to 1, as said below
- rel_index: int32 [200, 200], replicated, may hold values from 0 to 731
- qkv_weight: bfloat16 [768, 2304], replicated, may hold values from -0.21875 to 0.21875
- proj_weight: bfloat16 [768, 768], replicated, may hold values from -0.875 to 0.875
- up_weight: bfloat16 [768, 3072], P(None, 'narrow'), may hold values from -0.21875 to 0.21875
- down_weight: bfloat16 [768, 3072], P(None, 'narrow'), may hold values from -0.109375 to 0.109375
- vectors: float32 [10, 768], replicated
- up_bias: float32 [3072], replicated, may hold values from -1.5 to 1.5
- rel_table: float32 [732, 12], replicated, may hold values from -4 to 4
- qkv_master: float32 [768, 2304], P('wide', 'narrow'), may hold values from -0.21875 to 0.21875
- qkv_mean: float32 [768, 2304], P('wide', 'narrow'), may hold values from -0.00061035156 to 0.00061035156
- qkv_square: float32 [768, 2304], P('wide', 'narrow'), may hold values from 7.064254e-11 to 1.1302806e-09
- proj_master: float32 [768, 768], P('wide', 'narrow'), may hold values from -0.875 to 0.875
- proj_mean: float32 [768, 768], P('wide', 'narrow'), may hold values from -0.00061035156 to 0.00061035156
- proj_square: float32 [768, 768], P('wide', 'narrow'), may hold values from 7.064254e-11 to 1.1302806e-09
- up_master: float32 [768, 3072], P('wide', 'narrow'), may hold values from -0.21875 to 0.21875
- up_mean: float32 [768, 3072], P('wide', 'narrow'), may hold values from -0.00061035156 to 0.00061035156
- up_square: float32 [768, 3072], P('wide', 'narrow'), may hold values from 7.064254e-11 to 1.1302806e-09
- down_master: float32 [768, 3072], P('wide', 'narrow'), may hold values from -0.109375 to 0.109375
- down_mean: float32 [768, 3072], P('wide', 'narrow'), may hold values from -0.00061035156 to 0.00061035156
- down_square: float32 [768, 3072], P('wide', 'narrow'), may hold values from 7.064254e-11 to 1.1302806e-09
- vector_mean: float32 [10, 768], replicated, may hold values from -0.001953125 to 0.001953125
- vector_square: float32 [10, 768], replicated, may hold values from 6.3578287e-10 to 1.0172526e-08
- bias_mean: float32 [3072], replicated, may hold values from -0.001953125 to 0.001953125
- bias_square: float32 [3072], replicated, may hold values from 4.2385526e-11 to 1.695421e-10
- table_mean: float32 [732, 12], replicated, may hold values from -0.001953125 to 0.001953125
- table_square: float32 [732, 12], replicated, may hold values from 4.2385526e-11 to 1.695421e-10
Outputs:
- block_out: bfloat16 [160, 200, 768], P(('wide', 'narrow'))
- input_grad: float32 [160, 200, 768], P(('wide', 'narrow'))
- grad_norm: float32 [], replicated
- qkv_mean_new: float32 [768, 2304], P('wide', 'narrow')
- qkv_square_new: float32 [768, 2304], P('wide', 'narrow')
- qkv_new: float32 [768, 2304], P('wide', 'narrow')
- qkv_copy: bfloat16 [768, 2304], P('wide', 'narrow')
- proj_mean_new: float32 [768, 768], P('wide', 'narrow')
- proj_square_new: float32 [768, 768], P('wide', 'narrow')
- proj_new: float32 [768, 768], P('wide', 'narrow')
- proj_copy: bfloat16 [768, 768], P('wide', 'narrow')
- up_mean_new: float32 [768, 3072], P('wide', 'narrow')
- up_square_new: float32 [768, 3072], P('wide', 'narrow')
- up_new: float32 [768, 3072], P('wide', 'narrow')
- up_copy: bfloat16 [768, 3072], P('wide', 'narrow')
- down_mean_new: float32 [768, 3072], P('wide', 'narrow')
- down_square_new: float32 [768, 3072], P('wide', 'narrow')
- down_new: float32 [768, 3072], P('wide', 'narrow')
- down_copy: bfloat16 [768, 3072], P('wide', 'narrow')
- vector_mean_new: float32 [10, 768], replicated
- vector_square_new: float32 [10, 768], replicated
- vectors_new: float32 [10, 768], replicated
- bias_mean_new: float32 [3072], replicated
- bias_square_new: float32 [3072], replicated
- up_bias_new: float32 [3072], replicated
- table_mean_new: float32 [732, 12], replicated
- table_square_new: float32 [732, 12], replicated
- table_new: float32 [732, 12], replicated
Inputs may be any that keep to these rules, and one draw needn't show every extreme that they name: `mim_mask`: each image masks its own share of patches, from almost none to about three quarters, very unequal between images; position 0 and positions from 197 on are never masked.
All inputs are finite; a program needn't handle non-finite values.
Results may differ from a plain program's by a relative error of at most 0.012.
Values may be sent and summed in bfloat16 or wider, within the bound.
No kernel may reach another device: no remote copies, remote signals or barrier semaphores. Data moves between devices by JAX's collectives and lax.ppermute only.
A program may use at most 192 MiB of HBM per device.

v0:
```python
import jax
import jax.numpy as jnp
from jax import lax
from jax.sharding import PartitionSpec as P

VALID = 197
STEP = 10


norm_eps = 1e-06
clip_eps = 1e-06
max_norm = 1.0
beta_one = 0.9
beta_two = 0.999
adam_eps = 1e-08
rate_matrix = 0.05
rate_small = 0.4
weight_decay = 0.05
exact_prec = lax.Precision.HIGHEST
contract_rows = (((0,), (0,)), ((), ()))
contract_cols = (((1,), (1,)), ((), ()))


def split_up(shard, dim, peers):
    shape = shard.shape
    parts = shard.reshape(*shape[:dim], peers, shape[dim] // peers, *shape[dim + 1 :])
    return jnp.moveaxis(parts, dim, 0)


def sent_and_summed(shard, axis, dim):
    parts = split_up(shard, dim, lax.axis_size(axis))
    arrived = lax.all_to_all(parts, axis, split_axis=0, concat_axis=0, tiled=True)
    return arrived.astype(jnp.float32).sum(axis=0)


def in_one_piece(arrays, axis, dim, along):
    ends, at = ([], 0)
    for a in arrays[:-1]:
        at += a.shape[along]
        ends.append(at)
    both = jnp.concatenate(arrays, axis=along)
    return tuple(jnp.split(sent_and_summed(both, axis, dim), ends, axis=along))


def layer_stats(values, gain_vec, shift_vec):
    center = values - jnp.mean(values, -1, keepdims=True)
    factor = lax.rsqrt(jnp.mean(center * center, -1, keepdims=True) + norm_eps)
    normed = center * factor
    return (normed * gain_vec + shift_vec, normed, factor)


def layer_back(grad, normed, factor, gain_vec):
    scaled = grad * gain_vec
    return factor * (
        scaled
        - jnp.mean(scaled, -1, keepdims=True)
        - normed * jnp.mean(scaled * normed, -1, keepdims=True)
    )


def gelu_exact(values):
    return 0.5 * values * (1.0 + jax.scipy.special.erf(values * 0.7071067811865476))


def gelu_slope(values):
    return (
        0.5 * (1.0 + jax.scipy.special.erf(values * 0.7071067811865476))
        + values * jnp.exp(-0.5 * values * values) * 0.3989422804014327
    )


def rel_bias(rel_index, rel_table):
    seq_len = rel_index.shape[0]
    table_rows, heads = rel_table.shape
    blocks = rel_index.reshape(8, seq_len // 8, seq_len)

    def one_block(index_rows):
        onehot = (
            index_rows[:, :, None] == jnp.arange(table_rows, dtype=jnp.int32)[None, None, :]
        ).astype(jnp.float32)
        return jnp.einsum("qkr,rh->hqk", onehot, rel_table, precision=exact_prec)

    pieces = lax.map(one_block, blocks)
    return jnp.transpose(pieces, (1, 0, 2, 3)).reshape(heads, seq_len, seq_len)


def table_grad(rel_index, grad_rel, table_rows):
    heads, seq_len = (grad_rel.shape[0], grad_rel.shape[1])
    index_blocks = rel_index.reshape(8, seq_len // 8, seq_len)
    grad_blocks = jnp.moveaxis(grad_rel.reshape(heads, 8, seq_len // 8, seq_len), 1, 0)

    def add_block(total, paired):
        index_rows, grad_rows = paired
        onehot = (
            index_rows[:, :, None] == jnp.arange(table_rows, dtype=jnp.int32)[None, None, :]
        ).astype(jnp.float32)
        return (total + jnp.einsum("qkr,hqk->rh", onehot, grad_rows, precision=exact_prec), None)

    total, unused = lax.scan(
        add_block, jnp.zeros((table_rows, heads), jnp.float32), (index_blocks, grad_blocks)
    )
    return total


def adam_update(master, mean, square, grad, rate, decay):
    mean_new = beta_one * mean + (1.0 - beta_one) * grad
    square_new = beta_two * square + (1.0 - beta_two) * grad * grad
    fix_one = 1.0 - beta_one**STEP
    fix_two = 1.0 - beta_two**STEP
    direction = mean_new / fix_one / (jnp.sqrt(square_new / fix_two) + adam_eps)
    return (mean_new, square_new, master - rate * (direction + decay * master))


def shards(
    block_in,
    out_grad,
    mim_mask,
    rel_index,
    qkv_weight,
    proj_weight,
    up_weight,
    down_weight,
    vectors,
    up_bias,
    rel_table,
    qkv_master,
    qkv_mean,
    qkv_square,
    proj_master,
    proj_mean,
    proj_square,
    up_master,
    up_mean,
    up_square,
    down_master,
    down_mean,
    down_square,
    vector_mean,
    vector_square,
    bias_mean,
    bias_square,
    table_mean,
    table_square,
):
    images, seq_len, width = block_in.shape
    table_rows, heads = rel_table.shape
    head_dim = width // heads
    token_rows = images * seq_len
    factor_scale = head_dim ** (-0.5)
    local_ff = up_weight.shape[1]
    offset = lax.axis_index("narrow") * local_ff
    inputs = block_in.reshape(token_rows, width).astype(jnp.float32)
    first_norm, hat_one, factor_one = layer_stats(inputs, vectors[4], vectors[5])
    first_b = first_norm.astype(jnp.bfloat16)
    qkv_bias = jnp.concatenate([vectors[0], jnp.zeros_like(vectors[0]), vectors[1]])
    qkv_b = (jnp.dot(first_b, qkv_weight, preferred_element_type=jnp.float32) + qkv_bias).astype(
        jnp.bfloat16
    )
    parts = qkv_b.reshape(images, seq_len, 3, heads, head_dim)
    query, keys, values = (parts[:, :, 0], parts[:, :, 1], parts[:, :, 2])
    bias_all = rel_bias(rel_index, rel_table)
    key_keep = (jnp.arange(seq_len) < VALID)[None, None, None, :]

    def score_block():
        raw = (
            jnp.einsum("bqhd,bkhd->bhqk", query, keys, preferred_element_type=jnp.float32)
            * factor_scale
            + bias_all[None]
        )
        return jnp.where(key_keep, raw, -1e30)

    scores = score_block()
    log_total = jax.nn.logsumexp(scores, -1, keepdims=True)
    probs_b = jnp.exp(scores - log_total).astype(jnp.bfloat16)
    mixed = jnp.einsum("bhqk,bkhd->bqhd", probs_b, values, preferred_element_type=jnp.float32)
    heads_b = mixed.reshape(token_rows, width).astype(jnp.bfloat16)
    attn = jnp.dot(heads_b, proj_weight, preferred_element_type=jnp.float32) + vectors[2]
    middle = inputs + vectors[8] * attn
    second_norm, hat_two, factor_two = layer_stats(middle, vectors[6], vectors[7])
    second_b = second_norm.astype(jnp.bfloat16)
    gathered = lax.all_gather(second_b, "narrow", axis=0, tiled=True)
    local_bias = lax.dynamic_slice_in_dim(up_bias, offset, local_ff)
    hidden_pre = jnp.dot(gathered, up_weight, preferred_element_type=jnp.float32) + local_bias
    active_b = gelu_exact(hidden_pre).astype(jnp.bfloat16)
    block_rows = active_b
    branch = lax.psum_scatter(
        lax.dot_general(
            block_rows, down_weight, contract_cols, preferred_element_type=jnp.float32
        ).astype(jnp.bfloat16),
        "narrow",
        scatter_dimension=0,
        tiled=True,
    ).astype(jnp.float32)
    mlp_out = branch + vectors[3]
    block_out = (middle + vectors[9] * mlp_out).astype(jnp.bfloat16).reshape(images, seq_len, width)
    cotangent = out_grad.reshape(token_rows, width).astype(jnp.float32) * mim_mask.reshape(
        token_rows, 1
    ).astype(jnp.float32)
    grad_scale_two = jnp.sum(cotangent * mlp_out, 0)
    down_in_b = (vectors[9] * cotangent).astype(jnp.bfloat16)
    grad_down_bias = jnp.sum(down_in_b, 0, dtype=jnp.float32)
    down_all = lax.all_gather(down_in_b, "narrow", axis=0, tiled=True)
    active_grad = jnp.dot(down_all, down_weight, preferred_element_type=jnp.float32)
    grad_down = lax.dot_general(
        down_all, active_b, contract_rows, preferred_element_type=jnp.float32
    )
    pre_grad_b = (active_grad * gelu_slope(hidden_pre)).astype(jnp.bfloat16)
    grad_up = lax.dot_general(
        gathered, pre_grad_b, contract_rows, preferred_element_type=jnp.float32
    )
    local_bias_grad = jnp.sum(pre_grad_b, 0, dtype=jnp.float32)
    grad_bias = lax.dynamic_update_slice_in_dim(
        jnp.zeros(up_bias.shape, jnp.float32), local_bias_grad, offset, 0
    )
    block_rows = pre_grad_b
    grad_second = lax.psum_scatter(
        lax.dot_general(block_rows, up_weight, contract_cols, preferred_element_type=jnp.float32),
        "narrow",
        scatter_dimension=0,
        tiled=True,
    )
    grad_gain_two = jnp.sum(grad_second * hat_two, 0)
    grad_shift_two = jnp.sum(grad_second, 0)
    grad_middle = cotangent + layer_back(grad_second, hat_two, factor_two, vectors[6])
    grad_scale_one = jnp.sum(grad_middle * attn, 0)
    proj_in_b = (vectors[8] * grad_middle).astype(jnp.bfloat16)
    grad_proj_bias = jnp.sum(proj_in_b, 0, dtype=jnp.float32)
    grad_proj = lax.dot_general(
        heads_b, proj_in_b, contract_rows, preferred_element_type=jnp.float32
    )
    heads_grad_b = lax.dot_general(
        proj_in_b, proj_weight, contract_cols, preferred_element_type=jnp.float32
    ).astype(jnp.bfloat16)
    out_heads = heads_grad_b.reshape(images, seq_len, heads, head_dim)
    probs = jnp.exp(score_block() - log_total)
    probs_b = probs.astype(jnp.bfloat16)
    grad_values = jnp.einsum(
        "bhqk,bqhd->bkhd", probs_b, out_heads, preferred_element_type=jnp.float32
    )
    grad_probs = jnp.einsum(
        "bqhd,bkhd->bhqk", out_heads, values, preferred_element_type=jnp.float32
    )
    row_total = jnp.sum(grad_probs * probs, -1, keepdims=True)
    grad_scores_b = (probs * (grad_probs - row_total)).astype(jnp.bfloat16)
    grad_query = (
        jnp.einsum("bhqk,bkhd->bqhd", grad_scores_b, keys, preferred_element_type=jnp.float32)
        * factor_scale
    )
    grad_keys = (
        jnp.einsum("bhqk,bqhd->bkhd", grad_scores_b, query, preferred_element_type=jnp.float32)
        * factor_scale
    )
    grad_rel = jnp.sum(grad_scores_b, 0, dtype=jnp.float32)
    grad_table = table_grad(rel_index, grad_rel, table_rows)
    grad_qkv_b = (
        jnp.stack([grad_query, grad_keys, grad_values], 2)
        .reshape(token_rows, 3 * width)
        .astype(jnp.bfloat16)
    )
    column_sums = jnp.sum(grad_qkv_b, 0, dtype=jnp.float32)
    grad_qkv = lax.dot_general(
        first_b, grad_qkv_b, contract_rows, preferred_element_type=jnp.float32
    )
    grad_first = lax.dot_general(
        grad_qkv_b, qkv_weight, contract_cols, preferred_element_type=jnp.float32
    )
    grad_gain_one = jnp.sum(grad_first * hat_one, 0)
    grad_shift_one = jnp.sum(grad_first, 0)
    input_grad = (grad_middle + layer_back(grad_first, hat_one, factor_one, vectors[4])).reshape(
        images, seq_len, width
    )
    grad_vectors = jnp.stack(
        [
            column_sums[:width],
            column_sums[2 * width :],
            grad_proj_bias,
            grad_down_bias,
            grad_gain_one,
            grad_shift_one,
            grad_gain_two,
            grad_shift_two,
            grad_scale_one,
            grad_scale_two,
        ]
    )
    grad_vectors, grad_bias, grad_table = lax.psum(
        (grad_vectors, grad_bias, grad_table), ("wide", "narrow")
    )
    qkv_part, proj_part = (
        lax.psum_scatter(
            grad_qkv.astype(jnp.bfloat16), "narrow", scatter_dimension=1, tiled=True
        ).astype(jnp.float32),
        lax.psum_scatter(
            grad_proj.astype(jnp.bfloat16), "narrow", scatter_dimension=1, tiled=True
        ).astype(jnp.float32),
    )
    up_part, down_part = (grad_up, grad_down)
    qkv_shard, proj_shard, up_shard, down_shard = in_one_piece(
        (
            qkv_part.astype(jnp.bfloat16),
            proj_part.astype(jnp.bfloat16),
            up_part.astype(jnp.bfloat16),
            down_part.astype(jnp.bfloat16),
        ),
        "wide",
        0,
        1,
    )
    shard_squares = (
        jnp.sum(qkv_shard * qkv_shard)
        + jnp.sum(proj_shard * proj_shard)
        + jnp.sum(up_shard * up_shard)
        + jnp.sum(down_shard * down_shard)
    )
    large_squares = lax.psum(shard_squares, ("wide", "narrow"))
    small_squares = (
        jnp.sum(grad_vectors * grad_vectors)
        + jnp.sum(grad_bias * grad_bias)
        + jnp.sum(grad_table * grad_table)
    )
    grad_norm = jnp.sqrt(large_squares + small_squares)
    clip = jnp.minimum(1.0, max_norm / (grad_norm + clip_eps))
    results = [block_out, input_grad, grad_norm]
    for master, mean, square, grad in (
        (qkv_master, qkv_mean, qkv_square, qkv_shard),
        (proj_master, proj_mean, proj_square, proj_shard),
        (up_master, up_mean, up_square, up_shard),
        (down_master, down_mean, down_square, down_shard),
    ):
        mean_new, square_new, master_new = adam_update(
            master, mean, square, clip * grad, rate_matrix, weight_decay
        )
        results += [mean_new, square_new, master_new, master_new.astype(jnp.bfloat16)]
    for master, mean, square, grad in (
        (vectors, vector_mean, vector_square, grad_vectors),
        (up_bias, bias_mean, bias_square, grad_bias),
        (rel_table, table_mean, table_square, grad_table),
    ):
        mean_new, square_new, master_new = adam_update(
            master, mean, square, clip * grad, rate_small, 0.0
        )
        results += [mean_new, square_new, master_new]
    return tuple(results)


def solution(mesh):
    in_specs = (
        P(("wide", "narrow"), None, None),
        P(("wide", "narrow"), None, None),
        P(("wide", "narrow"), None),
        P(),
        P(),
        P(),
        P(None, "narrow"),
        P(None, "narrow"),
        P(),
        P(),
        P(),
        P("wide", "narrow"),
        P("wide", "narrow"),
        P("wide", "narrow"),
        P("wide", "narrow"),
        P("wide", "narrow"),
        P("wide", "narrow"),
        P("wide", "narrow"),
        P("wide", "narrow"),
        P("wide", "narrow"),
        P("wide", "narrow"),
        P("wide", "narrow"),
        P("wide", "narrow"),
        P(),
        P(),
        P(),
        P(),
        P(),
        P(),
    )
    out_specs = (
        P(("wide", "narrow"), None, None),
        P(("wide", "narrow"), None, None),
        P(),
        P("wide", "narrow"),
        P("wide", "narrow"),
        P("wide", "narrow"),
        P("wide", "narrow"),
        P("wide", "narrow"),
        P("wide", "narrow"),
        P("wide", "narrow"),
        P("wide", "narrow"),
        P("wide", "narrow"),
        P("wide", "narrow"),
        P("wide", "narrow"),
        P("wide", "narrow"),
        P("wide", "narrow"),
        P("wide", "narrow"),
        P("wide", "narrow"),
        P("wide", "narrow"),
        P(),
        P(),
        P(),
        P(),
        P(),
        P(),
        P(),
        P(),
        P(),
    )
    return jax.shard_map(shards, mesh=mesh, in_specs=in_specs, out_specs=out_specs, check_vma=False)
```

profile of v0, /device:TPU:0, one launch (start us, length us, event | category | flops | bytes accessed | tf_op | source)
XLA Modules:
  0.0 806.3 jit_solution(16619423688516278176)
XLA Ops:
  17.9 79.3 %while.21 = (s32[]{:T(128)}, f32[8,12,25,200]{3,1,2,0:T(8,128)}, s32[8,25,200]{2,1,0:T(8,128)}, f32[732,12]{0,1:T(8,128)}, s32[]{:T(128)}) while((s32[]{:T(128)}, f32[8,12,25,200]{3,1,2,0:T(8,128)}, s32[8,25,200]{2,1,0:T(8,128)}, f32[732,12]{0,1:T(8,128)}, s32[]{:T(128)}) %tuple.94), condition=%wide.region_3.4_spmd, body=%wide.region_2.3_spmd.sunk | while | flops 530700000 | bytes 518829 | solution.py:83
  18.6 9.1 %fusion.86 = f32[8,12,25,200]{3,1,2,0:T(8,128)} fusion(f32[8,12,25,200]{3,1,2,0:T(8,128)} %get-tuple-element.246, s32[]{:T(128)S(6)} %copy.134, s32[25,200]{1,0:T(8,128)S(1)} %dynamic-slice_bitcast_fusion.4, f32[732,12]{0,1:T(8,128)} %get-tuple-element.253), kind=kOutput, calls=%fused_computation.4.clone.1 | convolution fusion | flops 530700000 | bytes 478756 | tf_op jit(solution)/shard_map/while/body/eval_jaxpr/qkr,rh->hqk/dot_general | solution.py:81
  28.5 9.1 %fusion.86 = f32[8,12,25,200]{3,1,2,0:T(8,128)} fusion(f32[8,12,25,200]{3,1,2,0:T(8,128)} %get-tuple-element.246, s32[]{:T(128)S(6)} %copy.134, s32[25,200]{1,0:T(8,128)S(1)} %dynamic-slice_bitcast_fusion.4, f32[732,12]{0,1:T(8,128)} %get-tuple-element.253), kind=kOutput, calls=%fused_computation.4.clone.1 | convolution fusion | flops 530700000 | bytes 478756 | tf_op jit(solution)/shard_map/while/body/eval_jaxpr/qkr,rh->hqk/dot_general | solution.py:81
  38.5 9.2 %fusion.86 = f32[8,12,25,200]{3,1,2,0:T(8,128)} fusion(f32[8,12,25,200]{3,1,2,0:T(8,128)} %get-tuple-element.246, s32[]{:T(128)S(6)} %copy.134, s32[25,200]{1,0:T(8,128)S(1)} %dynamic-slice_bitcast_fusion.4, f32[732,12]{0,1:T(8,128)} %get-tuple-element.253), kind=kOutput, calls=%fused_computation.4.clone.1 | convolution fusion | flops 530700000 | bytes 478756 | tf_op jit(solution)/shard_map/while/body/eval_jaxpr/qkr,rh->hqk/dot_general | solution.py:81
  48.4 9.1 %fusion.86 = f32[8,12,25,200]{3,1,2,0:T(8,128)} fusion(f32[8,12,25,200]{3,1,2,0:T(8,128)} %get-tuple-element.246, s32[]{:T(128)S(6)} %copy.134, s32[25,200]{1,0:T(8,128)S(1)} %dynamic-slice_bitcast_fusion.4, f32[732,12]{0,1:T(8,128)} %get-tuple-element.253), kind=kOutput, calls=%fused_computation.4.clone.1 | convolution fusion | flops 530700000 | bytes 478756 | tf_op jit(solution)/shard_map/while/body/eval_jaxpr/qkr,rh->hqk/dot_general | solution.py:81
  58.3 9.1 %fusion.86 = f32[8,12,25,200]{3,1,2,0:T(8,128)} fusion(f32[8,12,25,200]{3,1,2,0:T(8,128)} %get-tuple-element.246, s32[]{:T(128)S(6)} %copy.134, s32[25,200]{1,0:T(8,128)S(1)} %dynamic-slice_bitcast_fusion.4, f32[732,12]{0,1:T(8,128)} %get-tuple-element.253), kind=kOutput, calls=%fused_computation.4.clone.1 | convolution fusion | flops 530700000 | bytes 478756 | tf_op jit(solution)/shard_map/while/body/eval_jaxpr/qkr,rh->hqk/dot_general | solution.py:81
  68.2 9.2 %fusion.86 = f32[8,12,25,200]{3,1,2,0:T(8,128)} fusion(f32[8,12,25,200]{3,1,2,0:T(8,128)} %get-tuple-element.246, s32[]{:T(128)S(6)} %copy.134, s32[25,200]{1,0:T(8,128)S(1)} %dynamic-slice_bitcast_fusion.4, f32[732,12]{0,1:T(8,128)} %get-tuple-element.253), kind=kOutput, calls=%fused_computation.4.clone.1 | convolution fusion | flops 530700000 | bytes 478756 | tf_op jit(solution)/shard_map/while/body/eval_jaxpr/qkr,rh->hqk/dot_general | solution.py:81
  78.1 9.2 %fusion.86 = f32[8,12,25,200]{3,1,2,0:T(8,128)} fusion(f32[8,12,25,200]{3,1,2,0:T(8,128)} %get-tuple-element.246, s32[]{:T(128)S(6)} %copy.134, s32[25,200]{1,0:T(8,128)S(1)} %dynamic-slice_bitcast_fusion.4, f32[732,12]{0,1:T(8,128)} %get-tuple-element.253), kind=kOutput, calls=%fused_computation.4.clone.1 | convolution fusion | flops 530700000 | bytes 478756 | tf_op jit(solution)/shard_map/while/body/eval_jaxpr/qkr,rh->hqk/dot_general | solution.py:81
  88.0 9.2 %fusion.86 = f32[8,12,25,200]{3,1,2,0:T(8,128)} fusion(f32[8,12,25,200]{3,1,2,0:T(8,128)} %get-tuple-element.246, s32[]{:T(128)S(6)} %copy.134, s32[25,200]{1,0:T(8,128)S(1)} %dynamic-slice_bitcast_fusion.4, f32[732,12]{0,1:T(8,128)} %get-tuple-element.253), kind=kOutput, calls=%fused_computation.4.clone.1 | convolution fusion | flops 530700000 | bytes 478756 | tf_op jit(solution)/shard_map/while/body/eval_jaxpr/qkr,rh->hqk/dot_general | solution.py:81
  97.2 4.7 copy.102
  102.6 8.1 %add_convert_fusion = bf16[1000,2304]{1,0:T(8,128)(2,1)} fusion(bf16[768,2304]{1,0:T(8,128)(2,1)S(1)} %copy-done, f32[2304]{0:T(1024)S(1)} %pad_maximum_fusion.1, f32[768]{0:T(1024)} %get-tuple-element.109, f32[768]{0:T(1024)S(1)} %copy-done.26, f32[1000]{0:T(1024)} %rsqrt.21, f32[1000]{0:T(1024)S(1)} %copy-done.28, bf16[1000,768]{1,0:T(8,128)(2,1)} %bitcast.124), kind=kOutput, calls=%fused_computation.34 | convolution fusion | flops 3548160000 | bytes 9706304 | tf_op jit(solution)/shard_map/dot_general | solution.py:156
  110.7 14.9 %reshape.239 = bf16[5,200,3,12,64]{4,3,2,1,0:T(8,128)(2,1)} reshape(bf16[1000,2304]{1,0:T(8,128)(2,1)} %add_convert_fusion) | data formatting | bytes 9216000 | tf_op jit(solution)/shard_map/reshape | solution.py:159
  125.6 8.4 %fusion.50 = (bf16[5,200,1,12,64]{4,3,2,1,0:T(8,128)(2,1)}, bf16[5,200,1,12,64]{4,3,2,1,0:T(8,128)(2,1)}, bf16[5,200,1,12,64]{4,3,2,1,0:T(8,128)(2,1)}) fusion(bf16[5,200,3,12,64]{4,3,2,1,0:T(8,128)(2,1)} %reshape.239), kind=kLoop, calls=%fused_computation.151 | loop fusion | bytes 9216000 | tf_op jit(solution)/shard_map/slice | solution.py:160
  134.0 6.0 copy.125
  140.0 6.0 copy.124
  146.0 6.2 copy.126
  152.2 6.2 fusion.52
  158.5 2.9 exponential_reduce_fusion
  165.5 3.1 copy.104
  168.6 6.0 convert_element_type.161
  174.6 6.4 multiply_add_fusion.2
  190.7 2.9 multiply_convert_fusion.4
  195.1 41.3 %all-gather.3.cloned.1.call-done = bf16[4000,768]{1,0:T(8,128)(2,1)} async-done(((bf16[1000,768]{1,0:T(8,128)(2,1)}), bf16[4000,768]{1,0:T(8,128)(2,1)}) %all-gather.3.cloned.1.call-update) | async-done | bytes 6144016 | tf_op jit(solution)/shard_map/all_gather | solution.py:181
  236.4 12.7 %multiply_convert_fusion.1 = (bf16[4000,768]{1,0:T(8,128)(2,1)}, f32[4000,768]{1,0:T(8,128)}) fusion(f32[768]{0:T(1024)} %dynamic_slice.14, bf16[4000,768]{1,0:T(8,128)(2,1)} %all-gather.3.cloned.1.call-done, bf16[768,768]{1,0:T(8,128)(2,1)} %param.39), kind=kOutput, calls=%fused_computation.26 | convolution fusion | flops 4737024000 | bytes 25758720 | tf_op jit(solution)/shard_map/dot_general | solution.py:183
  249.0 34.4 %all-gather.5.cloned.1.call-done = bf16[4000,768]{1,0:T(8,128)(2,1)} async-done(((bf16[1000,768]{1,0:T(8,128)(2,1)}), bf16[4000,768]{1,0:T(8,128)(2,1)}) %all-gather.5.cloned.1.call-update) | async-done | bytes 6144016 | tf_op jit(solution)/shard_map/all_gather | solution.py:202
  283.5 12.4 %convert_reduce_fusion.1 = (f32[768]{0:T(1024)}, bf16[4000,768]{1,0:T(8,128)(2,1)S(1)}) fusion(f32[4000,768]{1,0:T(8,128)} %get-tuple-element.182, f32[768]{0:T(1024)} %dynamic_slice.14, bf16[4000,768]{1,0:T(8,128)(2,1)} %all-gather.5.cloned.1.call-done, bf16[768,768]{1,0:T(8,128)(2,1)} %param.40), kind=kOutput, calls=%fused_computation.23 | convolution fusion | flops 4758526976 | bytes 25761792 | tf_op jit(solution)/shard_map/dot_general | solution.py:203
  298.6 7.9 fusion.54
  306.8 12.6 %convolution_convert_fusion = bf16[4000,768]{1,0:T(8,128)(2,1)} fusion(bf16[4000,768]{1,0:T(8,128)(2,1)} %get-tuple-element.181, bf16[768,768]{1,0:T(8,128)(2,1)} %param.40), kind=kOutput, calls=%fused_computation.36 | convolution fusion | flops 4721664000 | bytes 13467648 | tf_op jit(solution)/shard_map/dot_general | solution.py:187
  319.4 3.8 add_convert_fusion.1
  323.2 81.1 %reduce-scatter.7.cloned.1.call-done = f32[1000,768]{1,0:T(8,128)} async-done(((f32[4000,768]{1,0:T(8,128)}), f32[1000,768]{1,0:T(8,128)}) %reduce-scatter.7.cloned.1.call-update) | async-done | bytes 3072016 | tf_op jit(solution)/shard_map/reduce_scatter | solution.py:216
  404.3 4.2 multiply_reduce_fusion.3
  409.2 55.5 %reduce-scatter.5.cloned.1.call-done = bf16[1000,768]{1,0:T(8,128)(2,1)} async-done(((bf16[4000,768]{1,0:T(8,128)(2,1)}), bf16[1000,768]{1,0:T(8,128)(2,1)}) %reduce-scatter.5.cloned.1.call-update) | async-done | bytes 1536016 | tf_op jit(solution)/shard_map/reduce_scatter | solution.py:186
  464.6 8.4 %multiply_reduce_fusion.2 = (f32[768]{0:T(1024)}, f32[1000,768]{1,0:T(8,128)S(1)}, bf16[1000,768]{1,0:T(8,128)(2,1)}, f32[768]{0:T(1024)}) fusion(f32[1000,768]{1,0:T(8,128)} %get-tuple-element.180, f32[768]{0:T(1024)} %get-tuple-element.106, f32[1000]{0:T(1024)} %get-tuple-element.188, f32[1000,768]{1,0:T(8,128)} %get-tuple-element.179, ...), kind=kLoop, calls=%fused_computation.43 | loop fusion | flops 15358464 | bytes 16934432 | tf_op jit(solution)/shard_map/reduce_sum | solution.py:225
  479.4 4.3 convolution_convert_fusion.2
  484.2 5.8 reshape.240
  490.0 6.1 copy.106
  496.0 13.1 %multiply_reduce_fusion = (f32[5,12,200]{2,1,0:T(8,128)S(1)}, f32[5,12,200,200]{2,3,1,0:T(8,128)}) fusion(f32[5,12,200,200]{2,3,1,0:T(8,128)} %copy-done.1, f32[5,12,200]{2,1,0:T(8,128)} %copy-done.9, bf16[5,200,12,64]{1,3,2,0:T(8,128)(2,1)} %copy.106, bf16[5,200,1,12,64]{1,4,3,0,2:T(8,128)(2,1)} %copy.124), kind=kOutput, calls=%fused_computation.25 | convolution fusion | flops 314388000 | bytes 22368000 | tf_op jit(solution)/shard_map/bqhd,bkhd->bhqk/dot_general | solution.py:240
  509.1 12.1 %convert_reduce_fusion = (f32[12,200,200]{1,2,0:T(8,128)}, bf16[5,12,200,200]{2,3,1,0:T(8,128)(2,1)S(1)}) fusion(f32[5,12,200,200]{2,3,1,0:T(8,128)} %get-tuple-element.184, f32[5,12,200]{2,1,0:T(8,128)S(1)} %get-tuple-element.183, f32[5,12,200,200]{2,3,1,0:T(8,128)} %copy-done.1, f32[5,12,200]{2,1,0:T(8,128)S(1)} %copy-done.10), kind=kLoop, calls=%fused_computation.22 | loop fusion | flops 13920000 | bytes 26016000 | tf_op jit(solution)/shard_map/reduce_sum | solution.py:253
  521.2 5.1 multiply_bitcast_fusion
  529.0 5.1 convolution_bitcast_fusion
  534.1 6.6 convert_reduce_fusion.2
  540.7 11.3 %copy.111 = bf16[5,200,3,12,64]{1,0,4,3,2:T(8,128)(2,1)} copy(bf16[5,200,3,12,64]{1,4,3,0,2:T(8,128)(2,1)} %get-tuple-element.165) | data formatting | bytes 9216000 | tf_op jit(solution)/shard_map/convert_element_type | solution.py:258
  552.0 13.8 %convert_element_type.177 = bf16[1000,2304]{0,1:T(8,128)(2,1)} reshape(bf16[5,200,3,12,64]{1,0,4,3,2:T(8,128)(2,1)} %copy.111) | data formatting | bytes 9216000 | tf_op jit(solution)/shard_map/convert_element_type | solution.py:258
  565.8 8.4 %convolution_convert_fusion.1 = bf16[768,2304]{0,1:T(8,128)(2,1)} fusion(bf16[1000,768]{1,0:T(8,128)(2,1)} %bitcast.131, bf16[1000,2304]{0,1:T(8,128)(2,1)} %convert_element_type.177), kind=kOutput, calls=%fused_computation.37 | convolution fusion | flops 3540713472 | bytes 9682944 | tf_op jit(solution)/shard_map/dot_general | solution.py:261
  574.2 9.8 %convolution_convert_fusion.3 = bf16[768,768]{0,1:T(8,128)(2,1)} fusion(bf16[4000,768]{1,0:T(8,128)(2,1)} %all-gather.5.cloned.1.call-done, bf16[4000,768]{1,0:T(8,128)(2,1)} %get-tuple-element.181), kind=kOutput, calls=%fused_computation.79 | convolution fusion | flops 4719181824 | bytes 13467648 | tf_op jit(solution)/shard_map/dot_general | solution.py:204
  584.0 10.0 %convolution_convert_fusion.4 = bf16[768,768]{0,1:T(8,128)(2,1)} fusion(bf16[4000,768]{1,0:T(8,128)(2,1)} %all-gather.3.cloned.1.call-done, bf16[4000,768]{1,0:T(8,128)(2,1)} %copy-done.35), kind=kOutput, calls=%fused_computation.80 | convolution fusion | flops 4719181824 | bytes 13467648 | tf_op jit(solution)/shard_map/dot_general | solution.py:208
  594.1 20.7 %reduce-scatter.9.cloned.1.call-done = bf16[768,576]{0,1:T(8,128)(2,1)} async-done(((bf16[768,2304]{0,1:T(8,128)(2,1)}), bf16[768,576]{0,1:T(8,128)(2,1)}) %reduce-scatter.9.cloned.1.call-update) | async-done | bytes 884752 | tf_op jit(solution)/shard_map/reduce_scatter | solution.py:290
  614.7 3.5 pad_maximum_fusion
  618.2 5.8 copy.112
  624.0 5.9 all-to-all-start
  639.6 3.2 copy.113
  646.9 3.6 reshape.234
  650.4 10.1 %multiply_reduce_fusion.4 = (f32[768]{0:T(1024)S(1)}, f32[1000]{0:T(1024)}, f32[1000]{0:T(1024)}, f32[768]{0:T(1024)S(1)}, f32[1000,768]{1,0:T(8,128)}) fusion(f32[1000]{0:T(1024)} %rsqrt.21, f32[1000]{0:T(1024)} %div.123, bf16[5,200,768]{2,1,0:T(8,128)(2,1)} %param.33, f32[768]{0:T(1024)S(1)} %copy-done.27, bf16[1000,2304]{0,1:T(8,128)(2,1)} %convert_element_type.177, ...), kind=kOutput, calls=%fused_computation.45 | convolution fusion | flops 3548924416 | bytes 14316160 | tf_op jit(solution)/shard_map/dot_general | solution.py:264
  665.9 5.9 multiply_add_fusion
  671.8 60.1 %while.22 = (s32[]{:T(128)}, f32[732,12]{0,1:T(8,128)}, s32[8,25,200]{2,1,0:T(8,128)}, f32[8,12,25,200]{3,2,0,1:T(8,128)}, s32[]{:T(128)}, /*index=5*/s32[]{:T(128)}) while((s32[]{:T(128)}, f32[732,12]{0,1:T(8,128)}, s32[8,25,200]{2,1,0:T(8,128)}, f32[8,12,25,200]{3,2,0,1:T(8,128)}, s32[]{:T(128)}, /*index=5*/s32[]{:T(128)}) %tuple.113), condition=%wide.region_39.40_spmd.clone, body=%wide.region_38.39_spmd.clone.sunk | while | flops 530717568 | bytes 850367 | solution.py:99
  673.5 5.0 fusion.87
  680.3 5.8 fusion.87
  687.9 5.8 fusion.87
  695.5 5.8 fusion.87
  703.1 5.8 fusion.87
  710.7 5.8 fusion.87
  718.2 5.8 fusion.87
  725.8 5.8 fusion.87
  739.2 41.4 %all-reduce.2 = (f32[]{:T(128)}, f32[10,768]{1,0:T(8,128)}, f32[3072]{0:T(1024)}, f32[732,12]{0,1:T(8,128)}) all-reduce(f32[]{:T(128)S(6)} %add.302, f32[10,768]{1,0:T(8,128)} %stack.59, f32[3072]{0:T(1024)S(1)} %dynamic_update_slice.7, f32[732,12]{0,1:T(8,128)} %get-tuple-element.73), channel_id=1, replica_groups=mesh['wide'=8,'narrow'=4] {'wide','narrow'}, use_global_device_ids=true, to_apply=%region_22.23 | all-reduce | flops 19537 | bytes 156296 | tf_op jit(solution)/shard_map/psum | solution.py:315
  (175 shorter events, 98.1 us)
Async XLA Ops:
  7.2 95.4 %copy-start = (bf16[768,2304]{1,0:T(8,128)(2,1)S(1)}, bf16[768,2304]{1,0:T(8,128)(2,1)}, u32[]{:S(2)}) copy-start(bf16[768,2304]{1,0:T(8,128)(2,1)} %param.37) | copy-start | bytes 10616836
  7.2 229.1 %all-gather.3.cloned.1.call-start = ((), (), s32[]{:S(2)}) async-start(), calls=%async_computation.5 | async-start | bytes 7680000 | tf_op jit(solution)/shard_map/all_gather | solution.py:181
  13.7 4.2 copy-start.20
  97.2 5.4 copy-start.26
  97.2 5.4 copy-start.28
  146.0 6.2 copy-start.33
  158.5 4.8 copy-start.1
  158.5 4.8 copy-start.5
  163.3 2.2 copy-start.9
  168.6 6.0 copy-start.29
  168.6 6.0 copy-start.32
  183.1 3.1 copy-start.2
  183.1 3.1 copy-start.22
  183.1 3.1 copy-start.31
  185.6 0.6 copy-start.24
  186.2 4.4 copy-start.21
  188.0 95.5 %all-gather.5.cloned.1.call-start = ((), (), s32[]{:S(2)}) async-start(), calls=%async_computation.7 | async-start | bytes 7680000 | tf_op jit(solution)/shard_map/all_gather | solution.py:202
  193.6 210.7 %reduce-scatter.7.cloned.1.call-start = ((), (), s32[]{:S(2)}) async-start(), calls=%async_computation.8 | async-start | bytes 15360000 | tf_op jit(solution)/shard_map/reduce_scatter | solution.py:216
  283.5 15.1 %copy-start.34 = (bf16[768,768]{1,0:T(8,128)(2,1)S(1)}, bf16[768,768]{1,0:T(8,128)(2,1)}, u32[]{:S(2)}) copy-start(bf16[768,768]{1,0:T(8,128)(2,1)} %param.39) | copy-start | bytes 3538948
  295.9 2.7 copy-start.35
  306.5 158.1 %reduce-scatter.5.cloned.1.call-start = ((), (), s32[]{:S(2)}) async-start(), calls=%async_computation.6 | async-start | bytes 7680000 | tf_op jit(solution)/shard_map/reduce_scatter | solution.py:186
  319.4 274.7 %reduce-scatter.11.cloned.1.call-start = ((), (), s32[]{:S(2)}) async-start(), calls=%async_computation.10 | async-start | bytes 1474560 | tf_op jit(solution)/shard_map/reduce_scatter | solution.py:293
  323.2 141.5 %copy-start.23 = (f32[768]{0:T(1024)S(1)}, f32[768]{0:T(1024)}, u32[]{:S(2)}) copy-start(f32[768]{0:T(1024)} %get-tuple-element.105) | copy-start | bytes 9220
  323.2 141.5 %copy-start.25 = (f32[1000]{0:T(1024)S(1)}, f32[1000]{0:T(1024)}, u32[]{:S(2)}) copy-start(f32[1000]{0:T(1024)} %copy-done.24) | copy-start | bytes 12004
  464.6 10.0 %copy-start.30 = (f32[768]{0:T(1024)S(1)}, f32[768]{0:T(1024)}, u32[]{:S(2)}) copy-start(f32[768]{0:T(1024)} %get-tuple-element.111) | copy-start | bytes 9220
  473.0 1.6 copy-start.3
  473.0 3.9 copy-start.11
  475.7 1.2 copy-start.12
  483.7 131.0 %reduce-scatter.9.cloned.1.call-start = ((), (), s32[]{:S(2)}) async-start(), calls=%async_computation.9 | async-start | bytes 4423680 | tf_op jit(solution)/shard_map/reduce_scatter | solution.py:290
  496.0 13.1 %copy-start.10 = (f32[5,12,200]{2,1,0:T(8,128)S(1)}, f32[5,12,200]{2,1,0:T(8,128)}, u32[]{:S(2)}) copy-start(f32[5,12,200]{2,1,0:T(8,128)} %copy-done.9) | copy-start | bytes 144004
  509.1 19.9 %slice-start = ((s8[12288000]{0:T(1024)(128)(4,1)}), s8[4194304]{0:T(1024)(128)(4,1)S(1)}, s32[]{:S(2)}) async-start(s8[12288000]{0:T(1024)(128)(4,1)} %bitcast.122), calls=%async_computation.11 | async-start | bytes 8388608
  509.1 19.9 %slice-start.1 = ((s8[12288000]{0:T(1024)(128)(4,1)}), s8[4194304]{0:T(1024)(128)(4,1)S(1)}, s32[]{:S(2)}) async-start(s8[12288000]{0:T(1024)(128)(4,1)} %bitcast.122), calls=%async_computation.12 | async-start | bytes 8388608
  521.2 5.1 copy-start.4
  521.2 7.8 slice-start.2
  529.0 5.1 copy-start.8
  624.0 5.9 copy-start.19
  624.0 107.8 %all-to-all-start = ((bf16[8,96,2304]{2,1,0:T(8,128)(2,1)}), bf16[8,96,2304]{2,1,0:T(8,128)(2,1)}, u32[]{:S(2)}, u32[]{:S(2)}) async-start(bf16[8,96,2304]{2,1,0:T(8,128)(2,1)} %bitcast.126), calls=%async_computation.4 | async-start | bytes 7077888 | tf_op jit(solution)/shard_map/all_to_all | solution.py:32
  642.8 7.6 copy-start.27
  734.4 1.5 copy-start.6
  787.4 8.9 %copy-start.7 = (f32[96,2304]{1,0:T(8,128)S(1)}, f32[96,2304]{1,0:T(8,128)}, u32[]{:S(2)}) copy-start(f32[96,2304]{1,0:T(8,128)} %copy-done.6) | copy-start | bytes 2654212
  787.4 8.9 %copy-start.13 = (f32[96,768]{1,0:T(8,128)S(1)}, f32[96,768]{1,0:T(8,128)}, u32[]{:S(2)}) copy-start(f32[96,768]{1,0:T(8,128)} %param.53) | copy-start | bytes 884740
  787.4 8.9 %copy-start.14 = (f32[96,768]{1,0:T(8,128)S(1)}, f32[96,768]{1,0:T(8,128)}, u32[]{:S(2)}) copy-start(f32[96,768]{1,0:T(8,128)} %param.55) | copy-start | bytes 884740
  787.5 8.9 %copy-start.15 = (f32[96,768]{1,0:T(8,128)S(1)}, f32[96,768]{1,0:T(8,128)}, u32[]{:S(2)}) copy-start(f32[96,768]{1,0:T(8,128)} %param.54) | copy-start | bytes 884740
  787.5 8.9 %copy-start.16 = (f32[96,768]{1,0:T(8,128)S(1)}, f32[96,768]{1,0:T(8,128)}, u32[]{:S(2)}) copy-start(f32[96,768]{1,0:T(8,128)} %param.50) | copy-start | bytes 884740
  787.5 8.9 %copy-start.17 = (f32[96,768]{1,0:T(8,128)S(1)}, f32[96,768]{1,0:T(8,128)}, u32[]{:S(2)}) copy-start(f32[96,768]{1,0:T(8,128)} %param.52) | copy-start | bytes 884740
  787.5 8.9 %copy-start.18 = (f32[96,768]{1,0:T(8,128)S(1)}, f32[96,768]{1,0:T(8,128)}, u32[]{:S(2)}) copy-start(f32[96,768]{1,0:T(8,128)} %param.51) | copy-start | bytes 884740
Sparse Core Ops, SparseCore 0:
  188.1 48.2 all-gather.2
  237.9 45.5 all-gather.4
  306.6 97.6 reduce-scatter.6
  406.7 57.8 reduce-scatter.4
  483.8 25.5 reduce-scatter.10
  574.3 40.3 reduce-scatter.8
where the time goes:
time: 818 us; the launch traced here: 806 us
  matrix products  258 us (32%)
  waiting for transfers between devices  233 us (28%)
  local copies, waits for them, and re-layouts  157 us (19%)
  other arithmetic  88.3 us (11%)
  blocking collectives  41.4 us (5%)
  between operations  21.4 us (3%)
    reduce_scatter x1, waiting for transfers between devices, shards(): lax.psum_scatter(lax.dot_general(block_rows, up_weight, contract_cols, pr...  81.1 us
    dot_general x8, matrix products, one_block(): return jnp.einsum('qkr,rh->hqk', onehot, rel_table, precision=exact_prec)  73.2 us
    reduce_scatter x1, waiting for transfers between devices, shards(): lax.psum_scatter(lax.dot_general(block_rows, down_weight, contract_cols,...  55.5 us
    dot_general x8, matrix products, add_block(): jnp.einsum('qkr,hqk->rh', onehot, grad_rows, precision=exact_prec)  45.6 us
    psum x1, blocking collectives, shards(): large_squares = lax.psum(shard_squares, ('wide', 'narrow'))  41.4 us
    all_gather x1, waiting for transfers between devices, shards(): gathered = lax.all_gather(second_b, 'narrow', axis=0, tiled=True)  41.3 us
    all_gather x1, waiting for transfers between devices, shards(): down_all = lax.all_gather(down_in_b, 'narrow', axis=0, tiled=True)  34.4 us
    unnamed x81, local copies, waits for them, and re-layouts  26.3 us
  transfers between devices with their start and end apart: 7, of which 5 were waited for; matrix products, arithmetic and copies ran while one was open for 31% of the time, Pallas kernels for 0%

commit v1 on v0

v1 whole, which is shorter than its diff:
```python
import functools

import jax
import jax.numpy as jnp
from jax import lax
from jax.experimental import pallas as pl
from jax.experimental.pallas import tpu as pltpu
from jax.sharding import PartitionSpec as P

VALID = 197
STEP = 10
LANES = 128

norm_eps = 1e-06
clip_eps = 1e-06
max_norm = 1.0
beta_one = 0.9
beta_two = 0.999
adam_eps = 1e-08
rate_matrix = 0.05
rate_small = 0.4
weight_decay = 0.05
BF = jnp.bfloat16
F32 = jnp.float32
ROWS_ROWS = (((0,), (0,)), ((), ()))
COLS_COLS = (((1,), (1,)), ((), ()))
VMEM_LIMIT = 60000 * 1024


def mm(a, b):
    return jnp.dot(a, b, preferred_element_type=F32)


def mm_nt(a, b):
    return lax.dot_general(a, b, COLS_COLS, preferred_element_type=F32)


def mm_tn(a, b):
    return lax.dot_general(a, b, ROWS_ROWS, preferred_element_type=F32)


def params(steps=1):
    return pltpu.CompilerParams(
        dimension_semantics=("arbitrary",) * steps, vmem_limit_bytes=VMEM_LIMIT
    )


def whole(shape):
    zeros = (0,) * len(shape)
    return pl.BlockSpec(shape, lambda i: zeros)


def fixed(shape):
    zeros = (0,) * len(shape)
    return pl.BlockSpec(shape, lambda i: zeros, pipeline_mode=pl.Buffered(1))


def per_step(shape):
    rest = (0,) * (len(shape) - 1)
    return pl.BlockSpec((1,) + tuple(shape[1:]), lambda i: (i,) + rest)


def normalized(values):
    center = values - jnp.mean(values, -1, keepdims=True)
    factor = lax.rsqrt(jnp.mean(center * center, -1, keepdims=True) + norm_eps)
    return center * factor, factor


def layer_back(grad, normed, factor, gain_vec):
    scaled = grad * gain_vec
    return factor * (
        scaled
        - jnp.mean(scaled, -1, keepdims=True)
        - normed * jnp.mean(scaled * normed, -1, keepdims=True)
    )


def head_masks(pair_width, head_dim):
    lane = lax.broadcasted_iota(jnp.int32, (1, pair_width), 1)
    return [
        ((lane >= e * head_dim) & (lane < (e + 1) * head_dim)) for e in range(pair_width // head_dim)
    ]


def bias_kernel(idx_ref, tab_ref, out_ref):
    heads, seq = out_ref.shape[1], out_ref.shape[2]
    chunks = tab_ref.shape[1]

    def rows(step, carry):
        at = pl.multiple_of(step * 8, 8)
        for half in range(idx_ref.shape[2] // LANES):
            width = min(LANES, seq - half * LANES)
            index = idx_ref[0, pl.ds(at, 8), half * LANES : (half + 1) * LANES]
            low, high = index & (LANES - 1), index >> 7
            match = [high == c for c in range(chunks)]
            for h in range(heads):
                found = jnp.full((8, LANES), -1e30, F32)
                for c in range(chunks):
                    row = jnp.broadcast_to(tab_ref[h, c : c + 1, :], (8, LANES))
                    taken = jnp.take_along_axis(row, low, axis=1, mode="promise_in_bounds")
                    found = jnp.where(match[c], taken, found)
                out_ref[0, h, pl.ds(at, 8), half * LANES : half * LANES + width] = found[:, :width]
        return carry

    lax.fori_loop(0, seq // 8, rows, 0)


def bias_tables(indices, table_rows):
    both, seq, padded = indices.shape
    heads, chunks, _ = table_rows.shape
    return pl.pallas_call(
        bias_kernel,
        grid=(both,),
        in_specs=[per_step(indices.shape), whole(table_rows.shape)],
        out_specs=per_step((both, heads, seq, seq)),
        out_shape=jax.ShapeDtypeStruct((both, heads, seq, seq), F32),
        compiler_params=params(),
        name="bias_tables",
    )(indices, table_rows)


def table_kernel(idx_ref, ds_ref, out_ref):
    seq, heads, _ = ds_ref.shape
    chunks = out_ref.shape[0] // (2 * heads)
    out_ref[...] = jnp.zeros_like(out_ref)
    kinds = lax.broadcasted_iota(jnp.int32, (LANES, seq), 0)

    def one_key(j, total):
        index = idx_ref[pl.ds(j, 1), :]
        low, high = index & (LANES - 1), index >> 7
        onehot = jnp.where(jnp.broadcast_to(low, (LANES, seq)) == kinds, 1.0, 0.0).astype(BF)
        grads = ds_ref[j]
        top = grads.astype(BF).astype(F32)
        both = jnp.concatenate([top, grads - top], 0)
        high_all = jnp.broadcast_to(high, both.shape)
        parts = jnp.concatenate([jnp.where(high_all == c, both, 0.0) for c in range(chunks)], 0)
        return total + mm_nt(parts.astype(BF), onehot)

    out_ref[...] = lax.fori_loop(0, seq, one_key, jnp.zeros(out_ref.shape, F32), unroll=2)


def table_sums(index_t, grads, chunks):
    seq, heads, _ = grads.shape
    out = (chunks * 2 * heads, LANES)
    return pl.pallas_call(
        table_kernel,
        grid=(1,),
        in_specs=[whole(index_t.shape), whole(grads.shape)],
        out_specs=whole(out),
        out_shape=jax.ShapeDtypeStruct(out, F32),
        compiler_params=params(),
        name="table_sums",
    )(index_t, grads)


def front_kernel(heads, x_ref, wqkv_ref, wproj_ref, vec_ref, bias_ref, a_ref, qkv_ref, o_ref, attn_ref, hn_ref):
    width = x_ref.shape[2]
    head_dim = width // heads
    scale = head_dim ** (-0.5)
    x = x_ref[0].astype(F32)
    normed, _ = normalized(x)
    first = (normed * vec_ref[4:5, :] + vec_ref[5:6, :]).astype(BF)
    a_ref[0] = first
    for part, row in ((0, 0), (1, None), (2, 1)):
        cols = slice(part * width, (part + 1) * width)
        value = mm(first, wqkv_ref[:, cols])
        if row is not None:
            value = value + vec_ref[row : row + 1, :]
        qkv_ref[0, :, cols] = value.astype(BF)
    pair = LANES
    masks = head_masks(pair, head_dim)
    per = pair // head_dim

    def one_pair(g, carry):
        at = pl.multiple_of(g * pair, pair)
        q = qkv_ref[0, :, pl.ds(at, pair)]
        k = qkv_ref[0, :, pl.ds(at + width, pair)]
        v = qkv_ref[0, :, pl.ds(at + 2 * width, pair)]
        out = None
        for e in range(per):
            qm = q * jnp.where(masks[e], scale, 0.0).astype(BF)
            s = mm_nt(qm, k) + bias_ref[0, g * per + e]
            p = jnp.exp(s - jnp.max(s, -1, keepdims=True))
            p = p * (1.0 / jnp.sum(p, -1, keepdims=True))
            mixed = mm(p.astype(BF), v)
            out = mixed if out is None else jnp.where(masks[e], mixed, out)
        o_ref[0, :, pl.ds(at, pair)] = out.astype(BF)
        return carry

    lax.fori_loop(0, width // pair, one_pair, 0)
    attn = mm(o_ref[0], wproj_ref[...]) + vec_ref[2:3, :]
    attn_ref[0] = attn
    middle, _ = normalized(x + vec_ref[8:9, :] * attn)
    hn_ref[0] = (middle * vec_ref[6:7, :] + vec_ref[7:8, :]).astype(BF)


def front(x, qkv_weight, proj_weight, vectors, bias, heads):
    images, seq, width = x.shape
    shapes = [
        jax.ShapeDtypeStruct((images, seq, width), BF),
        jax.ShapeDtypeStruct((images, seq, 3 * width), BF),
        jax.ShapeDtypeStruct((images, seq, width), BF),
        jax.ShapeDtypeStruct((images, seq, width), F32),
        jax.ShapeDtypeStruct((images, seq, width), BF),
    ]
    return pl.pallas_call(
        functools.partial(front_kernel, heads),
        grid=(images,),
        in_specs=[
            per_step(x.shape),
            fixed(qkv_weight.shape),
            fixed(proj_weight.shape),
            fixed(vectors.shape),
            pl.BlockSpec((1,) + bias.shape[1:], lambda i: (0, 0, 0, 0), pipeline_mode=pl.Buffered(1)),
        ],
        out_specs=[per_step(s.shape) for s in shapes],
        out_shape=shapes,
        compiler_params=params(),
        name="front",
    )(x, qkv_weight, proj_weight, vectors, bias)


def mlp_kernel(chunk, hn_ref, gy_ref, vec_ref, bup_ref, wup_ref, wdn_ref, m_ref, dhn_ref, gup_ref, gdn_ref, gb_ref, dm_ref, z_ref, du_ref):
    tokens = hn_ref.shape[0]
    first = pl.program_id(0) == 0

    @pl.when(first)
    def _():
        m_ref[...] = jnp.zeros_like(m_ref)
        dhn_ref[...] = jnp.zeros_like(dhn_ref)

        def rows(step, carry):
            at = pl.ds(pl.multiple_of(step * chunk, chunk), chunk)
            dm_ref[at, :] = (vec_ref[9:10, :] * gy_ref[at, :].astype(F32)).astype(BF)
            return carry

        lax.fori_loop(0, tokens // chunk, rows, 0)

    gb_ref[...] = jnp.zeros_like(gb_ref)

    def rows(step, carry):
        at = pl.ds(pl.multiple_of(step * chunk, chunk), chunk)
        u = mm(hn_ref[at, :], wup_ref[0]) + bup_ref[0]
        gate = 0.5 * (1.0 + lax.erf(u * 0.7071067811865476))
        z = (u * gate).astype(BF)
        slope = gate + u * jnp.exp(-0.5 * u * u) * 0.3989422804014327
        z_ref[at, :] = z
        m_ref[at, :] += mm_nt(z, wdn_ref[0])
        du = (mm(dm_ref[at, :], wdn_ref[0]) * slope).astype(BF)
        du_ref[at, :] = du
        gb_ref[0] += jnp.sum(du.astype(F32), 0, keepdims=True)
        dhn_ref[at, :] += mm_nt(du, wup_ref[0])
        return carry

    lax.fori_loop(0, tokens // chunk, rows, 0)
    gdn_ref[0] = mm_tn(dm_ref[...], z_ref[...]).astype(BF)
    gup_ref[0] = mm_tn(hn_ref[...], du_ref[...]).astype(BF)


def mlp(hn, gy, vectors, up_bias, up_all, down_all, chunk):
    tokens, width = hn.shape
    blocks, _, hidden = up_all.shape
    shapes = [
        jax.ShapeDtypeStruct((tokens, width), F32),
        jax.ShapeDtypeStruct((tokens, width), F32),
        jax.ShapeDtypeStruct((blocks, width, hidden), BF),
        jax.ShapeDtypeStruct((blocks, width, hidden), BF),
        jax.ShapeDtypeStruct((blocks, 1, hidden), F32),
    ]
    return pl.pallas_call(
        functools.partial(mlp_kernel, chunk),
        grid=(blocks,),
        in_specs=[
            fixed(hn.shape),
            fixed(gy.shape),
            fixed(vectors.shape),
            per_step(up_bias.shape),
            per_step(up_all.shape),
            per_step(down_all.shape),
        ],
        out_specs=[fixed(s.shape) for s in shapes[:2]] + [per_step(s.shape) for s in shapes[2:]],
        out_shape=shapes,
        scratch_shapes=[
            pltpu.VMEM((tokens, width), BF),
            pltpu.VMEM((tokens, hidden), BF),
            pltpu.VMEM((tokens, hidden), BF),
        ],
        compiler_params=params(),
        name="mlp",
    )(hn, gy, vectors, up_bias, up_all, down_all)


def back_kernel(
    heads, x_ref, gy_ref, attn_ref, m_ref, dhn_ref, qkv_ref, wproj_ref, vec_ref, bias_ref,
    out_ref, dmid_ref, dat_ref, dqkv_ref, ds_ref, gvec_ref, gcol_ref, do_ref,
):
    seq, width = x_ref.shape[1], x_ref.shape[2]
    head_dim = width // heads
    scale = head_dim ** (-0.5)

    @pl.when(pl.program_id(0) == 0)
    def _():
        ds_ref[...] = jnp.zeros_like(ds_ref)
        gvec_ref[...] = jnp.zeros_like(gvec_ref)
        gcol_ref[...] = jnp.zeros_like(gcol_ref)

    attn = attn_ref[0]
    middle = x_ref[0].astype(F32) + vec_ref[8:9, :] * attn
    branch = m_ref[0] + vec_ref[3:4, :]
    out_ref[0] = (middle + vec_ref[9:10, :] * branch).astype(BF)
    cotangent = gy_ref[0].astype(F32)
    normed, factor = normalized(middle)
    dhn = dhn_ref[0]
    dmid = cotangent + layer_back(dhn, normed, factor, vec_ref[6:7, :])
    dmid_ref[0] = dmid
    dat = (vec_ref[8:9, :] * dmid).astype(BF)
    dat_ref[0] = dat
    down_in = (vec_ref[9:10, :] * cotangent).astype(BF)
    for row, value in enumerate(
        (dat.astype(F32), down_in.astype(F32), dhn * normed, dhn, dmid * attn, cotangent * branch)
    ):
        gvec_ref[row : row + 1, :] += jnp.sum(value, 0, keepdims=True)
    do_ref[...] = mm_nt(dat, wproj_ref[...]).astype(BF)
    pair = LANES
    masks = head_masks(pair, head_dim)
    per = pair // head_dim

    def one_pair(g, carry):
        at = pl.multiple_of(g * pair, pair)
        q = qkv_ref[0, :, pl.ds(at, pair)]
        k = qkv_ref[0, :, pl.ds(at + width, pair)]
        v = qkv_ref[0, :, pl.ds(at + 2 * width, pair)]
        do = do_ref[:, pl.ds(at, pair)]
        dq = dk = dv = None
        for e in range(per):
            pick = jnp.where(masks[e], scale, 0.0).astype(BF)
            keep = jnp.where(masks[e], 1.0, 0.0).astype(BF)
            qm, km, dom = q * pick, k * pick, do * keep
            s = mm_nt(k, qm) + bias_ref[0, g * per + e]
            p = jnp.exp(s - jnp.max(s, 0, keepdims=True))
            p = p * (1.0 / jnp.sum(p, 0, keepdims=True))
            dv_e = mm(p.astype(BF), dom)
            dp = mm_nt(v, dom)
            ds = (p * (dp - jnp.sum(dp * p, 0, keepdims=True))).astype(BF)
            ds_ref[g * per + e] += ds.astype(F32)
            dk_e = mm(ds, qm)
            dq_e = mm_tn(ds, km)
            dq = dq_e if dq is None else dq + dq_e
            dk = dk_e if dk is None else dk + dk_e
            dv = dv_e if dv is None else dv + dv_e
        for part, value in ((0, dq), (1, dk), (2, dv)):
            rounded = value.astype(BF)
            dqkv_ref[0, :, pl.ds(at + part * width, pair)] = rounded
            gcol_ref[:, pl.ds(at + part * width, pair)] += jnp.sum(rounded.astype(F32), 0, keepdims=True)
        return carry

    lax.fori_loop(0, width // pair, one_pair, 0)


def back(x, gy, attn, m, dhn, qkv, proj_weight, vectors, bias, heads):
    images, seq, width = x.shape
    shapes = [
        jax.ShapeDtypeStruct((images, seq, width), BF),
        jax.ShapeDtypeStruct((images, seq, width), F32),
        jax.ShapeDtypeStruct((images, seq, width), BF),
        jax.ShapeDtypeStruct((images, seq, 3 * width), BF),
        jax.ShapeDtypeStruct((heads, seq, seq), F32),
        jax.ShapeDtypeStruct((8, width), F32),
        jax.ShapeDtypeStruct((1, 3 * width), F32),
    ]
    return pl.pallas_call(
        functools.partial(back_kernel, heads),
        grid=(images,),
        in_specs=[per_step(v.shape) for v in (x, gy, attn, m, dhn, qkv)]
        + [
            fixed(proj_weight.shape),
            fixed(vectors.shape),
            pl.BlockSpec((1,) + bias.shape[1:], lambda i: (1, 0, 0, 0), pipeline_mode=pl.Buffered(1)),
        ],
        out_specs=[per_step(s.shape) for s in shapes[:4]] + [fixed(s.shape) for s in shapes[4:]],
        out_shape=shapes,
        scratch_shapes=[pltpu.VMEM((seq, width), BF)],
        compiler_params=params(),
        name="back",
    )(x, gy, attn, m, dhn, qkv, proj_weight, vectors, bias)


def grads_kernel(blocks, a_ref, dqkv_ref, o_ref, dat_ref, out_ref):
    wide_cols, thin_cols = dqkv_ref.shape[1] // blocks, dat_ref.shape[1] // blocks
    for n in range(blocks):
        out_ref[n, :, :wide_cols] = mm_tn(
            a_ref[...], dqkv_ref[:, n * wide_cols : (n + 1) * wide_cols]
        ).astype(BF)
        out_ref[n, :, wide_cols:] = mm_tn(
            o_ref[...], dat_ref[:, n * thin_cols : (n + 1) * thin_cols]
        ).astype(BF)


def attention_grads(first, dqkv, mixed, dat, blocks):
    width = first.shape[1]
    cols = (dqkv.shape[1] + dat.shape[1]) // blocks
    return pl.pallas_call(
        functools.partial(grads_kernel, blocks),
        grid=(1,),
        in_specs=[whole(v.shape) for v in (first, dqkv, mixed, dat)],
        out_specs=whole((blocks, width, cols)),
        out_shape=jax.ShapeDtypeStruct((blocks, width, cols), BF),
        compiler_params=params(),
        name="attention_grads",
    )(first, dqkv, mixed, dat)


def input_kernel(x_ref, dqkv_ref, dmid_ref, wqkv_ref, vec_ref, out_ref, gvec_ref):
    @pl.when(pl.program_id(0) == 0)
    def _():
        gvec_ref[...] = jnp.zeros_like(gvec_ref)

    da = mm_nt(dqkv_ref[0], wqkv_ref[...])
    normed, factor = normalized(x_ref[0].astype(F32))
    gvec_ref[0:1, :] += jnp.sum(da * normed, 0, keepdims=True)
    gvec_ref[1:2, :] += jnp.sum(da, 0, keepdims=True)
    out_ref[0] = dmid_ref[0] + layer_back(da, normed, factor, vec_ref[4:5, :])


def input_grads(x, dqkv, dmid, qkv_weight, vectors):
    images, seq, width = x.shape
    shapes = [
        jax.ShapeDtypeStruct((images, seq, width), F32),
        jax.ShapeDtypeStruct((8, width), F32),
    ]
    return pl.pallas_call(
        input_kernel,
        grid=(images,),
        in_specs=[per_step(v.shape) for v in (x, dqkv, dmid)]
        + [fixed(qkv_weight.shape), fixed(vectors.shape)],
        out_specs=[per_step(shapes[0].shape), fixed(shapes[1].shape)],
        out_shape=shapes,
        compiler_params=params(),
        name="input_grads",
    )(x, dqkv, dmid, qkv_weight, vectors)


def adam_update(master, mean, square, grad, rate, decay):
    mean_new = beta_one * mean + (1.0 - beta_one) * grad
    square_new = beta_two * square + (1.0 - beta_two) * grad * grad
    fix_one = 1.0 - beta_one**STEP
    fix_two = 1.0 - beta_two**STEP
    direction = mean_new / fix_one / (jnp.sqrt(square_new / fix_two) + adam_eps)
    return (mean_new, square_new, master - rate * (direction + decay * master))


def axis_bits():
    found = []
    for axis in ("narrow", "wide"):
        count = lax.axis_size(axis).bit_length() - 1
        found += [(axis, count - 1 - at) for at in range(count)]
    return found


def swap(value, axis, bit):
    size = lax.axis_size(axis)
    return lax.ppermute(value, axis, [(i, i ^ (1 << bit)) for i in range(size)])


def scattered_sum(grads, order):
    bits = axis_bits()
    pieces = [grads.reshape((2,) * len(bits) + grads.shape[2:])]
    for dim in order:
        axis, bit = bits[dim]
        mine = (lax.axis_index(axis) >> bit) & 1

        def half(piece, side):
            return lax.dynamic_slice_in_dim(piece, side, 1, dim)

        sent = sum(half(p, 1 - mine).astype(F32) for p in pieces).astype(BF)
        arrived = swap(sent, axis, bit)
        pieces = [half(p, mine) for p in pieces] + [arrived]
    return sum(p.astype(F32) for p in pieces).reshape(grads.shape[2:])


def summed(value):
    for axis, bit in reversed(axis_bits()):
        value = value + swap(value, axis, bit)
    return value


def local_work(
    block_in, out_grad, mim_mask, rel_index, qkv_weight, proj_weight, up_all, down_all, vectors, up_bias, rel_table
):
    images, seq, width = block_in.shape
    table_rows, heads = rel_table.shape
    blocks, _, hidden = up_all.shape
    tokens = images * seq
    chunks = -(-table_rows // LANES)
    padded_seq = -(-seq // LANES) * LANES
    key_at = jnp.arange(seq, dtype=jnp.int32)
    index = jnp.where(key_at[None, :] < VALID, rel_index, chunks * LANES)
    index_t = index.T
    indices = jnp.pad(jnp.stack([index, index_t]), ((0, 0), (0, 0), (0, padded_seq - seq)))
    table_t = jnp.pad(rel_table, ((0, chunks * LANES - table_rows), (0, 0))).T.reshape(heads, chunks, LANES)
    bias = bias_tables(indices, table_t)
    gy = out_grad * mim_mask.astype(BF)[:, :, None]
    first, qkv, mixed, attn, hn = front(block_in, qkv_weight, proj_weight, vectors, bias, heads)
    flat = lambda v: v.reshape(tokens, v.shape[-1])
    m, dhn, grad_up, grad_down, grad_bias = mlp(
        flat(hn), flat(gy), vectors, up_bias.reshape(blocks, 1, hidden), up_all, down_all, seq
    )
    fold = lambda v: v.reshape(images, seq, width)
    block_out, dmid, dat, dqkv, ds, gvec, gcol = back(
        block_in, gy, attn, fold(m), fold(dhn), qkv, proj_weight, vectors, bias, heads
    )
    grad_attn = attention_grads(flat(first), flat(dqkv), flat(mixed), flat(dat), blocks)
    input_grad, gvec_one = input_grads(block_in, dqkv, dmid, qkv_weight, vectors)
    by_key = jnp.pad(ds.transpose(1, 0, 2), ((0, 0), (0, (-heads) % 8), (0, 0)))
    sums = table_sums(index_t, by_key, chunks)
    sums = sums.reshape(chunks, 2, -1, LANES).sum(1)[:, :heads]
    grad_table = sums.transpose(1, 0, 2).reshape(heads * chunks * LANES // width, width)
    small = jnp.concatenate(
        [
            gcol[:, :width],
            gcol[:, 2 * width :],
            gvec[:2],
            gvec_one[:2],
            gvec[2:6],
            grad_bias.reshape(-1, width),
            grad_table,
        ]
    )
    return block_out, input_grad, grad_attn, grad_up, grad_down, small


def shards(
    block_in,
    out_grad,
    mim_mask,
    rel_index,
    qkv_weight,
    proj_weight,
    up_weight,
    down_weight,
    vectors,
    up_bias,
    rel_table,
    qkv_master,
    qkv_mean,
    qkv_square,
    proj_master,
    proj_mean,
    proj_square,
    up_master,
    up_mean,
    up_square,
    down_master,
    down_mean,
    down_square,
    vector_mean,
    vector_square,
    bias_mean,
    bias_square,
    table_mean,
    table_square,
):
    width = block_in.shape[2]
    table_rows, heads = rel_table.shape
    wide = lax.axis_size("wide")
    narrow = lax.axis_size("narrow")
    up_all = lax.all_gather(up_weight, "narrow", axis=0)
    down_all = lax.all_gather(down_weight, "narrow", axis=0)
    block_out, input_grad, grad_attn, grad_up, grad_down, small = local_work(
        block_in, out_grad, mim_mask, rel_index, qkv_weight, proj_weight, up_all, down_all, vectors, up_bias, rel_table
    )
    small = summed(small)
    lead = [n for n in range(narrow.bit_length() - 1)]
    trail = [len(lead) + n for n in range(wide.bit_length() - 1)]
    order_a = lead[::-1] + trail[::-1]
    order_b = lead[-1:] + trail[::-1] + lead[:-1]
    cut = lambda v: v.reshape(narrow, wide, width // wide, v.shape[-1])
    up_shard = scattered_sum(cut(grad_up), order_a)
    down_shard = scattered_sum(cut(grad_down), order_b)
    grad_attn = cut(grad_attn)
    half = grad_attn.shape[2] // 2
    attn_shard = jnp.concatenate(
        [scattered_sum(grad_attn[:, :, :half], order_a), scattered_sum(grad_attn[:, :, half:], order_b)]
    )
    split = qkv_master.shape[1]
    qkv_shard, proj_shard = attn_shard[:, :split], attn_shard[:, split:]
    shard_squares = jnp.sum(attn_shard * attn_shard) + jnp.sum(up_shard * up_shard) + jnp.sum(down_shard * down_shard)
    large_squares = summed(jnp.full((1, LANES), shard_squares))[0, 0]
    small_squares = jnp.sum(small * small)
    grad_vectors = small[:10]
    grad_bias = small[10 : 10 + up_bias.shape[0] // width].reshape(up_bias.shape)
    grad_table = small[10 + up_bias.shape[0] // width :].reshape(heads, -1).T[:table_rows]
    grad_norm = jnp.sqrt(large_squares + small_squares)
    clip = jnp.minimum(1.0, max_norm / (grad_norm + clip_eps))
    results = [block_out, input_grad, grad_norm]
    for master, mean, square, grad in (
        (qkv_master, qkv_mean, qkv_square, qkv_shard),
        (proj_master, proj_mean, proj_square, proj_shard),
        (up_master, up_mean, up_square, up_shard),
        (down_master, down_mean, down_square, down_shard),
    ):
        mean_new, square_new, master_new = adam_update(
            master, mean, square, clip * grad, rate_matrix, weight_decay
        )
        results += [mean_new, square_new, master_new, master_new.astype(jnp.bfloat16)]
    for master, mean, square, grad in (
        (vectors, vector_mean, vector_square, grad_vectors),
        (up_bias, bias_mean, bias_square, grad_bias),
        (rel_table, table_mean, table_square, grad_table),
    ):
        mean_new, square_new, master_new = adam_update(
            master, mean, square, clip * grad, rate_small, 0.0
        )
        results += [mean_new, square_new, master_new]
    return tuple(results)


def solution(mesh):
    token = P(("wide", "narrow"), None, None)
    whole_spec = P()
    shard = P("wide", "narrow")
    in_specs = (
        (token, token, P(("wide", "narrow"), None))
        + (whole_spec,) * 3
        + (P(None, "narrow"),) * 2
        + (whole_spec,) * 3
        + (shard,) * 12
        + (whole_spec,) * 6
    )
    out_specs = (token, token, whole_spec) + (shard,) * 16 + (whole_spec,) * 9
    return jax.shard_map(shards, mesh=mesh, in_specs=in_specs, out_specs=out_specs, check_vma=False)
```

time: 818 us -> 360 us (0.44); the launches traced: 806 us -> 359 us
  matrix products: 258 us -> 0 us
  Pallas kernels: 0 us -> 183 us
  waiting for transfers between devices: 233 us -> 62.2 us
  local copies, waits for them, and re-layouts: 157 us -> 18.1 us
  blocking collectives: 41.4 us -> 0 us
  other arithmetic: 88.3 us -> 48.9 us
  starting transfers between devices: 6.74 us -> 28.4 us
    dot_general x34 -> x0, matrix products: 258 us -> none  [the longest x8 73.2 us: one_block(): return jnp.einsum('qkr,rh->hqk', onehot, rel_table, precision=exact_prec)]
    pallas_call x0 -> x7, Pallas kernels: none -> 183 us  [the longest x1 44.5 us: mlp(): pl.pallas_call(functools.partial(mlp_kernel, chunk), grid=(blocks,), in_s...]
    reduce_scatter x4 -> x0, waiting for transfers between devices: 157 us -> none  [the longest x1 81.1 us: shards(): lax.psum_scatter(lax.dot_general(block_rows, up_weight, contract_cols, pr...]
    all_gather x2, waiting for transfers between devices: 75.7 us -> 23.5 us  [the longest x1 23.5 us: shards(): down_all = lax.all_gather(down_weight, 'narrow', axis=0)]
    reduce_sum x17 -> x4, other arithmetic: 54.4 us -> 4.07 us  [the longest x1 1.86 us: shards(): jnp.sum(up_shard * up_shard)]
    psum x1 -> x0, blocking collectives: 41.4 us -> none  [shards(): large_squares = lax.psum(shard_squares, ('wide', 'narrow'))]
    ppermute x0 -> x30, waiting for transfers between devices: none -> 37.3 us  [swap(): return lax.ppermute(value, axis, [(i, i ^ 1 << bit) for i in range(size)])]
    convert_element_type x5 -> x0, local copies, waits for them, and re-layouts: 35.5 us -> none  [the longest x2 25.1 us: shards(): grad_qkv_b = jnp.stack([grad_query, grad_keys, grad_values], 2).reshape(t...]
  transfers between devices with their start and end apart: 7 -> 32, of which waited for: 5 -> 13; matrix products, arithmetic and copies ran while one was open for 31% -> 15% of each run, Pallas kernels for 0% -> 39%
where the time goes in v1:
time: 360 us; the launch traced here: 359 us
  Pallas kernels  183 us (51%)
  waiting for transfers between devices  62.2 us (17%)
  other arithmetic  48.9 us (14%)
  starting transfers between devices  28.4 us (8%)
  between operations  18.5 us (5%)
  local copies, waits for them, and re-layouts  18.1 us (5%)
    pallas_call x1, Pallas kernels, mlp(): pl.pallas_call(functools.partial(mlp_kernel, chunk), grid=(blocks,), in_s...  44.5 us
    pallas_call x1, Pallas kernels, front(): pl.pallas_call(functools.partial(front_kernel, heads), grid=(images,), in...  39.9 us
    ppermute x30, waiting for transfers between devices, swap(): return lax.ppermute(value, axis, [(i, i ^ 1 << bit) for i in range(size)])  37.3 us
    pallas_call x1, Pallas kernels, back(): pl.pallas_call(functools.partial(back_kernel, heads), grid=(images,), in_...  35.5 us
    convert_element_type x16, other arithmetic, scattered_sum(): sent = sum((half(p, 1 - mine).astype(F32) for p in pieces)).astype(BF)  28.9 us
    ppermute x30, starting transfers between devices, swap(): return lax.ppermute(value, axis, [(i, i ^ 1 << bit) for i in range(size)])  28.4 us
    pallas_call x1, Pallas kernels, table_sums(): pl.pallas_call(table_kernel, grid=(1,), in_specs=[whole(index_t.shape), w...  24.9 us
    all_gather x1, waiting for transfers between devices, shards(): down_all = lax.all_gather(down_weight, 'narrow', axis=0)  23.5 us
  transfers between devices with their start and end apart: 32, of which 13 were waited for; matrix products, arithmetic and copies ran while one was open for 15% of the time, Pallas kernels for 39%

profile of v1, /device:TPU:0, one launch (start us, length us, event | category | flops | bytes accessed | tf_op | source)
XLA Modules:
  0.0 359.0 jit_solution(13921033185615196885)
XLA Ops:
  10.4 13.8 %bias_tables.1.bias_ref = f32[2,12,200,200]{3,2,1,0:T(8,128)} custom-call(s32[2,200,256]{2,1,0:T(8,128)} %pad.12.idx_ref, f32[12,6,128]{2,1,0:T(8,128)} %reshape.127.tab_ref), custom_call_target="tpu_custom_call" | custom-call | tf_op jit(solution)/shard_map/bias_tables/pallas_call | solution.py:111
  24.2 39.9 %front.1 = (bf16[5,200,768]{2,1,0:T(8,128)(2,1)}, bf16[5,200,2304]{2,1,0:T(8,128)(2,1)}, bf16[5,200,768]{2,1,0:T(8,128)(2,1)}, f32[5,200,768]{2,1,0:T(8,128)}, bf16[5,200,768]{2,1,0:T(8,128)(2,1)}) custom-call(bf16[5,200,768]{2,1,0:T(8,128)(2,1)} %x_ref.5, bf16[768,2304]{1,0:T(8,128)(2,1)} %wqkv_ref.3, bf16[768,768]{1,0:T(8,128)(2,1)} %wproj_ref.3, ...), custom_call_target="tpu_custom_call" | custom-call | tf_op jit(solution)/shard_map/front/pallas_call | solution.py:206
  64.1 1.3 broadcast_multiply_fusion.gy_ref
  65.5 23.5 %all-gather.7.cloned.1.call-done = bf16[3072,768]{1,0:T(8,128)(2,1)} async-done(((bf16[768,768]{1,0:T(8,128)(2,1)}), bf16[3072,768]{1,0:T(8,128)(2,1)}) %all-gather.7.cloned.1.call-update) | async-done | bytes 4718608 | tf_op jit(solution)/shard_map/all_gather | solution.py:568
  89.0 44.5 %mlp.1 = (f32[1000,768]{1,0:T(8,128)}, f32[1000,768]{1,0:T(8,128)}, bf16[4,768,768]{2,1,0:T(8,128)(2,1)}, bf16[4,768,768]{2,1,0:T(8,128)(2,1)}, f32[4,1,768]{2,1,0:T(1,128)}) custom-call(bf16[1000,768]{1,0:T(8,128)(2,1)} %bitcast.93, bf16[1000,768]{1,0:T(8,128)(2,1)} %bitcast.59, f32[10,768]{1,0:T(8,128)} %vec_ref.7, f32[4,1,768]{2,1,0:T(1,128)} %bitcast.98, ...), custom_call_target="tpu_custom_call" | custom-call | tf_op jit(solution)/shard_map/mlp/pallas_call | solution.py:270
  133.4 3.4 constant_dynamic-slice_fusion.1
  137.1 1.6 constant_dynamic-slice_fusion.2
  139.0 35.5 %back.1 = (bf16[5,200,768]{2,1,0:T(8,128)(2,1)}, f32[5,200,768]{2,1,0:T(8,128)}, bf16[5,200,768]{2,1,0:T(8,128)(2,1)}, bf16[5,200,2304]{2,1,0:T(8,128)(2,1)}, f3...) custom-call(bf16[5,200,768]{2,1,0:T(8,128)(2,1)} %x_ref.5, ...), custom_call_target="tpu_custom_call" | custom-call | tf_op jit(solution)/shard_map/back/pallas_call | solution.py:371
  174.5 12.7 %attention_grads.1 = bf16[4,768,768]{2,1,0:T(8,128)(2,1)} custom-call(bf16[1000,768]{1,0:T(8,128)(2,1)} %bitcast.91, bf16[1000,2304]{1,0:T(8,128)(2,1)} %bitcast.58, bf16[1000,768]{1,0:T(8,128)(2,1)} %bitcast.92, bf16[1000,768]{1,0:T(8,128)(2,1)} %bitcast.94), custom_call_target="tpu_custom_call" | custom-call | tf_op jit(solution)/shard_map/attention_grads/pallas_call | solution.py:402
  187.2 2.8 fusion.28
  190.0 1.3 constant_dynamic-slice_fusion.3
  191.5 1.1 constant_dynamic-slice_fusion
  192.9 3.0 add_convert_fusion
  195.8 1.4 collective-permute-start.16
  197.2 2.2 add_convert_fusion.5
  200.0 2.9 add_convert_fusion.1
  202.9 1.5 collective-permute-start.11
  204.4 1.1 add_convert_fusion.4
  206.9 1.3 slice.50
  208.2 11.7 %input_grads.1 = (f32[5,200,768]{2,1,0:T(8,128)}, f32[8,768]{1,0:T(8,128)}) custom-call(bf16[5,200,768]{2,1,0:T(8,128)(2,1)} %x_ref.5, bf16[5,200,2304]{2,1,0:T(8,128)(2,1)} %get-tuple-element.53.dqkv_ref, f32[5,200,768]{2,1,0:T(8,128)} %get-tuple-element.54.dmid_ref, bf16[768,2304]{1,0:T(8,128)(2,1)} %wqkv_ref.3, f32[10,768]{1,0:T(8,128)} %vec_ref.7), custom_call_target="tpu_custom_call" | custom-call | tf_op jit(solution)/shard_map/input_grads/pallas_call | solution.py:431
  221.5 2.0 pad.14.ds_ref
  223.5 24.9 %table_sums.1 = f32[192,128]{1,0:T(8,128)} custom-call(s32[200,200]{1,0:T(8,128)} %bitcast.90, f32[200,16,200]{2,1,0:T(8,128)} %pad.14.ds_ref), custom_call_target="tpu_custom_call" | custom-call | tf_op jit(solution)/shard_map/table_sums/pallas_call | solution.py:145
  250.0 1.5 collective-permute-start.25
  251.4 2.0 add_convert_fusion.9
  254.0 1.9 add_convert_fusion.8
  255.9 1.5 collective-permute-start.7
  258.0 2.5 add_convert_fusion.2
  260.5 1.5 collective-permute-start.17
  262.0 1.9 add_convert_fusion.13
  263.8 1.1 collective-permute-start.3
  264.9 1.1 collective-permute-done.7
  266.0 1.8 add_convert_fusion.12
  267.8 2.4 collective-permute-start.8
  270.2 2.5 add_convert_fusion.3
  272.7 1.4 collective-permute-start.12
  274.8 12.1 %collective-permute-done.3 = bf16[1,1,2,1,1,48,768]{6,5,4,3,2,1,0:T(8,128)(2,1)} collective-permute-done((bf16[1,1,2,1,1,48,768]{6,5,4,3,2,1,0:T(8,128)(2,1)}, bf16[1,1,2,1,1,48,768]{6,5,4,3,2,1,0:T(8,128)(2,1)}, u32[]{:S(2)}, u32[]{:S(2)}) %collective-permute-start.3) | collective-permute-done | bytes 147488 | tf_op jit(solution)/shard_map/ppermute | solution.py:462
  286.9 1.1 add_convert_fusion.15
  287.9 1.4 collective-permute-start.4
  291.0 1.3 add_convert_fusion.6
  292.3 1.4 collective-permute-start.18
  294.4 1.1 add_bitcast_fusion.1
  295.5 1.4 add_convert_fusion.7
  296.9 3.9 %collective-permute-start.13 = (bf16[1,1,2,1,1,96,768]{6,5,4,3,2,1,0:T(8,128)(2,1)S(1)}, bf16[1,1,2,1,1,96,768]{6,5,4,3,2,1,0:T(8,128)(2,1)S(1)}, u32[]{:S(2)}, u32[]{:S(2)}) collective-permute-start(bf16[1,1,2,1,1,96,768]{6,5,4,3,2,1,0:T(8,128)(2,1)S(1)} %add_convert_fusion.7), channel_id=1, source_target_pairs={{0,8},{4,12},{8,0},{12,4},{16,24},{20,28},{24,16},{28,20},{1,9},{5... | collective-permute-start | bytes 884744 | tf_op jit(solution)/shard_map/ppermute | solution.py:462
  300.8 6.0 %collective-permute-done.18 = bf16[2,1,1,1,1,96,768]{6,5,4,3,2,1,0:T(8,128)(2,1)S(1)} collective-permute-done((bf16[2,1,1,1,1,96,768]{6,5,4,3,2,1,0:T(8,128)(2,1)S(1)}, bf16[2,1,1,1,1,96,768]{6,5,4,3,2,1,0:T(8,128)(2,1)S(1)}, u32[]{:S(2)}, u32[]{:S(2)}) %collective-permute-start.18) | collective-permute-done | bytes 294944 | tf_op jit(solution)/shard_map/ppermute | solution.py:462
  306.8 1.1 add_convert_fusion.10
  308.4 1.1 add_bitcast_fusion
  310.2 1.3 add_convert_fusion.11
  311.6 1.6 collective-permute-done.19
  313.1 1.8 multiply_reduce_fusion
  314.9 5.2 %collective-permute-done.14 = bf16[1,1,1,1,1,96,768]{6,5,4,3,2,1,0:T(8,128)(2,1)S(1)} collective-permute-done((bf16[1,1,1,1,1,96,768]{6,5,4,3,2,1,0:T(8,128)(2,1)S(1)}, bf16[1,1,1,1,1,96,768]{6,5,4,3,2,1,0:T(8,128)(2,1)S(1)}, u32[]{:S(2)}, u32[]{:S(2)}) %collective-permute-start.14) | collective-permute-done | bytes 147488 | tf_op jit(solution)/shard_map/ppermute | solution.py:462
  320.2 1.9 multiply_reduce_fusion.1
  324.1 1.4 collective-permute-start.20
  326.6 1.2 collective-permute-done.20
  327.9 1.5 collective-permute-start.29
  329.3 2.0 collective-permute-done.21
  331.4 4.4 %collective-permute-done.22 = f32[1,128]{1,0:T(1,128)S(1)} collective-permute-done((f32[1,128]{1,0:T(1,128)S(1)}, f32[1,128]{1,0:T(1,128)S(1)}, u32[]{:S(2)}, u32[]{:S(2)}) %collective-permute-start.22) | collective-permute-done | bytes 544 | tf_op jit(solution)/shard_map/ppermute | solution.py:462
  337.0 1.3 collective-permute-start.24
  338.3 2.3 collective-permute-done.24
  341.4 1.5 multiply_subtract_fusion.5
  342.9 1.5 multiply_subtract_fusion.4
  344.4 1.3 multiply_subtract_fusion.6
  345.7 1.7 fusion.24
  347.5 2.1 fusion.26
  349.6 1.4 fusion.18
  (128 shorter events, 16.9 us)
Async XLA Ops:
  7.2 1.5 copy-start.7
  7.2 1.7 copy-start.16
  7.2 2.4 copy-start.23
  7.2 58.2 %all-gather.5.cloned.1.call-start = ((), (), s32[]{:S(2)}) async-start(), calls=%async_computation | async-start | bytes 5898240 | tf_op jit(solution)/shard_map/all_gather | solution.py:567
  8.0 81.0 %all-gather.7.cloned.1.call-start = ((), (), s32[]{:S(2)}) async-start(), calls=%async_computation.1 | async-start | bytes 5898240 | tf_op jit(solution)/shard_map/all_gather | solution.py:568
  8.9 15.3 %copy-start.3 = (s32[200,200]{0,1:T(8,128)}, s32[200,200]{0,1:T(8,128)S(1)}, u32[]{:S(2)}) copy-start(s32[200,200]{0,1:T(8,128)S(1)} %copy.61) | copy-start | bytes 480004
  24.2 39.9 %copy-start.4 = (bf16[5,200,768]{2,1,0:T(8,128)(2,1)S(1)}, bf16[5,200,768]{2,1,0:T(8,128)(2,1)}, u32[]{:S(2)}) copy-start(bf16[5,200,768]{2,1,0:T(8,128)(2,1)} %param.30) | copy-start | bytes 4608004
  133.4 3.7 %copy-start.1 = (bf16[4,768,768]{2,1,0:T(8,128)(2,1)S(1)}, bf16[4,768,768]{2,1,0:T(8,128)(2,1)}, u32[]{:S(2)}) copy-start(bf16[4,768,768]{2,1,0:T(8,128)(2,1)} %get-tuple-element.59) | copy-start | bytes 14155780
  136.9 56.0 %collective-permute-start.15 = (bf16[2,1,2,2,2,96,768]{6,5,4,3,2,1,0:T(8,128)(2,1)}, bf16[2,1,2,2,2,96,768]{6,5,4,3,2,1,0:T(8,128)(2,1)}, u32[]{:S(2)}, u32[]{:S(2)}) collective-permute-start(bf16[2,1,2,2,2,96,768]{6,5,4,3,2,1,0:T(8,128)(2,1)} %constant_dynamic-slice_fusion.1), channel_id=1, source_target_pairs={{0,1},{1,0},{2,3},{3,2},{4,5},{5,4},{6,7},{7,6},{8,9},{9,8},{10,11... | collective-permute-start | bytes 7077896 | tf_op jit(solution)/shard_map/ppermute | solution.py:462
  138.7 61.3 %collective-permute-start.10 = (bf16[2,1,2,2,2,96,768]{6,5,4,3,2,1,0:T(8,128)(2,1)}, bf16[2,1,2,2,2,96,768]{6,5,4,3,2,1,0:T(8,128)(2,1)}, u32[]{:S(2)}, u32[]{:S(2)}) collective-permute-start(bf16[2,1,2,2,2,96,768]{6,5,4,3,2,1,0:T(8,128)(2,1)} %constant_dynamic-slice_fusion.2), channel_id=1, source_target_pairs={{0,1},{1,0},{2,3},{3,2},{4,5},{5,4},{6,7},{7,6},{8,9},{9,8},{10,11... | collective-permute-start | bytes 7077896 | tf_op jit(solution)/shard_map/ppermute | solution.py:462
  190.0 2.6 copy-start
  191.3 6.0 %collective-permute-start = (bf16[2,1,2,2,2,48,768]{6,5,4,3,2,1,0:T(8,128)(2,1)}, bf16[2,1,2,2,2,48,768]{6,5,4,3,2,1,0:T(8,128)(2,1)}, u32[]{:S(2)}, u32[]{:S(2)}) collective-permute-start(bf16[2,1,2,2,2,48,768]{6,5,4,3,2,1,0:T(8,128)(2,1)} %constant_dynamic-slice_fusion.3), channel_id=1, source_target_pairs={{0,1},{1,0},{2,3},{3,2},{4,5},{5,4},{6,7},{7,6},{8,9},{9,8},{10,11... | collective-permute-start | bytes 3538952 | tf_op jit(solution)/shard_map/ppermute | solution.py:462
  192.6 11.8 %collective-permute-start.5 = (bf16[2,1,2,2,2,48,768]{6,5,4,3,2,1,0:T(8,128)(2,1)}, bf16[2,1,2,2,2,48,768]{6,5,4,3,2,1,0:T(8,128)(2,1)S(1)}, u32[]{:S(2)}, u32[]{:S(2)}) collective-permute-start(bf16[2,1,2,2,2,48,768]{6,5,4,3,2,1,0:T(8,128)(2,1)} %constant_dynamic-slice_fusion), channel_id=1, source_target_pairs={{0,1},{1,0},{2,3},{3,2},{4,5},{5,4},{6,7},{7,6},{8,9},{9,8},{10,11... | collective-permute-start | bytes 3538952 | tf_op jit(solution)/shard_map/ppermute | solution.py:462
  195.8 62.2 %collective-permute-start.16 = (bf16[2,1,2,2,1,96,768]{6,5,4,3,2,1,0:T(8,128)(2,1)}, bf16[2,1,2,2,1,96,768]{6,5,4,3,2,1,0:T(8,128)(2,1)}, u32[]{:S(2)}, u32[]{:S(2)}) collective-permute-start(bf16[2,1,2,2,1,96,768]{6,5,4,3,2,1,0:T(8,128)(2,1)} %add_convert_fusion), channel_id=1, source_target_pairs={{0,4},{4,0},{8,12},{12,8},{16,20},{20,16},{24,28},{28,24},{1,5},{5... | collective-permute-start | bytes 3538952 | tf_op jit(solution)/shard_map/ppermute | solution.py:462
  199.4 52.0 %collective-permute-start.1 = (bf16[1,1,2,2,2,48,768]{6,5,4,3,2,1,0:T(8,128)(2,1)}, bf16[1,1,2,2,2,48,768]{6,5,4,3,2,1,0:T(8,128)(2,1)}, u32[]{:S(2)}, u32[]{:S(2)}) collective-permute-start(bf16[1,1,2,2,2,48,768]{6,5,4,3,2,1,0:T(8,128)(2,1)} %add_convert_fusion.5), channel_id=1, source_target_pairs={{0,2},{1,3},{2,0},{3,1},{4,6},{5,7},{6,4},{7,5},{8,10},{9,11},{10,... | collective-permute-start | bytes 1769480 | tf_op jit(solution)/shard_map/ppermute | solution.py:462
  202.9 67.3 %collective-permute-start.11 = (bf16[1,1,2,2,2,96,768]{6,5,4,3,2,1,0:T(8,128)(2,1)}, bf16[1,1,2,2,2,96,768]{6,5,4,3,2,1,0:T(8,128)(2,1)}, u32[]{:S(2)}, u32[]{:S(2)}) collective-permute-start(bf16[1,1,2,2,2,96,768]{6,5,4,3,2,1,0:T(8,128)(2,1)} %add_convert_fusion.1), channel_id=1, source_target_pairs={{0,2},{1,3},{2,0},{3,1},{4,6},{5,7},{6,4},{7,5},{8,10},{9,11},{10,... | collective-permute-start | bytes 3538952 | tf_op jit(solution)/shard_map/ppermute | solution.py:462
  204.4 3.8 %copy-start.6 = (bf16[2,1,2,2,2,48,768]{6,5,4,3,2,1,0:T(8,128)(2,1)}, bf16[2,1,2,2,2,48,768]{6,5,4,3,2,1,0:T(8,128)(2,1)S(1)}, u32[]{:S(2)}) copy-start(bf16[2,1,2,2,2,48,768]{6,5,4,3,2,1,0:T(8,128)(2,1)S(1)} %collective-permute-done.5) | copy-start | bytes 3538948
  205.5 48.5 %collective-permute-start.6 = (bf16[2,1,2,2,1,48,768]{6,5,4,3,2,1,0:T(8,128)(2,1)}, bf16[2,1,2,2,1,48,768]{6,5,4,3,2,1,0:T(8,128)(2,1)}, u32[]{:S(2)}, u32[]{:S(2)}) collective-permute-start(bf16[2,1,2,2,1,48,768]{6,5,4,3,2,1,0:T(8,128)(2,1)} %add_convert_fusion.4), channel_id=1, source_target_pairs={{0,4},{4,0},{8,12},{12,8},{16,20},{20,16},{24,28},{28,24},{1,5},{5... | collective-permute-start | bytes 1769480 | tf_op jit(solution)/shard_map/ppermute | solution.py:462
  208.2 12.4 %copy-start.2 = (f32[12,200,200]{2,1,0:T(8,128)S(1)}, f32[12,200,200]{2,1,0:T(8,128)}, u32[]{:S(2)}) copy-start(f32[12,200,200]{2,1,0:T(8,128)} %get-tuple-element.65) | copy-start | bytes 5760004
  223.5 25.9 %copy-start.22 = (f32[4,1,768]{2,1,0:T(1,128)S(1)}, f32[4,1,768]{2,1,0:T(1,128)}, u32[]{:S(2)}) copy-start(f32[4,1,768]{2,1,0:T(1,128)} %get-tuple-element.64) | copy-start | bytes 36868
  223.5 25.9 %copy-start.24 = (f32[1,2304]{1,0:T(1,128)S(1)}, f32[1,2304]{1,0:T(1,128)}, u32[]{:S(2)}) copy-start(f32[1,2304]{1,0:T(1,128)} %get-tuple-element.61) | copy-start | bytes 27652
  223.5 25.9 %copy-start.21 = (f32[2,768]{1,0:T(2,128)S(1)}, f32[2,768]{1,0:T(2,128)}, u32[]{:S(2)}) copy-start(f32[2,768]{1,0:T(2,128)} %slice.50) | copy-start | bytes 18436
  250.0 7.4 %collective-permute-start.25 = (f32[26,768]{1,0:T(8,128)S(1)}, f32[26,768]{1,0:T(8,128)S(1)}, u32[]{:S(2)}, u32[]{:S(2)}) collective-permute-start(f32[26,768]{1,0:T(8,128)S(1)} %concatenate.7), channel_id=1, source_target_pairs={{0,4},{4,0},{8,12},{12,8},{16,20},{20,16},{24,28},{28,24},{1,5},{5... | collective-permute-start | bytes 239624 | tf_op jit(solution)/shard_map/ppermute | solution.py:462
  253.4 8.6 %collective-permute-start.2 = (bf16[1,1,2,2,1,48,768]{6,5,4,3,2,1,0:T(8,128)(2,1)}, bf16[1,1,2,2,1,48,768]{6,5,4,3,2,1,0:T(8,128)(2,1)}, u32[]{:S(2)}, u32[]{:S(2)}) collective-permute-start(bf16[1,1,2,2,1,48,768]{6,5,4,3,2,1,0:T(8,128)(2,1)} %add_convert_fusion.9), channel_id=1, source_target_pairs={{0,4},{4,0},{8,12},{12,8},{16,20},{20,16},{24,28},{28,24},{1,5},{5... | collective-permute-start | bytes 884744 | tf_op jit(solution)/shard_map/ppermute | solution.py:462
  255.9 10.1 %collective-permute-start.7 = (bf16[2,1,2,1,1,48,768]{6,5,4,3,2,1,0:T(8,128)(2,1)}, bf16[2,1,2,1,1,48,768]{6,5,4,3,2,1,0:T(8,128)(2,1)S(1)}, u32[]{:S(2)}, u32[]{:S(2)}) collective-permute-start(bf16[2,1,2,1,1,48,768]{6,5,4,3,2,1,0:T(8,128)(2,1)} %add_convert_fusion.8), channel_id=1, source_target_pairs={{0,8},{4,12},{8,0},{12,4},{16,24},{20,28},{24,16},{28,20},{1,9},{5... | collective-permute-start | bytes 884744 | tf_op jit(solution)/shard_map/ppermute | solution.py:462
  257.4 16.7 %collective-permute-start.26 = (f32[26,768]{1,0:T(8,128)S(1)}, f32[26,768]{1,0:T(8,128)S(1)}, u32[]{:S(2)}, u32[]{:S(2)}) collective-permute-start(f32[26,768]{1,0:T(8,128)S(1)} %add.1109), channel_id=1, source_target_pairs={{0,8},{4,12},{8,0},{12,4},{16,24},{20,28},{24,16},{28,20},{1,9},{5... | collective-permute-start | bytes 239624 | tf_op jit(solution)/shard_map/ppermute | solution.py:462
  260.5 30.5 %collective-permute-start.17 = (bf16[2,1,2,1,1,96,768]{6,5,4,3,2,1,0:T(8,128)(2,1)}, bf16[2,1,2,1,1,96,768]{6,5,4,3,2,1,0:T(8,128)(2,1)S(1)}, u32[]{:S(2)}, u32[]{:S(2)}) collective-permute-start(bf16[2,1,2,1,1,96,768]{6,5,4,3,2,1,0:T(8,128)(2,1)} %add_convert_fusion.2), channel_id=1, source_target_pairs={{0,8},{4,12},{8,0},{12,4},{16,24},{20,28},{24,16},{28,20},{1,9},{5... | collective-permute-start | bytes 1769480 | tf_op jit(solution)/shard_map/ppermute | solution.py:462
  263.8 23.0 %collective-permute-start.3 = (bf16[1,1,2,1,1,48,768]{6,5,4,3,2,1,0:T(8,128)(2,1)}, bf16[1,1,2,1,1,48,768]{6,5,4,3,2,1,0:T(8,128)(2,1)}, u32[]{:S(2)}, u32[]{:S(2)}) collective-permute-start(bf16[1,1,2,1,1,48,768]{6,5,4,3,2,1,0:T(8,128)(2,1)} %add_convert_fusion.13), channel_id=1, source_target_pairs={{0,8},{4,12},{8,0},{12,4},{16,24},{20,28},{24,16},{28,20},{1,9},{5... | collective-permute-start | bytes 442376 | tf_op jit(solution)/shard_map/ppermute | solution.py:462
  266.0 8.1 %copy-start.14 = (bf16[2,1,2,1,1,48,768]{6,5,4,3,2,1,0:T(8,128)(2,1)}, bf16[2,1,2,1,1,48,768]{6,5,4,3,2,1,0:T(8,128)(2,1)S(1)}, u32[]{:S(2)}) copy-start(bf16[2,1,2,1,1,48,768]{6,5,4,3,2,1,0:T(8,128)(2,1)S(1)} %collective-permute-done.7) | copy-start | bytes 884740
  267.8 21.5 %collective-permute-start.8 = (bf16[2,1,1,1,1,48,768]{6,5,4,3,2,1,0:T(8,128)(2,1)}, bf16[2,1,1,1,1,48,768]{6,5,4,3,2,1,0:T(8,128)(2,1)}, u32[]{:S(2)}, u32[]{:S(2)}) collective-permute-start(bf16[2,1,1,1,1,48,768]{6,5,4,3,2,1,0:T(8,128)(2,1)} %add_convert_fusion.12), channel_id=1, source_target_pairs={{0,16},{4,20},{8,24},{12,28},{16,0},{20,4},{24,8},{28,12},{1,17},{... | collective-permute-start | bytes 442376 | tf_op jit(solution)/shard_map/ppermute | solution.py:462
  272.7 22.8 %collective-permute-start.12 = (bf16[1,1,2,2,1,96,768]{6,5,4,3,2,1,0:T(8,128)(2,1)}, bf16[1,1,2,2,1,96,768]{6,5,4,3,2,1,0:T(8,128)(2,1)}, u32[]{:S(2)}, u32[]{:S(2)}) collective-permute-start(bf16[1,1,2,2,1,96,768]{6,5,4,3,2,1,0:T(8,128)(2,1)} %add_convert_fusion.3), channel_id=1, source_target_pairs={{0,4},{4,0},{8,12},{12,8},{16,20},{20,16},{24,28},{28,24},{1,5},{5... | collective-permute-start | bytes 1769480 | tf_op jit(solution)/shard_map/ppermute | solution.py:462
  274.2 51.4 %collective-permute-start.27 = (f32[26,768]{1,0:T(8,128)S(1)}, f32[26,768]{1,0:T(8,128)}, u32[]{:S(2)}, u32[]{:S(2)}) collective-permute-start(f32[26,768]{1,0:T(8,128)S(1)} %add.1110), channel_id=1, source_target_pairs={{0,16},{4,20},{8,24},{12,28},{16,0},{20,4},{24,8},{28,12},{1,17},{... | collective-permute-start | bytes 239624 | tf_op jit(solution)/shard_map/ppermute | solution.py:462
  287.9 6.5 %collective-permute-start.4 = (bf16[1,1,1,1,1,48,768]{6,5,4,3,2,1,0:T(8,128)(2,1)S(1)}, bf16[1,1,1,1,1,48,768]{6,5,4,3,2,1,0:T(8,128)(2,1)S(1)}, u32[]{:S(2)}, u32[]{:S(2)}) collective-permute-start(bf16[1,1,1,1,1,48,768]{6,5,4,3,2,1,0:T(8,128)(2,1)S(1)} %add_convert_fusion.15), channel_id=1, source_target_pairs={{0,16},{4,20},{8,24},{12,28},{16,0},{20,4},{24,8},{28,12},{1,17},{... | collective-permute-start | bytes 221192 | tf_op jit(solution)/shard_map/ppermute | solution.py:462
  290.4 18.0 %collective-permute-start.9 = (bf16[1,1,1,1,1,48,768]{6,5,4,3,2,1,0:T(8,128)(2,1)S(1)}, bf16[1,1,1,1,1,48,768]{6,5,4,3,2,1,0:T(8,128)(2,1)S(1)}, u32[]{:S(2)}, u32[]{:S(2)}) collective-permute-start(bf16[1,1,1,1,1,48,768]{6,5,4,3,2,1,0:T(8,128)(2,1)S(1)} %add_convert_fusion.14), channel_id=1, source_target_pairs={{0,2},{1,3},{2,0},{3,1},{4,6},{5,7},{6,4},{7,5},{8,10},{9,11},{10,... | collective-permute-start | bytes 221192 | tf_op jit(solution)/shard_map/ppermute | solution.py:462
  292.3 14.5 %collective-permute-start.18 = (bf16[2,1,1,1,1,96,768]{6,5,4,3,2,1,0:T(8,128)(2,1)S(1)}, bf16[2,1,1,1,1,96,768]{6,5,4,3,2,1,0:T(8,128)(2,1)S(1)}, u32[]{:S(2)}, u32[]{:S(2)}) collective-permute-start(bf16[2,1,1,1,1,96,768]{6,5,4,3,2,1,0:T(8,128)(2,1)S(1)} %add_convert_fusion.6), channel_id=1, source_target_pairs={{0,16},{4,20},{8,24},{12,28},{16,0},{20,4},{24,8},{28,12},{1,17},{... | collective-permute-start | bytes 884744 | tf_op jit(solution)/shard_map/ppermute | solution.py:462
  296.9 13.3 %collective-permute-start.13 = (bf16[1,1,2,1,1,96,768]{6,5,4,3,2,1,0:T(8,128)(2,1)S(1)}, bf16[1,1,2,1,1,96,768]{6,5,4,3,2,1,0:T(8,128)(2,1)S(1)}, u32[]{:S(2)}, u32[]{:S(2)}) collective-permute-start(bf16[1,1,2,1,1,96,768]{6,5,4,3,2,1,0:T(8,128)(2,1)S(1)} %add_convert_fusion.7), channel_id=1, source_target_pairs={{0,8},{4,12},{8,0},{12,4},{16,24},{20,28},{24,16},{28,20},{1,9},{5... | collective-permute-start | bytes 884744 | tf_op jit(solution)/shard_map/ppermute | solution.py:462
  307.9 5.2 %collective-permute-start.19 = (bf16[1,1,1,1,1,96,768]{6,5,4,3,2,1,0:T(8,128)(2,1)S(1)}, bf16[1,1,1,1,1,96,768]{6,5,4,3,2,1,0:T(8,128)(2,1)S(1)}, u32[]{:S(2)}, u32[]{:S(2)}) collective-permute-start(bf16[1,1,1,1,1,96,768]{6,5,4,3,2,1,0:T(8,128)(2,1)S(1)} %add_convert_fusion.10), channel_id=1, source_target_pairs={{0,2},{1,3},{2,0},{3,1},{4,6},{5,7},{6,4},{7,5},{8,10},{9,11},{10,... | collective-permute-start | bytes 442376 | tf_op jit(solution)/shard_map/ppermute | solution.py:462
  309.5 31.9 %copy-start.5 = (f32[10,768]{1,0:T(8,128)S(1)}, f32[10,768]{1,0:T(8,128)}, u32[]{:S(2)}) copy-start(f32[10,768]{1,0:T(8,128)} %vec_ref.7) | copy-start | bytes 92164
  310.2 32.7 %copy-start.17 = (f32[732,12]{0,1:T(8,128)S(1)}, f32[732,12]{0,1:T(8,128)}, u32[]{:S(2)}) copy-start(f32[732,12]{0,1:T(8,128)} %param.39) | copy-start | bytes 105412
  310.2 34.2 %copy-start.20 = (f32[3072]{0:T(1024)S(1)}, f32[3072]{0:T(1024)}, u32[]{:S(2)}) copy-start(f32[3072]{0:T(1024)} %param.38) | copy-start | bytes 36868
  310.2 35.6 %copy-start.18 = (f32[96,192]{1,0:T(8,128)S(1)}, f32[96,192]{1,0:T(8,128)}, u32[]{:S(2)}) copy-start(f32[96,192]{1,0:T(8,128)} %param.43) | copy-start | bytes 221188
  310.2 35.6 %copy-start.19 = (f32[96,192]{1,0:T(8,128)S(1)}, f32[96,192]{1,0:T(8,128)}, u32[]{:S(2)}) copy-start(f32[96,192]{1,0:T(8,128)} %param.45) | copy-start | bytes 221188
  311.5 36.0 %copy-start.15 = (f32[96,576]{1,0:T(8,128)S(1)}, f32[96,576]{1,0:T(8,128)}, u32[]{:S(2)}) copy-start(f32[96,576]{1,0:T(8,128)} %param.40) | copy-start | bytes 663556
  311.5 8.7 %collective-permute-start.14 = (bf16[1,1,1,1,1,96,768]{6,5,4,3,2,1,0:T(8,128)(2,1)S(1)}, bf16[1,1,1,1,1,96,768]{6,5,4,3,2,1,0:T(8,128)(2,1)S(1)}, u32[]{:S(2)}, u32[]{:S(2)}) collective-permute-start(bf16[1,1,1,1,1,96,768]{6,5,4,3,2,1,0:T(8,128)(2,1)S(1)} %add_convert_fusion.11), channel_id=1, source_target_pairs={{0,16},{4,20},{8,24},{12,28},{16,0},{20,4},{24,8},{28,12},{1,17},{... | collective-permute-start | bytes 442376 | tf_op jit(solution)/shard_map/ppermute | solution.py:462
  322.0 27.5 %copy-start.8 = (f32[96,768]{1,0:T(8,128)S(1)}, f32[96,768]{1,0:T(8,128)}, u32[]{:S(2)}) copy-start(f32[96,768]{1,0:T(8,128)} %param.49) | copy-start | bytes 884740
  322.0 27.5 %copy-start.9 = (f32[96,768]{1,0:T(8,128)S(1)}, f32[96,768]{1,0:T(8,128)}, u32[]{:S(2)}) copy-start(f32[96,768]{1,0:T(8,128)} %param.51) | copy-start | bytes 884740
  322.0 27.5 %copy-start.10 = (f32[96,768]{1,0:T(8,128)S(1)}, f32[96,768]{1,0:T(8,128)}, u32[]{:S(2)}) copy-start(f32[96,768]{1,0:T(8,128)} %param.50) | copy-start | bytes 884740
  322.0 27.5 %copy-start.11 = (f32[96,768]{1,0:T(8,128)S(1)}, f32[96,768]{1,0:T(8,128)}, u32[]{:S(2)}) copy-start(f32[96,768]{1,0:T(8,128)} %param.46) | copy-start | bytes 884740
  322.0 27.5 %copy-start.12 = (f32[96,768]{1,0:T(8,128)S(1)}, f32[96,768]{1,0:T(8,128)}, u32[]{:S(2)}) copy-start(f32[96,768]{1,0:T(8,128)} %param.48) | copy-start | bytes 884740
  322.0 27.6 %copy-start.13 = (f32[96,768]{1,0:T(8,128)S(1)}, f32[96,768]{1,0:T(8,128)}, u32[]{:S(2)}) copy-start(f32[96,768]{1,0:T(8,128)} %param.47) | copy-start | bytes 884740
  324.1 3.6 %collective-permute-start.20 = (f32[1,128]{1,0:T(1,128)S(1)}, f32[1,128]{1,0:T(1,128)S(1)}, u32[]{:S(2)}, u32[]{:S(2)}) collective-permute-start(f32[1,128]{1,0:T(1,128)S(1)} %broadcast_in_dim.19), channel_id=1, source_target_pairs={{0,4},{4,0},{8,12},{12,8},{16,20},{20,16},{24,28},{28,24},{1,5},{5... | collective-permute-start | bytes 1544 | tf_op jit(solution)/shard_map/ppermute | solution.py:462
  326.5 1.4 collective-permute-start.28
  327.8 3.6 collective-permute-start.21
  327.9 8.0 %collective-permute-start.29 = (f32[26,768]{1,0:T(8,128)S(1)}, f32[26,768]{1,0:T(8,128)S(1)}, u32[]{:S(2)}, u32[]{:S(2)}) collective-permute-start(f32[26,768]{1,0:T(8,128)S(1)} %add.1112), channel_id=1, source_target_pairs={{0,2},{1,3},{2,0},{3,1},{4,6},{5,7},{6,4},{7,5},{8,10},{9,11},{10,... | collective-permute-start | bytes 239624 | tf_op jit(solution)/shard_map/ppermute | solution.py:462
  331.4 4.5 %collective-permute-start.22 = (f32[1,128]{1,0:T(1,128)S(1)}, f32[1,128]{1,0:T(1,128)S(1)}, u32[]{:S(2)}, u32[]{:S(2)}) collective-permute-start(f32[1,128]{1,0:T(1,128)S(1)} %fusion.30), channel_id=1, source_target_pairs={{0,16},{4,20},{8,24},{12,28},{16,0},{20,4},{24,8},{28,12},{1,17},{... | collective-permute-start | bytes 1544 | tf_op jit(solution)/shard_map/ppermute | solution.py:462
  335.8 1.2 collective-permute-start.23
  337.0 3.6 collective-permute-start.24
Sparse Core Ops, SparseCore 0:
  9.6 40.1 all-gather.4
  51.4 37.5 all-gather.6

commit v2 on v1

--- a/solution.py
+++ b/solution.py
@@ -25,6 +25,9 @@
 ROWS_ROWS = (((0,), (0,)), ((), ()))
 COLS_COLS = (((1,), (1,)), ((), ()))
 VMEM_LIMIT = 60000 * 1024
+UNROLL_F = 3
+UNROLL_B = 3
+UNROLL_T = 8
 
 
 def mm(a, b):
@@ -82,15 +85,15 @@
     ]
 
 
-def bias_kernel(idx_ref, tab_ref, out_ref):
-    heads, seq = out_ref.shape[1], out_ref.shape[2]
+def bias_kernel(idx_ref, tab_ref, out_ref, back_ref, work_ref):
+    heads, seq = out_ref.shape[0], out_ref.shape[1]
     chunks = tab_ref.shape[1]
 
     def rows(step, carry):
         at = pl.multiple_of(step * 8, 8)
-        for half in range(idx_ref.shape[2] // LANES):
-            width = min(LANES, seq - half * LANES)
-            index = idx_ref[0, pl.ds(at, 8), half * LANES : (half + 1) * LANES]
+        for half in range(idx_ref.shape[1] // LANES):
+            cols = slice(half * LANES, (half + 1) * LANES)
+            index = idx_ref[pl.ds(at, 8), cols]
             low, high = index & (LANES - 1), index >> 7
             match = [high == c for c in range(chunks)]
             for h in range(heads):
@@ -99,24 +102,33 @@
                     row = jnp.broadcast_to(tab_ref[h, c : c + 1, :], (8, LANES))
                     taken = jnp.take_along_axis(row, low, axis=1, mode="promise_in_bounds")
                     found = jnp.where(match[c], taken, found)
-                out_ref[0, h, pl.ds(at, 8), half * LANES : half * LANES + width] = found[:, :width]
+                work_ref[h, pl.ds(at, 8), cols] = found
         return carry
 
     lax.fori_loop(0, seq // 8, rows, 0)
 
-
-def bias_tables(indices, table_rows):
-    both, seq, padded = indices.shape
+    def turn(h, carry):
+        out_ref[h] = work_ref[h, :seq, :seq]
+        back_ref[h] = work_ref[h].T[:seq, :seq]
+        return carry
+
+    lax.fori_loop(0, heads, turn, 0)
+
+
+def bias_tables(index, table_rows):
+    seq, padded = index.shape
     heads, chunks, _ = table_rows.shape
+    shape = (heads, seq, seq)
     return pl.pallas_call(
         bias_kernel,
-        grid=(both,),
-        in_specs=[per_step(indices.shape), whole(table_rows.shape)],
-        out_specs=per_step((both, heads, seq, seq)),
-        out_shape=jax.ShapeDtypeStruct((both, heads, seq, seq), F32),
+        grid=(1,),
+        in_specs=[whole(index.shape), whole(table_rows.shape)],
+        out_specs=[whole(shape)] * 2,
+        out_shape=[jax.ShapeDtypeStruct(shape, F32)] * 2,
+        scratch_shapes=[pltpu.VMEM((heads, padded, padded), F32)],
         compiler_params=params(),
         name="bias_tables",
-    )(indices, table_rows)
+    )(index, table_rows)
 
 
 def table_kernel(idx_ref, ds_ref, out_ref):
@@ -136,7 +148,7 @@
         parts = jnp.concatenate([jnp.where(high_all == c, both, 0.0) for c in range(chunks)], 0)
         return total + mm_nt(parts.astype(BF), onehot)
 
-    out_ref[...] = lax.fori_loop(0, seq, one_key, jnp.zeros(out_ref.shape, F32), unroll=2)
+    out_ref[...] = lax.fori_loop(0, seq, one_key, jnp.zeros(out_ref.shape, F32), unroll=UNROLL_T)
 
 
 def table_sums(index_t, grads, chunks):
@@ -179,7 +191,7 @@
         out = None
         for e in range(per):
             qm = q * jnp.where(masks[e], scale, 0.0).astype(BF)
-            s = mm_nt(qm, k) + bias_ref[0, g * per + e]
+            s = mm_nt(qm, k) + bias_ref[g * per + e]
             p = jnp.exp(s - jnp.max(s, -1, keepdims=True))
             p = p * (1.0 / jnp.sum(p, -1, keepdims=True))
             mixed = mm(p.astype(BF), v)
@@ -187,7 +199,7 @@
         o_ref[0, :, pl.ds(at, pair)] = out.astype(BF)
         return carry
 
-    lax.fori_loop(0, width // pair, one_pair, 0)
+    lax.fori_loop(0, width // pair, one_pair, 0, unroll=UNROLL_F)
     attn = mm(o_ref[0], wproj_ref[...]) + vec_ref[2:3, :]
     attn_ref[0] = attn
     middle, _ = normalized(x + vec_ref[8:9, :] * attn)
@@ -211,7 +223,7 @@
             fixed(qkv_weight.shape),
             fixed(proj_weight.shape),
             fixed(vectors.shape),
-            pl.BlockSpec((1,) + bias.shape[1:], lambda i: (0, 0, 0, 0), pipeline_mode=pl.Buffered(1)),
+            fixed(bias.shape),
         ],
         out_specs=[per_step(s.shape) for s in shapes],
         out_shape=shapes,
@@ -220,55 +232,41 @@
     )(x, qkv_weight, proj_weight, vectors, bias)
 
 
-def mlp_kernel(chunk, hn_ref, gy_ref, vec_ref, bup_ref, wup_ref, wdn_ref, m_ref, dhn_ref, gup_ref, gdn_ref, gb_ref, dm_ref, z_ref, du_ref):
+def mlp_in_kernel(chunk, hn_ref, gy_ref, vec_ref, bup_ref, wup_ref, z_ref, slope_ref, gdn_ref, dm_ref, turned_ref):
     tokens = hn_ref.shape[0]
-    first = pl.program_id(0) == 0
-
-    @pl.when(first)
+
+    @pl.when(pl.program_id(0) == 0)
     def _():
-        m_ref[...] = jnp.zeros_like(m_ref)
-        dhn_ref[...] = jnp.zeros_like(dhn_ref)
-
         def rows(step, carry):
             at = pl.ds(pl.multiple_of(step * chunk, chunk), chunk)
             dm_ref[at, :] = (vec_ref[9:10, :] * gy_ref[at, :].astype(F32)).astype(BF)
             return carry
 
         lax.fori_loop(0, tokens // chunk, rows, 0)
-
-    gb_ref[...] = jnp.zeros_like(gb_ref)
+        turned_ref[...] = dm_ref[...].T
 
     def rows(step, carry):
         at = pl.ds(pl.multiple_of(step * chunk, chunk), chunk)
         u = mm(hn_ref[at, :], wup_ref[0]) + bup_ref[0]
         gate = 0.5 * (1.0 + lax.erf(u * 0.7071067811865476))
-        z = (u * gate).astype(BF)
-        slope = gate + u * jnp.exp(-0.5 * u * u) * 0.3989422804014327
-        z_ref[at, :] = z
-        m_ref[at, :] += mm_nt(z, wdn_ref[0])
-        du = (mm(dm_ref[at, :], wdn_ref[0]) * slope).astype(BF)
-        du_ref[at, :] = du
-        gb_ref[0] += jnp.sum(du.astype(F32), 0, keepdims=True)
-        dhn_ref[at, :] += mm_nt(du, wup_ref[0])
+        z_ref[0, at, :] = (u * gate).astype(BF)
+        slope_ref[0, at, :] = (gate + u * jnp.exp(-0.5 * u * u) * 0.3989422804014327).astype(BF)
         return carry
 
     lax.fori_loop(0, tokens // chunk, rows, 0)
-    gdn_ref[0] = mm_tn(dm_ref[...], z_ref[...]).astype(BF)
-    gup_ref[0] = mm_tn(hn_ref[...], du_ref[...]).astype(BF)
-
-
-def mlp(hn, gy, vectors, up_bias, up_all, down_all, chunk):
+    gdn_ref[0] = mm(turned_ref[...], z_ref[0]).astype(BF)
+
+
+def mlp_in(hn, gy, vectors, up_bias, up_all, chunk):
     tokens, width = hn.shape
     blocks, _, hidden = up_all.shape
     shapes = [
-        jax.ShapeDtypeStruct((tokens, width), F32),
-        jax.ShapeDtypeStruct((tokens, width), F32),
+        jax.ShapeDtypeStruct((blocks, tokens, hidden), BF),
+        jax.ShapeDtypeStruct((blocks, tokens, hidden), BF),
         jax.ShapeDtypeStruct((blocks, width, hidden), BF),
-        jax.ShapeDtypeStruct((blocks, width, hidden), BF),
-        jax.ShapeDtypeStruct((blocks, 1, hidden), F32),
     ]
     return pl.pallas_call(
-        functools.partial(mlp_kernel, chunk),
+        functools.partial(mlp_in_kernel, chunk),
         grid=(blocks,),
         in_specs=[
             fixed(hn.shape),
@@ -276,18 +274,58 @@
             fixed(vectors.shape),
             per_step(up_bias.shape),
             per_step(up_all.shape),
-            per_step(down_all.shape),
         ],
+        out_specs=[per_step(s.shape) for s in shapes] + [fixed((tokens, width))],
+        out_shape=shapes + [jax.ShapeDtypeStruct((tokens, width), BF)],
+        scratch_shapes=[pltpu.VMEM((width, tokens), BF)],
+        compiler_params=params(),
+        name="mlp_in",
+    )(hn, gy, vectors, up_bias, up_all)
+
+
+def mlp_out_kernel(chunk, hn_ref, dm_ref, z_ref, slope_ref, wup_ref, wdn_ref, m_ref, dhn_ref, gup_ref, gb_ref, du_ref, turned_ref):
+    tokens = hn_ref.shape[0]
+
+    @pl.when(pl.program_id(0) == 0)
+    def _():
+        m_ref[...] = jnp.zeros_like(m_ref)
+        dhn_ref[...] = jnp.zeros_like(dhn_ref)
+        turned_ref[...] = hn_ref[...].T
+
+    gb_ref[...] = jnp.zeros_like(gb_ref)
+
+    def rows(step, carry):
+        at = pl.ds(pl.multiple_of(step * chunk, chunk), chunk)
+        m_ref[at, :] += mm_nt(z_ref[0, at, :], wdn_ref[0])
+        du = (mm(dm_ref[at, :], wdn_ref[0]) * slope_ref[0, at, :].astype(F32)).astype(BF)
+        du_ref[at, :] = du
+        gb_ref[0] += jnp.sum(du.astype(F32), 0, keepdims=True)
+        dhn_ref[at, :] += mm_nt(du, wup_ref[0])
+        return carry
+
+    lax.fori_loop(0, tokens // chunk, rows, 0)
+    gup_ref[0] = mm(turned_ref[...], du_ref[...]).astype(BF)
+
+
+def mlp_out(hn, dm, z, slope, up_all, down_all, chunk):
+    tokens, width = hn.shape
+    blocks, _, hidden = up_all.shape
+    shapes = [
+        jax.ShapeDtypeStruct((tokens, width), F32),
+        jax.ShapeDtypeStruct((tokens, width), F32),
+        jax.ShapeDtypeStruct((blocks, width, hidden), BF),
+        jax.ShapeDtypeStruct((blocks, 1, hidden), F32),
+    ]
+    return pl.pallas_call(
+        functools.partial(mlp_out_kernel, chunk),
+        grid=(blocks,),
+        in_specs=[fixed(hn.shape), fixed(dm.shape)] + [per_step(v.shape) for v in (z, slope, up_all, down_all)],
         out_specs=[fixed(s.shape) for s in shapes[:2]] + [per_step(s.shape) for s in shapes[2:]],
         out_shape=shapes,
-        scratch_shapes=[
-            pltpu.VMEM((tokens, width), BF),
-            pltpu.VMEM((tokens, hidden), BF),
-            pltpu.VMEM((tokens, hidden), BF),
-        ],
-        compiler_params=params(),
-        name="mlp",
-    )(hn, gy, vectors, up_bias, up_all, down_all)
+        scratch_shapes=[pltpu.VMEM((tokens, hidden), BF), pltpu.VMEM((width, tokens), BF)],
+        compiler_params=params(),
+        name="mlp_out",
+    )(hn, dm, z, slope, up_all, down_all)
 
 
 def back_kernel(
@@ -336,7 +374,7 @@
             pick = jnp.where(masks[e], scale, 0.0).astype(BF)
             keep = jnp.where(masks[e], 1.0, 0.0).astype(BF)
             qm, km, dom = q * pick, k * pick, do * keep
-            s = mm_nt(k, qm) + bias_ref[0, g * per + e]
+            s = mm_nt(k, qm) + bias_ref[g * per + e]
             p = jnp.exp(s - jnp.max(s, 0, keepdims=True))
             p = p * (1.0 / jnp.sum(p, 0, keepdims=True))
             dv_e = mm(p.astype(BF), dom)
@@ -354,7 +392,7 @@
             gcol_ref[:, pl.ds(at + part * width, pair)] += jnp.sum(rounded.astype(F32), 0, keepdims=True)
         return carry
 
-    lax.fori_loop(0, width // pair, one_pair, 0)
+    lax.fori_loop(0, width // pair, one_pair, 0, unroll=UNROLL_B)
 
 
 def back(x, gy, attn, m, dhn, qkv, proj_weight, vectors, bias, heads):
@@ -375,7 +413,7 @@
         + [
             fixed(proj_weight.shape),
             fixed(vectors.shape),
-            pl.BlockSpec((1,) + bias.shape[1:], lambda i: (1, 0, 0, 0), pipeline_mode=pl.Buffered(1)),
+            fixed(bias.shape),
         ],
         out_specs=[per_step(s.shape) for s in shapes[:4]] + [fixed(s.shape) for s in shapes[4:]],
         out_shape=shapes,
@@ -385,14 +423,16 @@
     )(x, gy, attn, m, dhn, qkv, proj_weight, vectors, bias)
 
 
-def grads_kernel(blocks, a_ref, dqkv_ref, o_ref, dat_ref, out_ref):
+def grads_kernel(blocks, a_ref, dqkv_ref, o_ref, dat_ref, out_ref, turned_a, turned_o):
     wide_cols, thin_cols = dqkv_ref.shape[1] // blocks, dat_ref.shape[1] // blocks
+    turned_a[...] = a_ref[...].T
+    turned_o[...] = o_ref[...].T
     for n in range(blocks):
-        out_ref[n, :, :wide_cols] = mm_tn(
-            a_ref[...], dqkv_ref[:, n * wide_cols : (n + 1) * wide_cols]
+        out_ref[n, :, :wide_cols] = mm(
+            turned_a[...], dqkv_ref[:, n * wide_cols : (n + 1) * wide_cols]
         ).astype(BF)
-        out_ref[n, :, wide_cols:] = mm_tn(
-            o_ref[...], dat_ref[:, n * thin_cols : (n + 1) * thin_cols]
+        out_ref[n, :, wide_cols:] = mm(
+            turned_o[...], dat_ref[:, n * thin_cols : (n + 1) * thin_cols]
         ).astype(BF)
 
 
@@ -405,6 +445,7 @@
         in_specs=[whole(v.shape) for v in (first, dqkv, mixed, dat)],
         out_specs=whole((blocks, width, cols)),
         out_shape=jax.ShapeDtypeStruct((blocks, width, cols), BF),
+        scratch_shapes=[pltpu.VMEM((width, first.shape[0]), BF)] * 2,
         compiler_params=params(),
         name="attention_grads",
     )(first, dqkv, mixed, dat)
@@ -496,18 +537,17 @@
     key_at = jnp.arange(seq, dtype=jnp.int32)
     index = jnp.where(key_at[None, :] < VALID, rel_index, chunks * LANES)
     index_t = index.T
-    indices = jnp.pad(jnp.stack([index, index_t]), ((0, 0), (0, 0), (0, padded_seq - seq)))
+    padded = jnp.pad(index, ((0, 0), (0, padded_seq - seq)))
     table_t = jnp.pad(rel_table, ((0, chunks * LANES - table_rows), (0, 0))).T.reshape(heads, chunks, LANES)
-    bias = bias_tables(indices, table_t)
+    bias, bias_t = bias_tables(padded, table_t)
     gy = out_grad * mim_mask.astype(BF)[:, :, None]
     first, qkv, mixed, attn, hn = front(block_in, qkv_weight, proj_weight, vectors, bias, heads)
     flat = lambda v: v.reshape(tokens, v.shape[-1])
-    m, dhn, grad_up, grad_down, grad_bias = mlp(
-        flat(hn), flat(gy), vectors, up_bias.reshape(blocks, 1, hidden), up_all, down_all, seq
-    )
+    z, slope, grad_down, dm = mlp_in(flat(hn), flat(gy), vectors, up_bias.reshape(blocks, 1, hidden), up_all, seq)
+    m, dhn, grad_up, grad_bias = mlp_out(flat(hn), dm, z, slope, up_all, down_all, seq)
     fold = lambda v: v.reshape(images, seq, width)
     block_out, dmid, dat, dqkv, ds, gvec, gcol = back(
-        block_in, gy, attn, fold(m), fold(dhn), qkv, proj_weight, vectors, bias, heads
+        block_in, gy, attn, fold(m), fold(dhn), qkv, proj_weight, vectors, bias_t, heads
     )
     grad_attn = attention_grads(flat(first), flat(dqkv), flat(mixed), flat(dat), blocks)
     input_grad, gvec_one = input_grads(block_in, dqkv, dmid, qkv_weight, vectors)

time: 360 us -> 335 us (0.931)
  Pallas kernels: 183 us -> 162 us
  waiting for transfers between devices: 62.2 us -> 54.7 us
    pallas_call x1, Pallas kernels: 39.9 us -> 26.7 us  [front(): pl.pallas_call(functools.partial(front_kernel, heads), grid=(images,), in...]
    pallas_call x1, Pallas kernels: 24.9 us -> 12.3 us  [table_sums(): pl.pallas_call(table_kernel, grid=(1,), in_specs=[whole(index_t.shape), w...]
    pallas_call x2 -> x3, Pallas kernels: 58.3 us -> 67.7 us  [the longest x1 36.7 us: mlp_out(): pl.pallas_call(functools.partial(mlp_out_kernel, chunk), grid=(blocks,),...]
    all_gather x1, waiting for transfers between devices: 23.5 us -> 14.9 us  [shards(): down_all = lax.all_gather(down_weight, 'narrow', axis=0)]
    pallas_call x1, Pallas kernels: 35.5 us -> 30.9 us  [back(): pl.pallas_call(functools.partial(back_kernel, heads), grid=(images,), in_...]
  transfers between devices with their start and end apart: 32 -> 32, of which waited for: 13 -> 15; matrix products, arithmetic and copies ran while one was open for 15% -> 18% of each run, Pallas kernels for 39% -> 49%
where the time goes in v2:
time: 335 us; the launch traced here: 334 us
  Pallas kernels  162 us (48%)
  waiting for transfers between devices  54.7 us (16%)
  other arithmetic  50.7 us (15%)
  starting transfers between devices  28.9 us (9%)
  local copies, waits for them, and re-layouts  19.1 us (6%)
  between operations  18.5 us (6%)
    ppermute x30, waiting for transfers between devices, swap(): return lax.ppermute(value, axis, [(i, i ^ 1 << bit) for i in range(size)])  37.6 us
    pallas_call x1, Pallas kernels, mlp_out(): pl.pallas_call(functools.partial(mlp_out_kernel, chunk), grid=(blocks,),...  36.7 us
    pallas_call x1, Pallas kernels, back(): pl.pallas_call(functools.partial(back_kernel, heads), grid=(images,), in_...  30.9 us
    convert_element_type x16, other arithmetic, scattered_sum(): sent = sum((half(p, 1 - mine).astype(F32) for p in pieces)).astype(BF)  29 us
    ppermute x30, starting transfers between devices, swap(): return lax.ppermute(value, axis, [(i, i ^ 1 << bit) for i in range(size)])  28.8 us
    pallas_call x1, Pallas kernels, front(): pl.pallas_call(functools.partial(front_kernel, heads), grid=(images,), in...  26.7 us
    pallas_call x1, Pallas kernels, mlp_in(): pl.pallas_call(functools.partial(mlp_in_kernel, chunk), grid=(blocks,), i...  20.7 us
    all_gather x1, waiting for transfers between devices, shards(): down_all = lax.all_gather(down_weight, 'narrow', axis=0)  14.9 us
  transfers between devices with their start and end apart: 32, of which 15 were waited for; matrix products, arithmetic and copies ran while one was open for 18% of the time, Pallas kernels for 49%

profile of v2, /device:TPU:0, one launch (start us, length us, event | category | flops | bytes accessed | tf_op | source)
XLA Modules:
  0.0 333.8 jit_solution(528512187751892322)
XLA Ops:
  10.4 10.4 %bias_tables.1 = (f32[12,200,200]{2,1,0:T(8,128)}, f32[12,200,200]{2,1,0:T(8,128)}) custom-call(s32[200,256]{1,0:T(8,128)} %pad.12.clone.idx_ref, f32[12,6,128]{2,1,0:T(8,128)} %reshape.128.tab_ref), custom_call_target="tpu_custom_call" | custom-call | tf_op jit(solution)/shard_map/bias_tables/pallas_call | solution.py:122
  20.8 26.7 %front.1 = (bf16[5,200,768]{2,1,0:T(8,128)(2,1)}, bf16[5,200,2304]{2,1,0:T(8,128)(2,1)}, bf16[5,200,768]{2,1,0:T(8,128)(2,1)}, f32[5,200,768]{2,1,0:T(8,128)}, bf16[5,200,768]{2,1,0:T(8,128)(2,1)}) custom-call(bf16[5,200,768]{2,1,0:T(8,128)(2,1)} %x_ref.5, bf16[768,2304]{1,0:T(8,128)(2,1)} %wqkv_ref.3, bf16[768,768]{1,0:T(8,128)(2,1)} %wproj_ref.3, ...), custom_call_target="tpu_custom_call" | custom-call | tf_op jit(solution)/shard_map/front/pallas_call | solution.py:218
  47.6 1.3 broadcast_multiply_fusion.gy_ref
  49.8 20.7 %mlp_in.1 = (bf16[4,1000,768]{2,1,0:T(8,128)(2,1)}, bf16[4,1000,768]{2,1,0:T(8,128)(2,1)}, bf16[4,768,768]{2,1,0:T(8,128)(2,1)}, bf16[1000,768]{1,0:T(8,128)(2,1)}) custom-call(bf16[1000,768]{1,0:T(8,128)(2,1)} %bitcast.72, bf16[1000,768]{1,0:T(8,128)(2,1)} %bitcast.58, f32[10,768]{1,0:T(8,128)} %vec_ref.7, f32[4,1,768]{2,1,0:T(1,128)} %bitcast.95, ...), custom_call_target="tpu_custom_call" | custom-call | tf_op jit(solution)/shard_map/mlp_in/pallas_call | solution.py:268
  70.5 3.2 constant_dynamic-slice_fusion.1
  73.9 14.9 %all-gather.7.cloned.1.call-done = bf16[3072,768]{1,0:T(8,128)(2,1)} async-done(((bf16[768,768]{1,0:T(8,128)(2,1)}), bf16[3072,768]{1,0:T(8,128)(2,1)}) %all-gather.7.cloned.1.call-update) | async-done | bytes 4718608 | tf_op jit(solution)/shard_map/all_gather | solution.py:608
  88.8 36.7 %mlp_out.1 = (f32[1000,768]{1,0:T(8,128)}, f32[1000,768]{1,0:T(8,128)}, bf16[4,768,768]{2,1,0:T(8,128)(2,1)}, f32[4,1,768]{2,1,0:T(1,128)}) custom-call(bf16[1000,768]{1,0:T(8,128)(2,1)} %bitcast.73, bf16[1000,768]{1,0:T(8,128)(2,1)} %get-tuple-element.55.dm_ref, bf16[4,1000,768]{2,1,0:T(8,128)(2,1)} %get-tuple-element.56.z_ref, ...), custom_call_target="tpu_custom_call" | custom-call | tf_op jit(solution)/shard_map/mlp_out/pallas_call | solution.py:319
  125.5 3.2 constant_dynamic-slice_fusion.2
  129.0 30.9 %back.1 = (bf16[5,200,768]{2,1,0:T(8,128)(2,1)}, f32[5,200,768]{2,1,0:T(8,128)}, bf16[5,200,768]{2,1,0:T(8,128)(2,1)}, bf16[5,200,2304]{2,1,0:T(8,128)(2,1)}, f3...) custom-call(bf16[5,200,768]{2,1,0:T(8,128)(2,1)} %x_ref.5, ...), custom_call_target="tpu_custom_call" | custom-call | tf_op jit(solution)/shard_map/back/pallas_call | solution.py:409
  159.9 12.7 %attention_grads.1 = bf16[4,768,768]{2,1,0:T(8,128)(2,1)} custom-call(bf16[1000,768]{1,0:T(8,128)(2,1)} %bitcast.89, bf16[1000,2304]{1,0:T(8,128)(2,1)} %bitcast.57, bf16[1000,768]{1,0:T(8,128)(2,1)} %bitcast.90, bf16[1000,768]{1,0:T(8,128)(2,1)} %bitcast.91), custom_call_target="tpu_custom_call" | custom-call | tf_op jit(solution)/shard_map/attention_grads/pallas_call | solution.py:442
  172.6 2.8 fusion.28
  175.4 1.2 constant_dynamic-slice_fusion.3
  176.9 1.1 constant_dynamic-slice_fusion
  178.3 1.6 collective-permute-done
  179.8 1.4 add_convert_fusion.5
  181.6 3.0 add_convert_fusion
  184.6 1.7 collective-permute-start.16
  186.3 2.1 add_convert_fusion.4
  188.7 3.0 add_convert_fusion.1
  191.6 1.7 collective-permute-start.11
  194.1 11.6 %input_grads.1 = (f32[5,200,768]{2,1,0:T(8,128)}, f32[8,768]{1,0:T(8,128)}) custom-call(bf16[5,200,768]{2,1,0:T(8,128)(2,1)} %x_ref.5, bf16[5,200,2304]{2,1,0:T(8,128)(2,1)} %get-tuple-element.63.dqkv_ref, f32[5,200,768]{2,1,0:T(8,128)} %get-tuple-element.64.dmid_ref, bf16[768,2304]{1,0:T(8,128)(2,1)} %wqkv_ref.3, f32[10,768]{1,0:T(8,128)} %vec_ref.7), custom_call_target="tpu_custom_call" | custom-call | tf_op jit(solution)/shard_map/input_grads/pallas_call | solution.py:472
  206.4 2.5 copy.72
  208.9 2.0 pad.14.ds_ref
  211.0 12.3 %table_sums.1 = f32[192,128]{1,0:T(8,128)} custom-call(s32[200,200]{1,0:T(8,128)} %fusion.30.idx_ref, f32[200,16,200]{2,1,0:T(8,128)} %pad.14.ds_ref), custom_call_target="tpu_custom_call" | custom-call | tf_op jit(solution)/shard_map/table_sums/pallas_call | solution.py:157
  224.8 1.5 collective-permute-start.25
  226.4 2.0 add_convert_fusion.9
  228.9 1.9 add_convert_fusion.8
  230.8 1.5 collective-permute-start.7
  233.8 2.4 add_convert_fusion.2
  236.2 1.5 collective-permute-start.17
  237.7 1.9 add_convert_fusion.13
  240.9 1.8 add_convert_fusion.12
  242.7 2.4 collective-permute-start.8
  245.1 2.5 add_convert_fusion.3
  247.6 1.5 collective-permute-start.12
  249.7 12.1 %collective-permute-done.3 = bf16[1,1,2,1,1,48,768]{6,5,4,3,2,1,0:T(8,128)(2,1)} collective-permute-done((bf16[1,1,2,1,1,48,768]{6,5,4,3,2,1,0:T(8,128)(2,1)}, bf16[1,1,2,1,1,48,768]{6,5,4,3,2,1,0:T(8,128)(2,1)}, u32[]{:S(2)}, u32[]{:S(2)}) %collective-permute-start.3) | collective-permute-done | bytes 147488 | tf_op jit(solution)/shard_map/ppermute | solution.py:503
  261.8 1.1 add_convert_fusion.15
  262.8 1.5 collective-permute-start.4
  266.0 1.3 add_convert_fusion.6
  267.3 1.4 collective-permute-start.18
  269.2 1.1 add_bitcast_fusion.1
  270.3 1.4 add_convert_fusion.7
  271.7 4.0 %collective-permute-start.13 = (bf16[1,1,2,1,1,96,768]{6,5,4,3,2,1,0:T(8,128)(2,1)S(1)}, bf16[1,1,2,1,1,96,768]{6,5,4,3,2,1,0:T(8,128)(2,1)S(1)}, u32[]{:S(2)}, u32[]{:S(2)}) collective-permute-start(bf16[1,1,2,1,1,96,768]{6,5,4,3,2,1,0:T(8,128)(2,1)S(1)} %add_convert_fusion.7), channel_id=1, source_target_pairs={{0,8},{4,12},{8,0},{12,4},{16,24},{20,28},{24,16},{28,20},{1,9},{5... | collective-permute-start | bytes 884744 | tf_op jit(solution)/shard_map/ppermute | solution.py:503
  275.8 5.9 %collective-permute-done.18 = bf16[2,1,1,1,1,96,768]{6,5,4,3,2,1,0:T(8,128)(2,1)S(1)} collective-permute-done((bf16[2,1,1,1,1,96,768]{6,5,4,3,2,1,0:T(8,128)(2,1)S(1)}, bf16[2,1,1,1,1,96,768]{6,5,4,3,2,1,0:T(8,128)(2,1)S(1)}, u32[]{:S(2)}, u32[]{:S(2)}) %collective-permute-start.18) | collective-permute-done | bytes 294944 | tf_op jit(solution)/shard_map/ppermute | solution.py:503
  281.7 1.1 add_convert_fusion.10
  283.4 1.1 add_bitcast_fusion
  285.2 1.3 add_convert_fusion.11
  286.6 1.5 collective-permute-done.19
  288.0 1.8 multiply_reduce_fusion
  289.8 5.1 %collective-permute-done.14 = bf16[1,1,1,1,1,96,768]{6,5,4,3,2,1,0:T(8,128)(2,1)S(1)} collective-permute-done((bf16[1,1,1,1,1,96,768]{6,5,4,3,2,1,0:T(8,128)(2,1)S(1)}, bf16[1,1,1,1,1,96,768]{6,5,4,3,2,1,0:T(8,128)(2,1)S(1)}, u32[]{:S(2)}, u32[]{:S(2)}) %collective-permute-start.14) | collective-permute-done | bytes 147488 | tf_op jit(solution)/shard_map/ppermute | solution.py:503
  295.0 1.9 multiply_reduce_fusion.1
  298.9 1.6 collective-permute-start.20
  301.5 1.1 collective-permute-done.20
  302.8 1.5 collective-permute-start.29
  304.3 1.8 collective-permute-done.21
  306.4 4.2 %collective-permute-done.22 = f32[1,128]{1,0:T(1,128)S(1)} collective-permute-done((f32[1,128]{1,0:T(1,128)S(1)}, f32[1,128]{1,0:T(1,128)S(1)}, u32[]{:S(2)}, u32[]{:S(2)}) %collective-permute-start.22) | collective-permute-done | bytes 544 | tf_op jit(solution)/shard_map/ppermute | solution.py:503
  311.8 1.5 collective-permute-start.24
  313.3 2.1 collective-permute-done.24
  316.2 1.5 multiply_subtract_fusion.5
  317.7 1.5 multiply_subtract_fusion.4
  319.2 1.3 multiply_subtract_fusion.6
  320.5 1.7 fusion.24
  322.3 2.1 fusion.26
  324.4 1.4 fusion.18
  (121 shorter events, 19.0 us)
Async XLA Ops:
  7.2 1.5 copy-start.11
  7.2 1.9 copy-start.12
  7.2 2.5 copy-start.19
  7.2 42.6 %all-gather.5.cloned.1.call-start = ((), (), s32[]{:S(2)}) async-start(), calls=%async_computation | async-start | bytes 5898240 | tf_op jit(solution)/shard_map/all_gather | solution.py:607
  8.0 80.9 %all-gather.7.cloned.1.call-start = ((), (), s32[]{:S(2)}) async-start(), calls=%async_computation.1 | async-start | bytes 5898240 | tf_op jit(solution)/shard_map/all_gather | solution.py:608
  20.8 26.8 %copy-start.1 = (bf16[5,200,768]{2,1,0:T(8,128)(2,1)S(1)}, bf16[5,200,768]{2,1,0:T(8,128)(2,1)}, u32[]{:S(2)}) copy-start(bf16[5,200,768]{2,1,0:T(8,128)(2,1)} %param.30) | copy-start | bytes 4608004
  73.7 107.9 %collective-permute-start.15 = (bf16[2,1,2,2,2,96,768]{6,5,4,3,2,1,0:T(8,128)(2,1)}, bf16[2,1,2,2,2,96,768]{6,5,4,3,2,1,0:T(8,128)(2,1)}, u32[]{:S(2)}, u32[]{:S(2)}) collective-permute-start(bf16[2,1,2,2,2,96,768]{6,5,4,3,2,1,0:T(8,128)(2,1)} %constant_dynamic-slice_fusion.1), channel_id=1, source_target_pairs={{0,1},{1,0},{2,3},{3,2},{4,5},{5,4},{6,7},{7,6},{8,9},{9,8},{10,11... | collective-permute-start | bytes 7077896 | tf_op jit(solution)/shard_map/ppermute | solution.py:503
  128.7 59.9 %collective-permute-start.10 = (bf16[2,1,2,2,2,96,768]{6,5,4,3,2,1,0:T(8,128)(2,1)}, bf16[2,1,2,2,2,96,768]{6,5,4,3,2,1,0:T(8,128)(2,1)}, u32[]{:S(2)}, u32[]{:S(2)}) collective-permute-start(bf16[2,1,2,2,2,96,768]{6,5,4,3,2,1,0:T(8,128)(2,1)} %constant_dynamic-slice_fusion.2), channel_id=1, source_target_pairs={{0,1},{1,0},{2,3},{3,2},{4,5},{5,4},{6,7},{7,6},{8,9},{9,8},{10,11... | collective-permute-start | bytes 7077896 | tf_op jit(solution)/shard_map/ppermute | solution.py:503
  175.4 2.6 copy-start
  176.6 3.2 collective-permute-start
  178.0 8.3 %collective-permute-start.5 = (bf16[2,1,2,2,2,48,768]{6,5,4,3,2,1,0:T(8,128)(2,1)}, bf16[2,1,2,2,2,48,768]{6,5,4,3,2,1,0:T(8,128)(2,1)}, u32[]{:S(2)}, u32[]{:S(2)}) collective-permute-start(bf16[2,1,2,2,2,48,768]{6,5,4,3,2,1,0:T(8,128)(2,1)} %constant_dynamic-slice_fusion), channel_id=1, source_target_pairs={{0,1},{1,0},{2,3},{3,2},{4,5},{5,4},{6,7},{7,6},{8,9},{9,8},{10,11... | collective-permute-start | bytes 3538952 | tf_op jit(solution)/shard_map/ppermute | solution.py:503
  181.2 45.2 %collective-permute-start.1 = (bf16[1,1,2,2,2,48,768]{6,5,4,3,2,1,0:T(8,128)(2,1)S(1)}, bf16[1,1,2,2,2,48,768]{6,5,4,3,2,1,0:T(8,128)(2,1)}, u32[]{:S(2)}, u32[]{:S(2)}) collective-permute-start(bf16[1,1,2,2,2,48,768]{6,5,4,3,2,1,0:T(8,128)(2,1)S(1)} %add_convert_fusion.5), channel_id=1, source_target_pairs={{0,2},{1,3},{2,0},{3,1},{4,6},{5,7},{6,4},{7,5},{8,10},{9,11},{10,... | collective-permute-start | bytes 1769480 | tf_op jit(solution)/shard_map/ppermute | solution.py:503
  184.6 49.2 %collective-permute-start.16 = (bf16[2,1,2,2,1,96,768]{6,5,4,3,2,1,0:T(8,128)(2,1)}, bf16[2,1,2,2,1,96,768]{6,5,4,3,2,1,0:T(8,128)(2,1)}, u32[]{:S(2)}, u32[]{:S(2)}) collective-permute-start(bf16[2,1,2,2,1,96,768]{6,5,4,3,2,1,0:T(8,128)(2,1)} %add_convert_fusion), channel_id=1, source_target_pairs={{0,4},{4,0},{8,12},{12,8},{16,20},{20,16},{24,28},{28,24},{1,5},{5... | collective-permute-start | bytes 3538952 | tf_op jit(solution)/shard_map/ppermute | solution.py:503
  188.3 5.8 %copy-start.17 = (f32[8,768]{1,0:T(8,128)S(1)}, f32[8,768]{1,0:T(8,128)}, u32[]{:S(2)}) copy-start(f32[8,768]{1,0:T(8,128)} %get-tuple-element.72) | copy-start | bytes 73732
  188.3 40.6 %collective-permute-start.6 = (bf16[2,1,2,2,1,48,768]{6,5,4,3,2,1,0:T(8,128)(2,1)}, bf16[2,1,2,2,1,48,768]{6,5,4,3,2,1,0:T(8,128)(2,1)}, u32[]{:S(2)}, u32[]{:S(2)}) collective-permute-start(bf16[2,1,2,2,1,48,768]{6,5,4,3,2,1,0:T(8,128)(2,1)} %add_convert_fusion.4), channel_id=1, source_target_pairs={{0,4},{4,0},{8,12},{12,8},{16,20},{20,16},{24,28},{28,24},{1,5},{5... | collective-permute-start | bytes 1769480 | tf_op jit(solution)/shard_map/ppermute | solution.py:503
  191.6 53.5 %collective-permute-start.11 = (bf16[1,1,2,2,2,96,768]{6,5,4,3,2,1,0:T(8,128)(2,1)}, bf16[1,1,2,2,2,96,768]{6,5,4,3,2,1,0:T(8,128)(2,1)}, u32[]{:S(2)}, u32[]{:S(2)}) collective-permute-start(bf16[1,1,2,2,2,96,768]{6,5,4,3,2,1,0:T(8,128)(2,1)} %add_convert_fusion.1), channel_id=1, source_target_pairs={{0,2},{1,3},{2,0},{3,1},{4,6},{5,7},{6,4},{7,5},{8,10},{9,11},{10,... | collective-permute-start | bytes 3538952 | tf_op jit(solution)/shard_map/ppermute | solution.py:503
  211.0 13.3 %copy-start.18 = (f32[4,1,768]{2,1,0:T(1,128)S(1)}, f32[4,1,768]{2,1,0:T(1,128)}, u32[]{:S(2)}) copy-start(f32[4,1,768]{2,1,0:T(1,128)} %get-tuple-element.74) | copy-start | bytes 36868
  211.0 13.3 %copy-start.20 = (f32[1,2304]{1,0:T(1,128)S(1)}, f32[1,2304]{1,0:T(1,128)}, u32[]{:S(2)}) copy-start(f32[1,2304]{1,0:T(1,128)} %get-tuple-element.71) | copy-start | bytes 27652
  224.8 7.4 %collective-permute-start.25 = (f32[26,768]{1,0:T(8,128)S(1)}, f32[26,768]{1,0:T(8,128)}, u32[]{:S(2)}, u32[]{:S(2)}) collective-permute-start(f32[26,768]{1,0:T(8,128)S(1)} %concatenate.7), channel_id=1, source_target_pairs={{0,4},{4,0},{8,12},{12,8},{16,20},{20,16},{24,28},{28,24},{1,5},{5... | collective-permute-start | bytes 239624 | tf_op jit(solution)/shard_map/ppermute | solution.py:503
  228.3 9.4 %collective-permute-start.2 = (bf16[1,1,2,2,1,48,768]{6,5,4,3,2,1,0:T(8,128)(2,1)}, bf16[1,1,2,2,1,48,768]{6,5,4,3,2,1,0:T(8,128)(2,1)}, u32[]{:S(2)}, u32[]{:S(2)}) collective-permute-start(bf16[1,1,2,2,1,48,768]{6,5,4,3,2,1,0:T(8,128)(2,1)} %add_convert_fusion.9), channel_id=1, source_target_pairs={{0,4},{4,0},{8,12},{12,8},{16,20},{20,16},{24,28},{28,24},{1,5},{5... | collective-permute-start | bytes 884744 | tf_op jit(solution)/shard_map/ppermute | solution.py:503
  230.8 10.1 %collective-permute-start.7 = (bf16[2,1,2,1,1,48,768]{6,5,4,3,2,1,0:T(8,128)(2,1)}, bf16[2,1,2,1,1,48,768]{6,5,4,3,2,1,0:T(8,128)(2,1)S(1)}, u32[]{:S(2)}, u32[]{:S(2)}) collective-permute-start(bf16[2,1,2,1,1,48,768]{6,5,4,3,2,1,0:T(8,128)(2,1)} %add_convert_fusion.8), channel_id=1, source_target_pairs={{0,8},{4,12},{8,0},{12,4},{16,24},{20,28},{24,16},{28,20},{1,9},{5... | collective-permute-start | bytes 884744 | tf_op jit(solution)/shard_map/ppermute | solution.py:503
  233.2 15.9 %collective-permute-start.26 = (f32[26,768]{1,0:T(8,128)S(1)}, f32[26,768]{1,0:T(8,128)S(1)}, u32[]{:S(2)}, u32[]{:S(2)}) collective-permute-start(f32[26,768]{1,0:T(8,128)S(1)} %add.1109), channel_id=1, source_target_pairs={{0,8},{4,12},{8,0},{12,4},{16,24},{20,28},{24,16},{28,20},{1,9},{5... | collective-permute-start | bytes 239624 | tf_op jit(solution)/shard_map/ppermute | solution.py:503
  236.2 29.8 %collective-permute-start.17 = (bf16[2,1,2,1,1,96,768]{6,5,4,3,2,1,0:T(8,128)(2,1)}, bf16[2,1,2,1,1,96,768]{6,5,4,3,2,1,0:T(8,128)(2,1)S(1)}, u32[]{:S(2)}, u32[]{:S(2)}) collective-permute-start(bf16[2,1,2,1,1,96,768]{6,5,4,3,2,1,0:T(8,128)(2,1)} %add_convert_fusion.2), channel_id=1, source_target_pairs={{0,8},{4,12},{8,0},{12,4},{16,24},{20,28},{24,16},{28,20},{1,9},{5... | collective-permute-start | bytes 1769480 | tf_op jit(solution)/shard_map/ppermute | solution.py:503
  239.6 22.2 %collective-permute-start.3 = (bf16[1,1,2,1,1,48,768]{6,5,4,3,2,1,0:T(8,128)(2,1)}, bf16[1,1,2,1,1,48,768]{6,5,4,3,2,1,0:T(8,128)(2,1)}, u32[]{:S(2)}, u32[]{:S(2)}) collective-permute-start(bf16[1,1,2,1,1,48,768]{6,5,4,3,2,1,0:T(8,128)(2,1)} %add_convert_fusion.13), channel_id=1, source_target_pairs={{0,8},{4,12},{8,0},{12,4},{16,24},{20,28},{24,16},{28,20},{1,9},{5... | collective-permute-start | bytes 442376 | tf_op jit(solution)/shard_map/ppermute | solution.py:503
  240.9 8.2 %copy-start.9 = (bf16[2,1,2,1,1,48,768]{6,5,4,3,2,1,0:T(8,128)(2,1)}, bf16[2,1,2,1,1,48,768]{6,5,4,3,2,1,0:T(8,128)(2,1)S(1)}, u32[]{:S(2)}) copy-start(bf16[2,1,2,1,1,48,768]{6,5,4,3,2,1,0:T(8,128)(2,1)S(1)} %collective-permute-done.7) | copy-start | bytes 884740
  242.7 21.6 %collective-permute-start.8 = (bf16[2,1,1,1,1,48,768]{6,5,4,3,2,1,0:T(8,128)(2,1)}, bf16[2,1,1,1,1,48,768]{6,5,4,3,2,1,0:T(8,128)(2,1)}, u32[]{:S(2)}, u32[]{:S(2)}) collective-permute-start(bf16[2,1,1,1,1,48,768]{6,5,4,3,2,1,0:T(8,128)(2,1)} %add_convert_fusion.12), channel_id=1, source_target_pairs={{0,16},{4,20},{8,24},{12,28},{16,0},{20,4},{24,8},{28,12},{1,17},{... | collective-permute-start | bytes 442376 | tf_op jit(solution)/shard_map/ppermute | solution.py:503
  247.6 22.7 %collective-permute-start.12 = (bf16[1,1,2,2,1,96,768]{6,5,4,3,2,1,0:T(8,128)(2,1)}, bf16[1,1,2,2,1,96,768]{6,5,4,3,2,1,0:T(8,128)(2,1)}, u32[]{:S(2)}, u32[]{:S(2)}) collective-permute-start(bf16[1,1,2,2,1,96,768]{6,5,4,3,2,1,0:T(8,128)(2,1)} %add_convert_fusion.3), channel_id=1, source_target_pairs={{0,4},{4,0},{8,12},{12,8},{16,20},{20,16},{24,28},{28,24},{1,5},{5... | collective-permute-start | bytes 1769480 | tf_op jit(solution)/shard_map/ppermute | solution.py:503
  249.1 51.4 %collective-permute-start.27 = (f32[26,768]{1,0:T(8,128)S(1)}, f32[26,768]{1,0:T(8,128)}, u32[]{:S(2)}, u32[]{:S(2)}) collective-permute-start(f32[26,768]{1,0:T(8,128)S(1)} %add.1110), channel_id=1, source_target_pairs={{0,16},{4,20},{8,24},{12,28},{16,0},{20,4},{24,8},{28,12},{1,17},{... | collective-permute-start | bytes 239624 | tf_op jit(solution)/shard_map/ppermute | solution.py:503
  262.8 6.4 %collective-permute-start.4 = (bf16[1,1,1,1,1,48,768]{6,5,4,3,2,1,0:T(8,128)(2,1)S(1)}, bf16[1,1,1,1,1,48,768]{6,5,4,3,2,1,0:T(8,128)(2,1)S(1)}, u32[]{:S(2)}, u32[]{:S(2)}) collective-permute-start(bf16[1,1,1,1,1,48,768]{6,5,4,3,2,1,0:T(8,128)(2,1)S(1)} %add_convert_fusion.15), channel_id=1, source_target_pairs={{0,16},{4,20},{8,24},{12,28},{16,0},{20,4},{24,8},{28,12},{1,17},{... | collective-permute-start | bytes 221192 | tf_op jit(solution)/shard_map/ppermute | solution.py:503
  265.4 18.1 %collective-permute-start.9 = (bf16[1,1,1,1,1,48,768]{6,5,4,3,2,1,0:T(8,128)(2,1)S(1)}, bf16[1,1,1,1,1,48,768]{6,5,4,3,2,1,0:T(8,128)(2,1)S(1)}, u32[]{:S(2)}, u32[]{:S(2)}) collective-permute-start(bf16[1,1,1,1,1,48,768]{6,5,4,3,2,1,0:T(8,128)(2,1)S(1)} %add_convert_fusion.14), channel_id=1, source_target_pairs={{0,2},{1,3},{2,0},{3,1},{4,6},{5,7},{6,4},{7,5},{8,10},{9,11},{10,... | collective-permute-start | bytes 221192 | tf_op jit(solution)/shard_map/ppermute | solution.py:503
  267.3 14.4 %collective-permute-start.18 = (bf16[2,1,1,1,1,96,768]{6,5,4,3,2,1,0:T(8,128)(2,1)S(1)}, bf16[2,1,1,1,1,96,768]{6,5,4,3,2,1,0:T(8,128)(2,1)S(1)}, u32[]{:S(2)}, u32[]{:S(2)}) collective-permute-start(bf16[2,1,1,1,1,96,768]{6,5,4,3,2,1,0:T(8,128)(2,1)S(1)} %add_convert_fusion.6), channel_id=1, source_target_pairs={{0,16},{4,20},{8,24},{12,28},{16,0},{20,4},{24,8},{28,12},{1,17},{... | collective-permute-start | bytes 884744 | tf_op jit(solution)/shard_map/ppermute | solution.py:503
  271.7 13.5 %collective-permute-start.13 = (bf16[1,1,2,1,1,96,768]{6,5,4,3,2,1,0:T(8,128)(2,1)S(1)}, bf16[1,1,2,1,1,96,768]{6,5,4,3,2,1,0:T(8,128)(2,1)S(1)}, u32[]{:S(2)}, u32[]{:S(2)}) collective-permute-start(bf16[1,1,2,1,1,96,768]{6,5,4,3,2,1,0:T(8,128)(2,1)S(1)} %add_convert_fusion.7), channel_id=1, source_target_pairs={{0,8},{4,12},{8,0},{12,4},{16,24},{20,28},{24,16},{28,20},{1,9},{5... | collective-permute-start | bytes 884744 | tf_op jit(solution)/shard_map/ppermute | solution.py:503
  282.8 5.2 %collective-permute-start.19 = (bf16[1,1,1,1,1,96,768]{6,5,4,3,2,1,0:T(8,128)(2,1)S(1)}, bf16[1,1,1,1,1,96,768]{6,5,4,3,2,1,0:T(8,128)(2,1)S(1)}, u32[]{:S(2)}, u32[]{:S(2)}) collective-permute-start(bf16[1,1,1,1,1,96,768]{6,5,4,3,2,1,0:T(8,128)(2,1)S(1)} %add_convert_fusion.10), channel_id=1, source_target_pairs={{0,2},{1,3},{2,0},{3,1},{4,6},{5,7},{6,4},{7,5},{8,10},{9,11},{10,... | collective-permute-start | bytes 442376 | tf_op jit(solution)/shard_map/ppermute | solution.py:503
  284.5 31.7 %copy-start.2 = (f32[10,768]{1,0:T(8,128)S(1)}, f32[10,768]{1,0:T(8,128)}, u32[]{:S(2)}) copy-start(f32[10,768]{1,0:T(8,128)} %vec_ref.7) | copy-start | bytes 92164
  285.2 32.5 %copy-start.13 = (f32[732,12]{0,1:T(8,128)S(1)}, f32[732,12]{0,1:T(8,128)}, u32[]{:S(2)}) copy-start(f32[732,12]{0,1:T(8,128)} %param.39) | copy-start | bytes 105412
  285.2 34.0 %copy-start.16 = (f32[3072]{0:T(1024)S(1)}, f32[3072]{0:T(1024)}, u32[]{:S(2)}) copy-start(f32[3072]{0:T(1024)} %param.38) | copy-start | bytes 36868
  285.2 35.4 %copy-start.14 = (f32[96,192]{1,0:T(8,128)S(1)}, f32[96,192]{1,0:T(8,128)}, u32[]{:S(2)}) copy-start(f32[96,192]{1,0:T(8,128)} %param.43) | copy-start | bytes 221188
  285.2 35.4 %copy-start.15 = (f32[96,192]{1,0:T(8,128)S(1)}, f32[96,192]{1,0:T(8,128)}, u32[]{:S(2)}) copy-start(f32[96,192]{1,0:T(8,128)} %param.45) | copy-start | bytes 221188
  286.5 35.8 %copy-start.10 = (f32[96,576]{1,0:T(8,128)S(1)}, f32[96,576]{1,0:T(8,128)}, u32[]{:S(2)}) copy-start(f32[96,576]{1,0:T(8,128)} %param.40) | copy-start | bytes 663556
  286.5 8.5 %collective-permute-start.14 = (bf16[1,1,1,1,1,96,768]{6,5,4,3,2,1,0:T(8,128)(2,1)S(1)}, bf16[1,1,1,1,1,96,768]{6,5,4,3,2,1,0:T(8,128)(2,1)S(1)}, u32[]{:S(2)}, u32[]{:S(2)}) collective-permute-start(bf16[1,1,1,1,1,96,768]{6,5,4,3,2,1,0:T(8,128)(2,1)S(1)} %add_convert_fusion.11), channel_id=1, source_target_pairs={{0,16},{4,20},{8,24},{12,28},{16,0},{20,4},{24,8},{28,12},{1,17},{... | collective-permute-start | bytes 442376 | tf_op jit(solution)/shard_map/ppermute | solution.py:503
  296.8 27.5 %copy-start.3 = (f32[96,768]{1,0:T(8,128)S(1)}, f32[96,768]{1,0:T(8,128)}, u32[]{:S(2)}) copy-start(f32[96,768]{1,0:T(8,128)} %param.49) | copy-start | bytes 884740
  296.8 27.5 %copy-start.4 = (f32[96,768]{1,0:T(8,128)S(1)}, f32[96,768]{1,0:T(8,128)}, u32[]{:S(2)}) copy-start(f32[96,768]{1,0:T(8,128)} %param.51) | copy-start | bytes 884740
  296.8 27.5 %copy-start.5 = (f32[96,768]{1,0:T(8,128)S(1)}, f32[96,768]{1,0:T(8,128)}, u32[]{:S(2)}) copy-start(f32[96,768]{1,0:T(8,128)} %param.50) | copy-start | bytes 884740
  296.8 27.5 %copy-start.6 = (f32[96,768]{1,0:T(8,128)S(1)}, f32[96,768]{1,0:T(8,128)}, u32[]{:S(2)}) copy-start(f32[96,768]{1,0:T(8,128)} %param.46) | copy-start | bytes 884740
  296.8 27.5 %copy-start.7 = (f32[96,768]{1,0:T(8,128)S(1)}, f32[96,768]{1,0:T(8,128)}, u32[]{:S(2)}) copy-start(f32[96,768]{1,0:T(8,128)} %param.48) | copy-start | bytes 884740
  296.9 27.6 %copy-start.8 = (f32[96,768]{1,0:T(8,128)S(1)}, f32[96,768]{1,0:T(8,128)}, u32[]{:S(2)}) copy-start(f32[96,768]{1,0:T(8,128)} %param.47) | copy-start | bytes 884740
  298.9 3.6 %collective-permute-start.20 = (f32[1,128]{1,0:T(1,128)S(1)}, f32[1,128]{1,0:T(1,128)S(1)}, u32[]{:S(2)}, u32[]{:S(2)}) collective-permute-start(f32[1,128]{1,0:T(1,128)S(1)} %broadcast_in_dim.19), channel_id=1, source_target_pairs={{0,4},{4,0},{8,12},{12,8},{16,20},{20,16},{24,28},{28,24},{1,5},{5... | collective-permute-start | bytes 1544 | tf_op jit(solution)/shard_map/ppermute | solution.py:503
  301.4 1.4 collective-permute-start.28
  302.6 3.6 %collective-permute-start.21 = (f32[1,128]{1,0:T(1,128)S(1)}, f32[1,128]{1,0:T(1,128)S(1)}, u32[]{:S(2)}, u32[]{:S(2)}) collective-permute-start(f32[1,128]{1,0:T(1,128)S(1)} %broadcast_add_fusion), channel_id=1, source_target_pairs={{0,8},{4,12},{8,0},{12,4},{16,24},{20,28},{24,16},{28,20},{1,9},{5... | collective-permute-start | bytes 1544 | tf_op jit(solution)/shard_map/ppermute | solution.py:503
  302.8 7.8 %collective-permute-start.29 = (f32[26,768]{1,0:T(8,128)S(1)}, f32[26,768]{1,0:T(8,128)S(1)}, u32[]{:S(2)}, u32[]{:S(2)}) collective-permute-start(f32[26,768]{1,0:T(8,128)S(1)} %add.1112), channel_id=1, source_target_pairs={{0,2},{1,3},{2,0},{3,1},{4,6},{5,7},{6,4},{7,5},{8,10},{9,11},{10,... | collective-permute-start | bytes 239624 | tf_op jit(solution)/shard_map/ppermute | solution.py:503
  306.2 4.5 %collective-permute-start.22 = (f32[1,128]{1,0:T(1,128)S(1)}, f32[1,128]{1,0:T(1,128)S(1)}, u32[]{:S(2)}, u32[]{:S(2)}) collective-permute-start(f32[1,128]{1,0:T(1,128)S(1)} %fusion.31), channel_id=1, source_target_pairs={{0,16},{4,20},{8,24},{12,28},{16,0},{20,4},{24,8},{28,12},{1,17},{... | collective-permute-start | bytes 1544 | tf_op jit(solution)/shard_map/ppermute | solution.py:503
  310.6 1.2 collective-permute-start.23
  311.8 3.6 %collective-permute-start.24 = (f32[1,128]{1,0:T(1,128)S(1)}, f32[1,128]{1,0:T(1,128)S(1)}, u32[]{:S(2)}, u32[]{:S(2)}) collective-permute-start(f32[1,128]{1,0:T(1,128)S(1)} %add.1107), channel_id=1, source_target_pairs={{0,2},{1,3},{2,0},{3,1},{4,6},{5,7},{6,4},{7,5},{8,10},{9,11},{10,... | collective-permute-start | bytes 1544 | tf_op jit(solution)/shard_map/ppermute | solution.py:503
Sparse Core Ops, SparseCore 0:
  9.6 40.1 all-gather.4
  51.4 37.4 all-gather.6

commit v3 on v2

--- a/solution.py
+++ b/solution.py
@@ -328,19 +328,12 @@
     )(hn, dm, z, slope, up_all, down_all)
 
 
-def back_kernel(
-    heads, x_ref, gy_ref, attn_ref, m_ref, dhn_ref, qkv_ref, wproj_ref, vec_ref, bias_ref,
-    out_ref, dmid_ref, dat_ref, dqkv_ref, ds_ref, gvec_ref, gcol_ref, do_ref,
+def middle_kernel(
+    x_ref, gy_ref, attn_ref, m_ref, dhn_ref, wproj_ref, vec_ref, out_ref, dmid_ref, dat_ref, do_ref, gvec_ref
 ):
-    seq, width = x_ref.shape[1], x_ref.shape[2]
-    head_dim = width // heads
-    scale = head_dim ** (-0.5)
-
     @pl.when(pl.program_id(0) == 0)
     def _():
-        ds_ref[...] = jnp.zeros_like(ds_ref)
         gvec_ref[...] = jnp.zeros_like(gvec_ref)
-        gcol_ref[...] = jnp.zeros_like(gcol_ref)
 
     attn = attn_ref[0]
     middle = x_ref[0].astype(F32) + vec_ref[8:9, :] * attn
@@ -358,7 +351,39 @@
         (dat.astype(F32), down_in.astype(F32), dhn * normed, dhn, dmid * attn, cotangent * branch)
     ):
         gvec_ref[row : row + 1, :] += jnp.sum(value, 0, keepdims=True)
-    do_ref[...] = mm_nt(dat, wproj_ref[...]).astype(BF)
+    do_ref[0] = mm_nt(dat, wproj_ref[...]).astype(BF)
+
+
+def middle_back(x, gy, attn, m, dhn, proj_weight, vectors):
+    images, seq, width = x.shape
+    shapes = [
+        jax.ShapeDtypeStruct((images, seq, width), BF),
+        jax.ShapeDtypeStruct((images, seq, width), F32),
+        jax.ShapeDtypeStruct((images, seq, width), BF),
+        jax.ShapeDtypeStruct((images, seq, width), BF),
+        jax.ShapeDtypeStruct((8, width), F32),
+    ]
+    return pl.pallas_call(
+        middle_kernel,
+        grid=(images,),
+        in_specs=[per_step(v.shape) for v in (x, gy, attn, m, dhn)] + [fixed(proj_weight.shape), fixed(vectors.shape)],
+        out_specs=[per_step(s.shape) for s in shapes[:4]] + [fixed(shapes[4].shape)],
+        out_shape=shapes,
+        compiler_params=params(),
+        name="middle_back",
+    )(x, gy, attn, m, dhn, proj_weight, vectors)
+
+
+def back_kernel(heads, qkv_ref, do_ref, bias_ref, dqkv_ref, ds_ref, gcol_ref):
+    width = do_ref.shape[2]
+    head_dim = width // heads
+    scale = head_dim ** (-0.5)
+
+    @pl.when(pl.program_id(0) == 0)
+    def _():
+        ds_ref[...] = jnp.zeros_like(ds_ref)
+        gcol_ref[...] = jnp.zeros_like(gcol_ref)
+
     pair = LANES
     masks = head_masks(pair, head_dim)
     per = pair // head_dim
@@ -368,7 +393,7 @@
         q = qkv_ref[0, :, pl.ds(at, pair)]
         k = qkv_ref[0, :, pl.ds(at + width, pair)]
         v = qkv_ref[0, :, pl.ds(at + 2 * width, pair)]
-        do = do_ref[:, pl.ds(at, pair)]
+        do = do_ref[0, :, pl.ds(at, pair)]
         dq = dk = dv = None
         for e in range(per):
             pick = jnp.where(masks[e], scale, 0.0).astype(BF)
@@ -395,32 +420,22 @@
     lax.fori_loop(0, width // pair, one_pair, 0, unroll=UNROLL_B)
 
 
-def back(x, gy, attn, m, dhn, qkv, proj_weight, vectors, bias, heads):
-    images, seq, width = x.shape
+def back(qkv, do, bias, heads):
+    images, seq, width = do.shape
     shapes = [
-        jax.ShapeDtypeStruct((images, seq, width), BF),
-        jax.ShapeDtypeStruct((images, seq, width), F32),
-        jax.ShapeDtypeStruct((images, seq, width), BF),
         jax.ShapeDtypeStruct((images, seq, 3 * width), BF),
         jax.ShapeDtypeStruct((heads, seq, seq), F32),
-        jax.ShapeDtypeStruct((8, width), F32),
         jax.ShapeDtypeStruct((1, 3 * width), F32),
     ]
     return pl.pallas_call(
         functools.partial(back_kernel, heads),
         grid=(images,),
-        in_specs=[per_step(v.shape) for v in (x, gy, attn, m, dhn, qkv)]
-        + [
-            fixed(proj_weight.shape),
-            fixed(vectors.shape),
-            fixed(bias.shape),
-        ],
-        out_specs=[per_step(s.shape) for s in shapes[:4]] + [fixed(s.shape) for s in shapes[4:]],
+        in_specs=[per_step(qkv.shape), per_step(do.shape), fixed(bias.shape)],
+        out_specs=[per_step(shapes[0].shape)] + [fixed(s.shape) for s in shapes[1:]],
         out_shape=shapes,
-        scratch_shapes=[pltpu.VMEM((seq, width), BF)],
         compiler_params=params(),
         name="back",
-    )(x, gy, attn, m, dhn, qkv, proj_weight, vectors, bias)
+    )(qkv, do, bias)
 
 
 def grads_kernel(blocks, a_ref, dqkv_ref, o_ref, dat_ref, out_ref, turned_a, turned_o):
@@ -490,6 +505,63 @@
     return (mean_new, square_new, master - rate * (direction + decay * master))
 
 
+def adam_kernel(rows, ours_ref, theirs_ref, attn_ref, up_ref, down_ref, *refs):
+    state, results = refs[:21], refs[21:]
+    sums = ours_ref[...] + theirs_ref[...]
+    heads, vec_at, bias_at, square_at = rows
+    row = lax.broadcasted_iota(jnp.int32, sums.shape, 0)
+    small = jnp.where(row < square_at, sums, 0.0)
+    total = jnp.sum(jnp.sum(small * small, 0, keepdims=True), 1, keepdims=True) + sums[square_at : square_at + 1, :1]
+    norm = jnp.sqrt(total)
+    results[0][...] = norm
+    clip = jnp.minimum(1.0, max_norm / (norm + clip_eps))
+    split = state[0].shape[1]
+    vec_rows, table_rows = state[12].shape[0], state[18].shape[1]
+    bias = jnp.concatenate([sums[r : r + 1] for r in range(bias_at, square_at)], 1)
+    grads = (
+        attn_ref[:, :split],
+        attn_ref[:, split:],
+        up_ref[...],
+        down_ref[...].astype(F32),
+        sums[vec_at : vec_at + vec_rows],
+        bias,
+        sums[:heads, :table_rows],
+    )
+    at = 1
+    for n, grad in enumerate(grads):
+        large = n < 4
+        mean_new, square_new, master_new = adam_update(
+            *(state[3 * n + k][...] for k in range(3)),
+            clip * grad,
+            rate_matrix if large else rate_small,
+            weight_decay if large else 0.0,
+        )
+        values = [mean_new, square_new, master_new]
+        if large:
+            values.append(master_new.astype(BF))
+        for value in values:
+            results[at][...] = value
+            at += 1
+
+
+def adam(rows, ours, theirs, shards, state):
+    shapes = [jax.ShapeDtypeStruct((1, 1), F32)]
+    for n in range(7):
+        shapes += [jax.ShapeDtypeStruct(state[3 * n].shape, F32)] * 3
+        if n < 4:
+            shapes.append(jax.ShapeDtypeStruct(state[3 * n].shape, BF))
+    inputs = [ours, theirs, *shards, *state]
+    return pl.pallas_call(
+        functools.partial(adam_kernel, rows),
+        grid=(1,),
+        in_specs=[whole(v.shape) for v in inputs],
+        out_specs=[whole(v.shape) for v in shapes],
+        out_shape=shapes,
+        compiler_params=params(),
+        name="adam",
+    )(*inputs)
+
+
 def axis_bits():
     found = []
     for axis in ("narrow", "wide"):
@@ -503,31 +575,107 @@
     return lax.ppermute(value, axis, [(i, i ^ (1 << bit)) for i in range(size)])
 
 
-def scattered_sum(grads, order):
-    bits = axis_bits()
-    pieces = [grads.reshape((2,) * len(bits) + grads.shape[2:])]
-    for dim in order:
-        axis, bit = bits[dim]
-        mine = (lax.axis_index(axis) >> bit) & 1
-
-        def half(piece, side):
-            return lax.dynamic_slice_in_dim(piece, side, 1, dim)
-
-        sent = sum(half(p, 1 - mine).astype(F32) for p in pieces).astype(BF)
-        arrived = swap(sent, axis, bit)
-        pieces = [half(p, mine) for p in pieces] + [arrived]
-    return sum(p.astype(F32) for p in pieces).reshape(grads.shape[2:])
-
-
-def summed(value):
-    for axis, bit in reversed(axis_bits()):
-        value = value + swap(value, axis, bit)
-    return value
+class Halving:
+    def __init__(self, grads, steps):
+        self.bits = axis_bits()
+        self.shape = grads.shape[2:]
+        self.parts = [[grads.reshape((2,) * len(self.bits) + self.shape)]]
+        self.steps = list(steps)
+
+    def send(self, *after):
+        dims = self.steps.pop(0)
+        last = [pieces[-1] for pieces in self.parts]
+        if after:
+            last = lax.optimization_barrier((*last, *after))
+        self.parts = [[*pieces[:-1], piece] for pieces, piece in zip(self.parts, last)]
+        if len(dims) > len(self.parts):
+            middle = self.shape[0] // 2
+            self.parts = [[p[..., :middle, :] for p in self.parts[0]], [p[..., middle:, :] for p in self.parts[0]]]
+        sent = []
+        for n, pieces in enumerate(self.parts):
+            dim = dims[n % len(dims)]
+            axis, bit = self.bits[dim]
+            mine = (lax.axis_index(axis) >> bit) & 1
+
+            def half(piece, side):
+                return lax.dynamic_slice_in_dim(piece, side, 1, dim)
+
+            sent.append(sum(half(p, 1 - mine).astype(F32) for p in pieces).astype(BF))
+            self.parts[n] = [half(p, mine) for p in pieces]
+        if len(dims) < len(sent):
+            sent = [jnp.concatenate(sent, -2)]
+        arrived = [swap(v, *self.bits[dim]) for v, dim in zip(sent, dims)]
+        if len(arrived) < len(self.parts):
+            arrived = jnp.split(arrived[0], 2, -2)
+        for pieces, piece in zip(self.parts, arrived):
+            pieces.append(piece)
+        return tuple(sent)
+
+    def result(self):
+        while self.steps:
+            self.send()
+        sums = [sum(p.astype(F32) for p in pieces).reshape(-1, self.shape[1]) for pieces in self.parts]
+        return jnp.concatenate(sums)
+
+
+def gated(value, *waits):
+    return lax.optimization_barrier((value,) + waits)[0] if waits else value
+
+
+class Plan:
+    def __init__(self, wide, narrow):
+        self.wide, self.narrow = wide, narrow
+        lead = list(range(narrow.bit_length() - 1))
+        trail = [len(lead) + n for n in range(wide.bit_length() - 1)][::-1]
+        pair = (lead[0], trail[0])
+        self.steps = [(d,) for d in lead[:0:-1]] + [pair, pair[::-1]] + [(d,) for d in trail[1:]]
+
+    def halving(self, grads):
+        return Halving(grads.reshape(self.narrow, self.wide, grads.shape[1] // self.wide, grads.shape[2]), self.steps)
+
+    def after_down(self, grads):
+        rows = grads.reshape(-1, grads.shape[2])
+        self.down = lax.psum_scatter(rows, ("narrow", "wide"), scatter_dimension=0, tiled=True)
+        return ()
+
+    def after_up(self, grads):
+        self.up = self.halving(grads)
+        return self.up.send()
+
+    def next_up(self, *after):
+        return self.up.send(*after)
+
+    def after_attention(self, grads):
+        self.attn = self.halving(grads)
+        return self.attn.send()
+
+    def next_all(self, *after):
+        return self.up.send(*after) + self.attn.send(*after)
+
+
+class Alone:
+    def after_down(self, grads):
+        self.down = grads
+        return ()
+
+    def after_up(self, grads):
+        self.up = grads
+        return ()
+
+    def after_attention(self, grads):
+        self.attn = grads
+        return ()
+
+    def next_up(self, *after):
+        return ()
+
+    next_all = next_up
 
 
 def local_work(
-    block_in, out_grad, mim_mask, rel_index, qkv_weight, proj_weight, up_all, down_all, vectors, up_bias, rel_table
+    block_in, out_grad, mim_mask, rel_index, qkv_weight, proj_weight, up_all, down_all, vectors, up_bias, rel_table, plan=None
 ):
+    plan = plan or Alone()
     images, seq, width = block_in.shape
     table_rows, heads = rel_table.shape
     blocks, _, hidden = up_all.shape
@@ -544,29 +692,35 @@
     first, qkv, mixed, attn, hn = front(block_in, qkv_weight, proj_weight, vectors, bias, heads)
     flat = lambda v: v.reshape(tokens, v.shape[-1])
     z, slope, grad_down, dm = mlp_in(flat(hn), flat(gy), vectors, up_bias.reshape(blocks, 1, hidden), up_all, seq)
+    dm = gated(dm, *plan.after_down(grad_down))
     m, dhn, grad_up, grad_bias = mlp_out(flat(hn), dm, z, slope, up_all, down_all, seq)
+    gy = gated(gy, *plan.after_up(grad_up))
     fold = lambda v: v.reshape(images, seq, width)
-    block_out, dmid, dat, dqkv, ds, gvec, gcol = back(
-        block_in, gy, attn, fold(m), fold(dhn), qkv, proj_weight, vectors, bias_t, heads
-    )
+    block_out, dmid, dat, do, gvec = middle_back(block_in, gy, attn, fold(m), fold(dhn), proj_weight, vectors)
+    do = gated(do, *plan.next_up(do))
+    dqkv, ds, gcol = back(qkv, do, bias_t, heads)
+    dat = gated(dat, *plan.next_up(dqkv))
     grad_attn = attention_grads(flat(first), flat(dqkv), flat(mixed), flat(dat), blocks)
+    dmid = gated(dmid, *plan.after_attention(grad_attn))
     input_grad, gvec_one = input_grads(block_in, dqkv, dmid, qkv_weight, vectors)
     by_key = jnp.pad(ds.transpose(1, 0, 2), ((0, 0), (0, (-heads) % 8), (0, 0)))
+    by_key = gated(by_key, *plan.next_all(input_grad))
     sums = table_sums(index_t, by_key, chunks)
-    sums = sums.reshape(chunks, 2, -1, LANES).sum(1)[:, :heads]
-    grad_table = sums.transpose(1, 0, 2).reshape(heads * chunks * LANES // width, width)
+    plan.next_all(sums)
+    sums = sums.reshape(chunks, 2, -1, LANES).sum(1)
+    grad_table = sums.transpose(1, 0, 2).reshape(-1, chunks * LANES)
     small = jnp.concatenate(
         [
+            grad_table,
             gcol[:, :width],
             gcol[:, 2 * width :],
             gvec[:2],
             gvec_one[:2],
             gvec[2:6],
             grad_bias.reshape(-1, width),
-            grad_table,
         ]
     )
-    return block_out, input_grad, grad_attn, grad_up, grad_down, small
+    return block_out, input_grad, small, plan
 
 
 def shards(
@@ -581,78 +735,43 @@
     vectors,
     up_bias,
     rel_table,
-    qkv_master,
-    qkv_mean,
-    qkv_square,
-    proj_master,
-    proj_mean,
-    proj_square,
-    up_master,
-    up_mean,
-    up_square,
-    down_master,
-    down_mean,
-    down_square,
-    vector_mean,
-    vector_square,
-    bias_mean,
-    bias_square,
-    table_mean,
-    table_square,
+    *state,
 ):
     width = block_in.shape[2]
-    table_rows, heads = rel_table.shape
-    wide = lax.axis_size("wide")
-    narrow = lax.axis_size("narrow")
+    heads = rel_table.shape[1]
     up_all = lax.all_gather(up_weight, "narrow", axis=0)
     down_all = lax.all_gather(down_weight, "narrow", axis=0)
-    block_out, input_grad, grad_attn, grad_up, grad_down, small = local_work(
-        block_in, out_grad, mim_mask, rel_index, qkv_weight, proj_weight, up_all, down_all, vectors, up_bias, rel_table
+    plan = Plan(lax.axis_size("wide"), lax.axis_size("narrow"))
+    block_out, input_grad, small, plan = local_work(
+        block_in, out_grad, mim_mask, rel_index, qkv_weight, proj_weight, up_all, down_all, vectors, up_bias, rel_table, plan
     )
-    small = summed(small)
-    lead = [n for n in range(narrow.bit_length() - 1)]
-    trail = [len(lead) + n for n in range(wide.bit_length() - 1)]
-    order_a = lead[::-1] + trail[::-1]
-    order_b = lead[-1:] + trail[::-1] + lead[:-1]
-    cut = lambda v: v.reshape(narrow, wide, width // wide, v.shape[-1])
-    up_shard = scattered_sum(cut(grad_up), order_a)
-    down_shard = scattered_sum(cut(grad_down), order_b)
-    grad_attn = cut(grad_attn)
-    half = grad_attn.shape[2] // 2
-    attn_shard = jnp.concatenate(
-        [scattered_sum(grad_attn[:, :, :half], order_a), scattered_sum(grad_attn[:, :, half:], order_b)]
+    up_shard = plan.up.result()
+    down_shard = plan.down
+    attn_shard = plan.attn.result()
+    squares = sum(jnp.sum(jnp.square(v.astype(F32))) for v in (down_shard, up_shard, attn_shard))
+    bias_rows = up_bias.shape[0] // width
+    vec_at = heads + (-heads) % 8
+    bias_at = vec_at + vectors.shape[0]
+    square_at = bias_at + bias_rows
+    ours = jnp.concatenate([small, jnp.full((1, width), squares)])
+    theirs = None
+    for axis, bit in reversed(axis_bits()):
+        ours = ours if theirs is None else ours + theirs
+        theirs = swap(ours, axis, bit)
+    line = lambda v: v.reshape(1, -1)
+    matrices = state[:12]
+    params_small = (vectors, state[12], state[13], line(up_bias), line(state[14]), line(state[15]), rel_table.T, *(v.T for v in state[16:]))
+    norm, *updated = adam(
+        (heads, vec_at, bias_at, square_at),
+        ours,
+        theirs,
+        (attn_shard, up_shard, down_shard),
+        [matrices[3 * n + k] for n in range(4) for k in range(3)] + [params_small[3 * n + k] for n in range(3) for k in range(3)],
     )
-    split = qkv_master.shape[1]
-    qkv_shard, proj_shard = attn_shard[:, :split], attn_shard[:, split:]
-    shard_squares = jnp.sum(attn_shard * attn_shard) + jnp.sum(up_shard * up_shard) + jnp.sum(down_shard * down_shard)
-    large_squares = summed(jnp.full((1, LANES), shard_squares))[0, 0]
-    small_squares = jnp.sum(small * small)
-    grad_vectors = small[:10]
-    grad_bias = small[10 : 10 + up_bias.shape[0] // width].reshape(up_bias.shape)
-    grad_table = small[10 + up_bias.shape[0] // width :].reshape(heads, -1).T[:table_rows]
-    grad_norm = jnp.sqrt(large_squares + small_squares)
-    clip = jnp.minimum(1.0, max_norm / (grad_norm + clip_eps))
-    results = [block_out, input_grad, grad_norm]
-    for master, mean, square, grad in (
-        (qkv_master, qkv_mean, qkv_square, qkv_shard),
-        (proj_master, proj_mean, proj_square, proj_shard),
-        (up_master, up_mean, up_square, up_shard),
-        (down_master, down_mean, down_square, down_shard),
-    ):
-        mean_new, square_new, master_new = adam_update(
-            master, mean, square, clip * grad, rate_matrix, weight_decay
-        )
-        results += [mean_new, square_new, master_new, master_new.astype(jnp.bfloat16)]
-    for master, mean, square, grad in (
-        (vectors, vector_mean, vector_square, grad_vectors),
-        (up_bias, bias_mean, bias_square, grad_bias),
-        (rel_table, table_mean, table_square, grad_table),
-    ):
-        mean_new, square_new, master_new = adam_update(
-            master, mean, square, clip * grad, rate_small, 0.0
-        )
-        results += [mean_new, square_new, master_new]
-    return tuple(results)
+    for n in range(19, 22):
+        updated[n] = updated[n].reshape(up_bias.shape)
+        updated[n + 3] = updated[n + 3].T
+    return (block_out, input_grad, norm.reshape(()), *updated)
 
 
 def solution(mesh):

time: 335 us -> 311 us (0.928)
  other arithmetic: 50.7 us -> 32 us
  starting transfers between devices: 28.9 us -> 17 us
  Pallas kernels: 162 us -> 171 us
  local copies, waits for them, and re-layouts: 19.1 us -> 24.4 us
  waiting for transfers between devices: 54.7 us -> 49.6 us
    convert_element_type x19 -> x10, other arithmetic: 34.3 us -> 18 us  [send(): sent.append(sum((half(p, 1 - mine).astype(F32) for p in pieces)).astype(BF))]
    pallas_call x0 -> x2, Pallas kernels: none -> 15.7 us  [the longest x1 10.9 us: middle_back(): pl.pallas_call(middle_kernel, grid=(images,), in_specs=[per_step(v.shape)...]
    ppermute x30 -> x19, starting transfers between devices: 28.8 us -> 16.9 us  [swap(): return lax.ppermute(value, axis, [(i, i ^ 1 << bit) for i in range(size)])]
    ppermute x30 -> x19, waiting for transfers between devices: 37.6 us -> 29 us  [swap(): return lax.ppermute(value, axis, [(i, i ^ 1 << bit) for i in range(size)])]
    pallas_call x1, Pallas kernels: 30.9 us -> 23.5 us  [back(): pl.pallas_call(functools.partial(back_kernel, heads), grid=(images,), in_...]
    concatenate x0 -> x5, other arithmetic: none -> 5.27 us  [the longest x4 2.81 us: send(): sent = [jnp.concatenate(sent, -2)]]
    sub x3 -> x0, other arithmetic: 4.35 us -> none  [adam_update(): return (mean_new, square_new, master - rate * (direction + decay * master))]
    all_gather x1, waiting for transfers between devices: 14.9 us -> 18.3 us  [shards(): down_all = lax.all_gather(down_weight, 'narrow', axis=0)]
  transfers between devices with their start and end apart: 32 -> 22, of which waited for: 15 -> 11; matrix products, arithmetic and copies ran while one was open for 18% -> 15% of each run, Pallas kernels for 49% -> 42%
where the time goes in v3:
time: 311 us; the launch traced here: 310 us
  Pallas kernels  171 us (55%)
  waiting for transfers between devices  49.6 us (16%)
  other arithmetic  32 us (10%)
  local copies, waits for them, and re-layouts  24.4 us (8%)
  starting transfers between devices  17 us (5%)
  between operations  16.2 us (5%)
    pallas_call x1, Pallas kernels, mlp_out(): pl.pallas_call(functools.partial(mlp_out_kernel, chunk), grid=(blocks,),...  36.7 us
    ppermute x19, waiting for transfers between devices, swap(): return lax.ppermute(value, axis, [(i, i ^ 1 << bit) for i in range(size)])  29 us
    pallas_call x1, Pallas kernels, front(): pl.pallas_call(functools.partial(front_kernel, heads), grid=(images,), in...  26.7 us
    pallas_call x1, Pallas kernels, back(): pl.pallas_call(functools.partial(back_kernel, heads), grid=(images,), in_...  23.5 us
    pallas_call x1, Pallas kernels, mlp_in(): pl.pallas_call(functools.partial(mlp_in_kernel, chunk), grid=(blocks,), i...  20.7 us
    all_gather x1, waiting for transfers between devices, shards(): down_all = lax.all_gather(down_weight, 'narrow', axis=0)  18.3 us
    convert_element_type x10, other arithmetic, send(): sent.append(sum((half(p, 1 - mine).astype(F32) for p in pieces)).astype(BF))  18 us
    ppermute x19, starting transfers between devices, swap(): return lax.ppermute(value, axis, [(i, i ^ 1 << bit) for i in range(size)])  16.9 us
  transfers between devices with their start and end apart: 22, of which 11 were waited for; matrix products, arithmetic and copies ran while one was open for 15% of the time, Pallas kernels for 42%

profile of v3, /device:TPU:0, one launch (start us, length us, event | category | flops | bytes accessed | tf_op | source)
XLA Modules:
  0.0 310.2 jit_solution(9754340527635503780)
XLA Ops:
  8.0 0.7 all-gather.7.cloned.1.call-update
  9.8 0.7 pad.12.clone.idx_ref
  10.5 10.4 %bias_tables.1 = (f32[12,200,200]{2,1,0:T(8,128)}, f32[12,200,200]{2,1,0:T(8,128)}) custom-call(s32[200,256]{1,0:T(8,128)} %pad.12.clone.idx_ref, f32[12,6,128]{2,1,0:T(8,128)} %reshape.138.tab_ref), custom_call_target="tpu_custom_call" | custom-call | tf_op jit(solution)/shard_map/bias_tables/pallas_call | solution.py:122
  20.9 26.7 %front.1 = (bf16[5,200,768]{2,1,0:T(8,128)(2,1)}, bf16[5,200,2304]{2,1,0:T(8,128)(2,1)}, bf16[5,200,768]{2,1,0:T(8,128)(2,1)}, f32[5,200,768]{2,1,0:T(8,128)}, bf16[5,200,768]{2,1,0:T(8,128)(2,1)}) custom-call(bf16[5,200,768]{2,1,0:T(8,128)(2,1)} %x_ref.5, bf16[768,2304]{1,0:T(8,128)(2,1)} %wqkv_ref.3, bf16[768,768]{1,0:T(8,128)(2,1)} %wproj_ref.3, ...), custom_call_target="tpu_custom_call" | custom-call | tf_op jit(solution)/shard_map/front/pallas_call | solution.py:218
  47.6 1.4 broadcast_multiply_fusion.gy_ref
  49.0 0.8 all-gather.5.cloned.1.call-done
  49.8 20.7 %mlp_in.1 = (bf16[4,1000,768]{2,1,0:T(8,128)(2,1)}, bf16[4,1000,768]{2,1,0:T(8,128)(2,1)}, bf16[4,768,768]{2,1,0:T(8,128)(2,1)}, bf16[1000,768]{1,0:T(8,128)(2,1)}) custom-call(bf16[1000,768]{1,0:T(8,128)(2,1)} %bitcast.64, bf16[1000,768]{1,0:T(8,128)(2,1)} %bitcast.62, f32[10,768]{1,0:T(8,128)} %refs_12_.1, f32[4,1,768]{2,1,0:T(1,128)} %bitcast.84, ...), custom_call_target="tpu_custom_call" | custom-call | tf_op jit(solution)/shard_map/mlp_in/pallas_call | solution.py:268
  70.5 18.3 %all-gather.7.cloned.1.call-done = bf16[3072,768]{1,0:T(8,128)(2,1)} async-done(((bf16[768,768]{1,0:T(8,128)(2,1)}), bf16[3072,768]{1,0:T(8,128)(2,1)}) %all-gather.7.cloned.1.call-update) | async-done | bytes 4718608 | tf_op jit(solution)/shard_map/all_gather | solution.py:743
  88.8 36.7 %mlp_out.1 = (f32[1000,768]{1,0:T(8,128)}, f32[1000,768]{1,0:T(8,128)}, bf16[4,768,768]{2,1,0:T(8,128)(2,1)}, f32[4,1,768]{2,1,0:T(1,128)}) custom-call(bf16[1000,768]{1,0:T(8,128)(2,1)} %bitcast.65, bf16[1000,768]{1,0:T(8,128)(2,1)} %get-tuple-element.96.dm_ref, bf16[4,1000,768]{2,1,0:T(8,128)(2,1)} %get-tuple-element.97.z_ref, ...), custom_call_target="tpu_custom_call" | custom-call | tf_op jit(solution)/shard_map/mlp_out/pallas_call | solution.py:319
  125.5 3.3 %constant_dynamic-slice_fusion.1 = bf16[2,1,2,2,2,96,768]{6,5,4,3,2,1,0:T(8,128)(2,1)} fusion(bf16[2,2,2,2,2,96,768]{6,5,4,3,2,1,0:T(8,128)(2,1)} %bitcast.68, s32[]{:T(128)S(6)} %select_n.41), kind=kLoop, calls=%fused_computation.35 | loop fusion | bytes 4718596 | tf_op jit(solution)/shard_map/dynamic_slice | solution.py:601
  129.0 10.9 %middle_back.1 = (bf16[5,200,768]{2,1,0:T(8,128)(2,1)}, f32[5,200,768]{2,1,0:T(8,128)}, bf16[5,200,768]{2,1,0:T(8,128)(2,1)}, bf16[5,200,768]{2,1,0:T(8,128)(2,1)}, f32[8,768]{1,0:T(8,128)}) custom-call(bf16[5,200,768]{2,1,0:T(8,128)(2,1)} %x_ref.5, bf16[5,200,768]{2,1,0:T(8,128)(2,1)} %broadcast_multiply_fusion.gy_ref, ...), custom_call_target="tpu_custom_call" | custom-call | tf_op jit(solution)/shard_map/middle_back/pallas_call | solution.py:366
  140.0 1.4 copy-done.2
  141.4 1.9 fusion.1
  143.3 2.1 add_convert_fusion.2
  145.4 1.4 collective-permute-start.2
  146.7 2.0 add_convert_fusion.3
  149.3 23.5 %back.1 = (bf16[5,200,2304]{2,1,0:T(8,128)(2,1)}, f32[12,200,200]{2,1,0:T(8,128)}, f32[1,2304]{1,0:T(1,128)}) custom-call(bf16[5,200,2304]{2,1,0:T(8,128)(2,1)} %get-tuple-element.105.qkv_ref, bf16[5,200,768]{2,1,0:T(8,128)(2,1)} %get-tuple-element.108.do_ref, f32[12,200,200]{2,1,0:T(8,128)} %get-tuple-element.109.bias_ref), custom_call_target="tpu_custom_call" | custom-call | tf_op jit(solution)/shard_map/back/pallas_call | solution.py:430
  172.9 2.5 add_convert_fusion.6
  175.4 13.3 %attention_grads.1 = bf16[4,768,768]{2,1,0:T(8,128)(2,1)} custom-call(bf16[1000,768]{1,0:T(8,128)(2,1)} %bitcast.77, bf16[1000,2304]{1,0:T(8,128)(2,1)} %bitcast.61, bf16[1000,768]{1,0:T(8,128)(2,1)} %bitcast.78, bf16[1000,768]{1,0:T(8,128)(2,1)} %bitcast.79), custom_call_target="tpu_custom_call" | custom-call | tf_op jit(solution)/shard_map/attention_grads/pallas_call | solution.py:457
  188.7 3.3 %constant_dynamic-slice_fusion = bf16[2,1,2,2,2,96,768]{6,5,4,3,2,1,0:T(8,128)(2,1)} fusion(bf16[2,2,2,2,2,96,768]{6,5,4,3,2,1,0:T(8,128)(2,1)} %bitcast.52, s32[]{:T(128)S(6)} %select_n.41), kind=kLoop, calls=%fused_computation.34 | loop fusion | bytes 4718596 | tf_op jit(solution)/shard_map/dynamic_slice | solution.py:601
  192.0 1.5 collective-permute-start.4
  193.5 11.6 %input_grads.1 = (f32[5,200,768]{2,1,0:T(8,128)}, f32[8,768]{1,0:T(8,128)}) custom-call(bf16[5,200,768]{2,1,0:T(8,128)(2,1)} %x_ref.5, bf16[5,200,2304]{2,1,0:T(8,128)(2,1)} %get-tuple-element.110.dqkv_ref, f32[5,200,768]{2,1,0:T(8,128)} %get-tuple-element.118.dmid_ref, bf16[768,2304]{1,0:T(8,128)(2,1)} %wqkv_ref.3, f32[10,768]{1,0:T(8,128)} %refs_12_.1), custom_call_target="tpu_custom_call" | custom-call | tf_op jit(solution)/shard_map/input_grads/pallas_call | solution.py:487
  205.1 1.8 fusion
  207.0 2.5 add_convert_fusion
  209.5 1.8 collective-permute-start.9
  211.3 2.0 add_convert_fusion.1
  213.3 0.8 collective-permute-start.8
  214.1 0.8 fusion.5.idx_ref
  216.1 0.8 copy.73
  216.9 2.1 pad.14.ds_ref
  219.1 1.4 add_convert_fusion.11
  220.5 0.7 pad_maximum_fusion
  221.2 1.3 collective-permute-start.6
  223.1 1.3 slice.50
  224.5 12.5 %table_sums.1 = f32[192,128]{1,0:T(8,128)} custom-call(s32[200,200]{1,0:T(8,128)} %fusion.5.idx_ref, f32[200,16,200]{2,1,0:T(8,128)} %pad.14.ds_ref), custom_call_target="tpu_custom_call" | custom-call | tf_op jit(solution)/shard_map/table_sums/pallas_call | solution.py:157
  237.0 1.6 add_convert_fusion.5
  238.9 1.4 collective-permute-start.11
  240.3 1.0 fusion.3
  241.3 1.3 add_convert_fusion.15
  242.6 4.0 %collective-permute-done.10 = bf16[1,1,2,2,1,48,768]{6,5,4,3,2,1,0:T(8,128)(2,1)S(1)} collective-permute-done((bf16[1,1,2,2,1,48,768]{6,5,4,3,2,1,0:T(8,128)(2,1)S(1)}, bf16[1,1,2,2,1,48,768]{6,5,4,3,2,1,0:T(8,128)(2,1)S(1)}, u32[]{:S(2)}, u32[]{:S(2)}) %collective-permute-start.10) | collective-permute-done | bytes 294944 | tf_op jit(solution)/shard_map/ppermute | solution.py:575
  246.8 1.3 add_convert_fusion.9
  248.2 0.7 pad_maximum_fusion.2
  248.9 0.7 collective-permute-start.12
  250.3 2.2 collective-permute-start.7
  252.5 1.5 reduce_sum.36
  254.0 1.5 copy_bitcast_fusion.1
  255.5 4.0 %collective-permute-done.12 = bf16[1,1,2,1,1,96,768]{6,5,4,3,2,1,0:T(8,128)(2,1)} collective-permute-done((bf16[1,1,2,1,1,96,768]{6,5,4,3,2,1,0:T(8,128)(2,1)}, bf16[1,1,2,1,1,96,768]{6,5,4,3,2,1,0:T(8,128)(2,1)}, u32[]{:S(2)}, u32[]{:S(2)}) %collective-permute-start.12) | collective-permute-done | bytes 294944 | tf_op jit(solution)/shard_map/ppermute | solution.py:575
  259.5 1.0 fusion.2
  261.1 1.2 add_convert_fusion.13
  263.0 0.8 collective-permute-start.13
  263.9 2.0 add_bitcast_fusion.3
  265.9 1.6 multiply_reduce_fusion.2
  267.5 3.0 collective-permute-done.13
  270.5 1.3 add_bitcast_fusion.1
  271.9 2.5 pad_maximum_fusion.1
  276.5 1.4 collective-permute-start.14
  277.9 3.2 %collective-permute-done.14 = f32[31,768]{1,0:T(8,128)S(1)} collective-permute-done((f32[31,768]{1,0:T(8,128)S(1)}, f32[31,768]{1,0:T(8,128)S(1)}, u32[]{:S(2)}, u32[]{:S(2)}) %collective-permute-start.14) | collective-permute-done | bytes 95264 | tf_op jit(solution)/shard_map/ppermute | solution.py:575
  281.3 4.6 %collective-permute-done.15 = f32[31,768]{1,0:T(8,128)S(1)} collective-permute-done((f32[31,768]{1,0:T(8,128)S(1)}, f32[31,768]{1,0:T(8,128)S(1)}, u32[]{:S(2)}, u32[]{:S(2)}) %collective-permute-start.15) | collective-permute-done | bytes 95264 | tf_op jit(solution)/shard_map/ppermute | solution.py:575
  285.9 0.8 collective-permute-start.16
  286.7 5.3 %collective-permute-done.16 = f32[31,768]{1,0:T(8,128)S(1)} collective-permute-done((f32[31,768]{1,0:T(8,128)S(1)}, f32[31,768]{1,0:T(8,128)S(1)}, u32[]{:S(2)}, u32[]{:S(2)}) %collective-permute-start.16) | collective-permute-done | bytes 95264 | tf_op jit(solution)/shard_map/ppermute | solution.py:575
  292.1 1.3 collective-permute-done.17
  293.4 1.6 collective-permute-start.18
  295.0 3.3 %collective-permute-done.18.theirs_ref = f32[31,768]{1,0:T(8,128)S(1)} collective-permute-done((f32[31,768]{1,0:T(8,128)S(1)}, f32[31,768]{1,0:T(8,128)S(1)}, u32[]{:S(2)}, u32[]{:S(2)}) %collective-permute-start.18) | collective-permute-done | bytes 95264 | tf_op jit(solution)/shard_map/ppermute | solution.py:575
  298.9 4.7 %adam.1 = (f32[1,1]{1,0:T(1,128)}, f32[96,576]{1,0:T(8,128)}, f32[96,576]{1,0:T(8,128)}, f32[96,576]{1,0:T(8,128)}, bf16[96,576]{1,0:T(8,128)(2,1)}, /*index=5*/...) custom-call(f32[31,768]{1,0:T(8,128)} %copy-done.15, ...), custom_call_target="tpu_custom_call" | custom-call | tf_op jit(solution)/shard_map/adam/pallas_call | solution.py:554
  (102 shorter events, 8.1 us)
Async XLA Ops:
  7.2 1.6 copy-start.18
  7.2 1.9 copy-start.19
  7.2 42.6 %all-gather.5.cloned.1.call-start = ((), (), s32[]{:S(2)}) async-start(), calls=%async_computation.2 | async-start | bytes 5898240 | tf_op jit(solution)/shard_map/all_gather | solution.py:742
  8.0 1.8 copy-start.28
  8.0 80.8 %all-gather.7.cloned.1.call-start = ((), (), s32[]{:S(2)}) async-start(), calls=%async_computation.3 | async-start | bytes 5898240 | tf_op jit(solution)/shard_map/all_gather | solution.py:743
  8.7 257.2 %reduce-scatter.2.cloned.1.call-start = ((), (), s32[]{:S(2)}) async-start(), calls=%async_computation.1 | async-start | bytes 4866048 | tf_op jit(solution)/shard_map/reduce_scatter | solution.py:638
  8.9 38.7 %copy-start.3 = (s32[200,200]{0,1:T(8,128)}, s32[200,200]{0,1:T(8,128)S(1)}, u32[]{:S(2)}) copy-start(s32[200,200]{0,1:T(8,128)S(1)} %copy.63) | copy-start | bytes 480004
  20.9 26.7 %copy-start.5 = (bf16[5,200,768]{2,1,0:T(8,128)(2,1)S(1)}, bf16[5,200,768]{2,1,0:T(8,128)(2,1)}, u32[]{:S(2)}) copy-start(bf16[5,200,768]{2,1,0:T(8,128)(2,1)} %param.30) | copy-start | bytes 4608004
  128.8 11.2 %collective-permute-start = (bf16[2,1,2,2,2,96,768]{6,5,4,3,2,1,0:T(8,128)(2,1)}, bf16[2,1,2,2,2,96,768]{6,5,4,3,2,1,0:T(8,128)(2,1)S(1)}, u32[]{:S(2)}, u32[]{:S(2)}) collective-permute-start(bf16[2,1,2,2,2,96,768]{6,5,4,3,2,1,0:T(8,128)(2,1)} %constant_dynamic-slice_fusion.1), channel_id=1, source_target_pairs={{0,1},{1,0},{2,3},{3,2},{4,5},{5,4},{6,7},{7,6},{8,9},{9,8},{10,11... | collective-permute-start | bytes 7077896 | tf_op jit(solution)/shard_map/ppermute | solution.py:575
  140.0 1.4 copy-start.2
  145.4 27.5 %collective-permute-start.2 = (bf16[2,1,2,2,1,48,768]{6,5,4,3,2,1,0:T(8,128)(2,1)}, bf16[2,1,2,2,1,48,768]{6,5,4,3,2,1,0:T(8,128)(2,1)S(1)}, u32[]{:S(2)}, u32[]{:S(2)}) collective-permute-start(bf16[2,1,2,2,1,48,768]{6,5,4,3,2,1,0:T(8,128)(2,1)} %add_convert_fusion.2), channel_id=1, source_target_pairs={{0,4},{4,0},{8,12},{12,8},{16,20},{20,16},{24,28},{28,24},{1,5},{5... | collective-permute-start | bytes 1769480 | tf_op jit(solution)/shard_map/ppermute | solution.py:575
  148.8 24.1 %collective-permute-start.1 = (bf16[1,1,2,2,2,48,768]{6,5,4,3,2,1,0:T(8,128)(2,1)}, bf16[1,1,2,2,2,48,768]{6,5,4,3,2,1,0:T(8,128)(2,1)S(1)}, u32[]{:S(2)}, u32[]{:S(2)}) collective-permute-start(bf16[1,1,2,2,2,48,768]{6,5,4,3,2,1,0:T(8,128)(2,1)} %add_convert_fusion.3), channel_id=1, source_target_pairs={{0,2},{1,3},{2,0},{3,1},{4,6},{5,7},{6,4},{7,5},{8,10},{9,11},{10,... | collective-permute-start | bytes 1769480 | tf_op jit(solution)/shard_map/ppermute | solution.py:575
  172.9 15.8 %copy-start.6 = (bf16[2,1,2,2,1,48,768]{6,5,4,3,2,1,0:T(8,128)(2,1)}, bf16[2,1,2,2,1,48,768]{6,5,4,3,2,1,0:T(8,128)(2,1)S(1)}, u32[]{:S(2)}) copy-start(bf16[2,1,2,2,1,48,768]{6,5,4,3,2,1,0:T(8,128)(2,1)S(1)} %collective-permute-done.2) | copy-start | bytes 1769476
  172.9 15.8 %copy-start.7 = (bf16[1,1,2,2,2,48,768]{6,5,4,3,2,1,0:T(8,128)(2,1)}, bf16[1,1,2,2,2,48,768]{6,5,4,3,2,1,0:T(8,128)(2,1)S(1)}, u32[]{:S(2)}) copy-start(bf16[1,1,2,2,2,48,768]{6,5,4,3,2,1,0:T(8,128)(2,1)S(1)} %collective-permute-done.1) | copy-start | bytes 1769476
  192.0 13.1 %collective-permute-start.5 = (bf16[2,1,2,2,2,96,768]{6,5,4,3,2,1,0:T(8,128)(2,1)}, bf16[2,1,2,2,2,96,768]{6,5,4,3,2,1,0:T(8,128)(2,1)}, u32[]{:S(2)}, u32[]{:S(2)}) collective-permute-start(bf16[2,1,2,2,2,96,768]{6,5,4,3,2,1,0:T(8,128)(2,1)} %constant_dynamic-slice_fusion), channel_id=1, source_target_pairs={{0,1},{1,0},{2,3},{3,2},{4,5},{5,4},{6,7},{7,6},{8,9},{9,8},{10,11... | collective-permute-start | bytes 7077896 | tf_op jit(solution)/shard_map/ppermute | solution.py:575
  192.0 27.1 %collective-permute-start.3 = (bf16[1,1,2,2,1,48,768]{6,5,4,3,2,1,0:T(8,128)(2,1)}, bf16[1,1,2,2,1,48,768]{6,5,4,3,2,1,0:T(8,128)(2,1)}, u32[]{:S(2)}, u32[]{:S(2)}) collective-permute-start(bf16[1,1,2,2,1,48,768]{6,5,4,3,2,1,0:T(8,128)(2,1)} %get-tuple-element.175), channel_id=1, source_target_pairs={{0,4},{4,0},{8,12},{12,8},{16,20},{20,16},{24,28},{28,24},{1,5},{5... | collective-permute-start | bytes 884744 | tf_op jit(solution)/shard_map/ppermute | solution.py:575
  192.0 27.1 %collective-permute-start.4 = (bf16[1,1,2,2,1,48,768]{6,5,4,3,2,1,0:T(8,128)(2,1)}, bf16[1,1,2,2,1,48,768]{6,5,4,3,2,1,0:T(8,128)(2,1)}, u32[]{:S(2)}, u32[]{:S(2)}) collective-permute-start(bf16[1,1,2,2,1,48,768]{6,5,4,3,2,1,0:T(8,128)(2,1)} %get-tuple-element.174), channel_id=1, source_target_pairs={{0,2},{1,3},{2,0},{3,1},{4,6},{5,7},{6,4},{7,5},{8,10},{9,11},{10,... | collective-permute-start | bytes 884744 | tf_op jit(solution)/shard_map/ppermute | solution.py:575
  206.9 39.9 %copy-start = (bf16[2,1,2,2,2,48,768]{6,5,4,3,2,1,0:T(8,128)(2,1)}, bf16[2,1,2,2,2,48,768]{6,5,4,3,2,1,0:T(8,128)(2,1)S(1)}, u32[]{:S(2)}) copy-start(bf16[2,1,2,2,2,48,768]{6,5,4,3,2,1,0:T(8,128)(2,1)S(1)} %get-tuple-element.177) | copy-start | bytes 3538948
  206.9 7.2 %copy-start.4 = (s32[200,200]{0,1:T(8,128)S(1)}, s32[200,200]{0,1:T(8,128)}, u32[]{:S(2)}) copy-start(s32[200,200]{0,1:T(8,128)} %copy-done.3) | copy-start | bytes 480004
  206.9 7.9 %copy-start.25 = (f32[8,768]{1,0:T(8,128)S(1)}, f32[8,768]{1,0:T(8,128)}, u32[]{:S(2)}) copy-start(f32[8,768]{1,0:T(8,128)} %get-tuple-element.126) | copy-start | bytes 73732
  207.0 9.1 %copy-start.1 = (f32[12,200,200]{2,1,0:T(8,128)S(1)}, f32[12,200,200]{2,1,0:T(8,128)}, u32[]{:S(2)}) copy-start(f32[12,200,200]{2,1,0:T(8,128)} %get-tuple-element.120) | copy-start | bytes 5760004
  209.5 6.0 %copy-start.26 = (f32[4,1,768]{2,1,0:T(1,128)S(1)}, f32[4,1,768]{2,1,0:T(1,128)}, u32[]{:S(2)}) copy-start(f32[4,1,768]{2,1,0:T(1,128)} %get-tuple-element.128) | copy-start | bytes 36868
  209.5 27.4 %collective-permute-start.9 = (bf16[2,1,2,2,1,48,768]{6,5,4,3,2,1,0:T(8,128)(2,1)}, bf16[2,1,2,2,1,48,768]{6,5,4,3,2,1,0:T(8,128)(2,1)S(1)}, u32[]{:S(2)}, u32[]{:S(2)}) collective-permute-start(bf16[2,1,2,2,1,48,768]{6,5,4,3,2,1,0:T(8,128)(2,1)} %add_convert_fusion), channel_id=1, source_target_pairs={{0,4},{4,0},{8,12},{12,8},{16,20},{20,16},{24,28},{28,24},{1,5},{5... | collective-permute-start | bytes 1769480 | tf_op jit(solution)/shard_map/ppermute | solution.py:575
  213.3 23.7 %collective-permute-start.8 = (bf16[1,1,2,2,2,48,768]{6,5,4,3,2,1,0:T(8,128)(2,1)}, bf16[1,1,2,2,2,48,768]{6,5,4,3,2,1,0:T(8,128)(2,1)}, u32[]{:S(2)}, u32[]{:S(2)}) collective-permute-start(bf16[1,1,2,2,2,48,768]{6,5,4,3,2,1,0:T(8,128)(2,1)} %add_convert_fusion.1), channel_id=1, source_target_pairs={{0,2},{1,3},{2,0},{3,1},{4,6},{5,7},{6,4},{7,5},{8,10},{9,11},{10,... | collective-permute-start | bytes 1769480 | tf_op jit(solution)/shard_map/ppermute | solution.py:575
  219.1 3.5 %copy-start.29 = (f32[1,2304]{1,0:T(1,128)S(1)}, f32[1,2304]{1,0:T(1,128)}, u32[]{:S(2)}) copy-start(f32[1,2304]{1,0:T(1,128)} %get-tuple-element.125) | copy-start | bytes 27652
  221.2 19.0 %collective-permute-start.6 = (bf16[1,1,2,1,1,96,768]{6,5,4,3,2,1,0:T(8,128)(2,1)}, bf16[1,1,2,1,1,96,768]{6,5,4,3,2,1,0:T(8,128)(2,1)}, u32[]{:S(2)}, u32[]{:S(2)}) collective-permute-start(bf16[1,1,2,1,1,96,768]{6,5,4,3,2,1,0:T(8,128)(2,1)} %pad_maximum_fusion), channel_id=1, source_target_pairs={{0,8},{4,12},{8,0},{12,4},{16,24},{20,28},{24,16},{28,20},{1,9},{5... | collective-permute-start | bytes 884744 | tf_op jit(solution)/shard_map/ppermute | solution.py:575
  237.0 9.9 %copy-start.8 = (bf16[2,1,2,2,1,48,768]{6,5,4,3,2,1,0:T(8,128)(2,1)}, bf16[2,1,2,2,1,48,768]{6,5,4,3,2,1,0:T(8,128)(2,1)S(1)}, u32[]{:S(2)}) copy-start(bf16[2,1,2,2,1,48,768]{6,5,4,3,2,1,0:T(8,128)(2,1)S(1)} %collective-permute-done.9) | copy-start | bytes 1769476
  238.5 8.0 %collective-permute-start.10 = (bf16[1,1,2,2,1,48,768]{6,5,4,3,2,1,0:T(8,128)(2,1)S(1)}, bf16[1,1,2,2,1,48,768]{6,5,4,3,2,1,0:T(8,128)(2,1)S(1)}, u32[]{:S(2)}, u32[]{:S(2)}) collective-permute-start(bf16[1,1,2,2,1,48,768]{6,5,4,3,2,1,0:T(8,128)(2,1)S(1)} %get-tuple-element.168), channel_id=1, source_target_pairs={{0,4},{4,0},{8,12},{12,8},{16,20},{20,16},{24,28},{28,24},{1,5},{5... | collective-permute-start | bytes 884744 | tf_op jit(solution)/shard_map/ppermute | solution.py:575
  238.9 8.0 %collective-permute-start.11 = (bf16[1,1,2,2,1,48,768]{6,5,4,3,2,1,0:T(8,128)(2,1)S(1)}, bf16[1,1,2,2,1,48,768]{6,5,4,3,2,1,0:T(8,128)(2,1)S(1)}, u32[]{:S(2)}, u32[]{:S(2)}) collective-permute-start(bf16[1,1,2,2,1,48,768]{6,5,4,3,2,1,0:T(8,128)(2,1)S(1)} %get-tuple-element.169), channel_id=1, source_target_pairs={{0,2},{1,3},{2,0},{3,1},{4,6},{5,7},{6,4},{7,5},{8,10},{9,11},{10,... | collective-permute-start | bytes 884744 | tf_op jit(solution)/shard_map/ppermute | solution.py:575
  241.3 5.3 %copy-start.9 = (bf16[1,1,2,1,1,48,768]{6,5,4,3,2,1,0:T(8,128)(2,1)}, bf16[1,1,2,1,1,48,768]{6,5,4,3,2,1,0:T(8,128)(2,1)S(1)}, u32[]{:S(2)}) copy-start(bf16[1,1,2,1,1,48,768]{6,5,4,3,2,1,0:T(8,128)(2,1)S(1)} %get-tuple-element.131) | copy-start | bytes 442372
  241.3 5.3 %copy-start.11 = (bf16[1,1,2,1,1,48,768]{6,5,4,3,2,1,0:T(8,128)(2,1)}, bf16[1,1,2,1,1,48,768]{6,5,4,3,2,1,0:T(8,128)(2,1)S(1)}, u32[]{:S(2)}) copy-start(bf16[1,1,2,1,1,48,768]{6,5,4,3,2,1,0:T(8,128)(2,1)S(1)} %get-tuple-element.130) | copy-start | bytes 442372
  246.6 2.3 copy-start.16
  246.8 2.8 copy-start.17
  248.9 10.6 %collective-permute-start.12 = (bf16[1,1,2,1,1,96,768]{6,5,4,3,2,1,0:T(8,128)(2,1)}, bf16[1,1,2,1,1,96,768]{6,5,4,3,2,1,0:T(8,128)(2,1)}, u32[]{:S(2)}, u32[]{:S(2)}) collective-permute-start(bf16[1,1,2,1,1,96,768]{6,5,4,3,2,1,0:T(8,128)(2,1)} %pad_maximum_fusion.2), channel_id=1, source_target_pairs={{0,8},{4,12},{8,0},{12,4},{16,24},{20,28},{24,16},{28,20},{1,9},{5... | collective-permute-start | bytes 884744 | tf_op jit(solution)/shard_map/ppermute | solution.py:575
  250.3 13.6 %collective-permute-start.7 = (bf16[1,1,1,1,1,96,768]{6,5,4,3,2,1,0:T(8,128)(2,1)}, bf16[1,1,1,1,1,96,768]{6,5,4,3,2,1,0:T(8,128)(2,1)}, u32[]{:S(2)}, u32[]{:S(2)}) collective-permute-start(bf16[1,1,1,1,1,96,768]{6,5,4,3,2,1,0:T(8,128)(2,1)} %pad_maximum_fusion.4), channel_id=1, source_target_pairs={{0,16},{4,20},{8,24},{12,28},{16,0},{20,4},{24,8},{28,12},{1,17},{... | collective-permute-start | bytes 442376 | tf_op jit(solution)/shard_map/ppermute | solution.py:575
  254.0 9.8 %copy-start.10 = (bf16[1,1,2,1,1,48,768]{6,5,4,3,2,1,0:T(8,128)(2,1)S(1)}, bf16[1,1,2,1,1,48,768]{6,5,4,3,2,1,0:T(8,128)(2,1)}, u32[]{:S(2)}) copy-start(bf16[1,1,2,1,1,48,768]{6,5,4,3,2,1,0:T(8,128)(2,1)} %copy-done.9) | copy-start | bytes 442372
  254.0 9.8 %copy-start.12 = (bf16[1,1,2,1,1,48,768]{6,5,4,3,2,1,0:T(8,128)(2,1)S(1)}, bf16[1,1,2,1,1,48,768]{6,5,4,3,2,1,0:T(8,128)(2,1)}, u32[]{:S(2)}) copy-start(bf16[1,1,2,1,1,48,768]{6,5,4,3,2,1,0:T(8,128)(2,1)} %copy-done.11) | copy-start | bytes 442372
  260.5 0.7 copy-start.13
  260.5 1.9 copy-start.14
  263.0 7.5 %collective-permute-start.13 = (bf16[1,1,1,1,1,96,768]{6,5,4,3,2,1,0:T(8,128)(2,1)}, bf16[1,1,1,1,1,96,768]{6,5,4,3,2,1,0:T(8,128)(2,1)}, u32[]{:S(2)}, u32[]{:S(2)}) collective-permute-start(bf16[1,1,1,1,1,96,768]{6,5,4,3,2,1,0:T(8,128)(2,1)} %pad_maximum_fusion.5), channel_id=1, source_target_pairs={{0,16},{4,20},{8,24},{12,28},{16,0},{20,4},{24,8},{28,12},{1,17},{... | collective-permute-start | bytes 442376 | tf_op jit(solution)/shard_map/ppermute | solution.py:575
  265.8 10.4 %copy-start.20 = (f32[16,768]{1,0:T(8,128)S(1)}, f32[16,768]{1,0:T(8,128)}, u32[]{:S(2)}) copy-start(f32[16,768]{1,0:T(8,128)} %copy_bitcast_fusion.1) | copy-start | bytes 147460
  265.9 10.4 %copy-start.22 = (f32[4,1,768]{2,0,1:T(4,128)S(1)}, f32[4,1,768]{2,0,1:T(4,128)}, u32[]{:S(2)}) copy-start(f32[4,1,768]{2,0,1:T(4,128)} %copy.74) | copy-start | bytes 36868
  265.9 10.5 %copy-start.23 = (f32[2,768]{1,0:T(2,128)S(1)}, f32[2,768]{1,0:T(2,128)}, u32[]{:S(2)}) copy-start(f32[2,768]{1,0:T(2,128)} %slice.49) | copy-start | bytes 18436
  265.9 10.5 %copy-start.24 = (f32[2,768]{1,0:T(2,128)S(1)}, f32[2,768]{1,0:T(2,128)}, u32[]{:S(2)}) copy-start(f32[2,768]{1,0:T(2,128)} %slice.50) | copy-start | bytes 18436
  265.9 10.5 %copy-start.27 = (f32[1,768]{1,0:T(1,128)S(1)}, f32[1,768]{1,0:T(1,128)}, u32[]{:S(2)}) copy-start(f32[1,768]{1,0:T(1,128)} %get-tuple-element.189) | copy-start | bytes 9220
  276.5 4.7 %collective-permute-start.14 = (f32[31,768]{1,0:T(8,128)S(1)}, f32[31,768]{1,0:T(8,128)S(1)}, u32[]{:S(2)}, u32[]{:S(2)}) collective-permute-start(f32[31,768]{1,0:T(8,128)S(1)} %concatenate.27), channel_id=1, source_target_pairs={{0,4},{4,0},{8,12},{12,8},{16,20},{20,16},{24,28},{28,24},{1,5},{5... | collective-permute-start | bytes 285704 | tf_op jit(solution)/shard_map/ppermute | solution.py:575
  281.2 4.7 %collective-permute-start.15 = (f32[31,768]{1,0:T(8,128)S(1)}, f32[31,768]{1,0:T(8,128)S(1)}, u32[]{:S(2)}, u32[]{:S(2)}) collective-permute-start(f32[31,768]{1,0:T(8,128)S(1)} %add.923), channel_id=1, source_target_pairs={{0,8},{4,12},{8,0},{12,4},{16,24},{20,28},{24,16},{28,20},{1,9},{5... | collective-permute-start | bytes 285704 | tf_op jit(solution)/shard_map/ppermute | solution.py:575
  285.9 6.1 %collective-permute-start.16 = (f32[31,768]{1,0:T(8,128)S(1)}, f32[31,768]{1,0:T(8,128)S(1)}, u32[]{:S(2)}, u32[]{:S(2)}) collective-permute-start(f32[31,768]{1,0:T(8,128)S(1)} %add.924), channel_id=1, source_target_pairs={{0,16},{4,20},{8,24},{12,28},{16,0},{20,4},{24,8},{28,12},{1,17},{... | collective-permute-start | bytes 285704 | tf_op jit(solution)/shard_map/ppermute | solution.py:575
  292.0 1.4 collective-permute-start.17
  293.4 4.9 %copy-start.15 = (f32[31,768]{1,0:T(8,128)}, f32[31,768]{1,0:T(8,128)S(1)}, u32[]{:S(2)}) copy-start(f32[31,768]{1,0:T(8,128)S(1)} %add.926.ours_ref) | copy-start | bytes 285700
  293.4 4.9 %collective-permute-start.18 = (f32[31,768]{1,0:T(8,128)S(1)}, f32[31,768]{1,0:T(8,128)S(1)}, u32[]{:S(2)}, u32[]{:S(2)}) collective-permute-start(f32[31,768]{1,0:T(8,128)S(1)} %add.926.ours_ref), channel_id=1, source_target_pairs={{0,2},{1,3},{2,0},{3,1},{4,6},{5,7},{6,4},{7,5},{8,10},{9,11},{10,... | collective-permute-start | bytes 285704 | tf_op jit(solution)/shard_map/ppermute | solution.py:575
  298.3 0.6 copy-start.21
Sparse Core Ops, SparseCore 0:
  9.6 40.1 all-gather.4
  51.3 37.4 all-gather.6
  129.2 107.7 reduce-scatter.1

commit v4 on v3

--- a/solution.py
+++ b/solution.py
@@ -283,7 +283,20 @@
     )(hn, gy, vectors, up_bias, up_all)
 
 
-def mlp_out_kernel(chunk, hn_ref, dm_ref, z_ref, slope_ref, wup_ref, wdn_ref, m_ref, dhn_ref, gup_ref, gb_ref, du_ref, turned_ref):
+def place(keep_ref, send_ref, at, core, mine, value):
+    @pl.when(core == mine)
+    def _():
+        keep_ref[at] = value
+
+    @pl.when(core != mine)
+    def _():
+        send_ref[at] = value
+
+
+def mlp_out_kernel(
+    chunk, mine, hn_ref, dm_ref, z_ref, slope_ref, wup_ref, wdn_ref,
+    m_ref, dhn_ref, keep_ref, send_ref, gb_ref, du_ref, turned_ref,
+):
     tokens = hn_ref.shape[0]
 
     @pl.when(pl.program_id(0) == 0)
@@ -304,23 +317,25 @@
         return carry
 
     lax.fori_loop(0, tokens // chunk, rows, 0)
-    gup_ref[0] = mm(turned_ref[...], du_ref[...]).astype(BF)
-
-
-def mlp_out(hn, dm, z, slope, up_all, down_all, chunk):
+    place(keep_ref, send_ref, 0, pl.program_id(0) & 1, mine(), mm(turned_ref[...], du_ref[...]).astype(BF))
+
+
+def mlp_out(hn, dm, z, slope, up_all, down_all, chunk, mine):
     tokens, width = hn.shape
     blocks, _, hidden = up_all.shape
     shapes = [
         jax.ShapeDtypeStruct((tokens, width), F32),
         jax.ShapeDtypeStruct((tokens, width), F32),
-        jax.ShapeDtypeStruct((blocks, width, hidden), BF),
+        jax.ShapeDtypeStruct((blocks // 2, width, hidden), BF),
+        jax.ShapeDtypeStruct((blocks // 2, width, hidden), BF),
         jax.ShapeDtypeStruct((blocks, 1, hidden), F32),
     ]
-    return pl.pallas_call(
-        functools.partial(mlp_out_kernel, chunk),
+    by_pair = pl.BlockSpec((1, width, hidden), lambda i: (i // 2, 0, 0))
+    return pl.pallas_call(
+        functools.partial(mlp_out_kernel, chunk, mine),
         grid=(blocks,),
         in_specs=[fixed(hn.shape), fixed(dm.shape)] + [per_step(v.shape) for v in (z, slope, up_all, down_all)],
-        out_specs=[fixed(s.shape) for s in shapes[:2]] + [per_step(s.shape) for s in shapes[2:]],
+        out_specs=[fixed(s.shape) for s in shapes[:2]] + [by_pair, by_pair, per_step(shapes[4].shape)],
         out_shape=shapes,
         scratch_shapes=[pltpu.VMEM((tokens, hidden), BF), pltpu.VMEM((width, tokens), BF)],
         compiler_params=params(),
@@ -438,28 +453,27 @@
     )(qkv, do, bias)
 
 
-def grads_kernel(blocks, a_ref, dqkv_ref, o_ref, dat_ref, out_ref, turned_a, turned_o):
+def grads_kernel(blocks, mine, a_ref, dqkv_ref, o_ref, dat_ref, keep_ref, send_ref, turned_a, turned_o):
     wide_cols, thin_cols = dqkv_ref.shape[1] // blocks, dat_ref.shape[1] // blocks
     turned_a[...] = a_ref[...].T
     turned_o[...] = o_ref[...].T
+    here = mine()
     for n in range(blocks):
-        out_ref[n, :, :wide_cols] = mm(
-            turned_a[...], dqkv_ref[:, n * wide_cols : (n + 1) * wide_cols]
-        ).astype(BF)
-        out_ref[n, :, wide_cols:] = mm(
-            turned_o[...], dat_ref[:, n * thin_cols : (n + 1) * thin_cols]
-        ).astype(BF)
-
-
-def attention_grads(first, dqkv, mixed, dat, blocks):
+        left = mm(turned_a[...], dqkv_ref[:, n * wide_cols : (n + 1) * wide_cols]).astype(BF)
+        right = mm(turned_o[...], dat_ref[:, n * thin_cols : (n + 1) * thin_cols]).astype(BF)
+        place(keep_ref, send_ref, n // 2, n & 1, here, jnp.concatenate([left, right], 1))
+
+
+def attention_grads(first, dqkv, mixed, dat, blocks, mine):
     width = first.shape[1]
     cols = (dqkv.shape[1] + dat.shape[1]) // blocks
-    return pl.pallas_call(
-        functools.partial(grads_kernel, blocks),
+    shape = (blocks // 2, width, cols)
+    return pl.pallas_call(
+        functools.partial(grads_kernel, blocks, mine),
         grid=(1,),
         in_specs=[whole(v.shape) for v in (first, dqkv, mixed, dat)],
-        out_specs=whole((blocks, width, cols)),
-        out_shape=jax.ShapeDtypeStruct((blocks, width, cols), BF),
+        out_specs=[whole(shape)] * 2,
+        out_shape=[jax.ShapeDtypeStruct(shape, BF)] * 2,
         scratch_shapes=[pltpu.VMEM((width, first.shape[0]), BF)] * 2,
         compiler_params=params(),
         name="attention_grads",
@@ -511,7 +525,9 @@
     heads, vec_at, bias_at, square_at = rows
     row = lax.broadcasted_iota(jnp.int32, sums.shape, 0)
     small = jnp.where(row < square_at, sums, 0.0)
-    total = jnp.sum(jnp.sum(small * small, 0, keepdims=True), 1, keepdims=True) + sums[square_at : square_at + 1, :1]
+    total = jnp.sum(
+        jnp.sum(small * small, 0, keepdims=True) + sums[square_at : square_at + 1], 1, keepdims=True
+    )
     norm = jnp.sqrt(total)
     results[0][...] = norm
     clip = jnp.minimum(1.0, max_norm / (norm + clip_eps))
@@ -575,47 +591,155 @@
     return lax.ppermute(value, axis, [(i, i ^ (1 << bit)) for i in range(size)])
 
 
+def split_kernel(mine, keep_ref, come_ref, keep_a, send_a, keep_b, send_b):
+    half = keep_ref.shape[4] // 2
+    for out_a, out_b, flip in ((keep_a, keep_b, 0), (send_a, send_b, 1)):
+        side_a, side_b = mine[0]() ^ flip, mine[1]() ^ flip
+        for n in range(2):
+            for out, at, cols in (
+                (out_a.at[0, n], (side_a, 0, n), slice(0, half)),
+                (out_b.at[n, 0], (n, 0, side_b), slice(half, 2 * half)),
+            ):
+                total = keep_ref[(*at, slice(None), cols)].astype(F32) + come_ref[(*at, slice(None), cols)].astype(F32)
+                out[...] = total.astype(BF)
+
+
+def split_step(keep, come, mine):
+    _, middle, _, rows, cols = keep.shape
+    side = cols // 2
+    block = pl.BlockSpec((2, 1, 2, rows, cols), lambda i: (0, i, 0, 0, 0))
+    out_a = pl.BlockSpec((1, 2, rows, side), lambda i: (i, 0, 0, 0))
+    out_b = pl.BlockSpec((2, 1, rows, side), lambda i: (0, i, 0, 0))
+    shape_a = jax.ShapeDtypeStruct((middle, 2, rows, side), BF)
+    shape_b = jax.ShapeDtypeStruct((2, middle, rows, side), BF)
+    return pl.pallas_call(
+        functools.partial(split_kernel, mine),
+        grid=(middle,),
+        in_specs=[block, block],
+        out_specs=[out_a, out_a, out_b, out_b],
+        out_shape=[shape_a, shape_a, shape_b, shape_b],
+        compiler_params=params(),
+        name="split_step",
+    )(keep, come)
+
+
+def halve_kernel(mine, places, join, *refs):
+    parts = len(places)
+    ins, outs = refs[: 2 * parts], refs[2 * parts :]
+    for n in range(parts):
+        keep_ref, come_ref = ins[2 * n : 2 * n + 2]
+        count, _, cols = keep_ref.shape
+        left = cols * n if join else 0
+        outputs = outs[:2] if join else outs[2 * n : 2 * n + 2]
+        low = places[n]
+
+        def one(c, carry):
+            for out, side in zip(outputs, (mine[n](), 1 - mine[n]())):
+                at = ((c >> low) << (low + 1)) | (side << low) | (c & ((1 << low) - 1))
+                total = keep_ref[at].astype(F32) + come_ref[at].astype(F32)
+                out[c, :, left : left + cols] = total.astype(BF)
+            return carry
+
+        lax.fori_loop(0, count // 2, one, 0)
+
+
+def halve_step(parts, places, mine, join):
+    inputs = [v for pair in parts for v in pair]
+    shapes = []
+    for keep, _ in parts[:1] if join else parts:
+        count, rows, cols = keep.shape
+        shapes += [jax.ShapeDtypeStruct((count // 2, rows, cols * len(parts) if join else cols), BF)] * 2
+    return pl.pallas_call(
+        functools.partial(halve_kernel, mine, places, join),
+        grid=(1,),
+        in_specs=[whole(v.shape) for v in inputs],
+        out_specs=[whole(v.shape) for v in shapes],
+        out_shape=shapes,
+        compiler_params=params(),
+        name="halve_step",
+    )(*inputs)
+
+
 class Halving:
-    def __init__(self, grads, steps):
+    def __init__(self, keep, send, rows):
         self.bits = axis_bits()
-        self.shape = grads.shape[2:]
-        self.parts = [[grads.reshape((2,) * len(self.bits) + self.shape)]]
-        self.steps = list(steps)
+        cores = [d for d, (axis, _) in enumerate(self.bits) if axis == "narrow"]
+        self.dims = [[d for d in range(len(self.bits)) if d != cores[-1]]]
+        first, last = self.dims[0][0], self.dims[0][-1]
+        self.steps = [(first, last), (last, first)] + [(d,) for d in self.dims[0][-2:0:-1]]
+        shape = (-1, rows, keep.shape[-1])
+        self.keep = [keep.reshape(shape)]
+        self.sent = (send.reshape(shape),)
+        self.come = [swap(self.sent[0], *self.bits[cores[-1]])]
+
+    def mine(self, dim):
+        axis, bit = self.bits[dim]
+        return lambda: (lax.axis_index(axis) >> bit) & 1
 
     def send(self, *after):
-        dims = self.steps.pop(0)
-        last = [pieces[-1] for pieces in self.parts]
-        if after:
-            last = lax.optimization_barrier((*last, *after))
-        self.parts = [[*pieces[:-1], piece] for pieces, piece in zip(self.parts, last)]
-        if len(dims) > len(self.parts):
-            middle = self.shape[0] // 2
-            self.parts = [[p[..., :middle, :] for p in self.parts[0]], [p[..., middle:, :] for p in self.parts[0]]]
-        sent = []
-        for n, pieces in enumerate(self.parts):
-            dim = dims[n % len(dims)]
-            axis, bit = self.bits[dim]
-            mine = (lax.axis_index(axis) >> bit) & 1
-
-            def half(piece, side):
-                return lax.dynamic_slice_in_dim(piece, side, 1, dim)
-
-            sent.append(sum(half(p, 1 - mine).astype(F32) for p in pieces).astype(BF))
-            self.parts[n] = [half(p, mine) for p in pieces]
-        if len(dims) < len(sent):
-            sent = [jnp.concatenate(sent, -2)]
-        arrived = [swap(v, *self.bits[dim]) for v, dim in zip(sent, dims)]
-        if len(arrived) < len(self.parts):
-            arrived = jnp.split(arrived[0], 2, -2)
-        for pieces, piece in zip(self.parts, arrived):
-            pieces.append(piece)
-        return tuple(sent)
-
-    def result(self):
+        target = self.steps.pop(0)
+        come = lax.optimization_barrier((*self.come, *after)) if after else self.come
+        parts = len(self.keep)
+        if len(target) > parts:
+            rows, cols = self.keep[0].shape[1:]
+            shape = (2, -1, 2, rows, cols)
+            made = split_step(self.keep[0].reshape(shape), come[0].reshape(shape), [self.mine(d) for d in target])
+            made = [v.reshape(-1, rows, cols // 2) for v in made]
+            self.dims = self.dims * 2
+        else:
+            dims = target * (parts // len(target))
+            places = [len(own) - 1 - own.index(d) for own, d in zip(self.dims, dims)]
+            made = halve_step(
+                list(zip(self.keep, come)), places, [self.mine(d) for d in dims], len(target) < parts
+            )
+        self.keep, self.sent = made[::2], tuple(made[1::2])
+        self.dims = [[d for d in own if d != gone] for own, gone in zip(self.dims, target)]
+        self.come = [swap(v, *self.bits[d]) for v, d in zip(self.sent, target)]
+        return self.sent
+
+    def last_pair(self):
         while self.steps:
             self.send()
-        sums = [sum(p.astype(F32) for p in pieces).reshape(-1, self.shape[1]) for pieces in self.parts]
-        return jnp.concatenate(sums)
+        return self.keep[0][0], self.come[0][0]
+
+
+def finish_kernel(rows, up_a, up_b, attn_a, attn_b, down_ref, table_ref, cols_ref, gvec_ref, gone_ref, gb_ref, up_ref, attn_ref, ours_ref):
+    _, vec_at, bias_at, square_at = rows
+    width = ours_ref.shape[1]
+    up = up_a[...].astype(F32) + up_b[...].astype(F32)
+    attn = attn_a[...].astype(F32) + attn_b[...].astype(F32)
+    down = down_ref[...].astype(F32)
+    up_ref[...] = up
+    attn_ref[...] = attn
+    squares = jnp.sum(up * up + attn * attn + down * down, 0, keepdims=True)
+    ours_ref[...] = jnp.zeros_like(ours_ref)
+    for c in range(table_ref.shape[0]):
+        ours_ref[:vec_at, c * LANES : (c + 1) * LANES] = table_ref[c, 0] + table_ref[c, 1]
+    ours_ref[vec_at : vec_at + 1, :] = cols_ref[:, :width]
+    ours_ref[vec_at + 1 : vec_at + 2, :] = cols_ref[:, 2 * width :]
+    for to, source, at in ((2, gvec_ref, 0), (3, gvec_ref, 1), (4, gone_ref, 0), (5, gone_ref, 1)) + tuple(
+        (6 + n, gvec_ref, 2 + n) for n in range(4)
+    ):
+        ours_ref[vec_at + to : vec_at + to + 1, :] = source[at : at + 1, :]
+    for n in range(square_at - bias_at):
+        ours_ref[bias_at + n : bias_at + n + 1, :] = gb_ref[n]
+    ours_ref[square_at : square_at + 1, :] = squares
+
+
+def finish(rows, up, attn, down, small):
+    inputs = [*up, *attn, down, *small]
+    width = down.shape[1]
+    shapes = [jax.ShapeDtypeStruct(v.shape, F32) for v in (up[0], attn[0])]
+    shapes.append(jax.ShapeDtypeStruct((-(-(rows[3] + 1) // 8) * 8, width), F32))
+    return pl.pallas_call(
+        functools.partial(finish_kernel, rows),
+        grid=(1,),
+        in_specs=[whole(v.shape) for v in inputs],
+        out_specs=[whole(v.shape) for v in shapes],
+        out_shape=shapes,
+        compiler_params=params(),
+        name="finish",
+    )(*inputs)
 
 
 def gated(value, *waits):
@@ -623,53 +747,56 @@
 
 
 class Plan:
-    def __init__(self, wide, narrow):
-        self.wide, self.narrow = wide, narrow
-        lead = list(range(narrow.bit_length() - 1))
-        trail = [len(lead) + n for n in range(wide.bit_length() - 1)][::-1]
-        pair = (lead[0], trail[0])
-        self.steps = [(d,) for d in lead[:0:-1]] + [pair, pair[::-1]] + [(d,) for d in trail[1:]]
-
-    def halving(self, grads):
-        return Halving(grads.reshape(self.narrow, self.wide, grads.shape[1] // self.wide, grads.shape[2]), self.steps)
+    def __init__(self, rows):
+        self.rows = rows
+
+    @staticmethod
+    def mine():
+        return lax.axis_index("narrow") & 1
 
     def after_down(self, grads):
         rows = grads.reshape(-1, grads.shape[2])
         self.down = lax.psum_scatter(rows, ("narrow", "wide"), scatter_dimension=0, tiled=True)
-        return ()
-
-    def after_up(self, grads):
-        self.up = self.halving(grads)
-        return self.up.send()
+
+    def after_up(self, keep, send):
+        self.up = Halving(keep, send, self.rows)
+        return self.up.sent
 
     def next_up(self, *after):
         return self.up.send(*after)
 
-    def after_attention(self, grads):
-        self.attn = self.halving(grads)
-        return self.attn.send()
-
-    def next_all(self, *after):
-        return self.up.send(*after) + self.attn.send(*after)
+    def after_attention(self, keep, send):
+        self.attn = Halving(keep, send, self.rows)
+        return self.attn.sent
+
+    def next_attention(self, *after):
+        return self.attn.send(*after)
+
+    def next_both(self, *after):
+        self.up.send(*after)
+        self.attn.send(*after)
 
 
 class Alone:
+    @staticmethod
+    def mine():
+        return 0
+
     def after_down(self, grads):
         self.down = grads
-        return ()
-
-    def after_up(self, grads):
+
+    def after_up(self, *grads):
         self.up = grads
         return ()
 
-    def after_attention(self, grads):
+    def after_attention(self, *grads):
         self.attn = grads
         return ()
 
     def next_up(self, *after):
         return ()
 
-    next_all = next_up
+    next_attention = next_both = next_up
 
 
 def local_work(
@@ -691,35 +818,23 @@
     gy = out_grad * mim_mask.astype(BF)[:, :, None]
     first, qkv, mixed, attn, hn = front(block_in, qkv_weight, proj_weight, vectors, bias, heads)
     flat = lambda v: v.reshape(tokens, v.shape[-1])
-    z, slope, grad_down, dm = mlp_in(flat(hn), flat(gy), vectors, up_bias.reshape(blocks, 1, hidden), up_all, seq)
-    dm = gated(dm, *plan.after_down(grad_down))
-    m, dhn, grad_up, grad_bias = mlp_out(flat(hn), dm, z, slope, up_all, down_all, seq)
-    gy = gated(gy, *plan.after_up(grad_up))
+    z, slope, grad_down, dm = mlp_in(flat(hn), flat(gy), vectors, up_bias.reshape(blocks, 1, hidden), up_all, tokens)
+    plan.after_down(grad_down)
+    m, dhn, keep, send, grad_bias = mlp_out(flat(hn), dm, z, slope, up_all, down_all, tokens, plan.mine)
+    gy = gated(gy, *plan.after_up(keep, send))
     fold = lambda v: v.reshape(images, seq, width)
     block_out, dmid, dat, do, gvec = middle_back(block_in, gy, attn, fold(m), fold(dhn), proj_weight, vectors)
     do = gated(do, *plan.next_up(do))
     dqkv, ds, gcol = back(qkv, do, bias_t, heads)
     dat = gated(dat, *plan.next_up(dqkv))
-    grad_attn = attention_grads(flat(first), flat(dqkv), flat(mixed), flat(dat), blocks)
-    dmid = gated(dmid, *plan.after_attention(grad_attn))
+    keep, send = attention_grads(flat(first), flat(dqkv), flat(mixed), flat(dat), blocks, plan.mine)
+    dmid = gated(dmid, *plan.after_attention(keep, send))
     input_grad, gvec_one = input_grads(block_in, dqkv, dmid, qkv_weight, vectors)
     by_key = jnp.pad(ds.transpose(1, 0, 2), ((0, 0), (0, (-heads) % 8), (0, 0)))
-    by_key = gated(by_key, *plan.next_all(input_grad))
+    by_key = gated(by_key, *plan.next_attention(input_grad))
     sums = table_sums(index_t, by_key, chunks)
-    plan.next_all(sums)
-    sums = sums.reshape(chunks, 2, -1, LANES).sum(1)
-    grad_table = sums.transpose(1, 0, 2).reshape(-1, chunks * LANES)
-    small = jnp.concatenate(
-        [
-            grad_table,
-            gcol[:, :width],
-            gcol[:, 2 * width :],
-            gvec[:2],
-            gvec_one[:2],
-            gvec[2:6],
-            grad_bias.reshape(-1, width),
-        ]
-    )
+    plan.next_both(sums)
+    small = (sums.reshape(chunks, 2, -1, LANES), gcol, gvec, gvec_one, grad_bias)
     return block_out, input_grad, small, plan
 
 
@@ -741,19 +856,15 @@
     heads = rel_table.shape[1]
     up_all = lax.all_gather(up_weight, "narrow", axis=0)
     down_all = lax.all_gather(down_weight, "narrow", axis=0)
-    plan = Plan(lax.axis_size("wide"), lax.axis_size("narrow"))
+    plan = Plan(width // lax.axis_size("wide"))
     block_out, input_grad, small, plan = local_work(
         block_in, out_grad, mim_mask, rel_index, qkv_weight, proj_weight, up_all, down_all, vectors, up_bias, rel_table, plan
     )
-    up_shard = plan.up.result()
-    down_shard = plan.down
-    attn_shard = plan.attn.result()
-    squares = sum(jnp.sum(jnp.square(v.astype(F32))) for v in (down_shard, up_shard, attn_shard))
-    bias_rows = up_bias.shape[0] // width
     vec_at = heads + (-heads) % 8
     bias_at = vec_at + vectors.shape[0]
-    square_at = bias_at + bias_rows
-    ours = jnp.concatenate([small, jnp.full((1, width), squares)])
+    rows = (heads, vec_at, bias_at, bias_at + up_bias.shape[0] // width)
+    down_shard = plan.down
+    up_shard, attn_shard, ours = finish(rows, plan.up.last_pair(), plan.attn.last_pair(), down_shard, small)
     theirs = None
     for axis, bit in reversed(axis_bits()):
         ours = ours if theirs is None else ours + theirs
@@ -762,7 +873,7 @@
     matrices = state[:12]
     params_small = (vectors, state[12], state[13], line(up_bias), line(state[14]), line(state[15]), rel_table.T, *(v.T for v in state[16:]))
     norm, *updated = adam(
-        (heads, vec_at, bias_at, square_at),
+        rows,
         ours,
         theirs,
         (attn_shard, up_shard, down_shard),

time: 311 us -> 291 us (0.936)
  other arithmetic: 32 us -> 3.2 us
  Pallas kernels: 171 us -> 187 us
  local copies, waits for them, and re-layouts: 24.4 us -> 13.7 us
  waiting for transfers between devices: 49.6 us -> 53.1 us
    pallas_call x2 -> x11, Pallas kernels: 50 us -> 68.5 us  [the longest x1 29 us: mlp_out(): pl.pallas_call(functools.partial(mlp_out_kernel, chunk, mine), grid=(bloc...]
    convert_element_type x10 -> x0, other arithmetic: 18 us -> none  [send(): sent.append(sum((half(p, 1 - mine).astype(F32) for p in pieces)).astype(BF))]
    dynamic_slice x2 -> x0, local copies, waits for them, and re-layouts: 6.53 us -> none  [half(): return lax.dynamic_slice_in_dim(piece, side, 1, dim)]
    slice x6 -> x0, local copies, waits for them, and re-layouts: 6.23 us -> none  [the longest x2 3.72 us: send(): p[..., middle:, :]]
    unnamed x63 -> x48, local copies, waits for them, and re-layouts: 3.64 us -> 9.45 us
    concatenate x5 -> x0, other arithmetic: 5.27 us -> none  [the longest x4 2.81 us: send(): sent = [jnp.concatenate(sent, -2)]]
    reshape x2 -> x0, other arithmetic: 3.31 us -> none  [result(): sum((p.astype(F32) for p in pieces)).reshape(-1, self.shape[1])]
    reduce_sum x2 -> x0, other arithmetic: 3.13 us -> none  [the longest x1 1.61 us: shards(): jnp.sum(jnp.square(v.astype(F32)))]
  transfers between devices with their start and end apart: 22 -> 22, of which waited for: 11 -> 11; matrix products, arithmetic and copies ran while one was open for 15% -> 2% of each run, Pallas kernels for 42% -> 52%
where the time goes in v4:
time: 291 us
  Pallas kernels  187 us (64%)
  waiting for transfers between devices  53.1 us (18%)
  starting transfers between devices  19.4 us (7%)
  between operations  14 us (5%)
  local copies, waits for them, and re-layouts  13.7 us (5%)
  other arithmetic  3.2 us (1%)
    ppermute x19, waiting for transfers between devices, swap(): return lax.ppermute(value, axis, [(i, i ^ 1 << bit) for i in range(size)])  29.6 us
    pallas_call x1, Pallas kernels, mlp_out(): pl.pallas_call(functools.partial(mlp_out_kernel, chunk, mine), grid=(bloc...  29 us
    pallas_call x1, Pallas kernels, front(): pl.pallas_call(functools.partial(front_kernel, heads), grid=(images,), in...  26.7 us
    pallas_call x1, Pallas kernels, back(): pl.pallas_call(functools.partial(back_kernel, heads), grid=(images,), in_...  23.5 us
    all_gather x1, waiting for transfers between devices, shards(): down_all = lax.all_gather(down_weight, 'narrow', axis=0)  21.3 us
    ppermute x19, starting transfers between devices, swap(): return lax.ppermute(value, axis, [(i, i ^ 1 << bit) for i in range(size)])  19.3 us
    pallas_call x1, Pallas kernels, mlp_in(): pl.pallas_call(functools.partial(mlp_in_kernel, chunk), grid=(blocks,), i...  17.8 us
    pallas_call x1, Pallas kernels, attention_grads(): pl.pallas_call(functools.partial(grads_kernel, blocks, mine), grid=(1,),...  14.6 us
  transfers between devices with their start and end apart: 22, of which 11 were waited for; matrix products, arithmetic and copies ran while one was open for 2% of the time, Pallas kernels for 52%

profile of v4, /device:TPU:0, one launch (start us, length us, event | category | flops | bytes accessed | tf_op | source)
XLA Modules:
  0.0 290.5 jit_solution(404567953210164384)
XLA Ops:
  7.3 0.7 all-gather.5.cloned.1.call-update
  8.0 0.7 all-gather.7.cloned.1.call-update
  8.8 0.6 reshape.156.tab_ref
  9.8 0.7 pad.12.clone.idx_ref
  10.5 10.4 %bias_tables.1 = (f32[12,200,200]{2,1,0:T(8,128)}, f32[12,200,200]{2,1,0:T(8,128)}) custom-call(s32[200,256]{1,0:T(8,128)} %pad.12.clone.idx_ref, f32[12,6,128]{2,1,0:T(8,128)} %reshape.156.tab_ref), custom_call_target="tpu_custom_call" | custom-call | tf_op jit(solution)/shard_map/bias_tables/pallas_call | solution.py:122
  20.8 26.7 %front.1 = (bf16[5,200,768]{2,1,0:T(8,128)(2,1)}, bf16[5,200,2304]{2,1,0:T(8,128)(2,1)}, bf16[5,200,768]{2,1,0:T(8,128)(2,1)}, f32[5,200,768]{2,1,0:T(8,128)}, bf16[5,200,768]{2,1,0:T(8,128)(2,1)}) custom-call(bf16[5,200,768]{2,1,0:T(8,128)(2,1)} %x_ref.5, bf16[768,2304]{1,0:T(8,128)(2,1)} %wqkv_ref.3, bf16[768,768]{1,0:T(8,128)(2,1)} %wproj_ref.3, ...), custom_call_target="tpu_custom_call" | custom-call | tf_op jit(solution)/shard_map/front/pallas_call | solution.py:218
  47.6 1.4 broadcast_multiply_fusion.gy_ref
  49.0 0.8 all-gather.5.cloned.1.call-done
  49.8 17.8 %mlp_in.1 = (bf16[4,1000,768]{2,1,0:T(8,128)(2,1)}, bf16[4,1000,768]{2,1,0:T(8,128)(2,1)}, bf16[4,768,768]{2,1,0:T(8,128)(2,1)}, bf16[1000,768]{1,0:T(8,128)(2,1)}) custom-call(bf16[1000,768]{1,0:T(8,128)(2,1)} %bitcast.56, bf16[1000,768]{1,0:T(8,128)(2,1)} %bitcast.54, f32[10,768]{1,0:T(8,128)} %refs_12_.1, f32[4,1,768]{2,1,0:T(1,128)} %bitcast.81, ...), custom_call_target="tpu_custom_call" | custom-call | tf_op jit(solution)/shard_map/mlp_in/pallas_call | solution.py:268
  67.6 21.3 %all-gather.7.cloned.1.call-done = bf16[3072,768]{1,0:T(8,128)(2,1)} async-done(((bf16[768,768]{1,0:T(8,128)(2,1)}), bf16[3072,768]{1,0:T(8,128)(2,1)}) %all-gather.7.cloned.1.call-update) | async-done | bytes 4718608 | tf_op jit(solution)/shard_map/all_gather | solution.py:858
  88.8 29.0 %mlp_out.1 = (f32[1000,768]{1,0:T(8,128)}, f32[1000,768]{1,0:T(8,128)}, bf16[2,768,768]{2,1,0:T(8,128)(2,1)}, bf16[2,768,768]{2,1,0:T(8,128)(2,1)}, f32[4,1,768]{2,1,0:T(1,128)}) custom-call(bf16[1000,768]{1,0:T(8,128)(2,1)} %bitcast.57, bf16[1000,768]{1,0:T(8,128)(2,1)} %get-tuple-element.124.dm_ref, bf16[4,1000,768]{2,1,0:T(8,128)(2,1)} %get-tuple-element.125.z_ref, ...), custom_call_target="tpu_custom_call" | custom-call | tf_op jit(solution)/shard_map/mlp_out/pallas_call | solution.py:334
  117.8 0.3 collective-permute-start
  118.1 11.2 %middle_back.1 = (bf16[5,200,768]{2,1,0:T(8,128)(2,1)}, f32[5,200,768]{2,1,0:T(8,128)}, bf16[5,200,768]{2,1,0:T(8,128)(2,1)}, bf16[5,200,768]{2,1,0:T(8,128)(2,1)}, f32[8,768]{1,0:T(8,128)}) custom-call(bf16[5,200,768]{2,1,0:T(8,128)(2,1)} %x_ref.5, bf16[5,200,768]{2,1,0:T(8,128)(2,1)} %broadcast_multiply_fusion.gy_ref, ...), custom_call_target="tpu_custom_call" | custom-call | tf_op jit(solution)/shard_map/middle_back/pallas_call | solution.py:381
  129.3 1.4 copy-done.1
  130.7 4.4 %split_step.2 = (bf16[4,2,96,384]{3,2,1,0:T(8,128)(2,1)}, bf16[4,2,96,384]{3,2,1,0:T(8,128)(2,1)}, bf16[2,4,96,384]{3,2,1,0:T(8,128)(2,1)}, bf16[2,4,96,384]{3,2,1,0:T(8,128)(2,1)}) custom-call(bf16[2,4,2,96,768]{4,3,2,1,0:T(8,128)(2,1)} %bitcast.62, bf16[2,4,2,96,768]{4,3,2,1,0:T(8,128)(2,1)} %bitcast.63), custom_call_target="tpu_custom_call" | custom-call | tf_op jit(solution)/shard_map/split_step/pallas_call | solution.py:615
  135.1 1.5 collective-permute-start.2
  136.5 0.5 collective-permute-start.1
  137.0 23.5 %back.1 = (bf16[5,200,2304]{2,1,0:T(8,128)(2,1)}, f32[12,200,200]{2,1,0:T(8,128)}, f32[1,2304]{1,0:T(1,128)}) custom-call(bf16[5,200,2304]{2,1,0:T(8,128)(2,1)} %get-tuple-element.133.qkv_ref, bf16[5,200,768]{2,1,0:T(8,128)(2,1)} %get-tuple-element.139.do_ref, f32[12,200,200]{2,1,0:T(8,128)} %get-tuple-element.140.bias_ref), custom_call_target="tpu_custom_call" | custom-call | tf_op jit(solution)/shard_map/back/pallas_call | solution.py:445
  160.6 0.8 copy-done.6
  161.4 0.2 copy-done.7
  161.6 3.0 %halve_step.6 = (bf16[4,96,384]{2,1,0:T(8,128)(2,1)}, bf16[4,96,384]{2,1,0:T(8,128)(2,1)}, bf16[4,96,384]{2,1,0:T(8,128)(2,1)}, bf16[4,96,384]{2,1,0:T(8,128)(2,1)}) custom-call(bf16[8,96,384]{2,1,0:T(8,128)(2,1)} %bitcast.71, bf16[8,96,384]{2,1,0:T(8,128)(2,1)} %copy-done.7, bf16[8,96,384]{2,1,0:T(8,128)(2,1)} %bitcast.72, bf16[8,96,384]{2,1,0:T(8,128)(2,1)} %copy-done.6), custom_call_target="tpu_custom_call" | custom-call | tf_op jit(solution)/shard_map/halve_step/pallas_call | solution.py:652
  164.5 14.6 %attention_grads.1 = (bf16[2,768,768]{2,1,0:T(8,128)(2,1)}, bf16[2,768,768]{2,1,0:T(8,128)(2,1)}) custom-call(bf16[1000,768]{1,0:T(8,128)(2,1)} %bitcast.66, bf16[1000,2304]{1,0:T(8,128)(2,1)} %bitcast.53, bf16[1000,768]{1,0:T(8,128)(2,1)} %bitcast.67, bf16[1000,768]{1,0:T(8,128)(2,1)} %bitcast.68), custom_call_target="tpu_custom_call" | custom-call | tf_op jit(solution)/shard_map/attention_grads/pallas_call | solution.py:471
  179.1 12.0 %input_grads.1 = (f32[5,200,768]{2,1,0:T(8,128)}, f32[8,768]{1,0:T(8,128)}) custom-call(bf16[5,200,768]{2,1,0:T(8,128)(2,1)} %x_ref.5, bf16[5,200,2304]{2,1,0:T(8,128)(2,1)} %get-tuple-element.141.dqkv_ref, f32[5,200,768]{2,1,0:T(8,128)} %get-tuple-element.154.dmid_ref, bf16[768,2304]{1,0:T(8,128)(2,1)} %wqkv_ref.3, f32[10,768]{1,0:T(8,128)} %refs_12_.1), custom_call_target="tpu_custom_call" | custom-call | tf_op jit(solution)/shard_map/input_grads/pallas_call | solution.py:501
  191.1 1.5 copy-done.2
  192.6 4.5 %split_step.3 = (bf16[4,2,96,384]{3,2,1,0:T(8,128)(2,1)}, bf16[4,2,96,384]{3,2,1,0:T(8,128)(2,1)}, bf16[2,4,96,384]{3,2,1,0:T(8,128)(2,1)}, bf16[2,4,96,384]{3,2,1,0:T(8,128)(2,1)}) custom-call(bf16[2,4,2,96,768]{4,3,2,1,0:T(8,128)(2,1)} %bitcast.64, bf16[2,4,2,96,768]{4,3,2,1,0:T(8,128)(2,1)} %bitcast.65), custom_call_target="tpu_custom_call" | custom-call | tf_op jit(solution)/shard_map/split_step/pallas_call | solution.py:615
  197.1 1.7 collective-permute-start.8
  198.8 0.8 fusion.idx_ref
  199.6 0.8 copy.62
  200.4 2.0 pad.14.ds_ref
  202.5 1.8 collective-permute-start.3
  204.3 0.6 collective-permute-start.4
  204.9 12.3 %table_sums.1 = f32[192,128]{1,0:T(8,128)} custom-call(s32[200,200]{1,0:T(8,128)} %fusion.idx_ref, f32[200,16,200]{2,1,0:T(8,128)} %pad.14.ds_ref), custom_call_target="tpu_custom_call" | custom-call | tf_op jit(solution)/shard_map/table_sums/pallas_call | solution.py:157
  217.2 0.8 copy-done.4
  218.0 0.2 copy-done.5
  218.2 3.0 %halve_step.9 = (bf16[4,96,384]{2,1,0:T(8,128)(2,1)}, bf16[4,96,384]{2,1,0:T(8,128)(2,1)}, bf16[4,96,384]{2,1,0:T(8,128)(2,1)}, bf16[4,96,384]{2,1,0:T(8,128)(2,1)}) custom-call(bf16[8,96,384]{2,1,0:T(8,128)(2,1)} %bitcast.69, bf16[8,96,384]{2,1,0:T(8,128)(2,1)} %copy-done.5, bf16[8,96,384]{2,1,0:T(8,128)(2,1)} %bitcast.70, bf16[8,96,384]{2,1,0:T(8,128)(2,1)} %copy-done.4), custom_call_target="tpu_custom_call" | custom-call | tf_op jit(solution)/shard_map/halve_step/pallas_call | solution.py:652
  221.3 1.6 collective-permute-start.11
  222.9 0.7 copy-done.11
  223.7 2.2 halve_step.7
  225.9 1.5 collective-permute-start.6
  227.4 2.1 collective-permute-done.10.refs_1_
  229.5 0.6 copy-done.13
  230.3 2.2 halve_step.10
  232.5 1.4 collective-permute-start.12
  233.9 0.7 copy-done.9
  234.6 1.8 halve_step.8
  236.4 2.6 collective-permute-start.7
  239.0 3.2 %collective-permute-done.12.refs_1_ = bf16[2,96,768]{2,1,0:T(8,128)(2,1)S(1)} collective-permute-done((bf16[2,96,768]{2,1,0:T(8,128)(2,1)}, bf16[2,96,768]{2,1,0:T(8,128)(2,1)S(1)}, u32[]{:S(2)}, u32[]{:S(2)}) %collective-permute-start.12) | collective-permute-done | bytes 294944 | tf_op jit(solution)/shard_map/ppermute | solution.py:591
  242.2 0.7 copy-done.10
  242.9 1.8 halve_step.11
  244.7 1.9 collective-permute-start.13
  246.6 5.9 %collective-permute-done.13 = bf16[1,96,768]{2,1,0:T(8,128)(2,1)S(1)} collective-permute-done((bf16[1,96,768]{2,1,0:T(8,128)(2,1)}, bf16[1,96,768]{2,1,0:T(8,128)(2,1)S(1)}, u32[]{:S(2)}, u32[]{:S(2)}) %collective-permute-start.13) | collective-permute-done | bytes 147488 | tf_op jit(solution)/shard_map/ppermute | solution.py:591
  252.5 0.7 copy-done.18
  253.2 2.1 finish.1
  255.3 1.4 collective-permute-start.14
  256.7 3.5 %collective-permute-done.14 = f32[32,768]{1,0:T(8,128)S(1)} collective-permute-done((f32[32,768]{1,0:T(8,128)}, f32[32,768]{1,0:T(8,128)S(1)}, u32[]{:S(2)}, u32[]{:S(2)}) %collective-permute-start.14) | collective-permute-done | bytes 98336 | tf_op jit(solution)/shard_map/ppermute | solution.py:591
  260.1 0.9 add.20
  261.2 4.8 %collective-permute-done.15 = f32[32,768]{1,0:T(8,128)S(1)} collective-permute-done((f32[32,768]{1,0:T(8,128)S(1)}, f32[32,768]{1,0:T(8,128)S(1)}, u32[]{:S(2)}, u32[]{:S(2)}) %collective-permute-start.15) | collective-permute-done | bytes 98336 | tf_op jit(solution)/shard_map/ppermute | solution.py:591
  266.0 1.1 collective-permute-start.16
  267.1 5.1 %collective-permute-done.16 = f32[32,768]{1,0:T(8,128)S(1)} collective-permute-done((f32[32,768]{1,0:T(8,128)S(1)}, f32[32,768]{1,0:T(8,128)S(1)}, u32[]{:S(2)}, u32[]{:S(2)}) %collective-permute-start.16) | collective-permute-done | bytes 98336 | tf_op jit(solution)/shard_map/ppermute | solution.py:591
  272.3 1.3 collective-permute-done.17
  273.6 1.3 collective-permute-start.18
  274.9 3.6 %collective-permute-done.18.theirs_ref = f32[32,768]{1,0:T(8,128)S(1)} collective-permute-done((f32[32,768]{1,0:T(8,128)S(1)}, f32[32,768]{1,0:T(8,128)S(1)}, u32[]{:S(2)}, u32[]{:S(2)}) %collective-permute-start.18) | collective-permute-done | bytes 98336 | tf_op jit(solution)/shard_map/ppermute | solution.py:591
  278.6 0.6 copy-done.19
  279.2 4.8 %adam.1 = (f32[1,1]{1,0:T(1,128)}, f32[96,576]{1,0:T(8,128)}, f32[96,576]{1,0:T(8,128)}, f32[96,576]{1,0:T(8,128)}, bf16[96,576]{1,0:T(8,128)(2,1)}, /*index=5*/...) custom-call(f32[32,768]{1,0:T(8,128)} %copy-done.8, ...), custom_call_target="tpu_custom_call" | custom-call | tf_op jit(solution)/shard_map/adam/pallas_call | solution.py:570
  (64 shorter events, 1.2 us)
Async XLA Ops:
  7.2 1.6 copy-start.20
  7.2 1.6 copy-start.16
  7.2 2.2 copy-start.15
  7.2 42.6 %all-gather.5.cloned.1.call-start = ((), (), s32[]{:S(2)}) async-start(), calls=%async_computation.2 | async-start | bytes 5898240 | tf_op jit(solution)/shard_map/all_gather | solution.py:857
  8.0 80.9 %all-gather.7.cloned.1.call-start = ((), (), s32[]{:S(2)}) async-start(), calls=%async_computation.3 | async-start | bytes 5898240 | tf_op jit(solution)/shard_map/all_gather | solution.py:858
  8.7 237.9 %reduce-scatter.2.cloned.1.call-start = ((), (), s32[]{:S(2)}) async-start(), calls=%async_computation.1 | async-start | bytes 4866048 | tf_op jit(solution)/shard_map/reduce_scatter | solution.py:759
  20.8 26.7 %copy-start.3 = (bf16[5,200,768]{2,1,0:T(8,128)(2,1)S(1)}, bf16[5,200,768]{2,1,0:T(8,128)(2,1)}, u32[]{:S(2)}) copy-start(bf16[5,200,768]{2,1,0:T(8,128)(2,1)} %param.30) | copy-start | bytes 4608004
  117.8 11.5 %collective-permute-start = (bf16[16,96,768]{2,1,0:T(8,128)(2,1)}, bf16[16,96,768]{2,1,0:T(8,128)(2,1)S(1)}, u32[]{:S(2)}, u32[]{:S(2)}) collective-permute-start(bf16[16,96,768]{2,1,0:T(8,128)(2,1)} %bitcast.85), channel_id=1, source_target_pairs={{0,1},{1,0},{2,3},{3,2},{4,5},{5,4},{6,7},{7,6},{8,9},{9,8},{10,11... | collective-permute-start | bytes 7077896 | tf_op jit(solution)/shard_map/ppermute | solution.py:591
  129.3 1.4 copy-start.1
  135.1 25.5 %collective-permute-start.2 = (bf16[8,96,384]{2,1,0:T(8,128)(2,1)}, bf16[8,96,384]{2,1,0:T(8,128)(2,1)S(1)}, u32[]{:S(2)}, u32[]{:S(2)}) collective-permute-start(bf16[8,96,384]{2,1,0:T(8,128)(2,1)} %bitcast.90), channel_id=1, source_target_pairs={{0,4},{4,0},{8,12},{12,8},{16,20},{20,16},{24,28},{28,24},{1,5},{5... | collective-permute-start | bytes 1769480 | tf_op jit(solution)/shard_map/ppermute | solution.py:591
  136.5 24.0 %collective-permute-start.1 = (bf16[8,96,384]{2,1,0:T(8,128)(2,1)}, bf16[8,96,384]{2,1,0:T(8,128)(2,1)S(1)}, u32[]{:S(2)}, u32[]{:S(2)}) collective-permute-start(bf16[8,96,384]{2,1,0:T(8,128)(2,1)} %bitcast.89), channel_id=1, source_target_pairs={{0,2},{1,3},{2,0},{3,1},{4,6},{5,7},{6,4},{7,5},{8,10},{9,11},{10,... | collective-permute-start | bytes 1769480 | tf_op jit(solution)/shard_map/ppermute | solution.py:591
  160.5 0.8 copy-start.6
  160.6 1.0 copy-start.7
  179.1 12.0 %collective-permute-start.5 = (bf16[16,96,768]{2,1,0:T(8,128)(2,1)}, bf16[16,96,768]{2,1,0:T(8,128)(2,1)S(1)}, u32[]{:S(2)}, u32[]{:S(2)}) collective-permute-start(bf16[16,96,768]{2,1,0:T(8,128)(2,1)} %bitcast.86), channel_id=1, source_target_pairs={{0,1},{1,0},{2,3},{3,2},{4,5},{5,4},{6,7},{7,6},{8,9},{9,8},{10,11... | collective-permute-start | bytes 7077896 | tf_op jit(solution)/shard_map/ppermute | solution.py:591
  191.1 1.5 copy-start.2
  192.6 7.0 %copy-start = (f32[12,200,200]{2,1,0:T(8,128)S(1)}, f32[12,200,200]{2,1,0:T(8,128)}, u32[]{:S(2)}) copy-start(f32[12,200,200]{2,1,0:T(8,128)} %get-tuple-element.157) | copy-start | bytes 5760004
  197.1 20.0 %collective-permute-start.9 = (bf16[8,96,384]{2,1,0:T(8,128)(2,1)}, bf16[8,96,384]{2,1,0:T(8,128)(2,1)S(1)}, u32[]{:S(2)}, u32[]{:S(2)}) collective-permute-start(bf16[8,96,384]{2,1,0:T(8,128)(2,1)} %bitcast.88), channel_id=1, source_target_pairs={{0,4},{4,0},{8,12},{12,8},{16,20},{20,16},{24,28},{28,24},{1,5},{5... | collective-permute-start | bytes 1769480 | tf_op jit(solution)/shard_map/ppermute | solution.py:591
  197.1 20.0 %collective-permute-start.8 = (bf16[8,96,384]{2,1,0:T(8,128)(2,1)}, bf16[8,96,384]{2,1,0:T(8,128)(2,1)S(1)}, u32[]{:S(2)}, u32[]{:S(2)}) collective-permute-start(bf16[8,96,384]{2,1,0:T(8,128)(2,1)} %bitcast.87), channel_id=1, source_target_pairs={{0,2},{1,3},{2,0},{3,1},{4,6},{5,7},{6,4},{7,5},{8,10},{9,11},{10,... | collective-permute-start | bytes 1769480 | tf_op jit(solution)/shard_map/ppermute | solution.py:591
  200.4 2.1 copy-start.22
  200.4 3.8 %copy-start.21 = (bf16[4,96,384]{2,1,0:T(8,128)(2,1)S(1)}, bf16[4,96,384]{2,1,0:T(8,128)(2,1)}, u32[]{:S(2)}) copy-start(bf16[4,96,384]{2,1,0:T(8,128)(2,1)} %get-tuple-element.151) | copy-start | bytes 884740
  202.5 20.4 %collective-permute-start.3 = (bf16[4,96,384]{2,1,0:T(8,128)(2,1)S(1)}, bf16[4,96,384]{2,1,0:T(8,128)(2,1)S(1)}, u32[]{:S(2)}, u32[]{:S(2)}) collective-permute-start(bf16[4,96,384]{2,1,0:T(8,128)(2,1)S(1)} %copy-done.22), channel_id=1, source_target_pairs={{0,4},{4,0},{8,12},{12,8},{16,20},{20,16},{24,28},{28,24},{1,5},{5... | collective-permute-start | bytes 884744 | tf_op jit(solution)/shard_map/ppermute | solution.py:591
  204.3 18.6 %collective-permute-start.4 = (bf16[4,96,384]{2,1,0:T(8,128)(2,1)S(1)}, bf16[4,96,384]{2,1,0:T(8,128)(2,1)S(1)}, u32[]{:S(2)}, u32[]{:S(2)}) collective-permute-start(bf16[4,96,384]{2,1,0:T(8,128)(2,1)S(1)} %copy-done.21), channel_id=1, source_target_pairs={{0,2},{1,3},{2,0},{3,1},{4,6},{5,7},{6,4},{7,5},{8,10},{9,11},{10,... | collective-permute-start | bytes 884744 | tf_op jit(solution)/shard_map/ppermute | solution.py:591
  217.2 0.8 copy-start.4
  217.2 1.0 copy-start.5
  221.2 8.3 %collective-permute-start.10 = (bf16[4,96,384]{2,1,0:T(8,128)(2,1)}, bf16[4,96,384]{2,1,0:T(8,128)(2,1)S(1)}, u32[]{:S(2)}, u32[]{:S(2)}) collective-permute-start(bf16[4,96,384]{2,1,0:T(8,128)(2,1)} %get-tuple-element.175), channel_id=1, source_target_pairs={{0,4},{4,0},{8,12},{12,8},{16,20},{20,16},{24,28},{28,24},{1,5},{5... | collective-permute-start | bytes 884744 | tf_op jit(solution)/shard_map/ppermute | solution.py:591
  221.3 8.2 %collective-permute-start.11 = (bf16[4,96,384]{2,1,0:T(8,128)(2,1)}, bf16[4,96,384]{2,1,0:T(8,128)(2,1)S(1)}, u32[]{:S(2)}, u32[]{:S(2)}) collective-permute-start(bf16[4,96,384]{2,1,0:T(8,128)(2,1)} %get-tuple-element.177), channel_id=1, source_target_pairs={{0,2},{1,3},{2,0},{3,1},{4,6},{5,7},{6,4},{7,5},{8,10},{9,11},{10,... | collective-permute-start | bytes 884744 | tf_op jit(solution)/shard_map/ppermute | solution.py:591
  222.9 0.7 copy-start.11
  222.9 0.8 copy-start.12
  225.9 7.9 %collective-permute-start.6 = (bf16[2,96,768]{2,1,0:T(8,128)(2,1)}, bf16[2,96,768]{2,1,0:T(8,128)(2,1)S(1)}, u32[]{:S(2)}, u32[]{:S(2)}) collective-permute-start(bf16[2,96,768]{2,1,0:T(8,128)(2,1)} %get-tuple-element.167), channel_id=1, source_target_pairs={{0,8},{4,12},{8,0},{12,4},{16,24},{20,28},{24,16},{28,20},{1,9},{5... | collective-permute-start | bytes 884744 | tf_op jit(solution)/shard_map/ppermute | solution.py:591
  229.5 0.7 copy-start.13
  229.5 0.7 copy-start.14
  232.5 9.7 %collective-permute-start.12 = (bf16[2,96,768]{2,1,0:T(8,128)(2,1)}, bf16[2,96,768]{2,1,0:T(8,128)(2,1)S(1)}, u32[]{:S(2)}, u32[]{:S(2)}) collective-permute-start(bf16[2,96,768]{2,1,0:T(8,128)(2,1)} %get-tuple-element.179), channel_id=1, source_target_pairs={{0,8},{4,12},{8,0},{12,4},{16,24},{20,28},{24,16},{28,20},{1,9},{5... | collective-permute-start | bytes 884744 | tf_op jit(solution)/shard_map/ppermute | solution.py:591
  233.9 0.7 copy-start.9
  236.4 10.2 %collective-permute-start.7 = (bf16[1,96,768]{2,1,0:T(8,128)(2,1)}, bf16[1,96,768]{2,1,0:T(8,128)(2,1)S(1)}, u32[]{:S(2)}, u32[]{:S(2)}) collective-permute-start(bf16[1,96,768]{2,1,0:T(8,128)(2,1)} %get-tuple-element.169), channel_id=1, source_target_pairs={{0,16},{4,20},{8,24},{12,28},{16,0},{20,4},{24,8},{28,12},{1,17},{... | collective-permute-start | bytes 442376 | tf_op jit(solution)/shard_map/ppermute | solution.py:591
  242.2 0.7 copy-start.10
  244.7 7.8 %collective-permute-start.13 = (bf16[1,96,768]{2,1,0:T(8,128)(2,1)}, bf16[1,96,768]{2,1,0:T(8,128)(2,1)S(1)}, u32[]{:S(2)}, u32[]{:S(2)}) collective-permute-start(bf16[1,96,768]{2,1,0:T(8,128)(2,1)} %get-tuple-element.181), channel_id=1, source_target_pairs={{0,16},{4,20},{8,24},{12,28},{16,0},{20,4},{24,8},{28,12},{1,17},{... | collective-permute-start | bytes 442376 | tf_op jit(solution)/shard_map/ppermute | solution.py:591
  246.6 6.0 %copy-start.17 = (bf16[1,96,768]{2,1,0:T(8,128)(2,1)}, bf16[1,96,768]{2,1,0:T(8,128)(2,1)S(1)}, u32[]{:S(2)}) copy-start(bf16[1,96,768]{2,1,0:T(8,128)(2,1)S(1)} %collective-permute-done.7) | copy-start | bytes 442372
  252.5 0.7 copy-start.18
  255.3 4.8 %collective-permute-start.14 = (f32[32,768]{1,0:T(8,128)}, f32[32,768]{1,0:T(8,128)S(1)}, u32[]{:S(2)}, u32[]{:S(2)}) collective-permute-start(f32[32,768]{1,0:T(8,128)} %get-tuple-element.187), channel_id=1, source_target_pairs={{0,4},{4,0},{8,12},{12,8},{16,20},{20,16},{24,28},{28,24},{1,5},{5... | collective-permute-start | bytes 294920 | tf_op jit(solution)/shard_map/ppermute | solution.py:591
  261.0 5.0 %collective-permute-start.15 = (f32[32,768]{1,0:T(8,128)S(1)}, f32[32,768]{1,0:T(8,128)S(1)}, u32[]{:S(2)}, u32[]{:S(2)}) collective-permute-start(f32[32,768]{1,0:T(8,128)S(1)} %add.20), channel_id=1, source_target_pairs={{0,8},{4,12},{8,0},{12,4},{16,24},{20,28},{24,16},{28,20},{1,9},{5... | collective-permute-start | bytes 294920 | tf_op jit(solution)/shard_map/ppermute | solution.py:591
  266.0 6.2 %collective-permute-start.16 = (f32[32,768]{1,0:T(8,128)S(1)}, f32[32,768]{1,0:T(8,128)S(1)}, u32[]{:S(2)}, u32[]{:S(2)}) collective-permute-start(f32[32,768]{1,0:T(8,128)S(1)} %add.21), channel_id=1, source_target_pairs={{0,16},{4,20},{8,24},{12,28},{16,0},{20,4},{24,8},{28,12},{1,17},{... | collective-permute-start | bytes 294920 | tf_op jit(solution)/shard_map/ppermute | solution.py:591
  272.3 1.4 collective-permute-start.17
  273.6 4.9 %copy-start.8 = (f32[32,768]{1,0:T(8,128)}, f32[32,768]{1,0:T(8,128)S(1)}, u32[]{:S(2)}) copy-start(f32[32,768]{1,0:T(8,128)S(1)} %add.23.ours_ref) | copy-start | bytes 294916
  273.6 4.9 %collective-permute-start.18 = (f32[32,768]{1,0:T(8,128)S(1)}, f32[32,768]{1,0:T(8,128)S(1)}, u32[]{:S(2)}, u32[]{:S(2)}) collective-permute-start(f32[32,768]{1,0:T(8,128)S(1)} %add.23.ours_ref), channel_id=1, source_target_pairs={{0,2},{1,3},{2,0},{3,1},{4,6},{5,7},{6,4},{7,5},{8,10},{9,11},{10,... | collective-permute-start | bytes 294920 | tf_op jit(solution)/shard_map/ppermute | solution.py:591
  278.6 0.6 copy-start.19
Sparse Core Ops, SparseCore 0:
  9.6 40.1 all-gather.4
  51.4 37.4 all-gather.6
  118.2 107.3 reduce-scatter.1

commit v5 on v4

--- a/solution.py
+++ b/solution.py
@@ -85,47 +85,39 @@
     ]
 
 
-def bias_kernel(idx_ref, tab_ref, out_ref, back_ref, work_ref):
+def bias_kernel(idx_ref, tab_ref, out_ref):
     heads, seq = out_ref.shape[0], out_ref.shape[1]
     chunks = tab_ref.shape[1]
 
     def rows(step, carry):
         at = pl.multiple_of(step * 8, 8)
-        for half in range(idx_ref.shape[1] // LANES):
-            cols = slice(half * LANES, (half + 1) * LANES)
-            index = idx_ref[pl.ds(at, 8), cols]
+        for left in range(0, seq, LANES):
+            index = idx_ref[pl.ds(at, 8), left : left + LANES]
             low, high = index & (LANES - 1), index >> 7
             match = [high == c for c in range(chunks)]
+            width = min(LANES, seq - left)
             for h in range(heads):
                 found = jnp.full((8, LANES), -1e30, F32)
                 for c in range(chunks):
                     row = jnp.broadcast_to(tab_ref[h, c : c + 1, :], (8, LANES))
                     taken = jnp.take_along_axis(row, low, axis=1, mode="promise_in_bounds")
                     found = jnp.where(match[c], taken, found)
-                work_ref[h, pl.ds(at, 8), cols] = found
+                out_ref[h, pl.ds(at, 8), left : left + width] = found[:, :width]
         return carry
 
     lax.fori_loop(0, seq // 8, rows, 0)
 
-    def turn(h, carry):
-        out_ref[h] = work_ref[h, :seq, :seq]
-        back_ref[h] = work_ref[h].T[:seq, :seq]
-        return carry
-
-    lax.fori_loop(0, heads, turn, 0)
-
 
 def bias_tables(index, table_rows):
-    seq, padded = index.shape
-    heads, chunks, _ = table_rows.shape
+    seq, _ = index.shape
+    heads, _, _ = table_rows.shape
     shape = (heads, seq, seq)
     return pl.pallas_call(
         bias_kernel,
         grid=(1,),
         in_specs=[whole(index.shape), whole(table_rows.shape)],
-        out_specs=[whole(shape)] * 2,
-        out_shape=[jax.ShapeDtypeStruct(shape, F32)] * 2,
-        scratch_shapes=[pltpu.VMEM((heads, padded, padded), F32)],
+        out_specs=whole(shape),
+        out_shape=jax.ShapeDtypeStruct(shape, F32),
         compiler_params=params(),
         name="bias_tables",
     )(index, table_rows)
@@ -137,7 +129,7 @@
     out_ref[...] = jnp.zeros_like(out_ref)
     kinds = lax.broadcasted_iota(jnp.int32, (LANES, seq), 0)
 
-    def one_key(j, total):
+    def one_query(j, total):
         index = idx_ref[pl.ds(j, 1), :]
         low, high = index & (LANES - 1), index >> 7
         onehot = jnp.where(jnp.broadcast_to(low, (LANES, seq)) == kinds, 1.0, 0.0).astype(BF)
@@ -148,24 +140,24 @@
         parts = jnp.concatenate([jnp.where(high_all == c, both, 0.0) for c in range(chunks)], 0)
         return total + mm_nt(parts.astype(BF), onehot)
 
-    out_ref[...] = lax.fori_loop(0, seq, one_key, jnp.zeros(out_ref.shape, F32), unroll=UNROLL_T)
-
-
-def table_sums(index_t, grads, chunks):
+    out_ref[...] = lax.fori_loop(0, seq, one_query, jnp.zeros(out_ref.shape, F32), unroll=UNROLL_T)
+
+
+def table_sums(index, grads, chunks):
     seq, heads, _ = grads.shape
     out = (chunks * 2 * heads, LANES)
     return pl.pallas_call(
         table_kernel,
         grid=(1,),
-        in_specs=[whole(index_t.shape), whole(grads.shape)],
+        in_specs=[whole(index.shape), whole(grads.shape)],
         out_specs=whole(out),
         out_shape=jax.ShapeDtypeStruct(out, F32),
         compiler_params=params(),
         name="table_sums",
-    )(index_t, grads)
-
-
-def front_kernel(heads, x_ref, wqkv_ref, wproj_ref, vec_ref, bias_ref, a_ref, qkv_ref, o_ref, attn_ref, hn_ref):
+    )(index, grads)
+
+
+def front_kernel(heads, x_ref, wqkv_ref, wproj_ref, vec_ref, bias_ref, a_ref, qkv_ref, p_ref, o_ref, attn_ref, hn_ref):
     width = x_ref.shape[2]
     head_dim = width // heads
     scale = head_dim ** (-0.5)
@@ -194,7 +186,9 @@
             s = mm_nt(qm, k) + bias_ref[g * per + e]
             p = jnp.exp(s - jnp.max(s, -1, keepdims=True))
             p = p * (1.0 / jnp.sum(p, -1, keepdims=True))
-            mixed = mm(p.astype(BF), v)
+            p = p.astype(BF)
+            p_ref[0, g * per + e] = p
+            mixed = mm(p, v)
             out = mixed if out is None else jnp.where(masks[e], mixed, out)
         o_ref[0, :, pl.ds(at, pair)] = out.astype(BF)
         return carry
@@ -211,6 +205,7 @@
     shapes = [
         jax.ShapeDtypeStruct((images, seq, width), BF),
         jax.ShapeDtypeStruct((images, seq, 3 * width), BF),
+        jax.ShapeDtypeStruct((images, heads, seq, seq), BF),
         jax.ShapeDtypeStruct((images, seq, width), BF),
         jax.ShapeDtypeStruct((images, seq, width), F32),
         jax.ShapeDtypeStruct((images, seq, width), BF),
@@ -232,8 +227,20 @@
     )(x, qkv_weight, proj_weight, vectors, bias)
 
 
-def mlp_in_kernel(chunk, hn_ref, gy_ref, vec_ref, bup_ref, wup_ref, z_ref, slope_ref, gdn_ref, dm_ref, turned_ref):
+def pick(refs, at, out_ref):
+    for n, ref in enumerate(refs):
+
+        @pl.when(at == n)
+        def _():
+            out_ref[...] = ref[...]
+
+
+def mlp_in_kernel(
+    chunk, owner, hn_ref, gy_ref, vec_ref, bup_ref, up_a, up_b, up_c, up_d,
+    z_ref, slope_ref, gdn_ref, dm_ref, turned_ref, wup_ref,
+):
     tokens = hn_ref.shape[0]
+    pick((up_a, up_b, up_c, up_d), pl.program_id(0) ^ owner(), wup_ref)
 
     @pl.when(pl.program_id(0) == 0)
     def _():
@@ -247,7 +254,7 @@
 
     def rows(step, carry):
         at = pl.ds(pl.multiple_of(step * chunk, chunk), chunk)
-        u = mm(hn_ref[at, :], wup_ref[0]) + bup_ref[0]
+        u = mm(hn_ref[at, :], wup_ref[...]) + bup_ref[0]
         gate = 0.5 * (1.0 + lax.erf(u * 0.7071067811865476))
         z_ref[0, at, :] = (u * gate).astype(BF)
         slope_ref[0, at, :] = (gate + u * jnp.exp(-0.5 * u * u) * 0.3989422804014327).astype(BF)
@@ -257,30 +264,30 @@
     gdn_ref[0] = mm(turned_ref[...], z_ref[0]).astype(BF)
 
 
-def mlp_in(hn, gy, vectors, up_bias, up_all, chunk):
+def mlp_in(hn, gy, vectors, up_bias, ups, chunk, owner):
     tokens, width = hn.shape
-    blocks, _, hidden = up_all.shape
+    blocks, hidden = len(ups), ups[0].shape[1]
     shapes = [
         jax.ShapeDtypeStruct((blocks, tokens, hidden), BF),
         jax.ShapeDtypeStruct((blocks, tokens, hidden), BF),
         jax.ShapeDtypeStruct((blocks, width, hidden), BF),
     ]
     return pl.pallas_call(
-        functools.partial(mlp_in_kernel, chunk),
+        functools.partial(mlp_in_kernel, chunk, owner),
         grid=(blocks,),
         in_specs=[
             fixed(hn.shape),
             fixed(gy.shape),
             fixed(vectors.shape),
             per_step(up_bias.shape),
-            per_step(up_all.shape),
+            *(fixed(v.shape) for v in ups),
         ],
         out_specs=[per_step(s.shape) for s in shapes] + [fixed((tokens, width))],
         out_shape=shapes + [jax.ShapeDtypeStruct((tokens, width), BF)],
-        scratch_shapes=[pltpu.VMEM((width, tokens), BF)],
+        scratch_shapes=[pltpu.VMEM((width, tokens), BF), pltpu.VMEM((width, hidden), BF)],
         compiler_params=params(),
         name="mlp_in",
-    )(hn, gy, vectors, up_bias, up_all)
+    )(hn, gy, vectors, up_bias, *ups)
 
 
 def place(keep_ref, send_ref, at, core, mine, value):
@@ -294,10 +301,11 @@
 
 
 def mlp_out_kernel(
-    chunk, mine, hn_ref, dm_ref, z_ref, slope_ref, wup_ref, wdn_ref,
-    m_ref, dhn_ref, keep_ref, send_ref, gb_ref, du_ref, turned_ref,
+    chunk, owner, hn_ref, dm_ref, z_ref, slope_ref, wdn_ref, up_a, up_b, up_c, up_d,
+    m_ref, dhn_ref, keep_ref, send_ref, gb_ref, du_ref, turned_ref, wup_ref,
 ):
     tokens = hn_ref.shape[0]
+    pick((up_a, up_b, up_c, up_d), pl.program_id(0) ^ owner(), wup_ref)
 
     @pl.when(pl.program_id(0) == 0)
     def _():
@@ -313,16 +321,16 @@
         du = (mm(dm_ref[at, :], wdn_ref[0]) * slope_ref[0, at, :].astype(F32)).astype(BF)
         du_ref[at, :] = du
         gb_ref[0] += jnp.sum(du.astype(F32), 0, keepdims=True)
-        dhn_ref[at, :] += mm_nt(du, wup_ref[0])
+        dhn_ref[at, :] += mm_nt(du, wup_ref[...])
         return carry
 
     lax.fori_loop(0, tokens // chunk, rows, 0)
-    place(keep_ref, send_ref, 0, pl.program_id(0) & 1, mine(), mm(turned_ref[...], du_ref[...]).astype(BF))
-
-
-def mlp_out(hn, dm, z, slope, up_all, down_all, chunk, mine):
+    place(keep_ref, send_ref, 0, pl.program_id(0) & 1, owner() & 1, mm(turned_ref[...], du_ref[...]).astype(BF))
+
+
+def mlp_out(hn, dm, z, slope, ups, down_all, chunk, owner):
     tokens, width = hn.shape
-    blocks, _, hidden = up_all.shape
+    blocks, _, hidden = down_all.shape
     shapes = [
         jax.ShapeDtypeStruct((tokens, width), F32),
         jax.ShapeDtypeStruct((tokens, width), F32),
@@ -332,15 +340,19 @@
     ]
     by_pair = pl.BlockSpec((1, width, hidden), lambda i: (i // 2, 0, 0))
     return pl.pallas_call(
-        functools.partial(mlp_out_kernel, chunk, mine),
+        functools.partial(mlp_out_kernel, chunk, owner),
         grid=(blocks,),
-        in_specs=[fixed(hn.shape), fixed(dm.shape)] + [per_step(v.shape) for v in (z, slope, up_all, down_all)],
+        in_specs=[fixed(hn.shape), fixed(dm.shape)] + [per_step(v.shape) for v in (z, slope, down_all)] + [fixed(v.shape) for v in ups],
         out_specs=[fixed(s.shape) for s in shapes[:2]] + [by_pair, by_pair, per_step(shapes[4].shape)],
         out_shape=shapes,
-        scratch_shapes=[pltpu.VMEM((tokens, hidden), BF), pltpu.VMEM((width, tokens), BF)],
+        scratch_shapes=[
+            pltpu.VMEM((tokens, hidden), BF),
+            pltpu.VMEM((width, tokens), BF),
+            pltpu.VMEM((width, hidden), BF),
+        ],
         compiler_params=params(),
         name="mlp_out",
-    )(hn, dm, z, slope, up_all, down_all)
+    )(hn, dm, z, slope, down_all, *ups)
 
 
 def middle_kernel(
@@ -389,7 +401,7 @@
     )(x, gy, attn, m, dhn, proj_weight, vectors)
 
 
-def back_kernel(heads, qkv_ref, do_ref, bias_ref, dqkv_ref, ds_ref, gcol_ref):
+def back_kernel(heads, qkv_ref, do_ref, p_ref, dqkv_ref, ds_ref, gcol_ref):
     width = do_ref.shape[2]
     head_dim = width // heads
     scale = head_dim ** (-0.5)
@@ -414,15 +426,14 @@
             pick = jnp.where(masks[e], scale, 0.0).astype(BF)
             keep = jnp.where(masks[e], 1.0, 0.0).astype(BF)
             qm, km, dom = q * pick, k * pick, do * keep
-            s = mm_nt(k, qm) + bias_ref[g * per + e]
-            p = jnp.exp(s - jnp.max(s, 0, keepdims=True))
-            p = p * (1.0 / jnp.sum(p, 0, keepdims=True))
-            dv_e = mm(p.astype(BF), dom)
-            dp = mm_nt(v, dom)
-            ds = (p * (dp - jnp.sum(dp * p, 0, keepdims=True))).astype(BF)
+            rounded = p_ref[0, g * per + e]
+            p = rounded.astype(F32)
+            dv_e = mm_tn(rounded, dom)
+            dp = mm_nt(dom, v)
+            ds = (p * (dp - jnp.sum(dp * p, -1, keepdims=True))).astype(BF)
             ds_ref[g * per + e] += ds.astype(F32)
-            dk_e = mm(ds, qm)
-            dq_e = mm_tn(ds, km)
+            dk_e = mm_tn(ds, qm)
+            dq_e = mm(ds, km)
             dq = dq_e if dq is None else dq + dq_e
             dk = dk_e if dk is None else dk + dk_e
             dv = dv_e if dv is None else dv + dv_e
@@ -435,7 +446,7 @@
     lax.fori_loop(0, width // pair, one_pair, 0, unroll=UNROLL_B)
 
 
-def back(qkv, do, bias, heads):
+def back(qkv, do, p, heads):
     images, seq, width = do.shape
     shapes = [
         jax.ShapeDtypeStruct((images, seq, 3 * width), BF),
@@ -445,31 +456,31 @@
     return pl.pallas_call(
         functools.partial(back_kernel, heads),
         grid=(images,),
-        in_specs=[per_step(qkv.shape), per_step(do.shape), fixed(bias.shape)],
+        in_specs=[per_step(v.shape) for v in (qkv, do, p)],
         out_specs=[per_step(shapes[0].shape)] + [fixed(s.shape) for s in shapes[1:]],
         out_shape=shapes,
         compiler_params=params(),
         name="back",
-    )(qkv, do, bias)
-
-
-def grads_kernel(blocks, mine, a_ref, dqkv_ref, o_ref, dat_ref, keep_ref, send_ref, turned_a, turned_o):
+    )(qkv, do, p)
+
+
+def grads_kernel(blocks, owner, a_ref, dqkv_ref, o_ref, dat_ref, keep_ref, send_ref, turned_a, turned_o):
     wide_cols, thin_cols = dqkv_ref.shape[1] // blocks, dat_ref.shape[1] // blocks
     turned_a[...] = a_ref[...].T
     turned_o[...] = o_ref[...].T
-    here = mine()
+    here = owner() & 1
     for n in range(blocks):
         left = mm(turned_a[...], dqkv_ref[:, n * wide_cols : (n + 1) * wide_cols]).astype(BF)
         right = mm(turned_o[...], dat_ref[:, n * thin_cols : (n + 1) * thin_cols]).astype(BF)
         place(keep_ref, send_ref, n // 2, n & 1, here, jnp.concatenate([left, right], 1))
 
 
-def attention_grads(first, dqkv, mixed, dat, blocks, mine):
+def attention_grads(first, dqkv, mixed, dat, blocks, owner):
     width = first.shape[1]
     cols = (dqkv.shape[1] + dat.shape[1]) // blocks
     shape = (blocks // 2, width, cols)
     return pl.pallas_call(
-        functools.partial(grads_kernel, blocks, mine),
+        functools.partial(grads_kernel, blocks, owner),
         grid=(1,),
         in_specs=[whole(v.shape) for v in (first, dqkv, mixed, dat)],
         out_specs=[whole(shape)] * 2,
@@ -660,6 +671,25 @@
     )(*inputs)
 
 
+class Spread:
+    def __init__(self, block):
+        rows = block.shape[0] // 2
+        self.block = block
+        self.side = lax.axis_index("wide") & 1
+        self.half = swap(lax.dynamic_slice_in_dim(block, self.side * rows, rows, 0), "narrow", 1)
+        self.other = swap(block, "narrow", 0)
+
+    def over_x(self, *after):
+        self.half = gated(self.half, *after)
+        self.rest = swap(self.half, "wide", 0)
+        return self.half
+
+    def blocks(self, *after):
+        half, rest = self.half, gated(self.rest, *after)
+        far = jnp.where(self.side == 0, jnp.concatenate([half, rest]), jnp.concatenate([rest, half]))
+        return self.block, self.other, far, swap(far, "narrow", 0)
+
+
 class Halving:
     def __init__(self, keep, send, rows):
         self.bits = axis_bits()
@@ -747,12 +777,21 @@
 
 
 class Plan:
-    def __init__(self, rows):
-        self.rows = rows
+    def __init__(self, rows, up_weight, down_weight):
+        self.rows, self.down_weight = rows, down_weight
+        self.spread = Spread(up_weight)
+
+    def after_bias(self, bias):
+        half = self.spread.over_x(bias)
+        self.down_all = lax.all_gather(gated(self.down_weight, half), "narrow", axis=0)
+        return (half,)
+
+    def after_front(self, hn):
+        return self.spread.blocks(hn), self.down_all
 
     @staticmethod
-    def mine():
-        return lax.axis_index("narrow") & 1
+    def owner():
+        return lax.axis_index("narrow")
 
     def after_down(self, grads):
         rows = grads.reshape(-1, grads.shape[2])
@@ -778,8 +817,17 @@
 
 
 class Alone:
+    def __init__(self, *weights):
+        self.weights = weights
+
+    def after_bias(self, bias):
+        return ()
+
+    def after_front(self, hn):
+        return self.weights
+
     @staticmethod
-    def mine():
+    def owner():
         return 0
 
     def after_down(self, grads):
@@ -800,39 +848,38 @@
 
 
 def local_work(
-    block_in, out_grad, mim_mask, rel_index, qkv_weight, proj_weight, up_all, down_all, vectors, up_bias, rel_table, plan=None
+    block_in, out_grad, mim_mask, rel_index, qkv_weight, proj_weight, vectors, up_bias, rel_table, plan
 ):
-    plan = plan or Alone()
     images, seq, width = block_in.shape
     table_rows, heads = rel_table.shape
-    blocks, _, hidden = up_all.shape
     tokens = images * seq
     chunks = -(-table_rows // LANES)
     padded_seq = -(-seq // LANES) * LANES
     key_at = jnp.arange(seq, dtype=jnp.int32)
     index = jnp.where(key_at[None, :] < VALID, rel_index, chunks * LANES)
-    index_t = index.T
     padded = jnp.pad(index, ((0, 0), (0, padded_seq - seq)))
     table_t = jnp.pad(rel_table, ((0, chunks * LANES - table_rows), (0, 0))).T.reshape(heads, chunks, LANES)
-    bias, bias_t = bias_tables(padded, table_t)
+    bias = bias_tables(padded, table_t)
     gy = out_grad * mim_mask.astype(BF)[:, :, None]
-    first, qkv, mixed, attn, hn = front(block_in, qkv_weight, proj_weight, vectors, bias, heads)
+    first, qkv, p, mixed, attn, hn = front(gated(block_in, gy, *plan.after_bias(bias)), qkv_weight, proj_weight, vectors, bias, heads)
     flat = lambda v: v.reshape(tokens, v.shape[-1])
-    z, slope, grad_down, dm = mlp_in(flat(hn), flat(gy), vectors, up_bias.reshape(blocks, 1, hidden), up_all, tokens)
+    ups, down_all = plan.after_front(hn)
+    blocks, _, hidden = down_all.shape
+    z, slope, grad_down, dm = mlp_in(flat(hn), flat(gy), vectors, up_bias.reshape(blocks, 1, hidden), ups, tokens, plan.owner)
     plan.after_down(grad_down)
-    m, dhn, keep, send, grad_bias = mlp_out(flat(hn), dm, z, slope, up_all, down_all, tokens, plan.mine)
+    m, dhn, keep, send, grad_bias = mlp_out(flat(hn), dm, z, slope, ups, down_all, tokens, plan.owner)
     gy = gated(gy, *plan.after_up(keep, send))
     fold = lambda v: v.reshape(images, seq, width)
     block_out, dmid, dat, do, gvec = middle_back(block_in, gy, attn, fold(m), fold(dhn), proj_weight, vectors)
     do = gated(do, *plan.next_up(do))
-    dqkv, ds, gcol = back(qkv, do, bias_t, heads)
+    dqkv, ds, gcol = back(qkv, do, p, heads)
     dat = gated(dat, *plan.next_up(dqkv))
-    keep, send = attention_grads(flat(first), flat(dqkv), flat(mixed), flat(dat), blocks, plan.mine)
+    keep, send = attention_grads(flat(first), flat(dqkv), flat(mixed), flat(dat), blocks, plan.owner)
     dmid = gated(dmid, *plan.after_attention(keep, send))
     input_grad, gvec_one = input_grads(block_in, dqkv, dmid, qkv_weight, vectors)
-    by_key = jnp.pad(ds.transpose(1, 0, 2), ((0, 0), (0, (-heads) % 8), (0, 0)))
-    by_key = gated(by_key, *plan.next_attention(input_grad))
-    sums = table_sums(index_t, by_key, chunks)
+    by_query = jnp.pad(ds.transpose(1, 0, 2), ((0, 0), (0, (-heads) % 8), (0, 0)))
+    by_query = gated(by_query, *plan.next_attention(input_grad))
+    sums = table_sums(index, by_query, chunks)
     plan.next_both(sums)
     small = (sums.reshape(chunks, 2, -1, LANES), gcol, gvec, gvec_one, grad_bias)
     return block_out, input_grad, small, plan
@@ -854,11 +901,9 @@
 ):
     width = block_in.shape[2]
     heads = rel_table.shape[1]
-    up_all = lax.all_gather(up_weight, "narrow", axis=0)
-    down_all = lax.all_gather(down_weight, "narrow", axis=0)
-    plan = Plan(width // lax.axis_size("wide"))
+    plan = Plan(width // lax.axis_size("wide"), up_weight, down_weight)
     block_out, input_grad, small, plan = local_work(
-        block_in, out_grad, mim_mask, rel_index, qkv_weight, proj_weight, up_all, down_all, vectors, up_bias, rel_table, plan
+        block_in, out_grad, mim_mask, rel_index, qkv_weight, proj_weight, vectors, up_bias, rel_table, plan
     )
     vec_at = heads + (-heads) % 8
     bias_at = vec_at + vectors.shape[0]

time: 291 us -> 283 us (0.973)
  waiting for transfers between devices: 53.1 us -> 36.5 us
  starting transfers between devices: 19.4 us -> 25.1 us
  Pallas kernels: 187 us -> 183 us
    all_gather x2 -> x1, waiting for transfers between devices: 22.1 us -> 0.01 us  [after_bias(): lax.all_gather(gated(self.down_weight, half), 'narrow', axis=0)]
    ppermute x19 -> x23, waiting for transfers between devices: 29.6 us -> 36.5 us  [swap(): return lax.ppermute(value, axis, [(i, i ^ 1 << bit) for i in range(size)])]
    ppermute x19 -> x23, starting transfers between devices: 19.3 us -> 25 us  [swap(): return lax.ppermute(value, axis, [(i, i ^ 1 << bit) for i in range(size)])]
    pallas_call x1, Pallas kernels: 23.5 us -> 19.4 us  [back(): pl.pallas_call(functools.partial(back_kernel, heads), grid=(images,), in_...]
    unnamed x48 -> x50, local copies, waits for them, and re-layouts: 9.45 us -> 10.5 us
  transfers between devices with their start and end apart: 22 -> 25, of which waited for: 11 -> 15; matrix products, arithmetic and copies ran while one was open for 2% -> 3% of each run, Pallas kernels for 52% -> 52%
where the time goes in v5:
time: 283 us; the launch traced here: 282 us
  Pallas kernels  183 us (65%)
  waiting for transfers between devices  36.5 us (13%)
  starting transfers between devices  25.1 us (9%)
  local copies, waits for them, and re-layouts  16.6 us (6%)
  between operations  15.7 us (6%)
  other arithmetic  5.16 us (2%)
    ppermute x23, waiting for transfers between devices, swap(): return lax.ppermute(value, axis, [(i, i ^ 1 << bit) for i in range(size)])  36.5 us
    pallas_call x1, Pallas kernels, mlp_out(): pl.pallas_call(functools.partial(mlp_out_kernel, chunk, owner), grid=(blo...  30.3 us
    pallas_call x1, Pallas kernels, front(): pl.pallas_call(functools.partial(front_kernel, heads), grid=(images,), in...  26.6 us
    ppermute x23, starting transfers between devices, swap(): return lax.ppermute(value, axis, [(i, i ^ 1 << bit) for i in range(size)])  25 us
    pallas_call x1, Pallas kernels, mlp_in(): pl.pallas_call(functools.partial(mlp_in_kernel, chunk, owner), grid=(bloc...  19.7 us
    pallas_call x1, Pallas kernels, back(): pl.pallas_call(functools.partial(back_kernel, heads), grid=(images,), in_...  19.4 us
    pallas_call x6, Pallas kernels, halve_step(): pl.pallas_call(functools.partial(halve_kernel, mine, places, join), grid=...  14 us
    pallas_call x1, Pallas kernels, attention_grads(): pl.pallas_call(functools.partial(grads_kernel, blocks, owner), grid=(1,),...  13.9 us
  transfers between devices with their start and end apart: 25, of which 15 were waited for; matrix products, arithmetic and copies ran while one was open for 3% of the time, Pallas kernels for 52%

profile of v5, /device:TPU:0, one launch (start us, length us, event | category | flops | bytes accessed | tf_op | source)
XLA Modules:
  0.0 282.2 jit_solution(12801633413350940749)
XLA Ops:
  8.1 1.1 constant_dynamic-slice_fusion
  9.2 3.1 %collective-permute-start = (bf16[384,768]{1,0:T(8,128)(2,1)S(1)}, bf16[384,768]{1,0:T(8,128)(2,1)S(1)}, u32[]{:S(2)}, u32[]{:S(2)}) collective-permute-start(bf16[384,768]{1,0:T(8,128)(2,1)S(1)} %constant_dynamic-slice_fusion), channel_id=1, source_target_pairs={{0,2},{1,3},{2,0},{3,1},{4,6},{5,7},{6,4},{7,5},{8,10},{9,11},{10,... | collective-permute-start | bytes 1769480 | tf_op jit(solution)/shard_map/ppermute | solution.py:602
  12.3 0.8 pad_bitcast_fusion
  13.1 0.6 reshape.156.tab_ref
  13.7 1.0 broadcast_select_fusion.idx_ref
  14.8 0.7 copy-done.7
  15.4 0.7 pad.12.idx_ref
  16.1 8.1 %bias_tables.1.bias_ref = f32[12,200,200]{2,1,0:T(8,128)} custom-call(s32[200,256]{1,0:T(8,128)} %pad.12.idx_ref, f32[12,6,128]{2,1,0:T(8,128)} %reshape.156.tab_ref), custom_call_target="tpu_custom_call" | custom-call | tf_op jit(solution)/shard_map/bias_tables/pallas_call | solution.py:115
  24.2 1.3 collective-permute-done
  25.7 1.8 collective-permute-start.2
  27.5 2.7 broadcast_multiply_fusion.gy_ref
  30.2 26.6 %front.1 = (bf16[5,200,768]{2,1,0:T(8,128)(2,1)}, bf16[5,200,2304]{2,1,0:T(8,128)(2,1)}, bf16[5,12,200,200]{3,2,1,0:T(8,128)(2,1)}, bf16[5,200,768]{2,1,0:T(8,12...) custom-call(bf16[5,200,768]{2,1,0:T(8,128)(2,1)} %x_ref.4, bf16[768,2304]{1,0:T(8,128)(2,1)} %wqkv_ref.3, ...), custom_call_target="tpu_custom_call" | custom-call | tf_op jit(solution)/shard_map/front/pallas_call | solution.py:213
  57.9 2.5 collective-permute-done.3.up_d
  60.3 1.0 copy-done.3
  61.3 19.7 %mlp_in.1 = (bf16[4,1000,768]{2,1,0:T(8,128)(2,1)}, bf16[4,1000,768]{2,1,0:T(8,128)(2,1)}, bf16[4,768,768]{2,1,0:T(8,128)(2,1)}, bf16[1000,768]{1,0:T(8,128)(2,1)}) custom-call(bf16[1000,768]{1,0:T(8,128)(2,1)} %bitcast.51, bf16[1000,768]{1,0:T(8,128)(2,1)} %bitcast.49, f32[10,768]{1,0:T(8,128)} %refs_12_.1, f32[4,1,768]{2,1,0:T(1,128)} %bitcast.76, ...), custom_call_target="tpu_custom_call" | custom-call | tf_op jit(solution)/shard_map/mlp_in/pallas_call | solution.py:275
  81.0 30.3 %mlp_out.1 = (f32[1000,768]{1,0:T(8,128)}, f32[1000,768]{1,0:T(8,128)}, bf16[2,768,768]{2,1,0:T(8,128)(2,1)}, bf16[2,768,768]{2,1,0:T(8,128)(2,1)}, f32[4,1,768]{2,1,0:T(1,128)}) custom-call(bf16[1000,768]{1,0:T(8,128)(2,1)} %bitcast.52, bf16[1000,768]{1,0:T(8,128)(2,1)} %get-tuple-element.129.dm_ref, bf16[4,1000,768]{2,1,0:T(8,128)(2,1)} %get-tuple-element.130.z_ref, ...), custom_call_target="tpu_custom_call" | custom-call | tf_op jit(solution)/shard_map/mlp_out/pallas_call | solution.py:342
  111.8 11.1 %middle_back.1 = (bf16[5,200,768]{2,1,0:T(8,128)(2,1)}, f32[5,200,768]{2,1,0:T(8,128)}, bf16[5,200,768]{2,1,0:T(8,128)(2,1)}, bf16[5,200,768]{2,1,0:T(8,128)(2,1)}, f32[8,768]{1,0:T(8,128)}) custom-call(bf16[5,200,768]{2,1,0:T(8,128)(2,1)} %x_ref.4, bf16[5,200,768]{2,1,0:T(8,128)(2,1)} %broadcast_multiply_fusion.gy_ref, ...), custom_call_target="tpu_custom_call" | custom-call | tf_op jit(solution)/shard_map/middle_back/pallas_call | solution.py:393
  122.9 1.4 copy-done.5
  124.3 4.4 %split_step.2 = (bf16[4,2,96,384]{3,2,1,0:T(8,128)(2,1)}, bf16[4,2,96,384]{3,2,1,0:T(8,128)(2,1)}, bf16[2,4,96,384]{3,2,1,0:T(8,128)(2,1)}, bf16[2,4,96,384]{3,2,1,0:T(8,128)(2,1)}) custom-call(bf16[2,4,2,96,768]{4,3,2,1,0:T(8,128)(2,1)} %bitcast.57, bf16[2,4,2,96,768]{4,3,2,1,0:T(8,128)(2,1)} %bitcast.58), custom_call_target="tpu_custom_call" | custom-call | tf_op jit(solution)/shard_map/split_step/pallas_call | solution.py:626
  129.0 1.6 collective-permute-start.5
  130.7 19.4 %back.1 = (bf16[5,200,2304]{2,1,0:T(8,128)(2,1)}, f32[12,200,200]{2,1,0:T(8,128)}, f32[1,2304]{1,0:T(1,128)}) custom-call(bf16[5,200,2304]{2,1,0:T(8,128)(2,1)} %get-tuple-element.139.qkv_ref, bf16[5,200,768]{2,1,0:T(8,128)(2,1)} %get-tuple-element.145.do_ref, bf16[5,12,200,200]{3,2,1,0:T(8,128)(2,1)} %get-tuple-element.146.p_ref), custom_call_target="tpu_custom_call" | custom-call | tf_op jit(solution)/shard_map/back/pallas_call | solution.py:456
  150.1 0.8 copy-done.10
  151.1 3.0 %halve_step.6 = (bf16[4,96,384]{2,1,0:T(8,128)(2,1)}, bf16[4,96,384]{2,1,0:T(8,128)(2,1)}, bf16[4,96,384]{2,1,0:T(8,128)(2,1)}, bf16[4,96,384]{2,1,0:T(8,128)(2,1)}) custom-call(bf16[8,96,384]{2,1,0:T(8,128)(2,1)} %bitcast.66, bf16[8,96,384]{2,1,0:T(8,128)(2,1)} %copy-done.11, bf16[8,96,384]{2,1,0:T(8,128)(2,1)} %bitcast.67, bf16[8,96,384]{2,1,0:T(8,128)(2,1)} %copy-done.10), custom_call_target="tpu_custom_call" | custom-call | tf_op jit(solution)/shard_map/halve_step/pallas_call | solution.py:663
  154.1 13.9 %attention_grads.1 = (bf16[2,768,768]{2,1,0:T(8,128)(2,1)}, bf16[2,768,768]{2,1,0:T(8,128)(2,1)}) custom-call(bf16[1000,768]{1,0:T(8,128)(2,1)} %bitcast.61, bf16[1000,2304]{1,0:T(8,128)(2,1)} %bitcast.48, bf16[1000,768]{1,0:T(8,128)(2,1)} %bitcast.62, bf16[1000,768]{1,0:T(8,128)(2,1)} %bitcast.63), custom_call_target="tpu_custom_call" | custom-call | tf_op jit(solution)/shard_map/attention_grads/pallas_call | solution.py:482
  168.0 11.9 %input_grads.1 = (f32[5,200,768]{2,1,0:T(8,128)}, f32[8,768]{1,0:T(8,128)}) custom-call(bf16[5,200,768]{2,1,0:T(8,128)(2,1)} %x_ref.4, bf16[5,200,2304]{2,1,0:T(8,128)(2,1)} %get-tuple-element.147.dqkv_ref, f32[5,200,768]{2,1,0:T(8,128)} %get-tuple-element.160.dmid_ref, bf16[768,2304]{1,0:T(8,128)(2,1)} %wqkv_ref.3, f32[10,768]{1,0:T(8,128)} %refs_12_.1), custom_call_target="tpu_custom_call" | custom-call | tf_op jit(solution)/shard_map/input_grads/pallas_call | solution.py:512
  179.9 1.4 copy-done.6
  181.2 4.5 %split_step.3 = (bf16[4,2,96,384]{3,2,1,0:T(8,128)(2,1)}, bf16[4,2,96,384]{3,2,1,0:T(8,128)(2,1)}, bf16[2,4,96,384]{3,2,1,0:T(8,128)(2,1)}, bf16[2,4,96,384]{3,2,1,0:T(8,128)(2,1)}) custom-call(bf16[2,4,2,96,768]{4,3,2,1,0:T(8,128)(2,1)} %bitcast.59, bf16[2,4,2,96,768]{4,3,2,1,0:T(8,128)(2,1)} %bitcast.60), custom_call_target="tpu_custom_call" | custom-call | tf_op jit(solution)/shard_map/split_step/pallas_call | solution.py:626
  185.8 1.7 collective-permute-start.13
  187.9 0.8 copy.59
  188.8 2.1 pad.14.ds_ref
  191.1 1.6 collective-permute-start.8
  192.7 12.3 %table_sums.1 = f32[192,128]{1,0:T(8,128)} custom-call(s32[200,200]{1,0:T(8,128)} %copy-done.7, f32[200,16,200]{2,1,0:T(8,128)} %pad.14.ds_ref), custom_call_target="tpu_custom_call" | custom-call | tf_op jit(solution)/shard_map/table_sums/pallas_call | solution.py:149
  206.5 3.0 %halve_step.9 = (bf16[4,96,384]{2,1,0:T(8,128)(2,1)}, bf16[4,96,384]{2,1,0:T(8,128)(2,1)}, bf16[4,96,384]{2,1,0:T(8,128)(2,1)}, bf16[4,96,384]{2,1,0:T(8,128)(2,1)}) custom-call(bf16[8,96,384]{2,1,0:T(8,128)(2,1)} %bitcast.64, bf16[8,96,384]{2,1,0:T(8,128)(2,1)} %copy-done.9, bf16[8,96,384]{2,1,0:T(8,128)(2,1)} %bitcast.65, bf16[8,96,384]{2,1,0:T(8,128)(2,1)} %copy-done.8), custom_call_target="tpu_custom_call" | custom-call | tf_op jit(solution)/shard_map/halve_step/pallas_call | solution.py:663
  209.5 1.6 collective-permute-start.14
  211.7 0.6 copy-done.15
  212.4 2.2 halve_step.7
  214.6 1.5 collective-permute-start.10
  216.1 3.0 %collective-permute-done.14.refs_1_ = bf16[4,96,384]{2,1,0:T(8,128)(2,1)S(1)} collective-permute-done((bf16[4,96,384]{2,1,0:T(8,128)(2,1)}, bf16[4,96,384]{2,1,0:T(8,128)(2,1)S(1)}, u32[]{:S(2)}, u32[]{:S(2)}) %collective-permute-start.14) | collective-permute-done | bytes 294944 | tf_op jit(solution)/shard_map/ppermute | solution.py:602
  219.2 0.6 copy-done.17
  219.9 2.2 halve_step.10
  222.1 1.5 collective-permute-start.16
  223.6 1.9 collective-permute-done.10.refs_1_
  225.5 0.7 copy-done.13
  226.2 1.8 halve_step.8
  228.0 2.0 collective-permute-start.11
  230.0 3.2 %collective-permute-done.16.refs_1_ = bf16[2,96,768]{2,1,0:T(8,128)(2,1)S(1)} collective-permute-done((bf16[2,96,768]{2,1,0:T(8,128)(2,1)}, bf16[2,96,768]{2,1,0:T(8,128)(2,1)S(1)}, u32[]{:S(2)}, u32[]{:S(2)}) %collective-permute-start.16) | collective-permute-done | bytes 294944 | tf_op jit(solution)/shard_map/ppermute | solution.py:602
  233.2 0.7 copy-done.14
  233.9 1.8 halve_step.11
  235.7 1.5 collective-permute-start.17
  237.2 1.5 collective-permute-done.11
  238.7 4.6 %collective-permute-done.17 = bf16[1,96,768]{2,1,0:T(8,128)(2,1)S(1)} collective-permute-done((bf16[1,96,768]{2,1,0:T(8,128)(2,1)}, bf16[1,96,768]{2,1,0:T(8,128)(2,1)S(1)}, u32[]{:S(2)}, u32[]{:S(2)}) %collective-permute-start.17) | collective-permute-done | bytes 147488 | tf_op jit(solution)/shard_map/ppermute | solution.py:602
  243.3 0.7 copy-done.20
  243.9 2.1 finish.1
  246.1 1.6 collective-permute-start.18
  247.7 3.2 %collective-permute-done.18 = f32[32,768]{1,0:T(8,128)S(1)} collective-permute-done((f32[32,768]{1,0:T(8,128)}, f32[32,768]{1,0:T(8,128)S(1)}, u32[]{:S(2)}, u32[]{:S(2)}) %collective-permute-start.18) | collective-permute-done | bytes 98336 | tf_op jit(solution)/shard_map/ppermute | solution.py:602
  250.9 0.9 add.24
  251.9 4.6 %collective-permute-done.19 = f32[32,768]{1,0:T(8,128)S(1)} collective-permute-done((f32[32,768]{1,0:T(8,128)S(1)}, f32[32,768]{1,0:T(8,128)S(1)}, u32[]{:S(2)}, u32[]{:S(2)}) %collective-permute-start.19) | collective-permute-done | bytes 98336 | tf_op jit(solution)/shard_map/ppermute | solution.py:602
  256.5 1.7 collective-permute-start.20
  258.2 4.8 %collective-permute-done.20 = f32[32,768]{1,0:T(8,128)S(1)} collective-permute-done((f32[32,768]{1,0:T(8,128)S(1)}, f32[32,768]{1,0:T(8,128)S(1)}, u32[]{:S(2)}, u32[]{:S(2)}) %collective-permute-start.20) | collective-permute-done | bytes 98336 | tf_op jit(solution)/shard_map/ppermute | solution.py:602
  263.1 1.3 collective-permute-done.21
  264.4 1.1 collective-permute-start.22
  265.5 3.8 %collective-permute-done.22.theirs_ref = f32[32,768]{1,0:T(8,128)S(1)} collective-permute-done((f32[32,768]{1,0:T(8,128)S(1)}, f32[32,768]{1,0:T(8,128)S(1)}, u32[]{:S(2)}, u32[]{:S(2)}) %collective-permute-start.22) | collective-permute-done | bytes 98336 | tf_op jit(solution)/shard_map/ppermute | solution.py:602
  269.3 0.6 copy-done.21
  269.9 4.8 %adam.1 = (f32[1,1]{1,0:T(1,128)}, f32[96,576]{1,0:T(8,128)}, f32[96,576]{1,0:T(8,128)}, f32[96,576]{1,0:T(8,128)}, bf16[96,576]{1,0:T(8,128)(2,1)}, /*index=5*/...) custom-call(f32[32,768]{1,0:T(8,128)} %copy-done.12, ...), custom_call_target="tpu_custom_call" | custom-call | tf_op jit(solution)/shard_map/adam/pallas_call | solution.py:581
  (72 shorter events, 5.6 us)
Async XLA Ops:
  8.0 73.0 %all-gather.3.cloned.1.call-start = ((), (), s32[]{:S(2)}) async-start(), calls=%async_computation.2 | async-start | bytes 5898240 | tf_op jit(solution)/shard_map/all_gather | solution.py:786
  9.2 16.4 %collective-permute-start = (bf16[384,768]{1,0:T(8,128)(2,1)S(1)}, bf16[384,768]{1,0:T(8,128)(2,1)S(1)}, u32[]{:S(2)}, u32[]{:S(2)}) collective-permute-start(bf16[384,768]{1,0:T(8,128)(2,1)S(1)} %constant_dynamic-slice_fusion), channel_id=1, source_target_pairs={{0,2},{1,3},{2,0},{3,1},{4,6},{5,7},{6,4},{7,5},{8,10},{9,11},{10,... | collective-permute-start | bytes 1769480 | tf_op jit(solution)/shard_map/ppermute | solution.py:602
  13.7 13.8 %copy-start.1 = (bf16[768,768]{1,0:T(8,128)(2,1)S(1)}, bf16[768,768]{1,0:T(8,128)(2,1)}, u32[]{:S(2)}) copy-start(bf16[768,768]{1,0:T(8,128)(2,1)} %up_a.3) | copy-start | bytes 3538948
  13.7 13.8 %copy-start.22 = (s32[5,200]{1,0:T(8,128)S(1)}, s32[5,200]{1,0:T(8,128)}, u32[]{:S(2)}) copy-start(s32[5,200]{1,0:T(8,128)} %param.31) | copy-start | bytes 12004
  14.7 0.7 copy-start.7
  25.6 211.6 %reduce-scatter.2.cloned.1.call-start = ((), (), s32[]{:S(2)}) async-start(), calls=%async_computation.1 | async-start | bytes 4866048 | tf_op jit(solution)/shard_map/reduce_scatter | solution.py:798
  25.7 31.1 %collective-permute-start.2 = (bf16[384,768]{1,0:T(8,128)(2,1)S(1)}, bf16[384,768]{1,0:T(8,128)(2,1)S(1)}, u32[]{:S(2)}, u32[]{:S(2)}) collective-permute-start(bf16[384,768]{1,0:T(8,128)(2,1)S(1)} %collective-permute-done), channel_id=1, source_target_pairs={{0,4},{4,0},{8,12},{12,8},{16,20},{20,16},{24,28},{28,24},{1,5},{5... | collective-permute-start | bytes 1769480 | tf_op jit(solution)/shard_map/ppermute | solution.py:602
  27.4 30.4 %collective-permute-start.1 = (bf16[768,768]{1,0:T(8,128)(2,1)S(1)}, bf16[768,768]{1,0:T(8,128)(2,1)S(1)}, u32[]{:S(2)}, u32[]{:S(2)}) collective-permute-start(bf16[768,768]{1,0:T(8,128)(2,1)S(1)} %copy-done.1), channel_id=1, source_target_pairs={{0,1},{1,0},{2,3},{3,2},{4,5},{5,4},{6,7},{7,6},{8,9},{9,8},{10,11... | collective-permute-start | bytes 3538952 | tf_op jit(solution)/shard_map/ppermute | solution.py:602
  57.2 3.1 %copy-start = (bf16[768,768]{1,0:T(8,128)(2,1)}, bf16[768,768]{1,0:T(8,128)(2,1)S(1)}, u32[]{:S(2)}) copy-start(bf16[768,768]{1,0:T(8,128)(2,1)S(1)} %maximum_select_fusion.up_c) | copy-start | bytes 3538948
  57.2 3.1 %collective-permute-start.3 = (bf16[768,768]{1,0:T(8,128)(2,1)S(1)}, bf16[768,768]{1,0:T(8,128)(2,1)S(1)}, u32[]{:S(2)}, u32[]{:S(2)}) collective-permute-start(bf16[768,768]{1,0:T(8,128)(2,1)S(1)} %maximum_select_fusion.up_c), channel_id=1, source_target_pairs={{0,1},{1,0},{2,3},{3,2},{4,5},{5,4},{6,7},{7,6},{8,9},{9,8},{10,11... | collective-permute-start | bytes 3538952 | tf_op jit(solution)/shard_map/ppermute | solution.py:602
  57.8 2.5 copy-start.2
  60.3 1.0 copy-start.3
  111.3 11.5 %collective-permute-start.4 = (bf16[16,96,768]{2,1,0:T(8,128)(2,1)}, bf16[16,96,768]{2,1,0:T(8,128)(2,1)S(1)}, u32[]{:S(2)}, u32[]{:S(2)}) collective-permute-start(bf16[16,96,768]{2,1,0:T(8,128)(2,1)} %bitcast.80), channel_id=1, source_target_pairs={{0,1},{1,0},{2,3},{3,2},{4,5},{5,4},{6,7},{7,6},{8,9},{9,8},{10,11... | collective-permute-start | bytes 7077896 | tf_op jit(solution)/shard_map/ppermute | solution.py:602
  122.9 1.4 copy-start.5
  128.7 21.4 %collective-permute-start.6 = (bf16[8,96,384]{2,1,0:T(8,128)(2,1)}, bf16[8,96,384]{2,1,0:T(8,128)(2,1)S(1)}, u32[]{:S(2)}, u32[]{:S(2)}) collective-permute-start(bf16[8,96,384]{2,1,0:T(8,128)(2,1)} %bitcast.85), channel_id=1, source_target_pairs={{0,4},{4,0},{8,12},{12,8},{16,20},{20,16},{24,28},{28,24},{1,5},{5... | collective-permute-start | bytes 1769480 | tf_op jit(solution)/shard_map/ppermute | solution.py:602
  129.0 21.1 %collective-permute-start.5 = (bf16[8,96,384]{2,1,0:T(8,128)(2,1)}, bf16[8,96,384]{2,1,0:T(8,128)(2,1)S(1)}, u32[]{:S(2)}, u32[]{:S(2)}) collective-permute-start(bf16[8,96,384]{2,1,0:T(8,128)(2,1)} %bitcast.84), channel_id=1, source_target_pairs={{0,2},{1,3},{2,0},{3,1},{4,6},{5,7},{6,4},{7,5},{8,10},{9,11},{10,... | collective-permute-start | bytes 1769480 | tf_op jit(solution)/shard_map/ppermute | solution.py:602
  150.1 0.8 copy-start.10
  150.1 1.0 copy-start.11
  168.0 11.9 %collective-permute-start.9 = (bf16[16,96,768]{2,1,0:T(8,128)(2,1)}, bf16[16,96,768]{2,1,0:T(8,128)(2,1)S(1)}, u32[]{:S(2)}, u32[]{:S(2)}) collective-permute-start(bf16[16,96,768]{2,1,0:T(8,128)(2,1)} %bitcast.81), channel_id=1, source_target_pairs={{0,1},{1,0},{2,3},{3,2},{4,5},{5,4},{6,7},{7,6},{8,9},{9,8},{10,11... | collective-permute-start | bytes 7077896 | tf_op jit(solution)/shard_map/ppermute | solution.py:602
  179.8 1.4 copy-start.6
  181.2 6.7 %copy-start.4 = (f32[12,200,200]{2,1,0:T(8,128)S(1)}, f32[12,200,200]{2,1,0:T(8,128)}, u32[]{:S(2)}) copy-start(f32[12,200,200]{2,1,0:T(8,128)} %get-tuple-element.163) | copy-start | bytes 5760004
  185.8 19.3 %collective-permute-start.13 = (bf16[8,96,384]{2,1,0:T(8,128)(2,1)}, bf16[8,96,384]{2,1,0:T(8,128)(2,1)S(1)}, u32[]{:S(2)}, u32[]{:S(2)}) collective-permute-start(bf16[8,96,384]{2,1,0:T(8,128)(2,1)} %bitcast.83), channel_id=1, source_target_pairs={{0,4},{4,0},{8,12},{12,8},{16,20},{20,16},{24,28},{28,24},{1,5},{5... | collective-permute-start | bytes 1769480 | tf_op jit(solution)/shard_map/ppermute | solution.py:602
  187.5 18.2 %collective-permute-start.12 = (bf16[8,96,384]{2,1,0:T(8,128)(2,1)}, bf16[8,96,384]{2,1,0:T(8,128)(2,1)S(1)}, u32[]{:S(2)}, u32[]{:S(2)}) collective-permute-start(bf16[8,96,384]{2,1,0:T(8,128)(2,1)} %bitcast.82), channel_id=1, source_target_pairs={{0,2},{1,3},{2,0},{3,1},{4,6},{5,7},{6,4},{7,5},{8,10},{9,11},{10,... | collective-permute-start | bytes 1769480 | tf_op jit(solution)/shard_map/ppermute | solution.py:602
  188.7 2.1 copy-start.24
  188.7 2.4 copy-start.23
  190.8 20.7 %collective-permute-start.7 = (bf16[4,96,384]{2,1,0:T(8,128)(2,1)S(1)}, bf16[4,96,384]{2,1,0:T(8,128)(2,1)S(1)}, u32[]{:S(2)}, u32[]{:S(2)}) collective-permute-start(bf16[4,96,384]{2,1,0:T(8,128)(2,1)S(1)} %copy-done.24), channel_id=1, source_target_pairs={{0,4},{4,0},{8,12},{12,8},{16,20},{20,16},{24,28},{28,24},{1,5},{5... | collective-permute-start | bytes 884744 | tf_op jit(solution)/shard_map/ppermute | solution.py:602
  191.1 20.5 %collective-permute-start.8 = (bf16[4,96,384]{2,1,0:T(8,128)(2,1)S(1)}, bf16[4,96,384]{2,1,0:T(8,128)(2,1)S(1)}, u32[]{:S(2)}, u32[]{:S(2)}) collective-permute-start(bf16[4,96,384]{2,1,0:T(8,128)(2,1)S(1)} %copy-done.23), channel_id=1, source_target_pairs={{0,2},{1,3},{2,0},{3,1},{4,6},{5,7},{6,4},{7,5},{8,10},{9,11},{10,... | collective-permute-start | bytes 884744 | tf_op jit(solution)/shard_map/ppermute | solution.py:602
  205.0 0.8 copy-start.8
  205.6 0.8 copy-start.9
  209.5 9.6 %collective-permute-start.14 = (bf16[4,96,384]{2,1,0:T(8,128)(2,1)}, bf16[4,96,384]{2,1,0:T(8,128)(2,1)S(1)}, u32[]{:S(2)}, u32[]{:S(2)}) collective-permute-start(bf16[4,96,384]{2,1,0:T(8,128)(2,1)} %get-tuple-element.181), channel_id=1, source_target_pairs={{0,4},{4,0},{8,12},{12,8},{16,20},{20,16},{24,28},{28,24},{1,5},{5... | collective-permute-start | bytes 884744 | tf_op jit(solution)/shard_map/ppermute | solution.py:602
  211.0 8.2 %collective-permute-start.15 = (bf16[4,96,384]{2,1,0:T(8,128)(2,1)}, bf16[4,96,384]{2,1,0:T(8,128)(2,1)S(1)}, u32[]{:S(2)}, u32[]{:S(2)}) collective-permute-start(bf16[4,96,384]{2,1,0:T(8,128)(2,1)} %get-tuple-element.183), channel_id=1, source_target_pairs={{0,2},{1,3},{2,0},{3,1},{4,6},{5,7},{6,4},{7,5},{8,10},{9,11},{10,... | collective-permute-start | bytes 884744 | tf_op jit(solution)/shard_map/ppermute | solution.py:602
  211.6 0.7 copy-start.15
  211.7 0.7 copy-start.16
  214.6 10.9 %collective-permute-start.10 = (bf16[2,96,768]{2,1,0:T(8,128)(2,1)}, bf16[2,96,768]{2,1,0:T(8,128)(2,1)S(1)}, u32[]{:S(2)}, u32[]{:S(2)}) collective-permute-start(bf16[2,96,768]{2,1,0:T(8,128)(2,1)} %get-tuple-element.173), channel_id=1, source_target_pairs={{0,8},{4,12},{8,0},{12,4},{16,24},{20,28},{24,16},{28,20},{1,9},{5... | collective-permute-start | bytes 884744 | tf_op jit(solution)/shard_map/ppermute | solution.py:602
  219.1 0.7 copy-start.17
  219.2 0.7 copy-start.18
  222.1 11.1 %collective-permute-start.16 = (bf16[2,96,768]{2,1,0:T(8,128)(2,1)}, bf16[2,96,768]{2,1,0:T(8,128)(2,1)S(1)}, u32[]{:S(2)}, u32[]{:S(2)}) collective-permute-start(bf16[2,96,768]{2,1,0:T(8,128)(2,1)} %get-tuple-element.185), channel_id=1, source_target_pairs={{0,8},{4,12},{8,0},{12,4},{16,24},{20,28},{24,16},{28,20},{1,9},{5... | collective-permute-start | bytes 884744 | tf_op jit(solution)/shard_map/ppermute | solution.py:602
  225.5 0.7 copy-start.13
  228.0 10.7 %collective-permute-start.11 = (bf16[1,96,768]{2,1,0:T(8,128)(2,1)}, bf16[1,96,768]{2,1,0:T(8,128)(2,1)S(1)}, u32[]{:S(2)}, u32[]{:S(2)}) collective-permute-start(bf16[1,96,768]{2,1,0:T(8,128)(2,1)} %get-tuple-element.175), channel_id=1, source_target_pairs={{0,16},{4,20},{8,24},{12,28},{16,0},{20,4},{24,8},{28,12},{1,17},{... | collective-permute-start | bytes 442376 | tf_op jit(solution)/shard_map/ppermute | solution.py:602
  233.2 0.7 copy-start.14
  235.7 7.6 %collective-permute-start.17 = (bf16[1,96,768]{2,1,0:T(8,128)(2,1)}, bf16[1,96,768]{2,1,0:T(8,128)(2,1)S(1)}, u32[]{:S(2)}, u32[]{:S(2)}) collective-permute-start(bf16[1,96,768]{2,1,0:T(8,128)(2,1)} %get-tuple-element.187), channel_id=1, source_target_pairs={{0,16},{4,20},{8,24},{12,28},{16,0},{20,4},{24,8},{28,12},{1,17},{... | collective-permute-start | bytes 442376 | tf_op jit(solution)/shard_map/ppermute | solution.py:602
  238.7 4.6 %copy-start.19 = (bf16[1,96,768]{2,1,0:T(8,128)(2,1)}, bf16[1,96,768]{2,1,0:T(8,128)(2,1)S(1)}, u32[]{:S(2)}) copy-start(bf16[1,96,768]{2,1,0:T(8,128)(2,1)S(1)} %collective-permute-done.11) | copy-start | bytes 442372
  243.3 0.7 copy-start.20
  246.1 4.8 %collective-permute-start.18 = (f32[32,768]{1,0:T(8,128)}, f32[32,768]{1,0:T(8,128)S(1)}, u32[]{:S(2)}, u32[]{:S(2)}) collective-permute-start(f32[32,768]{1,0:T(8,128)} %get-tuple-element.193), channel_id=1, source_target_pairs={{0,4},{4,0},{8,12},{12,8},{16,20},{20,16},{24,28},{28,24},{1,5},{5... | collective-permute-start | bytes 294920 | tf_op jit(solution)/shard_map/ppermute | solution.py:602
  251.8 4.7 %collective-permute-start.19 = (f32[32,768]{1,0:T(8,128)S(1)}, f32[32,768]{1,0:T(8,128)S(1)}, u32[]{:S(2)}, u32[]{:S(2)}) collective-permute-start(f32[32,768]{1,0:T(8,128)S(1)} %add.24), channel_id=1, source_target_pairs={{0,8},{4,12},{8,0},{12,4},{16,24},{20,28},{24,16},{28,20},{1,9},{5... | collective-permute-start | bytes 294920 | tf_op jit(solution)/shard_map/ppermute | solution.py:602
  256.5 6.5 %collective-permute-start.20 = (f32[32,768]{1,0:T(8,128)S(1)}, f32[32,768]{1,0:T(8,128)S(1)}, u32[]{:S(2)}, u32[]{:S(2)}) collective-permute-start(f32[32,768]{1,0:T(8,128)S(1)} %add.25), channel_id=1, source_target_pairs={{0,16},{4,20},{8,24},{12,28},{16,0},{20,4},{24,8},{28,12},{1,17},{... | collective-permute-start | bytes 294920 | tf_op jit(solution)/shard_map/ppermute | solution.py:602
  263.0 1.4 collective-permute-start.21
  264.4 4.9 %copy-start.12 = (f32[32,768]{1,0:T(8,128)}, f32[32,768]{1,0:T(8,128)S(1)}, u32[]{:S(2)}) copy-start(f32[32,768]{1,0:T(8,128)S(1)} %add.27.ours_ref) | copy-start | bytes 294916
  264.4 4.9 %collective-permute-start.22 = (f32[32,768]{1,0:T(8,128)S(1)}, f32[32,768]{1,0:T(8,128)S(1)}, u32[]{:S(2)}, u32[]{:S(2)}) collective-permute-start(f32[32,768]{1,0:T(8,128)S(1)} %add.27.ours_ref), channel_id=1, source_target_pairs={{0,2},{1,3},{2,0},{3,1},{4,6},{5,7},{6,4},{7,5},{8,10},{9,11},{10,... | collective-permute-start | bytes 294920 | tf_op jit(solution)/shard_map/ppermute | solution.py:602
  269.3 0.6 copy-start.21
Sparse Core Ops, SparseCore 0:
  25.7 38.8 all-gather.2
Sparse Core Ops, SparseCore 1:
  111.9 111.6 reduce-scatter.1

commit v6 on v5

--- a/solution.py
+++ b/solution.py
@@ -25,7 +25,9 @@
 ROWS_ROWS = (((0,), (0,)), ((), ()))
 COLS_COLS = (((1,), (1,)), ((), ()))
 VMEM_LIMIT = 60000 * 1024
+VMEM_WHOLE = 65536 * 1024
 UNROLL_F = 3
+PART = 256
 UNROLL_B = 3
 UNROLL_T = 8
 
@@ -42,9 +44,9 @@
     return lax.dot_general(a, b, ROWS_ROWS, preferred_element_type=F32)
 
 
-def params(steps=1):
+def params(steps=1, limit=VMEM_LIMIT):
     return pltpu.CompilerParams(
-        dimension_semantics=("arbitrary",) * steps, vmem_limit_bytes=VMEM_LIMIT
+        dimension_semantics=("arbitrary",) * steps, vmem_limit_bytes=limit
     )
 
 
@@ -252,15 +254,13 @@
         lax.fori_loop(0, tokens // chunk, rows, 0)
         turned_ref[...] = dm_ref[...].T
 
-    def rows(step, carry):
-        at = pl.ds(pl.multiple_of(step * chunk, chunk), chunk)
+    for low in range(0, tokens, PART):
+        at = slice(low, min(low + PART, tokens))
         u = mm(hn_ref[at, :], wup_ref[...]) + bup_ref[0]
         gate = 0.5 * (1.0 + lax.erf(u * 0.7071067811865476))
         z_ref[0, at, :] = (u * gate).astype(BF)
         slope_ref[0, at, :] = (gate + u * jnp.exp(-0.5 * u * u) * 0.3989422804014327).astype(BF)
-        return carry
-
-    lax.fori_loop(0, tokens // chunk, rows, 0)
+
     gdn_ref[0] = mm(turned_ref[...], z_ref[0]).astype(BF)
 
 
@@ -285,7 +285,7 @@
         out_specs=[per_step(s.shape) for s in shapes] + [fixed((tokens, width))],
         out_shape=shapes + [jax.ShapeDtypeStruct((tokens, width), BF)],
         scratch_shapes=[pltpu.VMEM((width, tokens), BF), pltpu.VMEM((width, hidden), BF)],
-        compiler_params=params(),
+        compiler_params=params(limit=VMEM_WHOLE),
         name="mlp_in",
     )(hn, gy, vectors, up_bias, *ups)
 
@@ -584,7 +584,7 @@
         in_specs=[whole(v.shape) for v in inputs],
         out_specs=[whole(v.shape) for v in shapes],
         out_shape=shapes,
-        compiler_params=params(),
+        compiler_params=params(limit=VMEM_WHOLE),
         name="adam",
     )(*inputs)
 
@@ -629,7 +629,7 @@
         in_specs=[block, block],
         out_specs=[out_a, out_a, out_b, out_b],
         out_shape=[shape_a, shape_a, shape_b, shape_b],
-        compiler_params=params(),
+        compiler_params=params(limit=VMEM_WHOLE),
         name="split_step",
     )(keep, come)
 
@@ -666,7 +666,7 @@
         in_specs=[whole(v.shape) for v in inputs],
         out_specs=[whole(v.shape) for v in shapes],
         out_shape=shapes,
-        compiler_params=params(),
+        compiler_params=params(limit=VMEM_WHOLE),
         name="halve_step",
     )(*inputs)
 
@@ -767,7 +767,7 @@
         in_specs=[whole(v.shape) for v in inputs],
         out_specs=[whole(v.shape) for v in shapes],
         out_shape=shapes,
-        compiler_params=params(),
+        compiler_params=params(limit=VMEM_WHOLE),
         name="finish",
     )(*inputs)
 
@@ -861,7 +861,7 @@
     table_t = jnp.pad(rel_table, ((0, chunks * LANES - table_rows), (0, 0))).T.reshape(heads, chunks, LANES)
     bias = bias_tables(padded, table_t)
     gy = out_grad * mim_mask.astype(BF)[:, :, None]
-    first, qkv, p, mixed, attn, hn = front(gated(block_in, gy, *plan.after_bias(bias)), qkv_weight, proj_weight, vectors, bias, heads)
+    first, qkv, p, mixed, attn, hn = front(gated(block_in, *plan.after_bias(bias)), qkv_weight, proj_weight, vectors, bias, heads)
     flat = lambda v: v.reshape(tokens, v.shape[-1])
     ups, down_all = plan.after_front(hn)
     blocks, _, hidden = down_all.shape

time: 283 us -> 278 us (0.982)
  local copies, waits for them, and re-layouts: 16.6 us -> 11.8 us
  waiting for transfers between devices: 36.5 us -> 40.6 us
    unnamed x50 -> x18, local copies, waits for them, and re-layouts: 10.5 us -> 4.01 us
    ppermute x23, waiting for transfers between devices: 36.5 us -> 40.6 us  [swap(): return lax.ppermute(value, axis, [(i, i ^ 1 << bit) for i in range(size)])]
where the time goes in v6:
time: 278 us; the launch traced here: 277 us
  Pallas kernels  182 us (65%)
  waiting for transfers between devices  40.6 us (15%)
  starting transfers between devices  23.3 us (8%)
  between operations  15.7 us (6%)
  local copies, waits for them, and re-layouts  11.8 us (4%)
  other arithmetic  3.79 us (1%)
    ppermute x23, waiting for transfers between devices, swap(): return lax.ppermute(value, axis, [(i, i ^ 1 << bit) for i in range(size)])  40.6 us
    pallas_call x1, Pallas kernels, mlp_out(): pl.pallas_call(functools.partial(mlp_out_kernel, chunk, owner), grid=(blo...  30.3 us
    pallas_call x1, Pallas kernels, front(): pl.pallas_call(functools.partial(front_kernel, heads), grid=(images,), in...  26.5 us
    ppermute x23, starting transfers between devices, swap(): return lax.ppermute(value, axis, [(i, i ^ 1 << bit) for i in range(size)])  23.2 us
    pallas_call x1, Pallas kernels, back(): pl.pallas_call(functools.partial(back_kernel, heads), grid=(images,), in_...  19.4 us
    pallas_call x1, Pallas kernels, mlp_in(): pl.pallas_call(functools.partial(mlp_in_kernel, chunk, owner), grid=(bloc...  18.8 us
    pallas_call x6, Pallas kernels, halve_step(): pl.pallas_call(functools.partial(halve_kernel, mine, places, join), grid=...  14.1 us
    pallas_call x1, Pallas kernels, attention_grads(): pl.pallas_call(functools.partial(grads_kernel, blocks, owner), grid=(1,),...  13.9 us
  transfers between devices with their start and end apart: 25, of which 15 were waited for; matrix products, arithmetic and copies ran while one was open for 3% of the time, Pallas kernels for 52%

profile of v6, /device:TPU:0, one launch (start us, length us, event | category | flops | bytes accessed | tf_op | source)
XLA Modules:
  0.0 277.1 jit_solution(13836264979452617878)
XLA Ops:
  8.1 1.1 constant_dynamic-slice_fusion
  9.2 3.1 %collective-permute-start = (bf16[384,768]{1,0:T(8,128)(2,1)S(1)}, bf16[384,768]{1,0:T(8,128)(2,1)S(1)}, u32[]{:S(2)}, u32[]{:S(2)}) collective-permute-start(bf16[384,768]{1,0:T(8,128)(2,1)S(1)} %constant_dynamic-slice_fusion), channel_id=1, source_target_pairs={{0,2},{1,3},{2,0},{3,1},{4,6},{5,7},{6,4},{7,5},{8,10},{9,11},{10,... | collective-permute-start | bytes 1769480 | tf_op jit(solution)/shard_map/ppermute | solution.py:602
  12.3 0.8 pad_bitcast_fusion
  13.1 0.6 reshape.156.tab_ref
  13.7 1.0 broadcast_select_fusion.idx_ref
  14.8 0.7 copy-done.4
  15.4 0.7 pad.12.idx_ref
  16.1 8.1 %bias_tables.1.bias_ref = f32[12,200,200]{2,1,0:T(8,128)} custom-call(s32[200,256]{1,0:T(8,128)} %pad.12.idx_ref, f32[12,6,128]{2,1,0:T(8,128)} %reshape.156.tab_ref), custom_call_target="tpu_custom_call" | custom-call | tf_op jit(solution)/shard_map/bias_tables/pallas_call | solution.py:117
  24.2 1.4 collective-permute-done
  25.7 1.8 collective-permute-start.2
  27.4 26.5 %front.1 = (bf16[5,200,768]{2,1,0:T(8,128)(2,1)}, bf16[5,200,2304]{2,1,0:T(8,128)(2,1)}, bf16[5,12,200,200]{3,2,1,0:T(8,128)(2,1)}, bf16[5,200,768]{2,1,0:T(8,12...) custom-call(bf16[5,200,768]{2,1,0:T(8,128)(2,1)} %x_ref.4, bf16[768,2304]{1,0:T(8,128)(2,1)} %wqkv_ref.3, ...), custom_call_target="tpu_custom_call" | custom-call | tf_op jit(solution)/shard_map/front/pallas_call | solution.py:215
  54.0 0.5 maximum_select_fusion.up_c
  54.4 1.0 copy-done
  55.5 0.5 collective-permute-start.3
  56.0 1.3 broadcast_multiply_fusion.gy_ref
  57.3 1.3 collective-permute-done.3.up_d
  58.6 1.0 copy-done.3
  59.6 18.8 %mlp_in.1 = (bf16[4,1000,768]{2,1,0:T(8,128)(2,1)}, bf16[4,1000,768]{2,1,0:T(8,128)(2,1)}, bf16[4,768,768]{2,1,0:T(8,128)(2,1)}, bf16[1000,768]{1,0:T(8,128)(2,1)}) custom-call(bf16[1000,768]{1,0:T(8,128)(2,1)} %bitcast.51, bf16[1000,768]{1,0:T(8,128)(2,1)} %bitcast.49, f32[10,768]{1,0:T(8,128)} %refs_12_.1, f32[4,1,768]{2,1,0:T(1,128)} %bitcast.72, ...), custom_call_target="tpu_custom_call" | custom-call | tf_op jit(solution)/shard_map/mlp_in/pallas_call | solution.py:275
  78.4 30.3 %mlp_out.1 = (f32[1000,768]{1,0:T(8,128)}, f32[1000,768]{1,0:T(8,128)}, bf16[2,768,768]{2,1,0:T(8,128)(2,1)}, bf16[2,768,768]{2,1,0:T(8,128)(2,1)}, f32[4,1,768]{2,1,0:T(1,128)}) custom-call(bf16[1000,768]{1,0:T(8,128)(2,1)} %bitcast.52, bf16[1000,768]{1,0:T(8,128)(2,1)} %get-tuple-element.129.dm_ref, bf16[4,1000,768]{2,1,0:T(8,128)(2,1)} %get-tuple-element.130.z_ref, ...), custom_call_target="tpu_custom_call" | custom-call | tf_op jit(solution)/shard_map/mlp_out/pallas_call | solution.py:342
  109.2 10.8 %middle_back.1 = (bf16[5,200,768]{2,1,0:T(8,128)(2,1)}, f32[5,200,768]{2,1,0:T(8,128)}, bf16[5,200,768]{2,1,0:T(8,128)(2,1)}, bf16[5,200,768]{2,1,0:T(8,128)(2,1)}, f32[8,768]{1,0:T(8,128)}) custom-call(bf16[5,200,768]{2,1,0:T(8,128)(2,1)} %x_ref.4, bf16[5,200,768]{2,1,0:T(8,128)(2,1)} %broadcast_multiply_fusion.gy_ref, ...), custom_call_target="tpu_custom_call" | custom-call | tf_op jit(solution)/shard_map/middle_back/pallas_call | solution.py:393
  120.0 4.4 %split_step.2 = (bf16[4,2,96,384]{3,2,1,0:T(8,128)(2,1)}, bf16[4,2,96,384]{3,2,1,0:T(8,128)(2,1)}, bf16[2,4,96,384]{3,2,1,0:T(8,128)(2,1)}, bf16[2,4,96,384]{3,2,1,0:T(8,128)(2,1)}) custom-call(bf16[2,4,2,96,768]{4,3,2,1,0:T(8,128)(2,1)} %bitcast.57, bf16[2,4,2,96,768]{4,3,2,1,0:T(8,128)(2,1)} %bitcast.9.come_ref), custom_call_target="tpu_custom_call" | custom-call | tf_op jit(solution)/shard_map/split_step/pallas_call | solution.py:626
  124.6 2.0 collective-permute-start.5
  126.6 19.4 %back.1 = (bf16[5,200,2304]{2,1,0:T(8,128)(2,1)}, f32[12,200,200]{2,1,0:T(8,128)}, f32[1,2304]{1,0:T(1,128)}) custom-call(bf16[5,200,2304]{2,1,0:T(8,128)(2,1)} %get-tuple-element.139.qkv_ref, bf16[5,200,768]{2,1,0:T(8,128)(2,1)} %get-tuple-element.145.do_ref, bf16[5,12,200,200]{3,2,1,0:T(8,128)(2,1)} %get-tuple-element.146.p_ref), custom_call_target="tpu_custom_call" | custom-call | tf_op jit(solution)/shard_map/back/pallas_call | solution.py:456
  146.1 3.0 %halve_step.6 = (bf16[4,96,384]{2,1,0:T(8,128)(2,1)}, bf16[4,96,384]{2,1,0:T(8,128)(2,1)}, bf16[4,96,384]{2,1,0:T(8,128)(2,1)}, bf16[4,96,384]{2,1,0:T(8,128)(2,1)}) custom-call(bf16[8,96,384]{2,1,0:T(8,128)(2,1)} %bitcast.64, bf16[8,96,384]{2,1,0:T(8,128)(2,1)} %collective-permute-done.5.refs_1_, bf16[8,96,384]{2,1,0:T(8,128)(2,1)} %bitcast.65, ...), custom_call_target="tpu_custom_call" | custom-call | tf_op jit(solution)/shard_map/halve_step/pallas_call | solution.py:663
  149.1 13.9 %attention_grads.1 = (bf16[2,768,768]{2,1,0:T(8,128)(2,1)}, bf16[2,768,768]{2,1,0:T(8,128)(2,1)}) custom-call(bf16[1000,768]{1,0:T(8,128)(2,1)} %bitcast.59, bf16[1000,2304]{1,0:T(8,128)(2,1)} %bitcast.48, bf16[1000,768]{1,0:T(8,128)(2,1)} %bitcast.60, bf16[1000,768]{1,0:T(8,128)(2,1)} %bitcast.61), custom_call_target="tpu_custom_call" | custom-call | tf_op jit(solution)/shard_map/attention_grads/pallas_call | solution.py:482
  162.9 11.9 %input_grads.1 = (f32[5,200,768]{2,1,0:T(8,128)}, f32[8,768]{1,0:T(8,128)}) custom-call(bf16[5,200,768]{2,1,0:T(8,128)(2,1)} %x_ref.4, bf16[5,200,2304]{2,1,0:T(8,128)(2,1)} %get-tuple-element.147.dqkv_ref, f32[5,200,768]{2,1,0:T(8,128)} %get-tuple-element.160.dmid_ref, bf16[768,2304]{1,0:T(8,128)(2,1)} %wqkv_ref.3, f32[10,768]{1,0:T(8,128)} %refs_12_.1), custom_call_target="tpu_custom_call" | custom-call | tf_op jit(solution)/shard_map/input_grads/pallas_call | solution.py:512
  174.8 4.5 %split_step.3 = (bf16[4,2,96,384]{3,2,1,0:T(8,128)(2,1)}, bf16[4,2,96,384]{3,2,1,0:T(8,128)(2,1)}, bf16[2,4,96,384]{3,2,1,0:T(8,128)(2,1)}, bf16[2,4,96,384]{3,2,1,0:T(8,128)(2,1)}) custom-call(bf16[2,4,2,96,768]{4,3,2,1,0:T(8,128)(2,1)} %bitcast.58, bf16[2,4,2,96,768]{4,3,2,1,0:T(8,128)(2,1)} %bitcast.21.come_ref), custom_call_target="tpu_custom_call" | custom-call | tf_op jit(solution)/shard_map/split_step/pallas_call | solution.py:626
  179.3 1.4 collective-permute-start.13
  180.7 0.5 collective-permute-start.12
  181.2 2.5 copy.59
  183.7 2.0 pad.14.ds_ref
  185.9 2.0 collective-permute-start.8
  187.9 12.3 %table_sums.1 = f32[192,128]{1,0:T(8,128)} custom-call(s32[200,200]{1,0:T(8,128)} %copy-done.4, f32[200,16,200]{2,1,0:T(8,128)} %pad.14.ds_ref), custom_call_target="tpu_custom_call" | custom-call | tf_op jit(solution)/shard_map/table_sums/pallas_call | solution.py:151
  200.3 1.1 collective-permute-done.12.refs_1_
  201.4 3.0 %halve_step.9 = (bf16[4,96,384]{2,1,0:T(8,128)(2,1)}, bf16[4,96,384]{2,1,0:T(8,128)(2,1)}, bf16[4,96,384]{2,1,0:T(8,128)(2,1)}, bf16[4,96,384]{2,1,0:T(8,128)(2,1)}) custom-call(bf16[8,96,384]{2,1,0:T(8,128)(2,1)} %bitcast.62, bf16[8,96,384]{2,1,0:T(8,128)(2,1)} %collective-permute-done.12.refs_1_, bf16[8,96,384]{2,1,0:T(8,128)(2,1)} %bitcast.63, ...), custom_call_target="tpu_custom_call" | custom-call | tf_op jit(solution)/shard_map/halve_step/pallas_call | solution.py:663
  204.4 0.7 collective-permute-start.14
  205.1 2.0 collective-permute-done.8.refs_3_
  207.1 2.3 halve_step.7
  209.4 1.6 collective-permute-start.10
  211.0 1.8 collective-permute-done.14.refs_1_
  212.8 1.3 collective-permute-done.15.refs_3_
  214.1 2.2 halve_step.10
  216.3 1.6 collective-permute-start.16
  217.9 3.8 %collective-permute-done.10.refs_1_ = bf16[2,96,768]{2,1,0:T(8,128)(2,1)} collective-permute-done((bf16[2,96,768]{2,1,0:T(8,128)(2,1)}, bf16[2,96,768]{2,1,0:T(8,128)(2,1)}, u32[]{:S(2)}, u32[]{:S(2)}) %collective-permute-start.10) | collective-permute-done | bytes 294944 | tf_op jit(solution)/shard_map/ppermute | solution.py:602
  221.7 1.8 halve_step.8
  223.5 1.9 collective-permute-start.11
  225.4 2.3 collective-permute-done.16.refs_1_
  227.8 1.8 halve_step.11
  229.6 2.2 collective-permute-start.17
  231.7 0.6 collective-permute-done.11
  232.3 6.0 %collective-permute-done.17 = bf16[1,96,768]{2,1,0:T(8,128)(2,1)} collective-permute-done((bf16[1,96,768]{2,1,0:T(8,128)(2,1)}, bf16[1,96,768]{2,1,0:T(8,128)(2,1)}, u32[]{:S(2)}, u32[]{:S(2)}) %collective-permute-start.17) | collective-permute-done | bytes 147488 | tf_op jit(solution)/shard_map/ppermute | solution.py:602
  238.3 2.1 finish.1
  240.4 1.0 collective-permute-start.18
  241.4 3.8 %collective-permute-done.18 = f32[32,768]{1,0:T(8,128)S(1)} collective-permute-done((f32[32,768]{1,0:T(8,128)}, f32[32,768]{1,0:T(8,128)S(1)}, u32[]{:S(2)}, u32[]{:S(2)}) %collective-permute-start.18) | collective-permute-done | bytes 98336 | tf_op jit(solution)/shard_map/ppermute | solution.py:602
  245.3 0.9 add.24
  246.2 4.6 %collective-permute-done.19 = f32[32,768]{1,0:T(8,128)S(1)} collective-permute-done((f32[32,768]{1,0:T(8,128)S(1)}, f32[32,768]{1,0:T(8,128)S(1)}, u32[]{:S(2)}, u32[]{:S(2)}) %collective-permute-start.19) | collective-permute-done | bytes 98336 | tf_op jit(solution)/shard_map/ppermute | solution.py:602
  250.9 0.9 collective-permute-start.20
  251.8 5.6 %collective-permute-done.20 = f32[32,768]{1,0:T(8,128)S(1)} collective-permute-done((f32[32,768]{1,0:T(8,128)S(1)}, f32[32,768]{1,0:T(8,128)S(1)}, u32[]{:S(2)}, u32[]{:S(2)}) %collective-permute-start.20) | collective-permute-done | bytes 98336 | tf_op jit(solution)/shard_map/ppermute | solution.py:602
  257.4 1.3 collective-permute-done.21
  258.7 0.6 copy-done.6
  259.4 1.2 collective-permute-start.22
  260.6 3.6 %collective-permute-done.22.theirs_ref = f32[32,768]{1,0:T(8,128)S(1)} collective-permute-done((f32[32,768]{1,0:T(8,128)S(1)}, f32[32,768]{1,0:T(8,128)S(1)}, u32[]{:S(2)}, u32[]{:S(2)}) %collective-permute-start.22) | collective-permute-done | bytes 98336 | tf_op jit(solution)/shard_map/ppermute | solution.py:602
  264.2 0.6 copy-done.7
  264.9 4.8 %adam.1 = (f32[1,1]{1,0:T(1,128)}, f32[96,576]{1,0:T(8,128)}, f32[96,576]{1,0:T(8,128)}, f32[96,576]{1,0:T(8,128)}, bf16[96,576]{1,0:T(8,128)(2,1)}, /*index=5*/...) custom-call(f32[32,768]{1,0:T(8,128)} %copy-done.6, ...), custom_call_target="tpu_custom_call" | custom-call | tf_op jit(solution)/shard_map/adam/pallas_call | solution.py:581
  (40 shorter events, 1.1 us)
Async XLA Ops:
  8.0 70.4 %all-gather.3.cloned.1.call-start = ((), (), s32[]{:S(2)}) async-start(), calls=%async_computation.2 | async-start | bytes 5898240 | tf_op jit(solution)/shard_map/all_gather | solution.py:786
  9.2 16.4 %collective-permute-start = (bf16[384,768]{1,0:T(8,128)(2,1)S(1)}, bf16[384,768]{1,0:T(8,128)(2,1)S(1)}, u32[]{:S(2)}, u32[]{:S(2)}) collective-permute-start(bf16[384,768]{1,0:T(8,128)(2,1)S(1)} %constant_dynamic-slice_fusion), channel_id=1, source_target_pairs={{0,2},{1,3},{2,0},{3,1},{4,6},{5,7},{6,4},{7,5},{8,10},{9,11},{10,... | collective-permute-start | bytes 1769480 | tf_op jit(solution)/shard_map/ppermute | solution.py:602
  13.7 13.8 %copy-start.1 = (bf16[768,768]{1,0:T(8,128)(2,1)S(1)}, bf16[768,768]{1,0:T(8,128)(2,1)}, u32[]{:S(2)}) copy-start(bf16[768,768]{1,0:T(8,128)(2,1)} %up_a.3) | copy-start | bytes 3538948
  14.7 0.7 copy-start.4
  25.6 206.1 %reduce-scatter.2.cloned.1.call-start = ((), (), s32[]{:S(2)}) async-start(), calls=%async_computation.1 | async-start | bytes 4866048 | tf_op jit(solution)/shard_map/reduce_scatter | solution.py:798
  25.7 28.3 %collective-permute-start.2 = (bf16[384,768]{1,0:T(8,128)(2,1)S(1)}, bf16[384,768]{1,0:T(8,128)(2,1)S(1)}, u32[]{:S(2)}, u32[]{:S(2)}) collective-permute-start(bf16[384,768]{1,0:T(8,128)(2,1)S(1)} %collective-permute-done), channel_id=1, source_target_pairs={{0,4},{4,0},{8,12},{12,8},{16,20},{20,16},{24,28},{28,24},{1,5},{5... | collective-permute-start | bytes 1769480 | tf_op jit(solution)/shard_map/ppermute | solution.py:602
  27.4 29.9 %collective-permute-start.1 = (bf16[768,768]{1,0:T(8,128)(2,1)S(1)}, bf16[768,768]{1,0:T(8,128)(2,1)S(1)}, u32[]{:S(2)}, u32[]{:S(2)}) collective-permute-start(bf16[768,768]{1,0:T(8,128)(2,1)S(1)} %copy-done.1), channel_id=1, source_target_pairs={{0,1},{1,0},{2,3},{3,2},{4,5},{5,4},{6,7},{7,6},{8,9},{9,8},{10,11... | collective-permute-start | bytes 3538952 | tf_op jit(solution)/shard_map/ppermute | solution.py:602
  53.9 2.0 copy-start.8
  53.9 2.0 copy-start.5
  54.4 1.0 copy-start
  55.5 3.1 %collective-permute-start.3 = (bf16[768,768]{1,0:T(8,128)(2,1)S(1)}, bf16[768,768]{1,0:T(8,128)(2,1)S(1)}, u32[]{:S(2)}, u32[]{:S(2)}) collective-permute-start(bf16[768,768]{1,0:T(8,128)(2,1)S(1)} %maximum_select_fusion.up_c), channel_id=1, source_target_pairs={{0,1},{1,0},{2,3},{3,2},{4,5},{5,4},{6,7},{7,6},{8,9},{9,8},{10,11... | collective-permute-start | bytes 3538952 | tf_op jit(solution)/shard_map/ppermute | solution.py:602
  57.3 1.3 copy-start.2
  58.6 1.0 copy-start.3
  108.7 11.3 %collective-permute-start.4 = (bf16[16,96,768]{2,1,0:T(8,128)(2,1)}, bf16[16,96,768]{2,1,0:T(8,128)(2,1)}, u32[]{:S(2)}, u32[]{:S(2)}) collective-permute-start(bf16[16,96,768]{2,1,0:T(8,128)(2,1)} %bitcast.76), channel_id=1, source_target_pairs={{0,1},{1,0},{2,3},{3,2},{4,5},{5,4},{6,7},{7,6},{8,9},{9,8},{10,11... | collective-permute-start | bytes 7077896 | tf_op jit(solution)/shard_map/ppermute | solution.py:602
  124.5 21.6 %collective-permute-start.6 = (bf16[8,96,384]{2,1,0:T(8,128)(2,1)}, bf16[8,96,384]{2,1,0:T(8,128)(2,1)}, u32[]{:S(2)}, u32[]{:S(2)}) collective-permute-start(bf16[8,96,384]{2,1,0:T(8,128)(2,1)} %bitcast.81), channel_id=1, source_target_pairs={{0,4},{4,0},{8,12},{12,8},{16,20},{20,16},{24,28},{28,24},{1,5},{5... | collective-permute-start | bytes 1769480 | tf_op jit(solution)/shard_map/ppermute | solution.py:602
  124.6 21.5 %collective-permute-start.5 = (bf16[8,96,384]{2,1,0:T(8,128)(2,1)}, bf16[8,96,384]{2,1,0:T(8,128)(2,1)}, u32[]{:S(2)}, u32[]{:S(2)}) collective-permute-start(bf16[8,96,384]{2,1,0:T(8,128)(2,1)} %bitcast.80), channel_id=1, source_target_pairs={{0,2},{1,3},{2,0},{3,1},{4,6},{5,7},{6,4},{7,5},{8,10},{9,11},{10,... | collective-permute-start | bytes 1769480 | tf_op jit(solution)/shard_map/ppermute | solution.py:602
  162.9 11.9 %collective-permute-start.9 = (bf16[16,96,768]{2,1,0:T(8,128)(2,1)}, bf16[16,96,768]{2,1,0:T(8,128)(2,1)}, u32[]{:S(2)}, u32[]{:S(2)}) collective-permute-start(bf16[16,96,768]{2,1,0:T(8,128)(2,1)} %bitcast.77), channel_id=1, source_target_pairs={{0,1},{1,0},{2,3},{3,2},{4,5},{5,4},{6,7},{7,6},{8,9},{9,8},{10,11... | collective-permute-start | bytes 7077896 | tf_op jit(solution)/shard_map/ppermute | solution.py:602
  179.3 21.0 %collective-permute-start.13 = (bf16[8,96,384]{2,1,0:T(8,128)(2,1)}, bf16[8,96,384]{2,1,0:T(8,128)(2,1)}, u32[]{:S(2)}, u32[]{:S(2)}) collective-permute-start(bf16[8,96,384]{2,1,0:T(8,128)(2,1)} %bitcast.79), channel_id=1, source_target_pairs={{0,4},{4,0},{8,12},{12,8},{16,20},{20,16},{24,28},{28,24},{1,5},{5... | collective-permute-start | bytes 1769480 | tf_op jit(solution)/shard_map/ppermute | solution.py:602
  180.7 20.7 %collective-permute-start.12 = (bf16[8,96,384]{2,1,0:T(8,128)(2,1)}, bf16[8,96,384]{2,1,0:T(8,128)(2,1)}, u32[]{:S(2)}, u32[]{:S(2)}) collective-permute-start(bf16[8,96,384]{2,1,0:T(8,128)(2,1)} %bitcast.78), channel_id=1, source_target_pairs={{0,2},{1,3},{2,0},{3,1},{4,6},{5,7},{6,4},{7,5},{8,10},{9,11},{10,... | collective-permute-start | bytes 1769480 | tf_op jit(solution)/shard_map/ppermute | solution.py:602
  185.8 19.3 %collective-permute-start.7 = (bf16[4,96,384]{2,1,0:T(8,128)(2,1)}, bf16[4,96,384]{2,1,0:T(8,128)(2,1)}, u32[]{:S(2)}, u32[]{:S(2)}) collective-permute-start(bf16[4,96,384]{2,1,0:T(8,128)(2,1)} %get-tuple-element.156), channel_id=1, source_target_pairs={{0,4},{4,0},{8,12},{12,8},{16,20},{20,16},{24,28},{28,24},{1,5},{5... | collective-permute-start | bytes 884744 | tf_op jit(solution)/shard_map/ppermute | solution.py:602
  185.9 21.2 %collective-permute-start.8 = (bf16[4,96,384]{2,1,0:T(8,128)(2,1)}, bf16[4,96,384]{2,1,0:T(8,128)(2,1)}, u32[]{:S(2)}, u32[]{:S(2)}) collective-permute-start(bf16[4,96,384]{2,1,0:T(8,128)(2,1)} %get-tuple-element.157), channel_id=1, source_target_pairs={{0,2},{1,3},{2,0},{3,1},{4,6},{5,7},{6,4},{7,5},{8,10},{9,11},{10,... | collective-permute-start | bytes 884744 | tf_op jit(solution)/shard_map/ppermute | solution.py:602
  204.4 8.4 %collective-permute-start.14 = (bf16[4,96,384]{2,1,0:T(8,128)(2,1)}, bf16[4,96,384]{2,1,0:T(8,128)(2,1)}, u32[]{:S(2)}, u32[]{:S(2)}) collective-permute-start(bf16[4,96,384]{2,1,0:T(8,128)(2,1)} %get-tuple-element.181), channel_id=1, source_target_pairs={{0,4},{4,0},{8,12},{12,8},{16,20},{20,16},{24,28},{28,24},{1,5},{5... | collective-permute-start | bytes 884744 | tf_op jit(solution)/shard_map/ppermute | solution.py:602
  205.0 9.1 %collective-permute-start.15 = (bf16[4,96,384]{2,1,0:T(8,128)(2,1)}, bf16[4,96,384]{2,1,0:T(8,128)(2,1)}, u32[]{:S(2)}, u32[]{:S(2)}) collective-permute-start(bf16[4,96,384]{2,1,0:T(8,128)(2,1)} %get-tuple-element.183), channel_id=1, source_target_pairs={{0,2},{1,3},{2,0},{3,1},{4,6},{5,7},{6,4},{7,5},{8,10},{9,11},{10,... | collective-permute-start | bytes 884744 | tf_op jit(solution)/shard_map/ppermute | solution.py:602
  209.4 12.3 %collective-permute-start.10 = (bf16[2,96,768]{2,1,0:T(8,128)(2,1)}, bf16[2,96,768]{2,1,0:T(8,128)(2,1)}, u32[]{:S(2)}, u32[]{:S(2)}) collective-permute-start(bf16[2,96,768]{2,1,0:T(8,128)(2,1)} %get-tuple-element.173), channel_id=1, source_target_pairs={{0,8},{4,12},{8,0},{12,4},{16,24},{20,28},{24,16},{28,20},{1,9},{5... | collective-permute-start | bytes 884744 | tf_op jit(solution)/shard_map/ppermute | solution.py:602
  216.3 11.5 %collective-permute-start.16 = (bf16[2,96,768]{2,1,0:T(8,128)(2,1)}, bf16[2,96,768]{2,1,0:T(8,128)(2,1)}, u32[]{:S(2)}, u32[]{:S(2)}) collective-permute-start(bf16[2,96,768]{2,1,0:T(8,128)(2,1)} %get-tuple-element.185), channel_id=1, source_target_pairs={{0,8},{4,12},{8,0},{12,4},{16,24},{20,28},{24,16},{28,20},{1,9},{5... | collective-permute-start | bytes 884744 | tf_op jit(solution)/shard_map/ppermute | solution.py:602
  223.5 8.8 %collective-permute-start.11 = (bf16[1,96,768]{2,1,0:T(8,128)(2,1)}, bf16[1,96,768]{2,1,0:T(8,128)(2,1)}, u32[]{:S(2)}, u32[]{:S(2)}) collective-permute-start(bf16[1,96,768]{2,1,0:T(8,128)(2,1)} %get-tuple-element.175), channel_id=1, source_target_pairs={{0,16},{4,20},{8,24},{12,28},{16,0},{20,4},{24,8},{28,12},{1,17},{... | collective-permute-start | bytes 442376 | tf_op jit(solution)/shard_map/ppermute | solution.py:602
  229.6 8.7 %collective-permute-start.17 = (bf16[1,96,768]{2,1,0:T(8,128)(2,1)}, bf16[1,96,768]{2,1,0:T(8,128)(2,1)}, u32[]{:S(2)}, u32[]{:S(2)}) collective-permute-start(bf16[1,96,768]{2,1,0:T(8,128)(2,1)} %get-tuple-element.187), channel_id=1, source_target_pairs={{0,16},{4,20},{8,24},{12,28},{16,0},{20,4},{24,8},{28,12},{1,17},{... | collective-permute-start | bytes 442376 | tf_op jit(solution)/shard_map/ppermute | solution.py:602
  240.4 4.8 %collective-permute-start.18 = (f32[32,768]{1,0:T(8,128)}, f32[32,768]{1,0:T(8,128)S(1)}, u32[]{:S(2)}, u32[]{:S(2)}) collective-permute-start(f32[32,768]{1,0:T(8,128)} %get-tuple-element.193), channel_id=1, source_target_pairs={{0,4},{4,0},{8,12},{12,8},{16,20},{20,16},{24,28},{28,24},{1,5},{5... | collective-permute-start | bytes 294920 | tf_op jit(solution)/shard_map/ppermute | solution.py:602
  246.2 4.7 %collective-permute-start.19 = (f32[32,768]{1,0:T(8,128)S(1)}, f32[32,768]{1,0:T(8,128)S(1)}, u32[]{:S(2)}, u32[]{:S(2)}) collective-permute-start(f32[32,768]{1,0:T(8,128)S(1)} %add.24), channel_id=1, source_target_pairs={{0,8},{4,12},{8,0},{12,4},{16,24},{20,28},{24,16},{28,20},{1,9},{5... | collective-permute-start | bytes 294920 | tf_op jit(solution)/shard_map/ppermute | solution.py:602
  250.9 6.5 %collective-permute-start.20 = (f32[32,768]{1,0:T(8,128)S(1)}, f32[32,768]{1,0:T(8,128)S(1)}, u32[]{:S(2)}, u32[]{:S(2)}) collective-permute-start(f32[32,768]{1,0:T(8,128)S(1)} %add.25), channel_id=1, source_target_pairs={{0,16},{4,20},{8,24},{12,28},{16,0},{20,4},{24,8},{28,12},{1,17},{... | collective-permute-start | bytes 294920 | tf_op jit(solution)/shard_map/ppermute | solution.py:602
  257.3 1.4 collective-permute-start.21
  258.7 0.6 copy-start.6
  259.4 4.9 %collective-permute-start.22 = (f32[32,768]{1,0:T(8,128)S(1)}, f32[32,768]{1,0:T(8,128)S(1)}, u32[]{:S(2)}, u32[]{:S(2)}) collective-permute-start(f32[32,768]{1,0:T(8,128)S(1)} %add.27.ours_ref), channel_id=1, source_target_pairs={{0,2},{1,3},{2,0},{3,1},{4,6},{5,7},{6,4},{7,5},{8,10},{9,11},{10,... | collective-permute-start | bytes 294920 | tf_op jit(solution)/shard_map/ppermute | solution.py:602
  264.2 0.6 copy-start.7
Sparse Core Ops, SparseCore 0:
  25.7 38.9 all-gather.2
Sparse Core Ops, SparseCore 1:
  109.3 112.5 reduce-scatter.1

commit v7 on v6

--- a/solution.py
+++ b/solution.py
@@ -350,7 +350,7 @@
             pltpu.VMEM((width, tokens), BF),
             pltpu.VMEM((width, hidden), BF),
         ],
-        compiler_params=params(),
+        compiler_params=params(limit=VMEM_WHOLE),
         name="mlp_out",
     )(hn, dm, z, slope, down_all, *ups)
 
@@ -450,7 +450,7 @@
     images, seq, width = do.shape
     shapes = [
         jax.ShapeDtypeStruct((images, seq, 3 * width), BF),
-        jax.ShapeDtypeStruct((heads, seq, seq), F32),
+        jax.ShapeDtypeStruct((heads + (-heads) % 8, seq, seq), F32),
         jax.ShapeDtypeStruct((1, 3 * width), F32),
     ]
     return pl.pallas_call(
@@ -877,7 +877,7 @@
     keep, send = attention_grads(flat(first), flat(dqkv), flat(mixed), flat(dat), blocks, plan.owner)
     dmid = gated(dmid, *plan.after_attention(keep, send))
     input_grad, gvec_one = input_grads(block_in, dqkv, dmid, qkv_weight, vectors)
-    by_query = jnp.pad(ds.transpose(1, 0, 2), ((0, 0), (0, (-heads) % 8), (0, 0)))
+    by_query = ds.transpose(1, 0, 2)
     by_query = gated(by_query, *plan.next_attention(input_grad))
     sums = table_sums(index, by_query, chunks)
     plan.next_both(sums)

time: 278 us -> 278 us (level)
  no operation moved by 1% of the time
where the time goes in v7:
time: 278 us; the launch traced here: 277 us
  Pallas kernels  182 us (65%)
  waiting for transfers between devices  39.1 us (14%)
  starting transfers between devices  24.4 us (9%)
  between operations  15.7 us (6%)
  local copies, waits for them, and re-layouts  11.9 us (4%)
  other arithmetic  3.79 us (1%)
    ppermute x23, waiting for transfers between devices, swap(): return lax.ppermute(value, axis, [(i, i ^ 1 << bit) for i in range(size)])  39 us
    pallas_call x1, Pallas kernels, mlp_out(): pl.pallas_call(functools.partial(mlp_out_kernel, chunk, owner), grid=(blo...  30.3 us
    pallas_call x1, Pallas kernels, front(): pl.pallas_call(functools.partial(front_kernel, heads), grid=(images,), in...  26.5 us
    ppermute x23, starting transfers between devices, swap(): return lax.ppermute(value, axis, [(i, i ^ 1 << bit) for i in range(size)])  24.3 us
    pallas_call x1, Pallas kernels, back(): pl.pallas_call(functools.partial(back_kernel, heads), grid=(images,), in_...  19.8 us
    pallas_call x1, Pallas kernels, mlp_in(): pl.pallas_call(functools.partial(mlp_in_kernel, chunk, owner), grid=(bloc...  18.8 us
    pallas_call x6, Pallas kernels, halve_step(): pl.pallas_call(functools.partial(halve_kernel, mine, places, join), grid=...  14.1 us
    pallas_call x1, Pallas kernels, attention_grads(): pl.pallas_call(functools.partial(grads_kernel, blocks, owner), grid=(1,),...  13.8 us
  transfers between devices with their start and end apart: 25, of which 15 were waited for; matrix products, arithmetic and copies ran while one was open for 3% of the time, Pallas kernels for 52%

profile of v7, /device:TPU:0, one launch (start us, length us, event | category | flops | bytes accessed | tf_op | source)
XLA Modules:
  0.0 277.1 jit_solution(6876214460842290833)
XLA Ops:
  8.1 1.1 constant_dynamic-slice_fusion
  9.2 3.1 %collective-permute-start = (bf16[384,768]{1,0:T(8,128)(2,1)S(1)}, bf16[384,768]{1,0:T(8,128)(2,1)S(1)}, u32[]{:S(2)}, u32[]{:S(2)}) collective-permute-start(bf16[384,768]{1,0:T(8,128)(2,1)S(1)} %constant_dynamic-slice_fusion), channel_id=1, source_target_pairs={{0,2},{1,3},{2,0},{3,1},{4,6},{5,7},{6,4},{7,5},{8,10},{9,11},{10,... | collective-permute-start | bytes 1769480 | tf_op jit(solution)/shard_map/ppermute | solution.py:602
  12.3 0.8 pad_bitcast_fusion
  13.1 0.6 reshape.156.tab_ref
  13.7 1.0 broadcast_select_fusion.idx_ref
  14.8 0.7 copy-done.4
  15.4 0.7 pad.8.idx_ref
  16.1 8.1 %bias_tables.1.bias_ref = f32[12,200,200]{2,1,0:T(8,128)} custom-call(s32[200,256]{1,0:T(8,128)} %pad.8.idx_ref, f32[12,6,128]{2,1,0:T(8,128)} %reshape.156.tab_ref), custom_call_target="tpu_custom_call" | custom-call | tf_op jit(solution)/shard_map/bias_tables/pallas_call | solution.py:117
  24.2 1.4 collective-permute-done
  25.7 1.8 collective-permute-start.2
  27.4 26.5 %front.1 = (bf16[5,200,768]{2,1,0:T(8,128)(2,1)}, bf16[5,200,2304]{2,1,0:T(8,128)(2,1)}, bf16[5,12,200,200]{3,2,1,0:T(8,128)(2,1)}, bf16[5,200,768]{2,1,0:T(8,12...) custom-call(bf16[5,200,768]{2,1,0:T(8,128)(2,1)} %x_ref.4, bf16[768,2304]{1,0:T(8,128)(2,1)} %wqkv_ref.3, ...), custom_call_target="tpu_custom_call" | custom-call | tf_op jit(solution)/shard_map/front/pallas_call | solution.py:215
  54.0 0.5 maximum_select_fusion.up_c
  54.4 1.0 copy-done
  55.5 0.5 collective-permute-start.3
  56.0 1.3 broadcast_multiply_fusion.gy_ref
  57.3 1.3 collective-permute-done.3.up_d
  58.6 1.0 copy-done.3
  59.6 18.8 %mlp_in.1 = (bf16[4,1000,768]{2,1,0:T(8,128)(2,1)}, bf16[4,1000,768]{2,1,0:T(8,128)(2,1)}, bf16[4,768,768]{2,1,0:T(8,128)(2,1)}, bf16[1000,768]{1,0:T(8,128)(2,1)}) custom-call(bf16[1000,768]{1,0:T(8,128)(2,1)} %bitcast.51, bf16[1000,768]{1,0:T(8,128)(2,1)} %bitcast.49, f32[10,768]{1,0:T(8,128)} %refs_12_.1, f32[4,1,768]{2,1,0:T(1,128)} %bitcast.72, ...), custom_call_target="tpu_custom_call" | custom-call | tf_op jit(solution)/shard_map/mlp_in/pallas_call | solution.py:275
  78.4 30.3 %mlp_out.1 = (f32[1000,768]{1,0:T(8,128)}, f32[1000,768]{1,0:T(8,128)}, bf16[2,768,768]{2,1,0:T(8,128)(2,1)}, bf16[2,768,768]{2,1,0:T(8,128)(2,1)}, f32[4,1,768]{2,1,0:T(1,128)}) custom-call(bf16[1000,768]{1,0:T(8,128)(2,1)} %bitcast.52, bf16[1000,768]{1,0:T(8,128)(2,1)} %get-tuple-element.129.dm_ref, bf16[4,1000,768]{2,1,0:T(8,128)(2,1)} %get-tuple-element.130.z_ref, ...), custom_call_target="tpu_custom_call" | custom-call | tf_op jit(solution)/shard_map/mlp_out/pallas_call | solution.py:342
  108.7 0.4 collective-permute-start.4
  109.2 10.8 %middle_back.1 = (bf16[5,200,768]{2,1,0:T(8,128)(2,1)}, f32[5,200,768]{2,1,0:T(8,128)}, bf16[5,200,768]{2,1,0:T(8,128)(2,1)}, bf16[5,200,768]{2,1,0:T(8,128)(2,1)}, f32[8,768]{1,0:T(8,128)}) custom-call(bf16[5,200,768]{2,1,0:T(8,128)(2,1)} %x_ref.4, bf16[5,200,768]{2,1,0:T(8,128)(2,1)} %broadcast_multiply_fusion.gy_ref, ...), custom_call_target="tpu_custom_call" | custom-call | tf_op jit(solution)/shard_map/middle_back/pallas_call | solution.py:393
  120.1 4.4 %split_step.2 = (bf16[4,2,96,384]{3,2,1,0:T(8,128)(2,1)}, bf16[4,2,96,384]{3,2,1,0:T(8,128)(2,1)}, bf16[2,4,96,384]{3,2,1,0:T(8,128)(2,1)}, bf16[2,4,96,384]{3,2,1,0:T(8,128)(2,1)}) custom-call(bf16[2,4,2,96,768]{4,3,2,1,0:T(8,128)(2,1)} %bitcast.57, bf16[2,4,2,96,768]{4,3,2,1,0:T(8,128)(2,1)} %bitcast.9.come_ref), custom_call_target="tpu_custom_call" | custom-call | tf_op jit(solution)/shard_map/split_step/pallas_call | solution.py:626
  124.6 2.0 collective-permute-start.5
  126.6 19.8 %back.1 = (bf16[5,200,2304]{2,1,0:T(8,128)(2,1)}, f32[16,200,200]{2,1,0:T(8,128)}, f32[1,2304]{1,0:T(1,128)}) custom-call(bf16[5,200,2304]{2,1,0:T(8,128)(2,1)} %get-tuple-element.139.qkv_ref, bf16[5,200,768]{2,1,0:T(8,128)(2,1)} %get-tuple-element.145.do_ref, bf16[5,12,200,200]{3,2,1,0:T(8,128)(2,1)} %get-tuple-element.146.p_ref), custom_call_target="tpu_custom_call" | custom-call | tf_op jit(solution)/shard_map/back/pallas_call | solution.py:456
  146.4 3.0 %halve_step.6 = (bf16[4,96,384]{2,1,0:T(8,128)(2,1)}, bf16[4,96,384]{2,1,0:T(8,128)(2,1)}, bf16[4,96,384]{2,1,0:T(8,128)(2,1)}, bf16[4,96,384]{2,1,0:T(8,128)(2,1)}) custom-call(bf16[8,96,384]{2,1,0:T(8,128)(2,1)} %bitcast.64, bf16[8,96,384]{2,1,0:T(8,128)(2,1)} %collective-permute-done.5.refs_1_, bf16[8,96,384]{2,1,0:T(8,128)(2,1)} %bitcast.65, ...), custom_call_target="tpu_custom_call" | custom-call | tf_op jit(solution)/shard_map/halve_step/pallas_call | solution.py:663
  149.5 13.8 %attention_grads.1 = (bf16[2,768,768]{2,1,0:T(8,128)(2,1)}, bf16[2,768,768]{2,1,0:T(8,128)(2,1)}) custom-call(bf16[1000,768]{1,0:T(8,128)(2,1)} %bitcast.59, bf16[1000,2304]{1,0:T(8,128)(2,1)} %bitcast.48, bf16[1000,768]{1,0:T(8,128)(2,1)} %bitcast.60, bf16[1000,768]{1,0:T(8,128)(2,1)} %bitcast.61), custom_call_target="tpu_custom_call" | custom-call | tf_op jit(solution)/shard_map/attention_grads/pallas_call | solution.py:482
  163.3 11.9 %input_grads.1 = (f32[5,200,768]{2,1,0:T(8,128)}, f32[8,768]{1,0:T(8,128)}) custom-call(bf16[5,200,768]{2,1,0:T(8,128)(2,1)} %x_ref.4, bf16[5,200,2304]{2,1,0:T(8,128)(2,1)} %get-tuple-element.147.dqkv_ref, f32[5,200,768]{2,1,0:T(8,128)} %get-tuple-element.160.dmid_ref, bf16[768,2304]{1,0:T(8,128)(2,1)} %wqkv_ref.3, f32[10,768]{1,0:T(8,128)} %refs_12_.1), custom_call_target="tpu_custom_call" | custom-call | tf_op jit(solution)/shard_map/input_grads/pallas_call | solution.py:512
  175.2 4.5 %split_step.3 = (bf16[4,2,96,384]{3,2,1,0:T(8,128)(2,1)}, bf16[4,2,96,384]{3,2,1,0:T(8,128)(2,1)}, bf16[2,4,96,384]{3,2,1,0:T(8,128)(2,1)}, bf16[2,4,96,384]{3,2,1,0:T(8,128)(2,1)}) custom-call(bf16[2,4,2,96,768]{4,3,2,1,0:T(8,128)(2,1)} %bitcast.58, bf16[2,4,2,96,768]{4,3,2,1,0:T(8,128)(2,1)} %bitcast.21.come_ref), custom_call_target="tpu_custom_call" | custom-call | tf_op jit(solution)/shard_map/split_step/pallas_call | solution.py:626
  179.6 1.4 collective-permute-start.13
  181.0 0.6 collective-permute-start.12
  181.6 4.6 %copy.59 = f32[16,200,200]{2,0,1:T(8,128)} copy(f32[16,200,200]{2,1,0:T(8,128)} %get-tuple-element.163) | data formatting | bytes 5120000 | tf_op jit(solution)/shard_map/back/pallas_call | solution.py:456
  186.3 2.0 collective-permute-start.8
  188.3 12.3 %table_sums.1 = f32[192,128]{1,0:T(8,128)} custom-call(s32[200,200]{1,0:T(8,128)} %copy-done.4, f32[200,16,200]{2,1,0:T(8,128)} %bitcast.50), custom_call_target="tpu_custom_call" | custom-call | tf_op jit(solution)/shard_map/table_sums/pallas_call | solution.py:151
  200.7 1.1 collective-permute-done.12.refs_1_
  201.7 3.0 %halve_step.9 = (bf16[4,96,384]{2,1,0:T(8,128)(2,1)}, bf16[4,96,384]{2,1,0:T(8,128)(2,1)}, bf16[4,96,384]{2,1,0:T(8,128)(2,1)}, bf16[4,96,384]{2,1,0:T(8,128)(2,1)}) custom-call(bf16[8,96,384]{2,1,0:T(8,128)(2,1)} %bitcast.62, bf16[8,96,384]{2,1,0:T(8,128)(2,1)} %collective-permute-done.12.refs_1_, bf16[8,96,384]{2,1,0:T(8,128)(2,1)} %bitcast.63, ...), custom_call_target="tpu_custom_call" | custom-call | tf_op jit(solution)/shard_map/halve_step/pallas_call | solution.py:663
  204.7 0.7 collective-permute-start.14
  205.5 1.8 collective-permute-done.8.refs_3_
  207.4 2.3 halve_step.7
  209.6 1.6 collective-permute-start.10
  211.2 1.9 collective-permute-done.14.refs_1_
  213.1 1.3 collective-permute-done.15.refs_3_
  214.4 2.2 halve_step.10
  216.6 1.6 collective-permute-start.16
  218.2 3.6 %collective-permute-done.10.refs_1_ = bf16[2,96,768]{2,1,0:T(8,128)(2,1)} collective-permute-done((bf16[2,96,768]{2,1,0:T(8,128)(2,1)}, bf16[2,96,768]{2,1,0:T(8,128)(2,1)}, u32[]{:S(2)}, u32[]{:S(2)}) %collective-permute-start.10) | collective-permute-done | bytes 294944 | tf_op jit(solution)/shard_map/ppermute | solution.py:602
  221.8 1.8 halve_step.8
  223.6 2.2 collective-permute-start.11
  225.8 2.1 collective-permute-done.16.refs_1_
  228.0 1.8 halve_step.11
  229.8 2.2 collective-permute-start.17
  232.0 0.2 collective-permute-done.11
  232.2 6.2 %collective-permute-done.17 = bf16[1,96,768]{2,1,0:T(8,128)(2,1)} collective-permute-done((bf16[1,96,768]{2,1,0:T(8,128)(2,1)}, bf16[1,96,768]{2,1,0:T(8,128)(2,1)}, u32[]{:S(2)}, u32[]{:S(2)}) %collective-permute-start.17) | collective-permute-done | bytes 147488 | tf_op jit(solution)/shard_map/ppermute | solution.py:602
  238.4 2.1 finish.1
  240.5 1.0 collective-permute-start.18
  241.6 3.8 %collective-permute-done.18 = f32[32,768]{1,0:T(8,128)S(1)} collective-permute-done((f32[32,768]{1,0:T(8,128)}, f32[32,768]{1,0:T(8,128)S(1)}, u32[]{:S(2)}, u32[]{:S(2)}) %collective-permute-start.18) | collective-permute-done | bytes 98336 | tf_op jit(solution)/shard_map/ppermute | solution.py:602
  245.3 0.9 add.22
  246.3 4.6 %collective-permute-done.19 = f32[32,768]{1,0:T(8,128)S(1)} collective-permute-done((f32[32,768]{1,0:T(8,128)S(1)}, f32[32,768]{1,0:T(8,128)S(1)}, u32[]{:S(2)}, u32[]{:S(2)}) %collective-permute-start.19) | collective-permute-done | bytes 98336 | tf_op jit(solution)/shard_map/ppermute | solution.py:602
  250.9 1.6 collective-permute-start.20
  252.5 4.7 %collective-permute-done.20 = f32[32,768]{1,0:T(8,128)S(1)} collective-permute-done((f32[32,768]{1,0:T(8,128)S(1)}, f32[32,768]{1,0:T(8,128)S(1)}, u32[]{:S(2)}, u32[]{:S(2)}) %collective-permute-start.20) | collective-permute-done | bytes 98336 | tf_op jit(solution)/shard_map/ppermute | solution.py:602
  257.4 1.3 collective-permute-done.21
  258.7 0.6 copy-done.6
  259.3 1.1 collective-permute-start.22
  260.5 3.7 %collective-permute-done.22.theirs_ref = f32[32,768]{1,0:T(8,128)S(1)} collective-permute-done((f32[32,768]{1,0:T(8,128)S(1)}, f32[32,768]{1,0:T(8,128)S(1)}, u32[]{:S(2)}, u32[]{:S(2)}) %collective-permute-start.22) | collective-permute-done | bytes 98336 | tf_op jit(solution)/shard_map/ppermute | solution.py:602
  264.2 0.6 copy-done.7
  264.8 4.8 %adam.1 = (f32[1,1]{1,0:T(1,128)}, f32[96,576]{1,0:T(8,128)}, f32[96,576]{1,0:T(8,128)}, f32[96,576]{1,0:T(8,128)}, bf16[96,576]{1,0:T(8,128)(2,1)}, /*index=5*/...) custom-call(f32[32,768]{1,0:T(8,128)} %copy-done.6, ...), custom_call_target="tpu_custom_call" | custom-call | tf_op jit(solution)/shard_map/adam/pallas_call | solution.py:581
  (39 shorter events, 0.7 us)
Async XLA Ops:
  8.0 70.4 %all-gather.3.cloned.1.call-start = ((), (), s32[]{:S(2)}) async-start(), calls=%async_computation.2 | async-start | bytes 5898240 | tf_op jit(solution)/shard_map/all_gather | solution.py:786
  9.2 16.4 %collective-permute-start = (bf16[384,768]{1,0:T(8,128)(2,1)S(1)}, bf16[384,768]{1,0:T(8,128)(2,1)S(1)}, u32[]{:S(2)}, u32[]{:S(2)}) collective-permute-start(bf16[384,768]{1,0:T(8,128)(2,1)S(1)} %constant_dynamic-slice_fusion), channel_id=1, source_target_pairs={{0,2},{1,3},{2,0},{3,1},{4,6},{5,7},{6,4},{7,5},{8,10},{9,11},{10,... | collective-permute-start | bytes 1769480 | tf_op jit(solution)/shard_map/ppermute | solution.py:602
  13.7 13.8 %copy-start.1 = (bf16[768,768]{1,0:T(8,128)(2,1)S(1)}, bf16[768,768]{1,0:T(8,128)(2,1)}, u32[]{:S(2)}) copy-start(bf16[768,768]{1,0:T(8,128)(2,1)} %up_a.3) | copy-start | bytes 3538948
  14.7 0.7 copy-start.4
  25.6 206.4 %reduce-scatter.2.cloned.1.call-start = ((), (), s32[]{:S(2)}) async-start(), calls=%async_computation.1 | async-start | bytes 4866048 | tf_op jit(solution)/shard_map/reduce_scatter | solution.py:798
  25.7 28.3 %collective-permute-start.2 = (bf16[384,768]{1,0:T(8,128)(2,1)S(1)}, bf16[384,768]{1,0:T(8,128)(2,1)S(1)}, u32[]{:S(2)}, u32[]{:S(2)}) collective-permute-start(bf16[384,768]{1,0:T(8,128)(2,1)S(1)} %collective-permute-done), channel_id=1, source_target_pairs={{0,4},{4,0},{8,12},{12,8},{16,20},{20,16},{24,28},{28,24},{1,5},{5... | collective-permute-start | bytes 1769480 | tf_op jit(solution)/shard_map/ppermute | solution.py:602
  27.4 29.9 %collective-permute-start.1 = (bf16[768,768]{1,0:T(8,128)(2,1)S(1)}, bf16[768,768]{1,0:T(8,128)(2,1)S(1)}, u32[]{:S(2)}, u32[]{:S(2)}) collective-permute-start(bf16[768,768]{1,0:T(8,128)(2,1)S(1)} %copy-done.1), channel_id=1, source_target_pairs={{0,1},{1,0},{2,3},{3,2},{4,5},{5,4},{6,7},{7,6},{8,9},{9,8},{10,11... | collective-permute-start | bytes 3538952 | tf_op jit(solution)/shard_map/ppermute | solution.py:602
  53.9 2.0 copy-start.8
  53.9 2.0 copy-start.5
  54.4 1.0 copy-start
  55.5 3.1 %collective-permute-start.3 = (bf16[768,768]{1,0:T(8,128)(2,1)S(1)}, bf16[768,768]{1,0:T(8,128)(2,1)S(1)}, u32[]{:S(2)}, u32[]{:S(2)}) collective-permute-start(bf16[768,768]{1,0:T(8,128)(2,1)S(1)} %maximum_select_fusion.up_c), channel_id=1, source_target_pairs={{0,1},{1,0},{2,3},{3,2},{4,5},{5,4},{6,7},{7,6},{8,9},{9,8},{10,11... | collective-permute-start | bytes 3538952 | tf_op jit(solution)/shard_map/ppermute | solution.py:602
  57.3 1.3 copy-start.2
  58.6 1.0 copy-start.3
  108.7 11.3 %collective-permute-start.4 = (bf16[16,96,768]{2,1,0:T(8,128)(2,1)}, bf16[16,96,768]{2,1,0:T(8,128)(2,1)}, u32[]{:S(2)}, u32[]{:S(2)}) collective-permute-start(bf16[16,96,768]{2,1,0:T(8,128)(2,1)} %bitcast.76), channel_id=1, source_target_pairs={{0,1},{1,0},{2,3},{3,2},{4,5},{5,4},{6,7},{7,6},{8,9},{9,8},{10,11... | collective-permute-start | bytes 7077896 | tf_op jit(solution)/shard_map/ppermute | solution.py:602
  124.5 22.0 %collective-permute-start.6 = (bf16[8,96,384]{2,1,0:T(8,128)(2,1)}, bf16[8,96,384]{2,1,0:T(8,128)(2,1)}, u32[]{:S(2)}, u32[]{:S(2)}) collective-permute-start(bf16[8,96,384]{2,1,0:T(8,128)(2,1)} %bitcast.81), channel_id=1, source_target_pairs={{0,4},{4,0},{8,12},{12,8},{16,20},{20,16},{24,28},{28,24},{1,5},{5... | collective-permute-start | bytes 1769480 | tf_op jit(solution)/shard_map/ppermute | solution.py:602
  124.6 21.8 %collective-permute-start.5 = (bf16[8,96,384]{2,1,0:T(8,128)(2,1)}, bf16[8,96,384]{2,1,0:T(8,128)(2,1)}, u32[]{:S(2)}, u32[]{:S(2)}) collective-permute-start(bf16[8,96,384]{2,1,0:T(8,128)(2,1)} %bitcast.80), channel_id=1, source_target_pairs={{0,2},{1,3},{2,0},{3,1},{4,6},{5,7},{6,4},{7,5},{8,10},{9,11},{10,... | collective-permute-start | bytes 1769480 | tf_op jit(solution)/shard_map/ppermute | solution.py:602
  163.3 11.9 %collective-permute-start.9 = (bf16[16,96,768]{2,1,0:T(8,128)(2,1)}, bf16[16,96,768]{2,1,0:T(8,128)(2,1)}, u32[]{:S(2)}, u32[]{:S(2)}) collective-permute-start(bf16[16,96,768]{2,1,0:T(8,128)(2,1)} %bitcast.77), channel_id=1, source_target_pairs={{0,1},{1,0},{2,3},{3,2},{4,5},{5,4},{6,7},{7,6},{8,9},{9,8},{10,11... | collective-permute-start | bytes 7077896 | tf_op jit(solution)/shard_map/ppermute | solution.py:602
  179.6 21.0 %collective-permute-start.13 = (bf16[8,96,384]{2,1,0:T(8,128)(2,1)}, bf16[8,96,384]{2,1,0:T(8,128)(2,1)}, u32[]{:S(2)}, u32[]{:S(2)}) collective-permute-start(bf16[8,96,384]{2,1,0:T(8,128)(2,1)} %bitcast.79), channel_id=1, source_target_pairs={{0,4},{4,0},{8,12},{12,8},{16,20},{20,16},{24,28},{28,24},{1,5},{5... | collective-permute-start | bytes 1769480 | tf_op jit(solution)/shard_map/ppermute | solution.py:602
  181.0 20.7 %collective-permute-start.12 = (bf16[8,96,384]{2,1,0:T(8,128)(2,1)}, bf16[8,96,384]{2,1,0:T(8,128)(2,1)}, u32[]{:S(2)}, u32[]{:S(2)}) collective-permute-start(bf16[8,96,384]{2,1,0:T(8,128)(2,1)} %bitcast.78), channel_id=1, source_target_pairs={{0,2},{1,3},{2,0},{3,1},{4,6},{5,7},{6,4},{7,5},{8,10},{9,11},{10,... | collective-permute-start | bytes 1769480 | tf_op jit(solution)/shard_map/ppermute | solution.py:602
  186.2 19.3 %collective-permute-start.7 = (bf16[4,96,384]{2,1,0:T(8,128)(2,1)}, bf16[4,96,384]{2,1,0:T(8,128)(2,1)}, u32[]{:S(2)}, u32[]{:S(2)}) collective-permute-start(bf16[4,96,384]{2,1,0:T(8,128)(2,1)} %get-tuple-element.156), channel_id=1, source_target_pairs={{0,4},{4,0},{8,12},{12,8},{16,20},{20,16},{24,28},{28,24},{1,5},{5... | collective-permute-start | bytes 884744 | tf_op jit(solution)/shard_map/ppermute | solution.py:602
  186.3 21.1 %collective-permute-start.8 = (bf16[4,96,384]{2,1,0:T(8,128)(2,1)}, bf16[4,96,384]{2,1,0:T(8,128)(2,1)}, u32[]{:S(2)}, u32[]{:S(2)}) collective-permute-start(bf16[4,96,384]{2,1,0:T(8,128)(2,1)} %get-tuple-element.157), channel_id=1, source_target_pairs={{0,2},{1,3},{2,0},{3,1},{4,6},{5,7},{6,4},{7,5},{8,10},{9,11},{10,... | collective-permute-start | bytes 884744 | tf_op jit(solution)/shard_map/ppermute | solution.py:602
  204.7 8.4 %collective-permute-start.14 = (bf16[4,96,384]{2,1,0:T(8,128)(2,1)}, bf16[4,96,384]{2,1,0:T(8,128)(2,1)}, u32[]{:S(2)}, u32[]{:S(2)}) collective-permute-start(bf16[4,96,384]{2,1,0:T(8,128)(2,1)} %get-tuple-element.181), channel_id=1, source_target_pairs={{0,4},{4,0},{8,12},{12,8},{16,20},{20,16},{24,28},{28,24},{1,5},{5... | collective-permute-start | bytes 884744 | tf_op jit(solution)/shard_map/ppermute | solution.py:602
  205.4 9.0 %collective-permute-start.15 = (bf16[4,96,384]{2,1,0:T(8,128)(2,1)}, bf16[4,96,384]{2,1,0:T(8,128)(2,1)}, u32[]{:S(2)}, u32[]{:S(2)}) collective-permute-start(bf16[4,96,384]{2,1,0:T(8,128)(2,1)} %get-tuple-element.183), channel_id=1, source_target_pairs={{0,2},{1,3},{2,0},{3,1},{4,6},{5,7},{6,4},{7,5},{8,10},{9,11},{10,... | collective-permute-start | bytes 884744 | tf_op jit(solution)/shard_map/ppermute | solution.py:602
  209.6 12.2 %collective-permute-start.10 = (bf16[2,96,768]{2,1,0:T(8,128)(2,1)}, bf16[2,96,768]{2,1,0:T(8,128)(2,1)}, u32[]{:S(2)}, u32[]{:S(2)}) collective-permute-start(bf16[2,96,768]{2,1,0:T(8,128)(2,1)} %get-tuple-element.173), channel_id=1, source_target_pairs={{0,8},{4,12},{8,0},{12,4},{16,24},{20,28},{24,16},{28,20},{1,9},{5... | collective-permute-start | bytes 884744 | tf_op jit(solution)/shard_map/ppermute | solution.py:602
  216.6 11.3 %collective-permute-start.16 = (bf16[2,96,768]{2,1,0:T(8,128)(2,1)}, bf16[2,96,768]{2,1,0:T(8,128)(2,1)}, u32[]{:S(2)}, u32[]{:S(2)}) collective-permute-start(bf16[2,96,768]{2,1,0:T(8,128)(2,1)} %get-tuple-element.185), channel_id=1, source_target_pairs={{0,8},{4,12},{8,0},{12,4},{16,24},{20,28},{24,16},{28,20},{1,9},{5... | collective-permute-start | bytes 884744 | tf_op jit(solution)/shard_map/ppermute | solution.py:602
  223.6 8.6 %collective-permute-start.11 = (bf16[1,96,768]{2,1,0:T(8,128)(2,1)}, bf16[1,96,768]{2,1,0:T(8,128)(2,1)}, u32[]{:S(2)}, u32[]{:S(2)}) collective-permute-start(bf16[1,96,768]{2,1,0:T(8,128)(2,1)} %get-tuple-element.175), channel_id=1, source_target_pairs={{0,16},{4,20},{8,24},{12,28},{16,0},{20,4},{24,8},{28,12},{1,17},{... | collective-permute-start | bytes 442376 | tf_op jit(solution)/shard_map/ppermute | solution.py:602
  229.8 8.6 %collective-permute-start.17 = (bf16[1,96,768]{2,1,0:T(8,128)(2,1)}, bf16[1,96,768]{2,1,0:T(8,128)(2,1)}, u32[]{:S(2)}, u32[]{:S(2)}) collective-permute-start(bf16[1,96,768]{2,1,0:T(8,128)(2,1)} %get-tuple-element.187), channel_id=1, source_target_pairs={{0,16},{4,20},{8,24},{12,28},{16,0},{20,4},{24,8},{28,12},{1,17},{... | collective-permute-start | bytes 442376 | tf_op jit(solution)/shard_map/ppermute | solution.py:602
  240.5 4.8 %collective-permute-start.18 = (f32[32,768]{1,0:T(8,128)}, f32[32,768]{1,0:T(8,128)S(1)}, u32[]{:S(2)}, u32[]{:S(2)}) collective-permute-start(f32[32,768]{1,0:T(8,128)} %get-tuple-element.193), channel_id=1, source_target_pairs={{0,4},{4,0},{8,12},{12,8},{16,20},{20,16},{24,28},{28,24},{1,5},{5... | collective-permute-start | bytes 294920 | tf_op jit(solution)/shard_map/ppermute | solution.py:602
  246.2 4.7 %collective-permute-start.19 = (f32[32,768]{1,0:T(8,128)S(1)}, f32[32,768]{1,0:T(8,128)S(1)}, u32[]{:S(2)}, u32[]{:S(2)}) collective-permute-start(f32[32,768]{1,0:T(8,128)S(1)} %add.22), channel_id=1, source_target_pairs={{0,8},{4,12},{8,0},{12,4},{16,24},{20,28},{24,16},{28,20},{1,9},{5... | collective-permute-start | bytes 294920 | tf_op jit(solution)/shard_map/ppermute | solution.py:602
  250.9 6.3 %collective-permute-start.20 = (f32[32,768]{1,0:T(8,128)S(1)}, f32[32,768]{1,0:T(8,128)S(1)}, u32[]{:S(2)}, u32[]{:S(2)}) collective-permute-start(f32[32,768]{1,0:T(8,128)S(1)} %add.23), channel_id=1, source_target_pairs={{0,16},{4,20},{8,24},{12,28},{16,0},{20,4},{24,8},{28,12},{1,17},{... | collective-permute-start | bytes 294920 | tf_op jit(solution)/shard_map/ppermute | solution.py:602
  257.3 1.4 collective-permute-start.21
  258.7 0.6 copy-start.6
  259.3 4.9 %collective-permute-start.22 = (f32[32,768]{1,0:T(8,128)S(1)}, f32[32,768]{1,0:T(8,128)S(1)}, u32[]{:S(2)}, u32[]{:S(2)}) collective-permute-start(f32[32,768]{1,0:T(8,128)S(1)} %add.25.ours_ref), channel_id=1, source_target_pairs={{0,2},{1,3},{2,0},{3,1},{4,6},{5,7},{6,4},{7,5},{8,10},{9,11},{10,... | collective-permute-start | bytes 294920 | tf_op jit(solution)/shard_map/ppermute | solution.py:602
  264.2 0.6 copy-start.7
Sparse Core Ops, SparseCore 0:
  25.7 38.9 all-gather.2
Sparse Core Ops, SparseCore 1:
  109.3 112.5 reduce-scatter.1
